TPU v7x, 128 devices: a whole 4x4x4 slice. The times are simulated.
128 devices in a mesh: rows: 8 (over z, core), cols: 16 (over x, y).
Axes of the slice: x: 4, y: 4, z: 4, core: 2. Of those that a mesh axis runs over, the one named last changes fastest.
Arguments:
- pixels: bfloat16 [3, 1024, 4096], P(None, 'rows', 'cols'), may hold values from -6 to 6
- patch_weight: bfloat16 [48, 256], replicated, may hold values from -0.875 to 0.875
- patch_bias: float32 [256], replicated, may hold values from -4 to 4
- conv_kernel: float32 [49, 256], replicated, may hold values from -0.875 to 0.875
- norm_gain: float32 [256], replicated, may hold values from 0.1 to 1.9
- kv_weight: bfloat16 [256, 2048], replicated, may hold values from -0.375 to 0.375
- latents: bfloat16 [256, 1024], replicated, may hold values from -80 to 80, as said below
- d_attended: bfloat16 [256, 1024], replicated, may hold values from -6 to 6
Outputs:
- attended: float32 [256, 1024], replicated
- grad_latents: float32 [256, 1024], replicated
- grad_kv_weight: float32 [256, 2048], replicated
- grad_norm_gain: float32 [256], replicated
- grad_conv_kernel: float32 [49, 256], replicated
- grad_patch_weight: float32 [48, 256], replicated
- grad_patch_bias: float32 [256], replicated
Inputs may be any that keep to these rules, and one draw needn't show every extreme that they name: `latents`: each latent row has its own scale.
All inputs are finite; a program needn't handle non-finite values.
Results may differ from a plain program's by a relative error of at most 0.035.
The roundings to bfloat16 on the way count: a program that leaves them out, or rounds other values in their place, can miss the bound.
Values may be sent and summed in bfloat16 or wider, within the bound.
No kernel may reach another device: no remote copies, remote signals or barrier semaphores. Data moves between devices by JAX's collectives and lax.ppermute only.
A program may use at most 576 MiB of HBM per device.

v0:
```python
import jax
import jax.numpy as jnp
from jax import lax
from jax.sharding import PartitionSpec as P

PATCH = 4
KSIZE = 7
HEADS = 8


norm_eps = 1e-05


def padded_2(x, sides, width):
    for axis, dim in sides:
        devices, length = (lax.axis_size(axis), x.shape[dim])
        up = [(i, (i + 1) % devices) for i in range(devices - 1)]
        down = [(j, i) for i, j in up]
        last = lax.slice_in_dim(x, length - width, length, axis=dim)
        leading = lax.slice_in_dim(x, 0, width, axis=dim)
        before = lax.ppermute(last, axis, up)
        after = lax.ppermute(leading, axis, down)
        x = jnp.concatenate([before, x, after], axis=dim)
    return x


def patch_rows(pixels):
    in_channels, height, image_width = pixels.shape
    blocks = pixels.reshape(in_channels, height // PATCH, PATCH, image_width // PATCH, PATCH)
    blocks = blocks.transpose(1, 3, 0, 2, 4)
    return blocks.reshape(height // PATCH * (image_width // PATCH), in_channels * PATCH * PATCH)


def depthwise(padded, kernel, tile_rows, tile_cols):
    result = jnp.zeros((tile_rows, tile_cols, kernel.shape[1]), jnp.float32)
    for offset_row in range(KSIZE):
        for offset_col in range(KSIZE):
            window = padded[
                offset_row : offset_row + tile_rows, offset_col : offset_col + tile_cols
            ].astype(jnp.float32)
            result = result + window * kernel[offset_row * KSIZE + offset_col]
    return result


def transposed(padded, kernel, tile_rows, tile_cols):
    result = jnp.zeros((tile_rows, tile_cols, kernel.shape[1]), jnp.float32)
    last = KSIZE - 1
    for offset_row in range(KSIZE):
        for offset_col in range(KSIZE):
            start_row = last - offset_row
            start_col = last - offset_col
            window = padded[
                start_row : start_row + tile_rows, start_col : start_col + tile_cols
            ].astype(jnp.float32)
            result = result + window * kernel[offset_row * KSIZE + offset_col]
    return result


def kernel_grad(padded, upstream, tile_rows, tile_cols):
    upstream_f = upstream.astype(jnp.float32)
    kernel_terms = []
    for offset_row in range(KSIZE):
        for offset_col in range(KSIZE):
            window = padded[
                offset_row : offset_row + tile_rows, offset_col : offset_col + tile_cols
            ].astype(jnp.float32)
            kernel_terms.append(jnp.sum(window * upstream_f, axis=(0, 1)))
    return jnp.stack(kernel_terms)


def normalize(mixed):
    centre = mixed - jnp.mean(mixed, axis=-1, keepdims=True)
    variance = jnp.mean(centre * centre, axis=-1, keepdims=True)
    inverse = lax.rsqrt(variance + norm_eps)
    return (centre * inverse, inverse)


def split_heads(matrix, head_count):
    return matrix.reshape(matrix.shape[0], head_count, -1).transpose(1, 0, 2)


def merge_heads(stacked):
    return stacked.transpose(1, 0, 2).reshape(stacked.shape[1], -1)


def head_state(pieces):
    queries, key_rows, values = pieces
    score_scale = queries.shape[-1] ** (-0.5)
    scores = (
        jnp.einsum("le,te->lt", queries, key_rows, preferred_element_type=jnp.float32) * score_scale
    )
    top_score = jnp.max(scores, axis=1)
    raised = jnp.exp(scores - top_score[:, None])
    weighted = jnp.dot(raised.astype(jnp.bfloat16), values, preferred_element_type=jnp.float32)
    return (top_score, jnp.sum(raised, axis=1), weighted)


def head_grads(pieces):
    queries, key_rows, values, top_score, sum_exp, row_dots, upstream = pieces
    score_scale = queries.shape[-1] ** (-0.5)
    scores = (
        jnp.einsum("le,te->lt", queries, key_rows, preferred_element_type=jnp.float32) * score_scale
    )
    probs = jnp.exp(scores - top_score[:, None]) / sum_exp[:, None]
    d_probs = jnp.einsum("le,te->lt", upstream, values, preferred_element_type=jnp.float32)
    d_scores = (probs * (d_probs - row_dots[:, None]) * score_scale).astype(jnp.bfloat16)
    q_grad = jnp.einsum("lt,te->le", d_scores, key_rows, preferred_element_type=jnp.float32)
    k_grad = jnp.einsum("lt,le->te", d_scores, queries, preferred_element_type=jnp.float32).astype(
        jnp.bfloat16
    )
    v_grad = jnp.einsum(
        "lt,le->te", probs.astype(jnp.bfloat16), upstream, preferred_element_type=jnp.float32
    )
    return (q_grad, k_grad, v_grad.astype(jnp.bfloat16))


def rescaled(local_top, local_sum, local_weighted, top_score):
    factor = jnp.exp(local_top - top_score)
    latent_count, head_count = factor.shape
    weighted = local_weighted.reshape(latent_count, head_count, -1) * factor[:, :, None]
    return (local_sum * factor, weighted.reshape(latent_count, -1))


def normalized(weighted, sum_exp):
    latent_count, head_count = sum_exp.shape
    return (weighted.reshape(latent_count, head_count, -1) / sum_exp[:, :, None]).reshape(
        latent_count, -1
    )


def per_device(
    pixels, patch_weight, patch_bias, conv_kernel, norm_gain, kv_weight, latents, d_attended
):
    tile_rows = pixels.shape[1] // PATCH
    tile_cols = pixels.shape[2] // PATCH
    channels = patch_weight.shape[1]
    model_dim = latents.shape[1]
    latent_count = latents.shape[0]
    patches = patch_rows(pixels)
    embedded = (
        jnp.dot(patches, patch_weight, preferred_element_type=jnp.float32) + patch_bias
    ).astype(jnp.bfloat16)
    embedded = embedded.reshape(tile_rows, tile_cols, channels)
    padded = padded_2(embedded, (("rows", 0), ("cols", 1)), KSIZE // 2)
    mixed = embedded.astype(jnp.float32) + depthwise(padded, conv_kernel, tile_rows, tile_cols)
    centred, inverse = normalize(mixed)
    normed = (centred * norm_gain).astype(jnp.bfloat16).reshape(tile_rows * tile_cols, channels)
    projected = jnp.dot(normed, kv_weight, preferred_element_type=jnp.float32).astype(jnp.bfloat16)
    query_heads = split_heads(latents, HEADS)
    key_heads = split_heads(projected[:, :model_dim], HEADS)
    value_heads = split_heads(projected[:, model_dim:], HEADS)
    tops, sums, weighteds = lax.map(head_state, (query_heads, key_heads, value_heads))
    local_top = tops.T
    local_sum = sums.T
    local_weighted = merge_heads(weighteds)
    top_score = lax.pmax(local_top, ("rows", "cols"))
    part_sum, part_weighted = rescaled(local_top, local_sum, local_weighted, top_score)
    sum_exp, weighted = lax.psum((part_sum, part_weighted), ("rows", "cols"))
    attended = normalized(weighted, sum_exp)
    row_dots = jnp.sum(
        d_attended.astype(jnp.float32).reshape(latent_count, HEADS, -1)
        * attended.reshape(latent_count, HEADS, -1),
        axis=2,
    )
    q_grads, k_grads, v_grads = lax.map(
        head_grads,
        (
            query_heads,
            key_heads,
            value_heads,
            top_score.T,
            sum_exp.T,
            row_dots.T,
            split_heads(d_attended, HEADS),
        ),
    )
    local_latents = merge_heads(q_grads)
    d_projected = jnp.concatenate([merge_heads(k_grads), merge_heads(v_grads)], axis=1)
    local_kv = jnp.einsum("tc,tk->ck", normed, d_projected, preferred_element_type=jnp.float32)
    d_normed = jnp.einsum("tk,ck->tc", d_projected, kv_weight, preferred_element_type=jnp.float32)
    d_normed = d_normed.reshape(tile_rows, tile_cols, channels)
    local_gain = jnp.sum(d_normed * centred, axis=(0, 1))
    scaled = d_normed * norm_gain
    d_mixed = inverse * (
        scaled
        - jnp.mean(scaled, axis=-1, keepdims=True)
        - centred * jnp.mean(scaled * centred, axis=-1, keepdims=True)
    )
    d_mixed = d_mixed.astype(jnp.bfloat16)
    local_kernel = kernel_grad(padded, d_mixed, tile_rows, tile_cols)
    d_padded = padded_2(d_mixed, (("rows", 0), ("cols", 1)), KSIZE // 2)
    d_embedded = (
        d_mixed.astype(jnp.float32) + transposed(d_padded, conv_kernel, tile_rows, tile_cols)
    ).astype(jnp.bfloat16)
    d_embedded = d_embedded.reshape(tile_rows * tile_cols, channels)
    local_patch = jnp.einsum("tp,tc->pc", patches, d_embedded, preferred_element_type=jnp.float32)
    local_bias = jnp.sum(d_embedded.astype(jnp.float32), axis=0)
    grad_latents, grad_kv, grad_gain, grad_kernel, grad_patch, grad_bias = lax.psum(
        (local_latents, local_kv, local_gain, local_kernel, local_patch, local_bias),
        ("rows", "cols"),
    )
    return (attended, grad_latents, grad_kv, grad_gain, grad_kernel, grad_patch, grad_bias)


def solution(mesh):
    return jax.shard_map(
        per_device,
        mesh=mesh,
        in_specs=(P(None, "rows", "cols"), P(), P(), P(), P(), P(), P(), P()),
        out_specs=(P(), P(), P(), P(), P(), P(), P()),
        check_vma=False,
    )
```

profile of v0, /device:TPU:1, one launch (start us, length us, event | category | flops | bytes accessed | tf_op | source)
XLA Modules:
  0.0 872.1 jit_solution(149863310632694244)
XLA Ops:
  7.2 15.3 %reshape.154 = bf16[3,32,4,64,4]{4,3,2,1,0:T(8,128)(2,1)} reshape(bf16[3,128,256]{2,1,0:T(8,128)(2,1)} %param.12) | data formatting | bytes 393216 | tf_op jit(solution)/shard_map/reshape | solution.py:29
  22.6 6.0 copy.22
  29.5 3.3 collective-permute-start.1
  32.8 3.5 collective-permute-start
  38.1 3.2 collective-permute-start.2
  48.9 19.2 %fusion.180 = (f32[32,64]{1,0:T(8,128)S(1)}, f32[32,64,256]{2,1,0:T(8,128)S(1)}) fusion(f32[256]{0:T(256)} %bitcast.382, bf16[38,67,256]{2,1,0:T(8,128)(2,1)S(1)} %get-tuple-element.249, f32[256]{0:T(256)} %bitcast.384, f32[256]{0:T(256)S(1)} %bitcast.290, f32[256]{0:T(256)S(1)} %bitcast.292, bf16[3,64,256]{2,1,0:T(8,128)(2,1)S(1)} %copy-done.16, ...), kind=kLoop, calls=%fused_computation.344 | loop fusion | flops 80738304 | bytes 47440896 | tf_op jit(solution)/shard_map/reduce_sum | solution.py:72
  69.6 2.4 convolution_convert_fusion.2
  72.0 3.6 fusion.182
  75.6 6.4 copy.24
  82.0 6.4 copy.23
  88.6 39.8 %while.28 = (s32[]{:T(128)}, f32[8,256]{1,0:T(8,128)S(1)}, f32[8,256]{1,0:T(8,128)}, f32[8,256,128]{2,1,0:T(8,128)S(1)}, bf16[8,256,128]{2,1,0:T(8,128)(2,1)}, /...) while((s32[]{:T(128)}, f32[8,256]{1,0:T(8,128)S(1)}, ...), condition=%wide.region_5.6_spmd, body=%wide.region_2.5_spmd.sunk | while | flops 271580672 | bytes 7546989 | solution.py:152
  128.9 69.0 %pmax.7 = f32[256,8]{0,1:T(8,128)S(1)} all-reduce(f32[256,8]{0,1:T(8,128)} %bitcast.284), channel_id=1, replica_groups=mesh['rows'=8,'cols'=16] {'rows','cols'}, use_global_device_ids=true, to_apply=%region_6.7 | all-reduce | flops 2048 | bytes 16384 | tf_op jit(solution)/shard_map/pmax | solution.py:156
  202.7 64.4 %psum.57 = f32[256,8]{0,1:T(8,128)S(1)} all-reduce(f32[256,8]{0,1:T(8,128)S(1)} %copy-done.32), channel_id=1, replica_groups=mesh['rows'=8,'cols'=16] {'rows','cols'}, use_global_device_ids=true, to_apply=%region_8.9 | all-reduce | flops 2048 | bytes 16384 | tf_op jit(solution)/shard_map/psum | solution.py:158
  267.1 78.4 %all-reduce.6.cloned.1.call-done = f32[256,1024]{1,0:T(8,128)} async-done(((f32[256,1024]{1,0:T(8,128)}), f32[256,1024]{1,0:T(8,128)}) %all-reduce.6.cloned.1.call-update) | async-done | bytes 1048592 | tf_op jit(solution)/shard_map/psum | solution.py:158
  350.0 126.1 %while.29 = (s32[]{:T(128)}, f32[8,256,128]{2,1,0:T(8,128)}, bf16[8,2048,128]{1,2,0:T(8,128)(2,1)}, bf16[8,2048,128]{1,2,0:T(8,128)(2,1)}, bf16[8,256,128]{2,1,0...) while((s32[]{:T(128)}, f32[8,256,128]{2,1,0:T(8,128)}, ...), condition=%wide.region_11.12_spmd, body=%wide.region_10.11_spmd.sunk | while | flops 675807232 | bytes 16658581 | solution.py:165
  352.3 2.1 fusion.238
  363.6 2.1 constant_dynamic-update-slice_fusion.3
  379.4 2.2 constant_dynamic-update-slice_fusion.3
  476.1 7.3 multiply_reduce_fusion.1
  484.1 4.5 multiply_reduce_fusion
  488.6 6.6 fusion.137
  495.3 6.5 fusion.141
  501.7 2.9 collective-permute-start.4
  504.7 2.4 collective-permute-start.5
  507.1 5.6 fusion.140
  512.8 8.2 fusion.43
  523.1 4.6 collective-permute-start.7
  529.4 9.1 %stack.199 = f32[49,256]{1,0:T(8,128)} concatenate(f32[1,256]{1,0:T(1,128)} %bitcast.434, f32[1,256]{1,0:T(1,128)} %bitcast.433, f32[1,256]{1,0:T(1,128)} %bitcast.432, f32[1,256]{1,0:T(1,128)} %bitcast.428, f32[1,256]{1,0:T(1,128)} %bitcast.424, f32[1,256]{1,0:T(1,128)} %bitcast.423, f32[1,256]{1,0:T(1,128)} %bitcast.405, f32[1,256]{1,0:T(1,128)S(1)} %bitcast.387, ...), dimensions={0} | concatenate | bytes 100352 | tf_op jit(solution)/shard_map/stack | solution.py:68
  541.0 21.4 %convert_reduce_fusion = (f32[256]{0:T(256)}, bf16[32,64,256]{2,1,0:T(8,128)(2,1)S(1)}) fusion(f32[256]{0:T(256)} %bitcast.383, bf16[38,67,256]{2,1,0:T(8,128)(2,1)S(1)} %get-tuple-element.245, f32[256]{0:T(256)} %bitcast.385, f32[256]{0:T(256)S(1)} %bitcast.291, f32[256]{0:T(256)S(1)} %bitcast.293, bf16[32,64,256]{2,1,0:T(8,128)(2,1)S(1)} %get-tuple-element.233, ...), kind=kLoop, calls=%fused_computation.283 | loop fusion | flops 81788672 | bytes 46385152 | tf_op jit(solution)/shard_map/reduce_sum | solution.py:197
  568.5 135.2 %all-reduce.8.cloned.1.call-done = (f32[256]{0:T(256)}, f32[49,256]{1,0:T(8,128)}, f32[48,256]{1,0:T(8,128)}, f32[256]{0:T(256)}) async-done(((f32[256]{0:T(256)}, f32[49,256]{1,0:T(8,128)}, f32[48,256]{1,0:T(8,128)}, f32[256]{0:T(256)}), (f32[256]{0:T(256)}, f32[49,256]{1,0:T(8,128)}, f32[48,256]{1,0:T(8,128)}, f32[256]{0:T(256)})) %all-reduce.8.cloned.1.call-update) | async-done | bytes 101392 | tf_op jit(solution)/shard_map/psum | solution.py:198
  703.7 155.7 %all-reduce.10.cloned.1.call-done = (f32[256,1024]{1,0:T(8,128)}, f32[256,2048]{1,0:T(8,128)}) async-done(((f32[256,1024]{1,0:T(8,128)}, f32[256,2048]{1,0:T(8,128)}), (f32[256,1024]{1,0:T(8,128)}, f32[256,2048]{1,0:T(8,128)})) %all-reduce.10.cloned.1.call-update) | async-done | bytes 3145744 | tf_op jit(solution)/shard_map/psum | solution.py:198
  859.4 2.5 copy.87
  (431 shorter events, 195.8 us)
Async XLA Ops:
  7.2 62.4 %copy-start = (bf16[256,2048]{1,0:T(8,128)(2,1)S(1)}, bf16[256,2048]{1,0:T(8,128)(2,1)}, u32[]{:S(2)}) copy-start(bf16[256,2048]{1,0:T(8,128)(2,1)} %param.17) | copy-start | bytes 3145732
  7.2 338.3 %all-reduce.6.cloned.1.call-start = ((), (), s32[]{:S(2)}) async-start(), calls=%async_computation | async-start | bytes 2097152 | tf_op jit(solution)/shard_map/psum | solution.py:158
  22.6 6.4 copy-start.33
  22.6 6.4 copy-start.121
  28.6 7.8 copy-start.30
  28.6 14.8 %copy-start.25 = (bf16[256,1024]{1,0:T(8,128)(2,1)S(1)}, bf16[256,1024]{1,0:T(8,128)(2,1)}, u32[]{:S(2)}) copy-start(bf16[256,1024]{1,0:T(8,128)(2,1)} %param.18) | copy-start | bytes 1572868
  29.0 14.4 %copy-start.13 = (bf16[2048,48]{0,1:T(8,128)(2,1)}, bf16[2048,48]{0,1:T(8,128)(2,1)S(1)}, u32[]{:S(2)}) copy-start(bf16[2048,48]{0,1:T(8,128)(2,1)S(1)} %reshape.155) | copy-start | bytes 589828
  29.5 19.1 %copy-start.5 = (bf16[2048,256]{1,0:T(8,128)(2,1)}, bf16[2048,256]{1,0:T(8,128)(2,1)S(1)}, u32[]{:S(2)}) copy-start(bf16[2048,256]{1,0:T(8,128)(2,1)S(1)} %fusion.44) | copy-start | bytes 3145732
  29.5 8.2 collective-permute-start.1
  32.8 5.2 collective-permute-start
  38.1 6.9 collective-permute-start.2
  41.3 5.6 collective-permute-start.3
  48.5 19.6 %copy-start.1 = (bf16[38,67,256]{2,1,0:T(8,128)(2,1)}, bf16[38,67,256]{2,1,0:T(8,128)(2,1)S(1)}, u32[]{:S(2)}) copy-start(bf16[38,67,256]{2,1,0:T(8,128)(2,1)S(1)} %get-tuple-element.249) | copy-start | bytes 3910660
  200.6 503.2 %all-reduce.8.cloned.1.call-start = ((), (), s32[]{:S(2)}) async-start(), calls=%async_computation.1 | async-start | bytes 217088 | tf_op jit(solution)/shard_map/psum | solution.py:198
  476.1 8.0 copy-start.109
  488.6 6.6 copy-start.2
  495.2 11.9 %copy-start.6 = (bf16[2048,256]{1,0:T(8,128)(2,1)S(1)}, bf16[2048,256]{1,0:T(8,128)(2,1)}, u32[]{:S(2)}) copy-start(bf16[2048,256]{1,0:T(8,128)(2,1)} %copy-done.5) | copy-start | bytes 3145732
  495.2 11.9 %copy-start.17 = (bf16[3,64,256]{2,1,0:T(8,128)(2,1)S(1)}, bf16[3,64,256]{2,1,0:T(8,128)(2,1)}, u32[]{:S(2)}) copy-start(bf16[3,64,256]{2,1,0:T(8,128)(2,1)} %copy-done.15) | copy-start | bytes 294916
  495.2 11.9 %copy-start.20 = (bf16[3,64,256]{2,1,0:T(8,128)(2,1)S(1)}, bf16[3,64,256]{2,1,0:T(8,128)(2,1)}, u32[]{:S(2)}) copy-start(bf16[3,64,256]{2,1,0:T(8,128)(2,1)} %copy-done.18) | copy-start | bytes 294916
  495.2 17.5 %copy-start.123 = (bf16[8,2048,128]{1,2,0:T(8,128)(2,1)S(1)}, bf16[8,2048,128]{1,2,0:T(8,128)(2,1)}, u32[]{:S(2)}) copy-start(bf16[8,2048,128]{1,2,0:T(8,128)(2,1)} %get-tuple-element.109) | copy-start | bytes 12582916
  501.7 19.3 %collective-permute-start.4 = (bf16[3,64,256]{2,1,0:T(8,128)(2,1)S(1)}, bf16[3,64,256]{2,1,0:T(8,128)(2,1)S(1)}, u32[]{:S(2)}, u32[]{:S(2)}) collective-permute-start(bf16[3,64,256]{2,1,0:T(8,128)(2,1)S(1)} %get-tuple-element.252), channel_id=1, source_target_pairs={{0,16},{16,32},{32,48},{48,64},{64,80},{80,96},{96,112},{1,17},{17... | collective-permute-start | bytes 294920 | tf_op jit(solution)/shard_map/ppermute | solution.py:21
  504.6 8.1 copy-start.9
  504.6 8.1 copy-start.122
  504.7 16.4 %collective-permute-start.5 = (bf16[3,64,256]{2,1,0:T(8,128)(2,1)S(1)}, bf16[3,64,256]{2,1,0:T(8,128)(2,1)S(1)}, u32[]{:S(2)}, u32[]{:S(2)}) collective-permute-start(bf16[3,64,256]{2,1,0:T(8,128)(2,1)S(1)} %get-tuple-element.253), channel_id=1, source_target_pairs={{16,0},{32,16},{48,32},{64,48},{80,64},{96,80},{112,96},{17,1},{33... | collective-permute-start | bytes 294920 | tf_op jit(solution)/shard_map/ppermute | solution.py:22
  521.0 8.3 copy-start.21
  521.0 8.3 copy-start.23
  521.8 17.1 %collective-permute-start.6 = (bf16[38,3,256]{2,1,0:T(4,128)(2,1)}, bf16[38,3,256]{2,1,0:T(4,128)(2,1)}, u32[]{:S(2)}, u32[]{:S(2)}) collective-permute-start(bf16[38,3,256]{2,1,0:T(4,128)(2,1)} %get-tuple-element.246), channel_id=1, source_target_pairs={{1,0},{2,1},{3,2},{4,3},{5,4},{6,5},{7,6},{8,7},{9,8},{10,9},{11,1... | collective-permute-start | bytes 175112 | tf_op jit(solution)/shard_map/ppermute | solution.py:22
  523.0 6.2 copy-start.110
  523.1 6.2 copy-start.111
  523.1 15.7 %collective-permute-start.7 = (bf16[38,3,256]{2,1,0:T(4,128)(2,1)}, bf16[38,3,256]{2,1,0:T(4,128)(2,1)}, u32[]{:S(2)}, u32[]{:S(2)}) collective-permute-start(bf16[38,3,256]{2,1,0:T(4,128)(2,1)} %get-tuple-element.247), channel_id=1, source_target_pairs={{0,1},{1,2},{2,3},{3,4},{4,5},{5,6},{6,7},{7,8},{8,9},{9,10},{10,1... | collective-permute-start | bytes 175112 | tf_op jit(solution)/shard_map/ppermute | solution.py:21
  541.0 21.4 %copy-start.14 = (bf16[2048,48]{0,1:T(8,128)(2,1)S(1)}, bf16[2048,48]{0,1:T(8,128)(2,1)}, u32[]{:S(2)}) copy-start(bf16[2048,48]{0,1:T(8,128)(2,1)} %copy-done.13) | copy-start | bytes 589828
  563.3 296.1 %all-reduce.10.cloned.1.call-start = ((), (), s32[]{:S(2)}) async-start(), calls=%async_computation.2 | async-start | bytes 6291456 | tf_op jit(solution)/shard_map/psum | solution.py:198
  (103 other events, 326.5 us)
Sparse Core Ops, SparseCore 0:
  200.7 144.7 all-reduce.5
  563.4 140.2 all-reduce.7
  709.1 150.2 all-reduce.9
where the time goes:
time: 877 us; the launch traced here: 872 us
  waiting for transfers between devices  371 us (42%)
  blocking collectives  133 us (15%)
  local copies, waits for them, and re-layouts  128 us (15%)
  matrix products  122 us (14%)
  other arithmetic  79.9 us (9%)
  starting transfers between devices  22.9 us (3%)
  between operations  15.6 us (2%)
    psum x2, waiting for transfers between devices, per_device(): lax.psum((local_latents, local_kv, local_gain, local_kernel, local_patch,...  291 us
    psum x1, waiting for transfers between devices, per_device(): sum_exp, weighted = lax.psum((part_sum, part_weighted), ('rows', 'cols'))  78.4 us
    pmax x1, blocking collectives, per_device(): top_score = lax.pmax(local_top, ('rows', 'cols'))  69 us
    psum x1, blocking collectives, per_device(): sum_exp, weighted = lax.psum((part_sum, part_weighted), ('rows', 'cols'))  64.4 us
    dynamic_update_slice x24, local copies, waits for them, and re-layouts, per_device(): lax.map(head_grads, (query_heads, key_heads, value_heads, top_score.T, su...  43.4 us
    reduce_sum x1, other arithmetic, per_device(): local_bias = jnp.sum(d_embedded.astype(jnp.float32), axis=0)  21.4 us
    reduce_sum x4, other arithmetic, kernel_grad(): kernel_terms.append(jnp.sum(window * upstream_f, axis=(0, 1)))  20.2 us
    reduce_sum x1, other arithmetic, normalize(): centre = mixed - jnp.mean(mixed, axis=-1, keepdims=True)  19.2 us
  transfers between devices with their start and end apart: 11, of which 5 were waited for; matrix products, arithmetic and copies ran while one was open for 4% of the time, Pallas kernels for 0%

commit v1 on v0

v1 whole, which is shorter than its diff:
```python
import functools

import jax
import jax.numpy as jnp
from jax import lax
from jax.experimental import pallas as pl
from jax.experimental.pallas import tpu as pltpu
from jax.sharding import PartitionSpec as P

PATCH = 4
KSIZE = 7
HEADS = 8
HALO = 3
norm_eps = 1e-05
BF = jnp.bfloat16
F32 = jnp.float32
NT = (((1,), (1,)), ((), ()))
TN = (((0,), (0,)), ((), ()))
NN = (((1,), (0,)), ((), ()))
ROWS = 32
COLS = 64
CH = 256
TOK = ROWS * COLS
WIDE = 14
VMEM = pltpu.CompilerParams(vmem_limit_bytes=58 << 20)


def dot(a, b, dims=NN):
    return lax.dot_general(a, b, dims, preferred_element_type=F32)


def iota(shape, dim):
    return lax.broadcasted_iota(jnp.int32, shape, dim)


def write_edges(src, top, bot, left, right, corners, l_sc, r_sc, c_sc):
    top[...] = src[0 : HALO * COLS, :]
    bot[...] = src[TOK - HALO * COLS : TOK, :]
    for a in range(ROWS):
        low = src[a * COLS : a * COLS + 32, :].astype(F32)
        high = src[a * COLS + 32 : a * COLS + 64, :].astype(F32)
        for k in range(HALO):
            l_sc[k * ROWS + a : k * ROWS + a + 1, :] = low[8 * k : 8 * k + 1, :]
            r_sc[k * ROWS + a : k * ROWS + a + 1, :] = high[8 * k + 15 : 8 * k + 16, :]
    left[...] = l_sc[...].astype(BF)
    right[...] = r_sc[...].astype(BF)
    c_sc[...] = jnp.zeros_like(c_sc)
    for k in range(HALO):
        for i in range(HALO):
            first = k * ROWS + i
            last = k * ROWS + ROWS - HALO + i
            row = k * HALO + i
            c_sc[0, row : row + 1, :] = l_sc[first : first + 1, :]
            c_sc[1, row : row + 1, :] = r_sc[first : first + 1, :]
            c_sc[2, row : row + 1, :] = l_sc[last : last + 1, :]
            c_sc[3, row : row + 1, :] = r_sc[last : last + 1, :]
    corners[...] = c_sc[...].astype(BF)


EDGE_SHAPES = [
    jax.ShapeDtypeStruct((HALO * COLS, CH), BF),
    jax.ShapeDtypeStruct((HALO * COLS, CH), BF),
    jax.ShapeDtypeStruct((HALO * ROWS, CH), BF),
    jax.ShapeDtypeStruct((HALO * ROWS, CH), BF),
    jax.ShapeDtypeStruct((4, 16, CH), BF),
]
EDGE_SCRATCH = [
    pltpu.VMEM((HALO * ROWS, CH), F32),
    pltpu.VMEM((HALO * ROWS, CH), F32),
    pltpu.VMEM((4, 16, CH), F32),
]


def exchange(edges):
    top, bot, left, right, corners = edges
    n_r, n_c = lax.axis_size("rows"), lax.axis_size("cols")

    def move(x, d_r, d_c):
        pairs = [
            (r * n_c + c, (r + d_r) * n_c + c + d_c)
            for r in range(n_r)
            for c in range(n_c)
            if 0 <= r + d_r < n_r and 0 <= c + d_c < n_c
        ]
        return lax.ppermute(x, ("rows", "cols"), pairs)

    return (
        move(bot, 1, 0),
        move(top, -1, 0),
        move(right, 0, 1),
        move(left, 0, -1),
        move(corners[3], 1, 1),
        move(corners[2], 1, -1),
        move(corners[1], -1, 1),
        move(corners[0], -1, -1),
    )


def assemble(wide, own, halo, l_sc, r_sc, c_sc):
    above, below, left, right, tl, tr, bl, br = halo
    l_sc[...] = left[...].astype(F32)
    r_sc[...] = right[...].astype(F32)
    for n, ref in enumerate((tl, tr, bl, br)):
        c_sc[n] = ref[...].astype(F32)
    sub = iota((8, CH), 0)

    def put(row, x, lefts, rights):
        x = x.astype(F32).reshape(8, 8, CH)
        for cb in range(8):
            wide[row, HALO + cb] = x[cb]
        for k in range(HALO):
            wide[row, k] = jnp.where(sub == 0, lefts[k], pltpu.roll(x[5 + k], 1, 0))
            wide[row, 11 + k] = jnp.where(sub == 7, rights[k], pltpu.roll(x[k], 7, 0))

    for i in range(HALO):
        row = [k * HALO + i for k in range(HALO)]
        put(
            i,
            above[i * COLS : (i + 1) * COLS, :],
            [c_sc[0, n : n + 1, :] for n in row],
            [c_sc[1, n : n + 1, :] for n in row],
        )
        put(
            HALO + ROWS + i,
            below[i * COLS : (i + 1) * COLS, :],
            [c_sc[2, n : n + 1, :] for n in row],
            [c_sc[3, n : n + 1, :] for n in row],
        )

    def body(a, carry):
        put(
            a + HALO,
            own[pl.ds(pl.multiple_of(a * COLS, COLS), COLS), :],
            [l_sc[pl.ds(k * ROWS + a, 1), :] for k in range(HALO)],
            [r_sc[pl.ds(k * ROWS + a, 1), :] for k in range(HALO)],
        )
        return carry

    lax.fori_loop(0, ROWS, body, 0)


def spread_weights(kernel_ref, w_sc):
    for n in range(KSIZE * KSIZE):
        w_sc[n] = jnp.broadcast_to(kernel_ref[n : n + 1, :], (8, CH))


def conv_row(wide, w_sc, a, half, flip):
    lanes = pl.ds(half * 128, 128)
    acc = [wide[a + HALO, HALO + cb, :, lanes] for cb in range(8)]
    for i in range(KSIZE):
        xs = [wide[a + i, c, :, lanes] for c in range(WIDE)]
        for j in range(KSIZE):
            n = i * KSIZE + j
            w = w_sc[KSIZE * KSIZE - 1 - n if flip else n, :, lanes]
            acc = [acc[cb] + xs[cb + j] * w for cb in range(8)]
    return acc


def norm_rows(x):
    centre = x - jnp.sum(x, axis=-1, keepdims=True) * (1.0 / CH)
    variance = jnp.sum(centre * centre, axis=-1, keepdims=True) * (1.0 / CH)
    inverse = lax.rsqrt(variance + norm_eps)
    return centre * inverse, inverse


def embed_kernel(pixels, weights, bias, emb, z_ref, top, bot, left, right, corners, w_sc, l_sc, r_sc, c_sc):
    out = iota((256, 256), 0)
    spread = (((out & 7) * 8 + ((out >> 3) & 7)) * 4 + (out >> 6)) == iota((256, 256), 1)
    spread = jnp.where(spread, 1.0, 0.0).astype(BF)
    by_cell = dot(spread, pixels[...], NT).astype(BF)
    row = iota((512, 384), 0)
    fu = row & 15
    target = (fu >> 2) * 128 + (row >> 4) * 4 + (fu & 3)
    order = jnp.where((target == iota((512, 384), 1)) & (fu < 12), 1.0, 0.0).astype(BF)
    z = dot(by_cell, order, NT).astype(BF)
    for g in range(4):
        for v in range(4):
            z_ref[g * 64 : (g + 1) * 64, v * 128 : (v + 1) * 128] = z[
                v * 64 : (v + 1) * 64, g * 128 : (g + 1) * 128
            ]
    w_sc[...] = jnp.zeros_like(w_sc)
    for v in range(4):
        for a8 in range(8):
            first = v * 128 + a8 * 16
            w_sc[first : first + 16, a8 * CH : (a8 + 1) * CH] = weights[v]
    for a8 in range(8):
        block = dot(z_ref[...], w_sc[:, a8 * CH : (a8 + 1) * CH]) + bias[...]
        block = block.astype(BF)
        for g in range(4):
            a = g * 8 + a8
            emb[a * COLS : (a + 1) * COLS, :] = block[g * 64 : (g + 1) * 64, :]
    write_edges(emb, top, bot, left, right, corners, l_sc, r_sc, c_sc)


def embed(pixels, patch_weight, patch_bias):
    weights = patch_weight.reshape(12, 4, CH).transpose(1, 0, 2)
    weights = jnp.pad(weights, ((0, 0), (0, 4), (0, 0)))
    outs = pl.pallas_call(
        embed_kernel,
        name="embed",
        out_shape=[
            jax.ShapeDtypeStruct((TOK, CH), BF),
            jax.ShapeDtypeStruct((256, 512), BF),
        ]
        + EDGE_SHAPES,
        scratch_shapes=[pltpu.VMEM((512, 2048), BF)] + EDGE_SCRATCH,
        compiler_params=VMEM,
    )(pixels.reshape(384, 256), weights, patch_bias.reshape(1, CH))
    return outs[0], outs[1], outs[2:]


def conv_kernel_body(emb, above, below, lh, rh, tl, tr, bl, br, kern, gain, wide, mixed, normed, w_sc, l_sc, r_sc, c_sc):
    assemble(wide, emb, (above, below, lh, rh, tl, tr, bl, br), l_sc, r_sc, c_sc)
    spread_weights(kern, w_sc)

    def body(a, carry):
        for half in range(2):
            acc = conv_row(wide, w_sc, a, half, False)
            for cb in range(8):
                rows = pl.ds(pl.multiple_of(a * COLS + cb * 8, 8), 8)
                mixed[rows, pl.ds(half * 128, 128)] = acc[cb]
        return carry

    lax.fori_loop(0, ROWS, body, 0)

    def norm_body(a, carry):
        rows = pl.ds(pl.multiple_of(a * COLS, COLS), COLS)
        centred, _ = norm_rows(mixed[rows, :])
        normed[rows, :] = (centred * gain[...]).astype(BF)
        return carry

    lax.fori_loop(0, ROWS, norm_body, 0)


def conv_forward(emb, halo, conv_kernel, gain):
    return pl.pallas_call(
        conv_kernel_body,
        name="conv_forward",
        out_shape=[
            jax.ShapeDtypeStruct((ROWS + 2 * HALO, WIDE, 8, CH), F32),
            jax.ShapeDtypeStruct((TOK, CH), F32),
            jax.ShapeDtypeStruct((TOK, CH), BF),
        ],
        scratch_shapes=[pltpu.VMEM((KSIZE * KSIZE, 8, CH), F32)] + EDGE_SCRATCH,
        compiler_params=VMEM,
    )(emb, *halo, conv_kernel, gain)


CHUNK = 512
SCALE = 128**-0.5


def attend_kernel(normed, wk, wv, q, up, k_out, v_out, weighted, stats, s_sc):
    h = pl.program_id(0)
    w = jnp.concatenate([wk[...], wv[...]], axis=1)
    peak = None
    for c in range(TOK // CHUNK):
        rows = slice(c * CHUNK, (c + 1) * CHUNK)
        kv = dot(normed[rows, :], w).astype(BF)
        k_out[rows, :] = kv[:, :128]
        v_out[rows, :] = kv[:, 128:]
        s = dot(kv[:, :128], q[...], NT) * SCALE
        s_sc[rows, :] = s
        top = jnp.max(s, axis=0, keepdims=True)
        peak = top if peak is None else jnp.maximum(peak, top)
    total = jnp.zeros((1, 256), F32)
    acc = jnp.zeros((128, 256), F32)
    for c in range(TOK // CHUNK):
        rows = slice(c * CHUNK, (c + 1) * CHUNK)
        p = jnp.exp(s_sc[rows, :] - peak)
        total = total + jnp.sum(p, axis=0, keepdims=True)
        acc = acc + dot(v_out[rows, :], p.astype(BF), TN)
    weighted[...] = acc.T
    dots = jnp.sum(acc * up[...].astype(F32).T, axis=0, keepdims=True)
    stats[0, pl.ds(h, 1), :] = peak
    stats[1, pl.ds(h, 1), :] = total
    stats[2, pl.ds(h, 1), :] = dots


def whole(shape):
    return pl.BlockSpec(shape, lambda h: (0,) * len(shape))


def column(rows, width, first=0):
    return pl.BlockSpec((rows, width), lambda h: (0, h + first))


def attend(normed, kv_weight, latents, d_attended):
    return pl.pallas_call(
        attend_kernel,
        name="attend",
        grid=(HEADS,),
        in_specs=[
            whole((TOK, CH)),
            column(CH, 128),
            column(CH, 128, HEADS),
            column(256, 128),
            column(256, 128),
        ],
        out_specs=[
            column(TOK, 128),
            column(TOK, 128),
            column(256, 128),
            whole((3, HEADS, 256)),
        ],
        out_shape=[
            jax.ShapeDtypeStruct((TOK, 1024), BF),
            jax.ShapeDtypeStruct((TOK, 1024), BF),
            jax.ShapeDtypeStruct((256, 1024), F32),
            jax.ShapeDtypeStruct((3, HEADS, 256), F32),
        ],
        scratch_shapes=[pltpu.VMEM((TOK, 256), F32)],
        compiler_params=VMEM,
    )(normed, kv_weight, kv_weight, latents, d_attended)


def attend_grad_kernel(
    normed, k_in, v_in, wk, wv, q, up, lse, dots, mixed, gain,
    q_grad, k_weight, v_weight, d_mixed, gain_grad, top, bot, left, right, corners,
    dn_sc, nt_sc, l_sc, r_sc, c_sc,
):
    h = pl.program_id(0)

    @pl.when(h == 0)
    def _():
        nt_sc[...] = normed[...].astype(F32).T.astype(BF)
        dn_sc[...] = jnp.zeros_like(dn_sc)

    w = jnp.concatenate([wk[...], wv[...]], axis=1)
    level = lse[pl.ds(h, 1), :]
    row_dots = dots[pl.ds(h, 1), :]
    qg = jnp.zeros((128, 256), F32)
    wg = jnp.zeros((256, 256), F32)
    for c in range(TOK // CHUNK):
        rows = slice(c * CHUNK, (c + 1) * CHUNK)
        k = k_in[rows, :]
        p = jnp.exp(dot(k, q[...], NT) * SCALE - level)
        dp = dot(v_in[rows, :], up[...], NT)
        ds = (p * (dp - row_dots) * SCALE).astype(BF)
        qg = qg + dot(k, ds, TN)
        kg = dot(ds, q[...]).astype(BF)
        vg = dot(p.astype(BF), up[...]).astype(BF)
        d_proj = jnp.concatenate([kg, vg], axis=1)
        wg = wg + dot(nt_sc[:, rows], d_proj)
        dn_sc[rows, :] += dot(d_proj, w, NT)
    q_grad[...] = qg.T
    k_weight[...] = wg[:, :128]
    v_weight[...] = wg[:, 128:]

    @pl.when(h == HEADS - 1)
    def _():
        def body(a, total):
            rows = pl.ds(pl.multiple_of(a * COLS, COLS), COLS)
            centred, inverse = norm_rows(mixed[rows, :])
            dn = dn_sc[rows, :]
            total = total + jnp.sum(dn * centred, axis=0, keepdims=True)
            g = dn * gain[...]
            mean = jnp.sum(g, axis=-1, keepdims=True) * (1.0 / CH)
            slope = jnp.sum(g * centred, axis=-1, keepdims=True) * (1.0 / CH)
            d_mixed[rows, :] = (inverse * (g - mean - centred * slope)).astype(BF)
            return total

        gain_grad[...] = lax.fori_loop(0, ROWS, body, jnp.zeros((1, CH), F32))
        write_edges(d_mixed, top, bot, left, right, corners, l_sc, r_sc, c_sc)


def attend_grad(normed, k, v, kv_weight, latents, d_attended, lse, dots, mixed, gain):
    outs = pl.pallas_call(
        attend_grad_kernel,
        name="attend_grad",
        grid=(HEADS,),
        in_specs=[
            whole((TOK, CH)),
            column(TOK, 128),
            column(TOK, 128),
            column(CH, 128),
            column(CH, 128, HEADS),
            column(256, 128),
            column(256, 128),
            whole((HEADS, 256)),
            whole((HEADS, 256)),
            whole((TOK, CH)),
            whole((1, CH)),
        ],
        out_specs=[column(256, 128), column(CH, 128), column(CH, 128), whole((TOK, CH)), whole((1, CH))]
        + [whole(s.shape) for s in EDGE_SHAPES],
        out_shape=[
            jax.ShapeDtypeStruct((256, 1024), F32),
            jax.ShapeDtypeStruct((CH, 1024), F32),
            jax.ShapeDtypeStruct((CH, 1024), F32),
            jax.ShapeDtypeStruct((TOK, CH), BF),
            jax.ShapeDtypeStruct((1, CH), F32),
        ]
        + EDGE_SHAPES,
        scratch_shapes=[pltpu.VMEM((TOK, CH), F32), pltpu.VMEM((CH, TOK), BF)] + EDGE_SCRATCH,
        compiler_params=VMEM,
    )(normed, k, v, kv_weight, kv_weight, latents, d_attended, lse, dots, mixed, gain)
    return outs[:5], outs[5:]


def kernel_grad_body(wide, d_mixed, out, d_sc):
    d_sc[...] = d_mixed[...].astype(F32)
    for half in range(2):
        lanes = pl.ds(half * 128, 128)
        for i in range(KSIZE):

            def body(a, acc):
                xs = [wide[a + i, c, :, lanes] for c in range(WIDE)]
                base = pl.multiple_of(a * COLS, COLS)
                ds = [d_sc[pl.ds(base + cb * 8, 8), lanes] for cb in range(8)]
                acc = list(acc)
                for cb in range(8):
                    for j in range(KSIZE):
                        acc[j] = acc[j] + xs[cb + j] * ds[cb]
                return tuple(acc)

            zero = jnp.zeros((8, 128), F32)
            acc = lax.fori_loop(0, ROWS, body, (zero,) * KSIZE)
            for j in range(KSIZE):
                n = i * KSIZE + j
                out[n : n + 1, lanes] = jnp.sum(acc[j], axis=0, keepdims=True)


def kernel_grad(wide, d_mixed):
    return pl.pallas_call(
        kernel_grad_body,
        name="kernel_grad",
        out_shape=jax.ShapeDtypeStruct((KSIZE * KSIZE, CH), F32),
        scratch_shapes=[pltpu.VMEM((TOK, CH), F32)],
        compiler_params=VMEM,
    )(wide, d_mixed)


def conv_back_body(d_mixed, above, below, lh, rh, tl, tr, bl, br, kern, z, patch_grad, bias_grad, wide, d_sc, w_sc, l_sc, r_sc, c_sc):
    assemble(wide, d_mixed, (above, below, lh, rh, tl, tr, bl, br), l_sc, r_sc, c_sc)
    spread_weights(kern, w_sc)
    zero = jnp.zeros((8, 128), F32)

    def body(a, bias):
        bias = list(bias)
        for half in range(2):
            acc = conv_row(wide, w_sc, a, half, True)
            acc = jnp.concatenate(acc, axis=0).astype(BF)
            d_sc[a & 7, pl.ds(pl.multiple_of((a >> 3) * 64, 64), 64), pl.ds(half * 128, 128)] = acc
            bias[half] = bias[half] + jnp.sum(acc.astype(F32).reshape(8, 8, 128), axis=0)
        return tuple(bias)

    bias = lax.fori_loop(0, ROWS, body, (zero, zero))
    for half in range(2):
        bias_grad[:, half * 128 : (half + 1) * 128] = jnp.sum(bias[half], axis=0, keepdims=True)
    total = [jnp.zeros((16, CH), F32) for _ in range(4)]
    for a8 in range(8):
        part = dot(z[...], d_sc[a8], TN)
        for v in range(4):
            first = v * 128 + a8 * 16
            total[v] = total[v] + part[first : first + 16, :]
    for v in range(4):
        patch_grad[v] = total[v]


def conv_back(d_mixed, halo, conv_kernel, z):
    return pl.pallas_call(
        conv_back_body,
        name="conv_back",
        out_shape=[jax.ShapeDtypeStruct((4, 16, CH), F32), jax.ShapeDtypeStruct((1, CH), F32)],
        scratch_shapes=[
            pltpu.VMEM((ROWS + 2 * HALO, WIDE, 8, CH), F32),
            pltpu.VMEM((8, 256, CH), BF),
            pltpu.VMEM((KSIZE * KSIZE, 8, CH), F32),
        ]
        + EDGE_SCRATCH,
        compiler_params=VMEM,
    )(d_mixed, *halo, conv_kernel, z)


def rings():
    n_r, n_c = lax.axis_size("rows"), lax.axis_size("cols")
    side = 4
    out = []
    for axis, size, inner in (("rows", 2, 1), ("rows", n_r // 2, 2), ("cols", side, 1), ("cols", n_c // side, side)):
        total = lax.axis_size(axis)
        shifts = []
        for d in range(1, size):
            pairs = []
            for i in range(total):
                pos = i // inner % size
                pairs.append((i, i + ((pos + d) % size - pos) * inner))
            shifts.append(pairs)
        out.append((axis, shifts))
    return out


def combine_stats(stats):
    for axis, shifts in rings():
        group = [stats] + [lax.ppermute(stats, axis, pairs) for pairs in shifts]
        peak = functools.reduce(jnp.maximum, [g[0] for g in group])
        factors = [jnp.exp(g[0] - peak) for g in group]
        total = sum(g[1] * f for g, f in zip(group, factors))
        dots = sum(g[2] * f for g, f in zip(group, factors))
        stats = jnp.stack([peak, total, dots])
    return stats


AXES = ("rows", "cols")


def all_sum(x):
    count = lax.axis_size(AXES)
    rows = x.shape[0] // count
    parts = lax.all_to_all(x, AXES, 0, 0, tiled=True)
    mine = jnp.sum(parts.reshape(count, rows, -1), axis=0)
    copies = jnp.broadcast_to(mine[None], (count,) + mine.shape).reshape(x.shape)
    return lax.all_to_all(copies, AXES, 0, 0, tiled=True)


def per_device(
    pixels, patch_weight, patch_bias, conv_kernel, norm_gain, kv_weight, latents, d_attended
):
    gain = norm_gain.reshape(1, CH)
    emb, z, edges = embed(pixels, patch_weight, patch_bias)
    wide, mixed, normed = conv_forward(emb, exchange(edges), conv_kernel, gain)
    k, v, weighted, local = attend(normed, kv_weight, latents, d_attended)
    stats = combine_stats(local)
    lse = stats[0] + jnp.log(stats[1])
    row_dots = stats[2] / stats[1]
    factor = (jnp.exp(local[0] - stats[0]) / stats[1]).T
    attended = (weighted.reshape(256, HEADS, 128) * factor[:, :, None]).reshape(256, 1024)
    (q_grad, k_weight, v_weight, d_mixed, gain_grad), d_edges = attend_grad(
        normed, k, v, kv_weight, latents, d_attended, lse, row_dots, mixed, gain
    )
    big = all_sum(jnp.concatenate([attended, q_grad, k_weight, v_weight], axis=0))
    halo = exchange(d_edges)
    kern = kernel_grad(wide, d_mixed)
    patch, bias = conv_back(d_mixed, halo, conv_kernel, z)
    small = jnp.concatenate([patch.reshape(64, CH), kern, gain_grad, bias], axis=0)
    small = all_sum(jnp.pad(small, ((0, 128 - small.shape[0]), (0, 0))))
    patch = small[:64].reshape(4, 16, CH)[:, :12].transpose(1, 0, 2).reshape(48, CH)
    return (
        big[:256],
        big[256:512],
        jnp.concatenate([big[512:768], big[768:]], axis=1),
        small[64 + 49],
        small[64 : 64 + 49],
        patch,
        small[64 + 50],
    )


def solution(mesh):
    return jax.shard_map(
        per_device,
        mesh=mesh,
        in_specs=(P(None, "rows", "cols"), P(), P(), P(), P(), P(), P(), P()),
        out_specs=(P(), P(), P(), P(), P(), P(), P()),
        check_vma=False,
    )
```

time: 877 us -> 360 us (0.41)
  waiting for transfers between devices: 371 us -> 139 us
  blocking collectives: 133 us -> 0 us
  matrix products: 122 us -> 0 us
  local copies, waits for them, and re-layouts: 128 us -> 14.5 us
  Pallas kernels: 0 us -> 98.2 us
  starting transfers between devices: 22.9 us -> 92.3 us
  other arithmetic: 79.9 us -> 13.2 us
  between operations: 15.6 us -> 1.18 us
    psum x3 -> x0, waiting for transfers between devices: 369 us -> none  [the longest x2 291 us: per_device(): lax.psum((local_latents, local_kv, local_gain, local_kernel, local_patch,...]
    dot_general x61 -> x0, matrix products: 122 us -> none  [the longest x8 17.1 us: head_grads(): jnp.einsum('lt,le->te', probs.astype(jnp.bfloat16), upstream, preferred_e...]
    all_to_all x0 -> x4, waiting for transfers between devices: none -> 117 us  [the longest x2 58.7 us: all_sum(): parts = lax.all_to_all(x, AXES, 0, 0, tiled=True)]
    pallas_call x0 -> x6, Pallas kernels: none -> 98.2 us  [the longest x1 34.4 us: attend_grad(): pl.pallas_call(attend_grad_kernel, name='attend_grad', grid=(HEADS,), in_...]
    pmax x1 -> x0, blocking collectives: 69 us -> none  [per_device(): top_score = lax.pmax(local_top, ('rows', 'cols'))]
    reduce_sum x17 -> x2, other arithmetic: 71.2 us -> 2.62 us  [all_sum(): mine = jnp.sum(parts.reshape(count, rows, -1), axis=0)]
    psum x1 -> x0, blocking collectives: 64.4 us -> none  [per_device(): sum_exp, weighted = lax.psum((part_sum, part_weighted), ('rows', 'cols'))]
    dynamic_update_slice x40 -> x0, local copies, waits for them, and re-layouts: 54.1 us -> none  [the longest x24 43.4 us: per_device(): lax.map(head_grads, (query_heads, key_heads, value_heads, top_score.T, su...]
  transfers between devices with their start and end apart: 11 -> 30, of which waited for: 5 -> 15; matrix products, arithmetic and copies ran while one was open for 4% -> 3% of each run, Pallas kernels for 0% -> 4%
where the time goes in v1:
time: 360 us; the launch traced here: 359 us
  waiting for transfers between devices  139 us (39%)
  Pallas kernels  98.2 us (27%)
  starting transfers between devices  92.3 us (26%)
  local copies, waits for them, and re-layouts  14.5 us (4%)
  other arithmetic  13.2 us (4%)
    all_to_all x2, waiting for transfers between devices, all_sum(): parts = lax.all_to_all(x, AXES, 0, 0, tiled=True)  58.7 us
    all_to_all x2, waiting for transfers between devices, all_sum(): return lax.all_to_all(copies, AXES, 0, 0, tiled=True)  58.1 us
    ppermute x16, starting transfers between devices, move(): return lax.ppermute(x, ('rows', 'cols'), pairs)  47.5 us
    pallas_call x1, Pallas kernels, attend_grad(): pl.pallas_call(attend_grad_kernel, name='attend_grad', grid=(HEADS,), in_...  34.4 us
    all_to_all x2, starting transfers between devices, all_sum(): parts = lax.all_to_all(x, AXES, 0, 0, tiled=True)  18.8 us
    pallas_call x1, Pallas kernels, attend(): pl.pallas_call(attend_kernel, name='attend', grid=(HEADS,), in_specs=[who...  17.8 us
    pallas_call x1, Pallas kernels, conv_forward(): pl.pallas_call(conv_kernel_body, name='conv_forward', out_shape=[jax.Shap...  17.6 us
    ppermute x10, starting transfers between devices, combine_stats(): group = [stats] + [lax.ppermute(stats, axis, pairs) for pairs in shifts]  16.6 us
  transfers between devices with their start and end apart: 30, of which 15 were waited for; matrix products, arithmetic and copies ran while one was open for 3% of the time, Pallas kernels for 4%

profile of v1, /device:TPU:1, one launch (start us, length us, event | category | flops | bytes accessed | tf_op | source)
XLA Modules:
  0.0 358.6 jit_solution(4488729493944755832)
XLA Ops:
  2.0 3.1 embed.1
  5.1 4.0 %collective-permute-start.2 = (bf16[96,256]{1,0:T(8,128)(2,1)}, bf16[96,256]{1,0:T(8,128)(2,1)S(1)}, u32[]{:S(2)}, u32[]{:S(2)}) collective-permute-start(bf16[96,256]{1,0:T(8,128)(2,1)} %get-tuple-element.36), channel_id=1, source_target_pairs={{0,1},{1,2},{2,3},{3,4},{4,5},{5,6},{6,7},{7,8},{8,9},{9,10},{10,1... | collective-permute-start | bytes 147464 | tf_op jit(solution)/shard_map/ppermute | solution.py:85
  10.5 4.4 %collective-permute-start = (bf16[192,256]{1,0:T(8,128)(2,1)}, bf16[192,256]{1,0:T(8,128)(2,1)S(1)}, u32[]{:S(2)}, u32[]{:S(2)}) collective-permute-start(bf16[192,256]{1,0:T(8,128)(2,1)} %get-tuple-element.34), channel_id=1, source_target_pairs={{0,16},{1,17},{2,18},{3,19},{4,20},{5,21},{6,22},{7,23},{8,24},{9,... | collective-permute-start | bytes 294920 | tf_op jit(solution)/shard_map/ppermute | solution.py:85
  18.8 5.7 %collective-permute-done.7.br = bf16[16,256]{1,0:T(8,128)(2,1)S(1)} collective-permute-done((bf16[16,256]{1,0:T(8,128)(2,1)S(1)}, bf16[16,256]{1,0:T(8,128)(2,1)S(1)}, u32[]{:S(2)}, u32[]{:S(2)}) %collective-permute-start.7) | collective-permute-done | bytes 8224 | tf_op jit(solution)/shard_map/ppermute | solution.py:85
  28.7 3.7 %collective-permute-done.5.tr = bf16[16,256]{1,0:T(8,128)(2,1)S(1)} collective-permute-done((bf16[16,256]{1,0:T(8,128)(2,1)S(1)}, bf16[16,256]{1,0:T(8,128)(2,1)S(1)}, u32[]{:S(2)}, u32[]{:S(2)}) %collective-permute-start.5) | collective-permute-done | bytes 8224 | tf_op jit(solution)/shard_map/ppermute | solution.py:85
  32.4 7.0 %collective-permute-start.4 = (bf16[16,256]{1,0:T(8,128)(2,1)S(1)}, bf16[16,256]{1,0:T(8,128)(2,1)S(1)}, u32[]{:S(2)}, u32[]{:S(2)}) collective-permute-start(bf16[16,256]{1,0:T(8,128)(2,1)S(1)} %get-tuple-element.83), channel_id=1, source_target_pairs={{0,17},{1,18},{2,19},{3,20},{4,21},{5,22},{6,23},{7,24},{8,25},{9,... | collective-permute-start | bytes 24584 | tf_op jit(solution)/shard_map/ppermute | solution.py:85
  40.8 17.6 %conv_forward.1 = (f32[38,14,8,256]{3,2,1,0:T(8,128)}, f32[2048,256]{1,0:T(8,128)}, bf16[2048,256]{1,0:T(8,128)(2,1)}) custom-call(bf16[2048,256]{1,0:T(8,128)(2,1)} %get-tuple-element.33.emb, bf16[192,256]{1,0:T(8,128)(2,1)} %copy-done.3, bf16[192,256]{1,0:T(8,128)(2,1)} %copy-done.4, bf16[96,256]{1,0:T(8,128)(2,1)} %copy-done.7, ...), custom_call_target="tpu_custom_call" | custom-call | tf_op jit(solution)/shard_map/conv_forward/pallas_call | solution.py:236
  58.4 17.8 %attend.1 = (bf16[2048,1024]{1,0:T(8,128)(2,1)}, bf16[2048,1024]{1,0:T(8,128)(2,1)}, f32[256,1024]{1,0:T(8,128)}, f32[3,8,256]{2,1,0:T(8,128)}) custom-call(bf16[2048,256]{1,0:T(8,128)(2,1)} %get-tuple-element.39.normed, bf16[256,2048]{1,0:T(8,128)(2,1)} %wv.3, bf16[256,2048]{1,0:T(8,128)(2,1)} %wv.3, bf16[256,1024]{1,0:T(8,128)(2,1)} %q.3, bf16[256,1024]{1,0:T(8,128)(2,1)} %up.3), custom_call_target="tpu_custom_call" | custom-call | tf_op jit(solution)/shard_map/attend/pallas_call | solution.py:289
  79.1 3.6 collective-permute-start.11
  83.6 3.2 collective-permute-done.10
  86.9 7.4 %collective-permute-start.14 = (f32[3,8,256]{2,1,0:T(8,128)S(1)}, f32[3,8,256]{2,1,0:T(8,128)S(1)}, u32[]{:S(2)}, u32[]{:S(2)}) collective-permute-start(f32[3,8,256]{2,1,0:T(8,128)S(1)} %pad_maximum_fusion.2), channel_id=1, source_target_pairs={{0,3},{1,0},{2,1},{3,2},{4,7},{5,4},{6,5},{7,6},{8,11},{9,8},{10,9... | collective-permute-start | bytes 73736 | tf_op jit(solution)/shard_map/ppermute | solution.py:495
  95.3 3.2 collective-permute-done.13
  98.6 2.8 collective-permute-start.17
  102.5 3.1 collective-permute-done.16
  108.5 34.4 %attend_grad.1 = (f32[256,1024]{1,0:T(8,128)}, f32[256,1024]{1,0:T(8,128)}, f32[256,1024]{1,0:T(8,128)}, bf16[2048,256]{1,0:T(8,128)(2,1)}, f32[1,256]{1,0:T(1,1...) custom-call(bf16[2048,256]{1,0:T(8,128)(2,1)} %get-tuple-element.39., ...), custom_call_target="tpu_custom_call" | custom-call | tf_op jit(solution)/shard_map/attend_grad/pallas_call | solution.py:368
  145.0 7.2 %collective-permute-start.24 = (bf16[16,256]{1,0:T(8,128)(2,1)S(1)}, bf16[16,256]{1,0:T(8,128)(2,1)S(1)}, u32[]{:S(2)}, u32[]{:S(2)}) collective-permute-start(bf16[16,256]{1,0:T(8,128)(2,1)S(1)} %get-tuple-element.77), channel_id=1, source_target_pairs={{16,1},{17,2},{18,3},{19,4},{20,5},{21,6},{22,7},{23,8},{24,9},{25... | collective-permute-start | bytes 24584 | tf_op jit(solution)/shard_map/ppermute | solution.py:85
  153.5 5.8 %collective-permute-start.22 = (bf16[16,256]{1,0:T(8,128)(2,1)S(1)}, bf16[16,256]{1,0:T(8,128)(2,1)S(1)}, u32[]{:S(2)}, u32[]{:S(2)}) collective-permute-start(bf16[16,256]{1,0:T(8,128)(2,1)S(1)} %get-tuple-element.79), channel_id=1, source_target_pairs={{0,17},{1,18},{2,19},{3,20},{4,21},{5,22},{6,23},{7,24},{8,25},{9,... | collective-permute-start | bytes 24584 | tf_op jit(solution)/shard_map/ppermute | solution.py:85
  159.3 2.8 collective-permute-start.20
  163.6 2.5 collective-permute-start.18
  168.9 13.2 %kernel_grad.1 = f32[49,256]{1,0:T(8,128)} custom-call(f32[38,14,8,256]{3,2,1,0:T(8,128)} %get-tuple-element.56.wide, bf16[2048,256]{1,0:T(8,128)(2,1)} %get-tuple-element.48.d_mixed), custom_call_target="tpu_custom_call" | custom-call | tf_op jit(solution)/shard_map/kernel_grad/pallas_call | solution.py:425
  182.9 12.2 %conv_back.1 = (f32[4,16,256]{2,1,0:T(8,128)}, f32[1,256]{1,0:T(1,128)}) custom-call(bf16[2048,256]{1,0:T(8,128)(2,1)} %get-tuple-element.48.d_mixed, bf16[192,256]{1,0:T(8,128)(2,1)} %copy-done.5, bf16[192,256]{1,0:T(8,128)(2,1)} %copy-done.6, bf16[96,256]{1,0:T(8,128)(2,1)} %copy-done.9, bf16[96,256]{1,0:T(8,128)(2,1)} %copy-done.10, ...), custom_call_target="tpu_custom_call" | custom-call | tf_op jit(solution)/shard_map/conv_back/pallas_call | solution.py:462
  196.7 13.7 %all-to-all-start.2 = ((f32[128,1,256]{2,1,0:T(1,128)}), f32[128,1,256]{2,1,0:T(1,128)S(1)}, u32[]{:S(2)}, u32[]{:S(2)}) async-start(f32[128,1,256]{2,1,0:T(1,128)} %all_to_all.23), calls=%async_computation.2 | async-start | bytes 262144 | tf_op jit(solution)/shard_map/all_to_all | solution.py:510
  210.4 3.7 %maximum_bitcast_fusion = f32[128,8,1024]{2,1,0:T(8,128)} fusion(f32[256,1024]{1,0:T(8,128)} %get-tuple-element.47, f32[256,1024]{1,0:T(8,128)S(1)} %copy-done.2, f32[256,1024]{1,0:T(8,128)S(1)} %copy-done.1, f32[256,1024]{1,0:T(8,128)S(1)} %bitcast_multiply_fusion), kind=kLoop, calls=%fused_computation | loop fusion | flops 3145728 | bytes 8388608 | tf_op jit(solution)/shard_map/all_to_all | solution.py:510
  214.1 6.4 %all-to-all-done.2 = f32[128,1,256]{2,1,0:T(1,128)S(1)} async-done(((f32[128,1,256]{2,1,0:T(1,128)}), f32[128,1,256]{2,1,0:T(1,128)S(1)}, u32[]{:S(2)}, u32[]{:S(2)}) %all-to-all-start.2) | async-done | bytes 131104 | tf_op jit(solution)/shard_map/all_to_all | solution.py:510
  220.5 5.1 %all-to-all-start = ((f32[128,8,1024]{2,1,0:T(8,128)}), f32[128,8,1024]{2,1,0:T(8,128)}, u32[]{:S(2)}, u32[]{:S(2)}) async-start(f32[128,8,1024]{2,1,0:T(8,128)} %maximum_bitcast_fusion), calls=%async_computation | async-start | bytes 8388608 | tf_op jit(solution)/shard_map/all_to_all | solution.py:510
  225.8 52.3 %all-to-all-done = f32[128,8,1024]{2,1,0:T(8,128)} async-done(((f32[128,8,1024]{2,1,0:T(8,128)}), f32[128,8,1024]{2,1,0:T(8,128)}, u32[]{:S(2)}, u32[]{:S(2)}) %all-to-all-start) | async-done | bytes 4194336 | tf_op jit(solution)/shard_map/all_to_all | solution.py:510
  278.8 4.2 %all-to-all-start.3 = ((f32[128,1,256]{2,1,0:T(1,128)}), f32[128,1,256]{2,1,0:T(1,128)S(1)}, u32[]{:S(2)}, u32[]{:S(2)}) async-start(f32[128,1,256]{2,1,0:T(1,128)} %reshape.80), calls=%async_computation.3 | async-start | bytes 262144 | tf_op jit(solution)/shard_map/all_to_all | solution.py:513
  285.5 7.6 %all-to-all-done.3 = f32[128,1,256]{2,1,0:T(1,128)S(1)} async-done(((f32[128,1,256]{2,1,0:T(1,128)}), f32[128,1,256]{2,1,0:T(1,128)S(1)}, u32[]{:S(2)}, u32[]{:S(2)}) %all-to-all-start.3) | async-done | bytes 131104 | tf_op jit(solution)/shard_map/all_to_all | solution.py:513
  293.1 2.5 broadcast_in_dim.2
  295.6 5.2 %all-to-all-start.1 = ((f32[128,8,1024]{2,1,0:T(8,128)}), f32[128,8,1024]{2,1,0:T(8,128)}, u32[]{:S(2)}, u32[]{:S(2)}) async-start(f32[128,8,1024]{2,1,0:T(8,128)} %broadcast_in_dim.2), calls=%async_computation.1 | async-start | bytes 8388608 | tf_op jit(solution)/shard_map/all_to_all | solution.py:513
  302.7 50.5 %all-to-all-done.1 = f32[128,8,1024]{2,1,0:T(8,128)} async-done(((f32[128,8,1024]{2,1,0:T(8,128)}), f32[128,8,1024]{2,1,0:T(8,128)}, u32[]{:S(2)}, u32[]{:S(2)}) %all-to-all-start.1) | async-done | bytes 4194336 | tf_op jit(solution)/shard_map/all_to_all | solution.py:513
  353.2 3.9 %slice_bitcast_fusion.1 = (f32[256,1024]{1,0:T(8,128)S(1)}, f32[256,1024]{1,0:T(8,128)S(1)}, f32[256,1024]{1,0:T(8,128)}, f32[256,1024]{1,0:T(8,128)}) fusion(f32[128,8,1024]{2,1,0:T(8,128)} %all-to-all-done.1), kind=kLoop, calls=%fused_computation.4 | loop fusion | bytes 8388608 | tf_op jit(solution)/shard_map/slice | solution.py:541
  (111 shorter events, 37.7 us)
Async XLA Ops:
  5.1 35.0 %collective-permute-start.2 = (bf16[96,256]{1,0:T(8,128)(2,1)}, bf16[96,256]{1,0:T(8,128)(2,1)S(1)}, u32[]{:S(2)}, u32[]{:S(2)}) collective-permute-start(bf16[96,256]{1,0:T(8,128)(2,1)} %get-tuple-element.36), channel_id=1, source_target_pairs={{0,1},{1,2},{2,3},{3,4},{4,5},{5,6},{6,7},{7,8},{8,9},{9,10},{10,1... | collective-permute-start | bytes 147464 | tf_op jit(solution)/shard_map/ppermute | solution.py:85
  9.2 30.9 %collective-permute-start.3 = (bf16[96,256]{1,0:T(8,128)(2,1)}, bf16[96,256]{1,0:T(8,128)(2,1)S(1)}, u32[]{:S(2)}, u32[]{:S(2)}) collective-permute-start(bf16[96,256]{1,0:T(8,128)(2,1)} %get-tuple-element.37), channel_id=1, source_target_pairs={{1,0},{2,1},{3,2},{4,3},{5,4},{6,5},{7,6},{8,7},{9,8},{10,9},{11,1... | collective-permute-start | bytes 147464 | tf_op jit(solution)/shard_map/ppermute | solution.py:85
  10.5 29.7 %collective-permute-start = (bf16[192,256]{1,0:T(8,128)(2,1)}, bf16[192,256]{1,0:T(8,128)(2,1)S(1)}, u32[]{:S(2)}, u32[]{:S(2)}) collective-permute-start(bf16[192,256]{1,0:T(8,128)(2,1)} %get-tuple-element.34), channel_id=1, source_target_pairs={{0,16},{1,17},{2,18},{3,19},{4,20},{5,21},{6,22},{7,23},{8,24},{9,... | collective-permute-start | bytes 294920 | tf_op jit(solution)/shard_map/ppermute | solution.py:85
  14.9 25.3 %collective-permute-start.1 = (bf16[192,256]{1,0:T(8,128)(2,1)}, bf16[192,256]{1,0:T(8,128)(2,1)S(1)}, u32[]{:S(2)}, u32[]{:S(2)}) collective-permute-start(bf16[192,256]{1,0:T(8,128)(2,1)} %get-tuple-element.35), channel_id=1, source_target_pairs={{16,0},{17,1},{18,2},{19,3},{20,4},{21,5},{22,6},{23,7},{24,8},{25... | collective-permute-start | bytes 294920 | tf_op jit(solution)/shard_map/ppermute | solution.py:85
  17.5 7.0 %collective-permute-start.7 = (bf16[16,256]{1,0:T(8,128)(2,1)S(1)}, bf16[16,256]{1,0:T(8,128)(2,1)S(1)}, u32[]{:S(2)}, u32[]{:S(2)}) collective-permute-start(bf16[16,256]{1,0:T(8,128)(2,1)S(1)} %get-tuple-element.80), channel_id=1, source_target_pairs={{17,0},{18,1},{19,2},{20,3},{21,4},{22,5},{23,6},{24,7},{25,8},{26... | collective-permute-start | bytes 24584 | tf_op jit(solution)/shard_map/ppermute | solution.py:85
  24.6 2.8 collective-permute-start.6
  27.4 5.0 %collective-permute-start.5 = (bf16[16,256]{1,0:T(8,128)(2,1)S(1)}, bf16[16,256]{1,0:T(8,128)(2,1)S(1)}, u32[]{:S(2)}, u32[]{:S(2)}) collective-permute-start(bf16[16,256]{1,0:T(8,128)(2,1)S(1)} %get-tuple-element.82), channel_id=1, source_target_pairs={{1,16},{2,17},{3,18},{4,19},{5,20},{6,21},{7,22},{8,23},{9,24},{10... | collective-permute-start | bytes 24584 | tf_op jit(solution)/shard_map/ppermute | solution.py:85
  32.4 7.7 %collective-permute-start.4 = (bf16[16,256]{1,0:T(8,128)(2,1)S(1)}, bf16[16,256]{1,0:T(8,128)(2,1)S(1)}, u32[]{:S(2)}, u32[]{:S(2)}) collective-permute-start(bf16[16,256]{1,0:T(8,128)(2,1)S(1)} %get-tuple-element.83), channel_id=1, source_target_pairs={{0,17},{1,18},{2,19},{3,20},{4,21},{5,22},{6,23},{7,24},{8,25},{9,... | collective-permute-start | bytes 24584 | tf_op jit(solution)/shard_map/ppermute | solution.py:85
  76.1 1.5 collective-permute-start.8
  79.1 4.5 %collective-permute-start.11 = (f32[3,8,256]{2,1,0:T(8,128)S(1)}, f32[3,8,256]{2,1,0:T(8,128)S(1)}, u32[]{:S(2)}, u32[]{:S(2)}) collective-permute-start(f32[3,8,256]{2,1,0:T(8,128)S(1)} %pad_maximum_fusion.1), channel_id=1, source_target_pairs={{0,96},{16,112},{32,0},{48,16},{64,32},{80,48},{96,64},{112,80},{1... | collective-permute-start | bytes 73736 | tf_op jit(solution)/shard_map/ppermute | solution.py:495
  82.7 4.2 %collective-permute-start.10 = (f32[3,8,256]{2,1,0:T(8,128)S(1)}, f32[3,8,256]{2,1,0:T(8,128)S(1)}, u32[]{:S(2)}, u32[]{:S(2)}) collective-permute-start(f32[3,8,256]{2,1,0:T(8,128)S(1)} %pad_maximum_fusion.1), channel_id=1, source_target_pairs={{0,64},{16,80},{32,96},{48,112},{64,0},{80,16},{96,32},{112,48},{1... | collective-permute-start | bytes 73736 | tf_op jit(solution)/shard_map/ppermute | solution.py:495
  82.7 4.2 %collective-permute-start.9 = (f32[3,8,256]{2,1,0:T(8,128)S(1)}, f32[3,8,256]{2,1,0:T(8,128)S(1)}, u32[]{:S(2)}, u32[]{:S(2)}) collective-permute-start(f32[3,8,256]{2,1,0:T(8,128)S(1)} %pad_maximum_fusion.1), channel_id=1, source_target_pairs={{0,32},{16,48},{32,64},{48,80},{64,96},{80,112},{96,0},{112,16},{1... | collective-permute-start | bytes 73736 | tf_op jit(solution)/shard_map/ppermute | solution.py:495
  86.9 8.4 %collective-permute-start.14 = (f32[3,8,256]{2,1,0:T(8,128)S(1)}, f32[3,8,256]{2,1,0:T(8,128)S(1)}, u32[]{:S(2)}, u32[]{:S(2)}) collective-permute-start(f32[3,8,256]{2,1,0:T(8,128)S(1)} %pad_maximum_fusion.2), channel_id=1, source_target_pairs={{0,3},{1,0},{2,1},{3,2},{4,7},{5,4},{6,5},{7,6},{8,11},{9,8},{10,9... | collective-permute-start | bytes 73736 | tf_op jit(solution)/shard_map/ppermute | solution.py:495
  94.3 4.2 %collective-permute-start.13 = (f32[3,8,256]{2,1,0:T(8,128)S(1)}, f32[3,8,256]{2,1,0:T(8,128)S(1)}, u32[]{:S(2)}, u32[]{:S(2)}) collective-permute-start(f32[3,8,256]{2,1,0:T(8,128)S(1)} %pad_maximum_fusion.2), channel_id=1, source_target_pairs={{0,2},{1,3},{2,0},{3,1},{4,6},{5,7},{6,4},{7,5},{8,10},{9,11},{10,... | collective-permute-start | bytes 73736 | tf_op jit(solution)/shard_map/ppermute | solution.py:495
  94.3 4.2 %collective-permute-start.12 = (f32[3,8,256]{2,1,0:T(8,128)S(1)}, f32[3,8,256]{2,1,0:T(8,128)S(1)}, u32[]{:S(2)}, u32[]{:S(2)}) collective-permute-start(f32[3,8,256]{2,1,0:T(8,128)S(1)} %pad_maximum_fusion.2), channel_id=1, source_target_pairs={{0,1},{1,2},{2,3},{3,0},{4,5},{5,6},{6,7},{7,4},{8,9},{9,10},{10,1... | collective-permute-start | bytes 73736 | tf_op jit(solution)/shard_map/ppermute | solution.py:495
  98.6 3.9 %collective-permute-start.17 = (f32[3,8,256]{2,1,0:T(8,128)S(1)}, f32[3,8,256]{2,1,0:T(8,128)S(1)}, u32[]{:S(2)}, u32[]{:S(2)}) collective-permute-start(f32[3,8,256]{2,1,0:T(8,128)S(1)} %pad_maximum_fusion.3), channel_id=1, source_target_pairs={{0,12},{1,13},{2,14},{3,15},{4,0},{5,1},{6,2},{7,3},{8,4},{9,5},{1... | collective-permute-start | bytes 73736 | tf_op jit(solution)/shard_map/ppermute | solution.py:495
  101.4 4.2 %collective-permute-start.16 = (f32[3,8,256]{2,1,0:T(8,128)S(1)}, f32[3,8,256]{2,1,0:T(8,128)S(1)}, u32[]{:S(2)}, u32[]{:S(2)}) collective-permute-start(f32[3,8,256]{2,1,0:T(8,128)S(1)} %pad_maximum_fusion.3), channel_id=1, source_target_pairs={{0,8},{1,9},{2,10},{3,11},{4,12},{5,13},{6,14},{7,15},{8,0},{9,1},... | collective-permute-start | bytes 73736 | tf_op jit(solution)/shard_map/ppermute | solution.py:495
  101.9 3.9 %collective-permute-start.15 = (f32[3,8,256]{2,1,0:T(8,128)S(1)}, f32[3,8,256]{2,1,0:T(8,128)S(1)}, u32[]{:S(2)}, u32[]{:S(2)}) collective-permute-start(f32[3,8,256]{2,1,0:T(8,128)S(1)} %pad_maximum_fusion.3), channel_id=1, source_target_pairs={{0,4},{1,5},{2,6},{3,7},{4,8},{5,9},{6,10},{7,11},{8,12},{9,13},{1... | collective-permute-start | bytes 73736 | tf_op jit(solution)/shard_map/ppermute | solution.py:495
  108.5 60.0 %copy-start = (f32[256,1024]{1,0:T(8,128)S(1)}, f32[256,1024]{1,0:T(8,128)}, u32[]{:S(2)}) copy-start(f32[256,1024]{1,0:T(8,128)} %get-tuple-element.40) | copy-start | bytes 3145732
  143.7 18.6 %collective-permute-start.25 = (bf16[16,256]{1,0:T(8,128)(2,1)S(1)}, bf16[16,256]{1,0:T(8,128)(2,1)S(1)}, u32[]{:S(2)}, u32[]{:S(2)}) collective-permute-start(bf16[16,256]{1,0:T(8,128)(2,1)S(1)} %get-tuple-element.76), channel_id=1, source_target_pairs={{17,0},{18,1},{19,2},{20,3},{21,4},{22,5},{23,6},{24,7},{25,8},{26... | collective-permute-start | bytes 24584 | tf_op jit(solution)/shard_map/ppermute | solution.py:85
  145.0 18.6 %collective-permute-start.24 = (bf16[16,256]{1,0:T(8,128)(2,1)S(1)}, bf16[16,256]{1,0:T(8,128)(2,1)S(1)}, u32[]{:S(2)}, u32[]{:S(2)}) collective-permute-start(bf16[16,256]{1,0:T(8,128)(2,1)S(1)} %get-tuple-element.77), channel_id=1, source_target_pairs={{16,1},{17,2},{18,3},{19,4},{20,5},{21,6},{22,7},{23,8},{24,9},{25... | collective-permute-start | bytes 24584 | tf_op jit(solution)/shard_map/ppermute | solution.py:85
  152.2 13.9 %collective-permute-start.23 = (bf16[16,256]{1,0:T(8,128)(2,1)S(1)}, bf16[16,256]{1,0:T(8,128)(2,1)S(1)}, u32[]{:S(2)}, u32[]{:S(2)}) collective-permute-start(bf16[16,256]{1,0:T(8,128)(2,1)S(1)} %get-tuple-element.78), channel_id=1, source_target_pairs={{1,16},{2,17},{3,18},{4,19},{5,20},{6,21},{7,22},{8,23},{9,24},{10... | collective-permute-start | bytes 24584 | tf_op jit(solution)/shard_map/ppermute | solution.py:85
  153.5 28.7 %collective-permute-start.22 = (bf16[16,256]{1,0:T(8,128)(2,1)S(1)}, bf16[16,256]{1,0:T(8,128)(2,1)S(1)}, u32[]{:S(2)}, u32[]{:S(2)}) collective-permute-start(bf16[16,256]{1,0:T(8,128)(2,1)S(1)} %get-tuple-element.79), channel_id=1, source_target_pairs={{0,17},{1,18},{2,19},{3,20},{4,21},{5,22},{6,23},{7,24},{8,25},{9,... | collective-permute-start | bytes 24584 | tf_op jit(solution)/shard_map/ppermute | solution.py:85
  159.3 22.9 %collective-permute-start.20 = (bf16[96,256]{1,0:T(8,128)(2,1)}, bf16[96,256]{1,0:T(8,128)(2,1)S(1)}, u32[]{:S(2)}, u32[]{:S(2)}) collective-permute-start(bf16[96,256]{1,0:T(8,128)(2,1)} %get-tuple-element.51), channel_id=1, source_target_pairs={{0,1},{1,2},{2,3},{3,4},{4,5},{5,6},{6,7},{7,8},{8,9},{9,10},{10,1... | collective-permute-start | bytes 147464 | tf_op jit(solution)/shard_map/ppermute | solution.py:85
  162.3 19.9 %collective-permute-start.21 = (bf16[96,256]{1,0:T(8,128)(2,1)}, bf16[96,256]{1,0:T(8,128)(2,1)S(1)}, u32[]{:S(2)}, u32[]{:S(2)}) collective-permute-start(bf16[96,256]{1,0:T(8,128)(2,1)} %get-tuple-element.52), channel_id=1, source_target_pairs={{1,0},{2,1},{3,2},{4,3},{5,4},{6,5},{7,6},{8,7},{9,8},{10,9},{11,1... | collective-permute-start | bytes 147464 | tf_op jit(solution)/shard_map/ppermute | solution.py:85
  163.6 18.6 %collective-permute-start.18 = (bf16[192,256]{1,0:T(8,128)(2,1)}, bf16[192,256]{1,0:T(8,128)(2,1)S(1)}, u32[]{:S(2)}, u32[]{:S(2)}) collective-permute-start(bf16[192,256]{1,0:T(8,128)(2,1)} %get-tuple-element.49), channel_id=1, source_target_pairs={{0,16},{1,17},{2,18},{3,19},{4,20},{5,21},{6,22},{7,23},{8,24},{9,... | collective-permute-start | bytes 294920 | tf_op jit(solution)/shard_map/ppermute | solution.py:85
  166.1 16.1 %collective-permute-start.19 = (bf16[192,256]{1,0:T(8,128)(2,1)}, bf16[192,256]{1,0:T(8,128)(2,1)S(1)}, u32[]{:S(2)}, u32[]{:S(2)}) collective-permute-start(bf16[192,256]{1,0:T(8,128)(2,1)} %get-tuple-element.50), channel_id=1, source_target_pairs={{16,0},{17,1},{18,2},{19,3},{20,4},{21,5},{22,6},{23,7},{24,8},{25... | collective-permute-start | bytes 294920 | tf_op jit(solution)/shard_map/ppermute | solution.py:85
  168.9 41.5 %copy-start.1 = (f32[256,1024]{1,0:T(8,128)S(1)}, f32[256,1024]{1,0:T(8,128)}, u32[]{:S(2)}) copy-start(f32[256,1024]{1,0:T(8,128)} %get-tuple-element.45) | copy-start | bytes 3145732
  196.7 23.7 %all-to-all-start.2 = ((f32[128,1,256]{2,1,0:T(1,128)}), f32[128,1,256]{2,1,0:T(1,128)S(1)}, u32[]{:S(2)}, u32[]{:S(2)}) async-start(f32[128,1,256]{2,1,0:T(1,128)} %all_to_all.23), calls=%async_computation.2 | async-start | bytes 262144 | tf_op jit(solution)/shard_map/all_to_all | solution.py:510
  220.5 57.6 %all-to-all-start = ((f32[128,8,1024]{2,1,0:T(8,128)}), f32[128,8,1024]{2,1,0:T(8,128)}, u32[]{:S(2)}, u32[]{:S(2)}) async-start(f32[128,8,1024]{2,1,0:T(8,128)} %maximum_bitcast_fusion), calls=%async_computation | async-start | bytes 8388608 | tf_op jit(solution)/shard_map/all_to_all | solution.py:510
  278.8 14.3 %all-to-all-start.3 = ((f32[128,1,256]{2,1,0:T(1,128)}), f32[128,1,256]{2,1,0:T(1,128)S(1)}, u32[]{:S(2)}, u32[]{:S(2)}) async-start(f32[128,1,256]{2,1,0:T(1,128)} %reshape.80), calls=%async_computation.3 | async-start | bytes 262144 | tf_op jit(solution)/shard_map/all_to_all | solution.py:513
  295.6 57.6 %all-to-all-start.1 = ((f32[128,8,1024]{2,1,0:T(8,128)}), f32[128,8,1024]{2,1,0:T(8,128)}, u32[]{:S(2)}, u32[]{:S(2)}) async-start(f32[128,8,1024]{2,1,0:T(8,128)} %broadcast_in_dim.2), calls=%async_computation.1 | async-start | bytes 8388608 | tf_op jit(solution)/shard_map/all_to_all | solution.py:513
  (18 other events, 164.7 us)

commit v2 on v1

--- a/solution.py
+++ b/solution.py
@@ -1,10 +1,9 @@
-import functools
-
 import jax
 import jax.numpy as jnp
 from jax import lax
 from jax.experimental import pallas as pl
 from jax.experimental.pallas import tpu as pltpu
+from jax.sharding import Mesh
 from jax.sharding import PartitionSpec as P
 
 PATCH = 4
@@ -22,6 +21,9 @@
 CH = 256
 TOK = ROWS * COLS
 WIDE = 14
+WIRE = BF
+ROW_AXES = ("z", "core")
+COL_AXES = ("x", "y")
 VMEM = pltpu.CompilerParams(vmem_limit_bytes=58 << 20)
 
 
@@ -33,9 +35,7 @@
     return lax.broadcasted_iota(jnp.int32, shape, dim)
 
 
-def write_edges(src, top, bot, left, right, corners, l_sc, r_sc, c_sc):
-    top[...] = src[0 : HALO * COLS, :]
-    bot[...] = src[TOK - HALO * COLS : TOK, :]
+def write_edges(src, top, bot, left, right, l_sc, r_sc, c_sc):
     for a in range(ROWS):
         low = src[a * COLS : a * COLS + 32, :].astype(F32)
         high = src[a * COLS + 32 : a * COLS + 64, :].astype(F32)
@@ -54,15 +54,19 @@
             c_sc[1, row : row + 1, :] = r_sc[first : first + 1, :]
             c_sc[2, row : row + 1, :] = l_sc[last : last + 1, :]
             c_sc[3, row : row + 1, :] = r_sc[last : last + 1, :]
-    corners[...] = c_sc[...].astype(BF)
+    side = HALO * COLS
+    top[:side, :] = src[0:side, :]
+    bot[:side, :] = src[TOK - side : TOK, :]
+    for n, ref in enumerate((top, bot)):
+        ref[side : side + 16, :] = c_sc[2 * n].astype(BF)
+        ref[side + 16 : side + 32, :] = c_sc[2 * n + 1].astype(BF)
 
 
 EDGE_SHAPES = [
-    jax.ShapeDtypeStruct((HALO * COLS, CH), BF),
-    jax.ShapeDtypeStruct((HALO * COLS, CH), BF),
+    jax.ShapeDtypeStruct((HALO * COLS + 32, CH), BF),
+    jax.ShapeDtypeStruct((HALO * COLS + 32, CH), BF),
     jax.ShapeDtypeStruct((HALO * ROWS, CH), BF),
     jax.ShapeDtypeStruct((HALO * ROWS, CH), BF),
-    jax.ShapeDtypeStruct((4, 16, CH), BF),
 ]
 EDGE_SCRATCH = [
     pltpu.VMEM((HALO * ROWS, CH), F32),
@@ -71,37 +75,33 @@
 ]
 
 
-def exchange(edges):
-    top, bot, left, right, corners = edges
-    n_r, n_c = lax.axis_size("rows"), lax.axis_size("cols")
-
-    def move(x, d_r, d_c):
-        pairs = [
-            (r * n_c + c, (r + d_r) * n_c + c + d_c)
-            for r in range(n_r)
-            for c in range(n_c)
-            if 0 <= r + d_r < n_r and 0 <= c + d_c < n_c
-        ]
-        return lax.ppermute(x, ("rows", "cols"), pairs)
-
-    return (
-        move(bot, 1, 0),
-        move(top, -1, 0),
-        move(right, 0, 1),
-        move(left, 0, -1),
-        move(corners[3], 1, 1),
-        move(corners[2], 1, -1),
-        move(corners[1], -1, 1),
-        move(corners[0], -1, -1),
-    )
+def exchange_rows(edges):
+    top, bot = edges[:2]
+    n = lax.axis_size(ROW_AXES)
+    above = lax.ppermute(bot, ROW_AXES, [(i, i + 1) for i in range(n - 1)])
+    below = lax.ppermute(top, ROW_AXES, [(i + 1, i) for i in range(n - 1)])
+    return above, below
+
+
+def exchange_cols(edges, above, below):
+    left, right = edges[2:]
+    n = lax.axis_size(COL_AXES)
+    side = HALO * COLS
+    right = jnp.concatenate([right, above[side + 16 : side + 32], below[side + 16 : side + 32]])
+    left = jnp.concatenate([left, above[side : side + 16], below[side : side + 16]])
+    from_left = lax.ppermute(right, COL_AXES, [(i, i + 1) for i in range(n - 1)])
+    from_right = lax.ppermute(left, COL_AXES, [(i + 1, i) for i in range(n - 1)])
+    return from_left, from_right
 
 
 def assemble(wide, own, halo, l_sc, r_sc, c_sc):
-    above, below, left, right, tl, tr, bl, br = halo
-    l_sc[...] = left[...].astype(F32)
-    r_sc[...] = right[...].astype(F32)
-    for n, ref in enumerate((tl, tr, bl, br)):
-        c_sc[n] = ref[...].astype(F32)
+    above, below, left, right = halo
+    edge = HALO * ROWS
+    l_sc[...] = left[:edge, :].astype(F32)
+    r_sc[...] = right[:edge, :].astype(F32)
+    for n in range(2):
+        c_sc[2 * n] = left[edge + 16 * n : edge + 16 * (n + 1), :].astype(F32)
+        c_sc[2 * n + 1] = right[edge + 16 * n : edge + 16 * (n + 1), :].astype(F32)
     sub = iota((8, CH), 0)
 
     def put(row, x, lefts, rights):
@@ -163,7 +163,7 @@
     return centre * inverse, inverse
 
 
-def embed_kernel(pixels, weights, bias, emb, z_ref, top, bot, left, right, corners, w_sc, l_sc, r_sc, c_sc):
+def embed_kernel(pixels, weights, bias, emb, z_ref, top, bot, left, right, w_sc, l_sc, r_sc, c_sc):
     out = iota((256, 256), 0)
     spread = (((out & 7) * 8 + ((out >> 3) & 7)) * 4 + (out >> 6)) == iota((256, 256), 1)
     spread = jnp.where(spread, 1.0, 0.0).astype(BF)
@@ -189,7 +189,7 @@
         for g in range(4):
             a = g * 8 + a8
             emb[a * COLS : (a + 1) * COLS, :] = block[g * 64 : (g + 1) * 64, :]
-    write_edges(emb, top, bot, left, right, corners, l_sc, r_sc, c_sc)
+    write_edges(emb, top, bot, left, right, l_sc, r_sc, c_sc)
 
 
 def embed(pixels, patch_weight, patch_bias):
@@ -209,8 +209,8 @@
     return outs[0], outs[1], outs[2:]
 
 
-def conv_kernel_body(emb, above, below, lh, rh, tl, tr, bl, br, kern, gain, wide, mixed, normed, w_sc, l_sc, r_sc, c_sc):
-    assemble(wide, emb, (above, below, lh, rh, tl, tr, bl, br), l_sc, r_sc, c_sc)
+def conv_kernel_body(emb, above, below, lh, rh, kern, gain, wide, mixed, normed, w_sc, l_sc, r_sc, c_sc):
+    assemble(wide, emb, (above, below, lh, rh), l_sc, r_sc, c_sc)
     spread_weights(kern, w_sc)
 
     def body(a, carry):
@@ -248,6 +248,7 @@
 
 CHUNK = 512
 SCALE = 128**-0.5
+COST = pl.CostEstimate(flops=14_000_000_000, transcendentals=0, bytes_accessed=16_000_000)
 
 
 def attend_kernel(normed, wk, wv, q, up, k_out, v_out, weighted, stats, s_sc):
@@ -270,7 +271,7 @@
         p = jnp.exp(s_sc[rows, :] - peak)
         total = total + jnp.sum(p, axis=0, keepdims=True)
         acc = acc + dot(v_out[rows, :], p.astype(BF), TN)
-    weighted[...] = acc.T
+    weighted[0] = acc.T
     dots = jnp.sum(acc * up[...].astype(F32).T, axis=0, keepdims=True)
     stats[0, pl.ds(h, 1), :] = peak
     stats[1, pl.ds(h, 1), :] = total
@@ -300,13 +301,13 @@
         out_specs=[
             column(TOK, 128),
             column(TOK, 128),
-            column(256, 128),
+            pl.BlockSpec((1, 256, 128), lambda h: (h, 0, 0)),
             whole((3, HEADS, 256)),
         ],
         out_shape=[
             jax.ShapeDtypeStruct((TOK, 1024), BF),
             jax.ShapeDtypeStruct((TOK, 1024), BF),
-            jax.ShapeDtypeStruct((256, 1024), F32),
+            jax.ShapeDtypeStruct((HEADS, 256, 128), F32),
             jax.ShapeDtypeStruct((3, HEADS, 256), F32),
         ],
         scratch_shapes=[pltpu.VMEM((TOK, 256), F32)],
@@ -314,18 +315,7 @@
     )(normed, kv_weight, kv_weight, latents, d_attended)
 
 
-def attend_grad_kernel(
-    normed, k_in, v_in, wk, wv, q, up, lse, dots, mixed, gain,
-    q_grad, k_weight, v_weight, d_mixed, gain_grad, top, bot, left, right, corners,
-    dn_sc, nt_sc, l_sc, r_sc, c_sc,
-):
-    h = pl.program_id(0)
-
-    @pl.when(h == 0)
-    def _():
-        nt_sc[...] = normed[...].astype(F32).T.astype(BF)
-        dn_sc[...] = jnp.zeros_like(dn_sc)
-
+def head_grads(h, normed, k_in, v_in, wk, wv, q, up, lse, dots, grads, dn_sc, nt_sc):
     w = jnp.concatenate([wk[...], wv[...]], axis=1)
     level = lse[pl.ds(h, 1), :]
     row_dots = dots[pl.ds(h, 1), :]
@@ -343,11 +333,35 @@
         d_proj = jnp.concatenate([kg, vg], axis=1)
         wg = wg + dot(nt_sc[:, rows], d_proj)
         dn_sc[rows, :] += dot(d_proj, w, NT)
-    q_grad[...] = qg.T
-    k_weight[...] = wg[:, :128]
-    v_weight[...] = wg[:, 128:]
-
-    @pl.when(h == HEADS - 1)
+    grads[0, 0] = qg.T
+    grads[1, 0] = wg[:, :128]
+    grads[2, 0] = wg[:, 128:]
+
+
+def first_half_kernel(normed, k_in, v_in, wk, wv, q, up, lse, dots, grads, dn, nt):
+    h = pl.program_id(0)
+
+    @pl.when(h == 0)
+    def _():
+        nt[...] = normed[...].astype(F32).T.astype(BF)
+        dn[...] = jnp.zeros_like(dn)
+
+    head_grads(h, normed, k_in, v_in, wk, wv, q, up, lse, dots, grads, dn, nt)
+
+
+def second_half_kernel(
+    nt, k_in, v_in, wk, wv, q, up, lse, dots, dn_in, mixed, gain,
+    grads, d_mixed, gain_grad, top, bot, left, right, dn_sc, l_sc, r_sc, c_sc,
+):
+    h = pl.program_id(0)
+
+    @pl.when(h == 0)
+    def _():
+        dn_sc[...] = dn_in[...]
+
+    head_grads(h + HEADS // 2, None, k_in, v_in, wk, wv, q, up, lse, dots, grads, dn_sc, nt)
+
+    @pl.when(h == HEADS // 2 - 1)
     def _():
         def body(a, total):
             rows = pl.ds(pl.multiple_of(a * COLS, COLS), COLS)
@@ -361,41 +375,67 @@
             return total
 
         gain_grad[...] = lax.fori_loop(0, ROWS, body, jnp.zeros((1, CH), F32))
-        write_edges(d_mixed, top, bot, left, right, corners, l_sc, r_sc, c_sc)
-
-
-def attend_grad(normed, k, v, kv_weight, latents, d_attended, lse, dots, mixed, gain):
+        write_edges(d_mixed, top, bot, left, right, l_sc, r_sc, c_sc)
+
+
+HALF = HEADS // 2
+
+
+def head_specs(first):
+    return [
+        column(TOK, 128, first),
+        column(TOK, 128, first),
+        column(CH, 128, first),
+        column(CH, 128, HEADS + first),
+        column(256, 128, first),
+        column(256, 128, first),
+        whole((HEADS, 256)),
+        whole((HEADS, 256)),
+    ]
+
+
+GRADS_SPEC = pl.BlockSpec((3, 1, 256, 128), lambda h: (0, h, 0, 0))
+GRADS = jax.ShapeDtypeStruct((3, HALF, 256, 128), F32)
+
+
+def first_half(normed, k, v, kv_weight, latents, d_attended, lse, dots):
+    return pl.pallas_call(
+        first_half_kernel,
+        name="first_half",
+        grid=(HALF,),
+        in_specs=[whole((TOK, CH))] + head_specs(0),
+        out_specs=[GRADS_SPEC, whole((TOK, CH)), whole((CH, TOK))],
+        out_shape=[
+            GRADS,
+            jax.ShapeDtypeStruct((TOK, CH), F32),
+            jax.ShapeDtypeStruct((CH, TOK), BF),
+        ],
+        compiler_params=VMEM,
+        cost_estimate=COST,
+    )(normed, k, v, kv_weight, kv_weight, latents, d_attended, lse, dots)
+
+
+def second_half(nt, k, v, kv_weight, latents, d_attended, lse, dots, dn, mixed, gain):
     outs = pl.pallas_call(
-        attend_grad_kernel,
-        name="attend_grad",
-        grid=(HEADS,),
-        in_specs=[
-            whole((TOK, CH)),
-            column(TOK, 128),
-            column(TOK, 128),
-            column(CH, 128),
-            column(CH, 128, HEADS),
-            column(256, 128),
-            column(256, 128),
-            whole((HEADS, 256)),
-            whole((HEADS, 256)),
-            whole((TOK, CH)),
-            whole((1, CH)),
-        ],
-        out_specs=[column(256, 128), column(CH, 128), column(CH, 128), whole((TOK, CH)), whole((1, CH))]
+        second_half_kernel,
+        name="second_half",
+        grid=(HALF,),
+        in_specs=[whole((CH, TOK))]
+        + head_specs(HALF)
+        + [whole((TOK, CH)), whole((TOK, CH)), whole((1, CH))],
+        out_specs=[GRADS_SPEC, whole((TOK, CH)), whole((1, CH))]
         + [whole(s.shape) for s in EDGE_SHAPES],
         out_shape=[
-            jax.ShapeDtypeStruct((256, 1024), F32),
-            jax.ShapeDtypeStruct((CH, 1024), F32),
-            jax.ShapeDtypeStruct((CH, 1024), F32),
+            GRADS,
             jax.ShapeDtypeStruct((TOK, CH), BF),
             jax.ShapeDtypeStruct((1, CH), F32),
         ]
         + EDGE_SHAPES,
-        scratch_shapes=[pltpu.VMEM((TOK, CH), F32), pltpu.VMEM((CH, TOK), BF)] + EDGE_SCRATCH,
+        scratch_shapes=[pltpu.VMEM((TOK, CH), F32)] + EDGE_SCRATCH,
         compiler_params=VMEM,
-    )(normed, k, v, kv_weight, kv_weight, latents, d_attended, lse, dots, mixed, gain)
-    return outs[:5], outs[5:]
+        cost_estimate=COST,
+    )(nt, k, v, kv_weight, kv_weight, latents, d_attended, lse, dots, dn, mixed, gain)
+    return outs[:3], outs[3:]
 
 
 def kernel_grad_body(wide, d_mixed, out, d_sc):
@@ -428,11 +468,12 @@
         out_shape=jax.ShapeDtypeStruct((KSIZE * KSIZE, CH), F32),
         scratch_shapes=[pltpu.VMEM((TOK, CH), F32)],
         compiler_params=VMEM,
+        cost_estimate=COST,
     )(wide, d_mixed)
 
 
-def conv_back_body(d_mixed, above, below, lh, rh, tl, tr, bl, br, kern, z, patch_grad, bias_grad, wide, d_sc, w_sc, l_sc, r_sc, c_sc):
-    assemble(wide, d_mixed, (above, below, lh, rh, tl, tr, bl, br), l_sc, r_sc, c_sc)
+def conv_back_body(d_mixed, above, below, lh, rh, kern, z, patch_grad, bias_grad, wide, d_sc, w_sc, l_sc, r_sc, c_sc):
+    assemble(wide, d_mixed, (above, below, lh, rh), l_sc, r_sc, c_sc)
     spread_weights(kern, w_sc)
     zero = jnp.zeros((8, 128), F32)
 
@@ -470,47 +511,72 @@
         ]
         + EDGE_SCRATCH,
         compiler_params=VMEM,
+        cost_estimate=COST,
     )(d_mixed, *halo, conv_kernel, z)
 
 
-def rings():
-    n_r, n_c = lax.axis_size("rows"), lax.axis_size("cols")
-    side = 4
-    out = []
-    for axis, size, inner in (("rows", 2, 1), ("rows", n_r // 2, 2), ("cols", side, 1), ("cols", n_c // side, side)):
-        total = lax.axis_size(axis)
-        shifts = []
-        for d in range(1, size):
-            pairs = []
-            for i in range(total):
-                pos = i // inner % size
-                pairs.append((i, i + ((pos + d) % size - pos) * inner))
-            shifts.append(pairs)
-        out.append((axis, shifts))
-    return out
+CHIPS = ("z", "x", "y")
+PAIR = [(0, 1), (1, 0)]
+
+
+def gather(x, axes):
+    n = lax.axis_size(axes)
+    copies = jnp.broadcast_to(x[None], (n,) + x.shape)
+    return lax.all_to_all(copies, axes, 0, 0, tiled=True)
 
 
 def combine_stats(stats):
-    for axis, shifts in rings():
-        group = [stats] + [lax.ppermute(stats, axis, pairs) for pairs in shifts]
-        peak = functools.reduce(jnp.maximum, [g[0] for g in group])
-        factors = [jnp.exp(g[0] - peak) for g in group]
-        total = sum(g[1] * f for g, f in zip(group, factors))
-        dots = sum(g[2] * f for g, f in zip(group, factors))
+    for axes in (("z", "core"), ("x", "y")):
+        group = gather(stats, axes)
+        peak = jnp.max(group[:, 0], axis=0)
+        factors = jnp.exp(group[:, 0] - peak)
+        total = jnp.sum(group[:, 1] * factors, axis=0)
+        dots = jnp.sum(group[:, 2] * factors, axis=0)
         stats = jnp.stack([peak, total, dots])
     return stats
 
 
-AXES = ("rows", "cols")
-
-
-def all_sum(x):
-    count = lax.axis_size(AXES)
-    rows = x.shape[0] // count
-    parts = lax.all_to_all(x, AXES, 0, 0, tiled=True)
-    mine = jnp.sum(parts.reshape(count, rows, -1), axis=0)
-    copies = jnp.broadcast_to(mine[None], (count,) + mine.shape).reshape(x.shape)
-    return lax.all_to_all(copies, AXES, 0, 0, tiled=True)
+def pair_sum(x):
+    core = lax.axis_index("core")
+    keep = lax.dynamic_index_in_dim(x, core, 0, keepdims=False)
+    send = lax.dynamic_index_in_dim(x, 1 - core, 0, keepdims=False)
+    return (keep + lax.ppermute(send, "core", PAIR)).astype(WIRE)
+
+
+def swap(half):
+    other = lax.ppermute(half, "core", PAIR)
+    first = lax.axis_index("core") == 0
+    return jnp.stack([jnp.where(first, half, other), jnp.where(first, other, half)]).astype(F32)
+
+
+def block_sum(parts):
+    return jnp.sum(parts.astype(F32), axis=0)
+
+
+def copies(x):
+    return jnp.broadcast_to(x.astype(WIRE)[None], (64,) + x.shape)
+
+
+def send(x):
+    return lax.all_to_all(x, CHIPS, 0, 0, tiled=True)
+
+
+def small_sum(x):
+    x = x + lax.ppermute(x, "core", PAIR)
+    x = jnp.sum(gather(x, ("z",)), axis=0)
+    return jnp.sum(gather(x, ("x", "y")), axis=0)
+
+
+def blocks(x):
+    return x.reshape(2, 64, -1, x.shape[-1])
+
+
+def tie(x, *others):
+    return lax.optimization_barrier((x,) + others)
+
+
+def columns(x):
+    return x.transpose(1, 0, 2).reshape(256, -1)
 
 
 def per_device(
@@ -518,27 +584,56 @@
 ):
     gain = norm_gain.reshape(1, CH)
     emb, z, edges = embed(pixels, patch_weight, patch_bias)
-    wide, mixed, normed = conv_forward(emb, exchange(edges), conv_kernel, gain)
+    rows = exchange_rows(edges)
+    halo = rows + exchange_cols(edges, *rows)
+    wide, mixed, normed = conv_forward(emb, halo, conv_kernel, gain)
     k, v, weighted, local = attend(normed, kv_weight, latents, d_attended)
     stats = combine_stats(local)
     lse = stats[0] + jnp.log(stats[1])
     row_dots = stats[2] / stats[1]
-    factor = (jnp.exp(local[0] - stats[0]) / stats[1]).T
-    attended = (weighted.reshape(256, HEADS, 128) * factor[:, :, None]).reshape(256, 1024)
-    (q_grad, k_weight, v_weight, d_mixed, gain_grad), d_edges = attend_grad(
-        normed, k, v, kv_weight, latents, d_attended, lse, row_dots, mixed, gain
+    factor = jnp.exp(local[0] - stats[0]) / stats[1]
+    attended = pair_sum(blocks((weighted * factor[:, :, None]).reshape(2048, 128)))
+    lse, attended = tie(lse, attended)
+    attended = send(attended)
+    grads_a, dn, nt = first_half(normed, k, v, kv_weight, latents, d_attended, lse, row_dots)
+    dn, nt, grads_a, attended = tie(dn, nt, grads_a, attended)
+    sums_a = pair_sum(blocks(grads_a.reshape(3072, 128)))
+    message = jnp.concatenate([sums_a, copies(block_sum(attended))], axis=1)
+    dn, message = tie(dn, message)
+    message = send(message)
+    (grads_b, d_mixed, gain_grad), d_edges = second_half(
+        nt, k, v, kv_weight, latents, d_attended, lse, row_dots, dn, mixed, gain
     )
-    big = all_sum(jnp.concatenate([attended, q_grad, k_weight, v_weight], axis=0))
-    halo = exchange(d_edges)
+    grads_b, d_mixed, message, *d_edges = tie(grads_b, d_mixed, message, *d_edges)
+    attended = message[:, 24:]
+    d_rows = exchange_rows(d_edges)
+    sums_b = pair_sum(blocks(grads_b.reshape(3072, 128)))
+    message = jnp.concatenate([sums_b, copies(block_sum(message[:, :24]))], axis=1)
+    d_mixed, message, *d_rows = tie(d_mixed, message, *d_rows)
+    message = send(message)
+    d_cols = exchange_cols(d_edges, *d_rows)
     kern = kernel_grad(wide, d_mixed)
-    patch, bias = conv_back(d_mixed, halo, conv_kernel, z)
+    d_mixed, message, kern, *d_cols = tie(d_mixed, message, kern, *d_cols)
+    grads_a = message[:, 24:]
+    grads_b = copies(block_sum(message[:, :24]))
+    d_mixed, grads_b = tie(d_mixed, grads_b)
+    grads_b = send(grads_b)
+    patch, bias = conv_back(d_mixed, tuple(d_rows) + tuple(d_cols), conv_kernel, z)
+    patch, bias, grads_b = tie(patch, bias, grads_b)
     small = jnp.concatenate([patch.reshape(64, CH), kern, gain_grad, bias], axis=0)
-    small = all_sum(jnp.pad(small, ((0, 128 - small.shape[0]), (0, 0))))
+    small = small_sum(jnp.pad(small, ((0, 5), (0, 0))))
+    attended = swap(attended)
+    grads = [
+        jnp.concatenate([a, b], axis=0)
+        for a, b in zip(
+            swap(grads_a).reshape(3, HALF, 256, 128), swap(grads_b).reshape(3, HALF, 256, 128)
+        )
+    ]
     patch = small[:64].reshape(4, 16, CH)[:, :12].transpose(1, 0, 2).reshape(48, CH)
     return (
-        big[:256],
-        big[256:512],
-        jnp.concatenate([big[512:768], big[768:]], axis=1),
+        columns(attended.reshape(HEADS, 256, 128)),
+        columns(grads[0]),
+        columns(jnp.concatenate([grads[1], grads[2]], axis=0)),
         small[64 + 49],
         small[64 : 64 + 49],
         patch,
@@ -547,10 +642,11 @@
 
 
 def solution(mesh):
+    split = Mesh(mesh.devices.reshape(4, 2, 4, 4), ("z", "core", "x", "y"))
     return jax.shard_map(
         per_device,
-        mesh=mesh,
-        in_specs=(P(None, "rows", "cols"), P(), P(), P(), P(), P(), P(), P()),
+        mesh=split,
+        in_specs=(P(None, ("z", "core"), ("x", "y")), P(), P(), P(), P(), P(), P(), P()),
         out_specs=(P(), P(), P(), P(), P(), P(), P()),
         check_vma=False,
     )

time: 360 us -> 280 us (0.78); the launches traced: 359 us -> 275 us
  waiting for transfers between devices: 139 us -> 46.6 us
  blocking collectives: 0 us -> 11 us
  starting transfers between devices: 92.3 us -> 82.2 us
  local copies, waits for them, and re-layouts: 14.5 us -> 20.2 us
  Pallas kernels: 98.2 us -> 102 us
    all_to_all x4 -> x7, waiting for transfers between devices: 117 us -> 28.3 us  [the longest x3 28.3 us: gather(): return lax.all_to_all(copies, axes, 0, 0, tiled=True)]
    ppermute x26 -> x15, starting transfers between devices: 64.1 us -> 27.9 us  [the longest x2 7.86 us: exchange_rows(): above = lax.ppermute(bot, ROW_AXES, [(i, i + 1) for i in range(n - 1)])]
    all_to_all x4 -> x7, starting transfers between devices: 28.2 us -> 54.4 us  [the longest x4 35.8 us: send(): return lax.all_to_all(x, CHIPS, 0, 0, tiled=True)]
    all_to_all x0 -> x1, blocking collectives: none -> 11 us  [gather(): return lax.all_to_all(copies, axes, 0, 0, tiled=True)]
    unnamed x42 -> x33, local copies, waits for them, and re-layouts: 1.95 us -> 6.77 us
    pallas_call x1 -> x2, Pallas kernels: 34.4 us -> 38.6 us  [the longest x1 23.7 us: second_half(): pl.pallas_call(second_half_kernel, name='second_half', grid=(HALF,), in_s...]
    ppermute x26 -> x15, waiting for transfers between devices: 22.5 us -> 18.3 us  [the longest x2 7.37 us: exchange_rows(): below = lax.ppermute(top, ROW_AXES, [(i + 1, i) for i in range(n - 1)])]
    slice x1 -> x5, local copies, waits for them, and re-layouts: 3.94 us -> 0.07 us  [the longest x1 0.04 us: per_device(): grads_a = message[:, 24:]]
  transfers between devices with their start and end apart: 30 -> 22, of which waited for: 15 -> 12; matrix products, arithmetic and copies ran while one was open for 3% -> 5% of each run, Pallas kernels for 4% -> 23%
where the time goes in v2:
time: 280 us; the launch traced here: 275 us
  Pallas kernels  102 us (36%)
  starting transfers between devices  82.2 us (29%)
  waiting for transfers between devices  46.6 us (17%)
  local copies, waits for them, and re-layouts  20.2 us (7%)
  blocking collectives  11 us (4%)
  other arithmetic  10.9 us (4%)
    all_to_all x4, starting transfers between devices, send(): return lax.all_to_all(x, CHIPS, 0, 0, tiled=True)  35.8 us
    all_to_all x3, waiting for transfers between devices, gather(): return lax.all_to_all(copies, axes, 0, 0, tiled=True)  28.3 us
    pallas_call x1, Pallas kernels, second_half(): pl.pallas_call(second_half_kernel, name='second_half', grid=(HALF,), in_s...  23.7 us
    all_to_all x3, starting transfers between devices, gather(): return lax.all_to_all(copies, axes, 0, 0, tiled=True)  18.6 us
    pallas_call x1, Pallas kernels, attend(): pl.pallas_call(attend_kernel, name='attend', grid=(HEADS,), in_specs=[who...  17.8 us
    pallas_call x1, Pallas kernels, conv_forward(): pl.pallas_call(conv_kernel_body, name='conv_forward', out_shape=[jax.Shap...  17.6 us
    pallas_call x1, Pallas kernels, first_half(): pl.pallas_call(first_half_kernel, name='first_half', grid=(HALF,), in_spe...  14.9 us
    pallas_call x1, Pallas kernels, kernel_grad(): pl.pallas_call(kernel_grad_body, name='kernel_grad', out_shape=jax.ShapeD...  13.1 us
  transfers between devices with their start and end apart: 22, of which 12 were waited for; matrix products, arithmetic and copies ran while one was open for 5% of the time, Pallas kernels for 23%

profile of v2, /device:TPU:1, one launch (start us, length us, event | category | flops | bytes accessed | tf_op | source)
XLA Modules:
  0.0 274.6 jit_solution(16024447449932579760)
XLA Ops:
  2.0 3.2 %embed.1 = (bf16[2048,256]{1,0:T(8,128)(2,1)}, bf16[256,512]{1,0:T(8,128)(2,1)}, bf16[224,256]{1,0:T(8,128)(2,1)}, bf16[224,256]{1,0:T(8,128)(2,1)}, bf16[96,256]{1,0:T(8,128)(2,1)}, /*index=5*/bf16[96,256]{1,0:T(8,128)(2,1)}) custom-call(bf16[384,256]{1,0:T(8,128)(2,1)} %bitcast.146, bf16[4,16,256]{2,1,0:T(8,128)(2,1)} %pad.8.weights, f32[1,256]{1,0:T(1,128)} %bitcast.151), custom_call_target="tpu_custom_call" | custom-call | tf_op jit(solution)/shard_map/embed/pallas_call | solution.py:198
  5.2 4.9 %collective-permute-start = (bf16[224,256]{1,0:T(8,128)(2,1)}, bf16[224,256]{1,0:T(8,128)(2,1)S(1)}, u32[]{:S(2)}, u32[]{:S(2)}) collective-permute-start(bf16[224,256]{1,0:T(8,128)(2,1)} %get-tuple-element.62), channel_id=1, source_target_pairs={{0,16},{16,32},{32,48},{48,64},{64,80},{80,96},{96,112},{1,17},{17... | collective-permute-start | bytes 344072 | tf_op jit(solution)/shard_map/ppermute | solution.py:81
  10.1 1.9 collective-permute-start.1
  12.2 4.2 %collective-permute-done.1.below = bf16[224,256]{1,0:T(8,128)(2,1)S(1)} collective-permute-done((bf16[224,256]{1,0:T(8,128)(2,1)}, bf16[224,256]{1,0:T(8,128)(2,1)S(1)}, u32[]{:S(2)}, u32[]{:S(2)}) %collective-permute-start.1) | collective-permute-done | bytes 114720 | tf_op jit(solution)/shard_map/ppermute | solution.py:82
  17.2 3.2 %collective-permute-start.2 = (bf16[128,256]{1,0:T(8,128)(2,1)S(1)}, bf16[128,256]{1,0:T(8,128)(2,1)S(1)}, u32[]{:S(2)}, u32[]{:S(2)}) collective-permute-start(bf16[128,256]{1,0:T(8,128)(2,1)S(1)} %pad_maximum_fusion.5), channel_id=1, source_target_pairs={{0,1},{1,2},{2,3},{3,4},{4,5},{5,6},{6,7},{7,8},{8,9},{9,10},{10,1... | collective-permute-start | bytes 196616 | tf_op jit(solution)/shard_map/ppermute | solution.py:92
  22.6 3.7 %collective-permute-done.3.rh = bf16[128,256]{1,0:T(8,128)(2,1)S(1)} collective-permute-done((bf16[128,256]{1,0:T(8,128)(2,1)S(1)}, bf16[128,256]{1,0:T(8,128)(2,1)S(1)}, u32[]{:S(2)}, u32[]{:S(2)}) %collective-permute-start.3) | collective-permute-done | bytes 65568 | tf_op jit(solution)/shard_map/ppermute | solution.py:93
  26.9 17.6 %conv_forward.1 = (f32[38,14,8,256]{3,2,1,0:T(8,128)}, f32[2048,256]{1,0:T(8,128)}, bf16[2048,256]{1,0:T(8,128)(2,1)}) custom-call(bf16[2048,256]{1,0:T(8,128)(2,1)} %get-tuple-element.61.emb, bf16[224,256]{1,0:T(8,128)(2,1)} %copy-done.4, bf16[224,256]{1,0:T(8,128)(2,1)} %copy-done.5, bf16[128,256]{1,0:T(8,128)(2,1)} %copy-done.6, ...), custom_call_target="tpu_custom_call" | custom-call | tf_op jit(solution)/shard_map/conv_forward/pallas_call | solution.py:236
  44.4 17.8 %attend.1 = (bf16[2048,1024]{1,0:T(8,128)(2,1)}, bf16[2048,1024]{1,0:T(8,128)(2,1)}, f32[8,256,128]{2,1,0:T(8,128)}, f32[3,8,256]{2,1,0:T(8,128)}) custom-call(bf16[2048,256]{1,0:T(8,128)(2,1)} %get-tuple-element.66.normed, bf16[256,2048]{1,0:T(8,128)(2,1)} %wv.5, bf16[256,2048]{1,0:T(8,128)(2,1)} %wv.5, bf16[256,1024]{1,0:T(8,128)(2,1)} %q.5, ...), custom_call_target="tpu_custom_call" | custom-call | tf_op jit(solution)/shard_map/attend/pallas_call | solution.py:290
  63.1 11.0 %all_to_all.40 = f32[8,3,8,256]{3,2,1,0:T(8,128)S(1)} all-to-all(f32[8,3,8,256]{3,2,1,0:T(8,128)S(1)} %broadcast_in_dim.14), channel_id=1, replica_groups=mesh['z'=4,'core'=2,'x'=4,'y'=4] {'z','core'}, dimensions={0} | all-to-all | bytes 393216 | tf_op jit(solution)/shard_map/all_to_all | solution.py:525
  74.9 8.0 %all-to-all-start.1 = ((f32[16,3,8,256]{3,2,1,0:T(8,128)}), f32[16,3,8,256]{3,2,1,0:T(8,128)S(1)}, u32[]{:S(2)}, u32[]{:S(2)}) async-start(f32[16,3,8,256]{3,2,1,0:T(8,128)} %broadcast_in_dim.15), calls=%async_computation.1 | async-start | bytes 786432 | tf_op jit(solution)/shard_map/all_to_all | solution.py:525
  82.9 8.1 %all-to-all-done.1 = f32[16,3,8,256]{3,2,1,0:T(8,128)S(1)} async-done(((f32[16,3,8,256]{3,2,1,0:T(8,128)}), f32[16,3,8,256]{3,2,1,0:T(8,128)S(1)}, u32[]{:S(2)}, u32[]{:S(2)}) %all-to-all-start.1) | async-done | bytes 393248 | tf_op jit(solution)/shard_map/all_to_all | solution.py:525
  92.8 2.7 collective-permute-start.4
  97.9 4.9 %all-to-all-start.2 = ((bf16[64,16,128]{2,1,0:T(8,128)(2,1)}), bf16[64,16,128]{2,1,0:T(8,128)(2,1)S(1)}, u32[]{:S(2)}, u32[]{:S(2)}) async-start(bf16[64,16,128]{2,1,0:T(8,128)(2,1)} %fusion.2), calls=%async_computation.2 | async-start | bytes 524288 | tf_op jit(solution)/shard_map/all_to_all | solution.py:561
  102.8 14.9 %first_half.1 = (f32[3,4,256,128]{3,2,1,0:T(8,128)}, f32[2048,256]{1,0:T(8,128)}, bf16[256,2048]{1,0:T(8,128)(2,1)}) custom-call(bf16[2048,256]{1,0:T(8,128)(2,1)} %get-tuple-element.66.normed, bf16[2048,1024]{1,0:T(8,128)(2,1)} %get-tuple-element.67.k_in, bf16[2048,1024]{1,0:T(8,128)(2,1)} %get-tuple-element.68.v_in, bf16[256,2048]{1,0:T(8,128)(2,1)} %wv.5, ...), custom_call_target="tpu_custom_call" | custom-call | flops 14000000000 | bytes 16000000 | tf_op jit(solution)/shard_map/first_half/pallas_call | solution.py:402
  119.9 1.8 collective-permute-done.5
  122.7 10.2 %all-to-all-start.3 = ((bf16[64,40,128]{2,1,0:T(8,128)(2,1)}), bf16[64,40,128]{2,1,0:T(8,128)(2,1)S(1)}, u32[]{:S(2)}, u32[]{:S(2)}) async-start(bf16[64,40,128]{2,1,0:T(8,128)(2,1)} %pad_maximum_fusion.3), calls=%async_computation.3 | async-start | bytes 1310720 | tf_op jit(solution)/shard_map/all_to_all | solution.py:561
  133.0 23.7 %second_half.1 = (f32[3,4,256,128]{3,2,1,0:T(8,128)}, bf16[2048,256]{1,0:T(8,128)(2,1)}, f32[1,256]{1,0:T(1,128)}, bf16[224,256]{1,0:T(8,128)(2,1)}, bf16[224,25...) custom-call(bf16[256,2048]{1,0:T(8,128)(2,1)} %get-tuple-element.76.nt, ...), custom_call_target="tpu_custom_call" | custom-call | flops 14000000000 | bytes 16000000 | tf_op jit(solution)/shard_map/second_half/pallas_call | solution.py:419
  158.8 2.9 %collective-permute-start.8 = (bf16[224,256]{1,0:T(8,128)(2,1)}, bf16[224,256]{1,0:T(8,128)(2,1)S(1)}, u32[]{:S(2)}, u32[]{:S(2)}) collective-permute-start(bf16[224,256]{1,0:T(8,128)(2,1)} %get-tuple-element.92), channel_id=1, source_target_pairs={{0,16},{16,32},{32,48},{48,64},{64,80},{80,96},{96,112},{1,17},{17... | collective-permute-start | bytes 344072 | tf_op jit(solution)/shard_map/ppermute | solution.py:81
  161.7 1.9 collective-permute-start.9
  164.9 3.1 %collective-permute-done.9.below = bf16[224,256]{1,0:T(8,128)(2,1)S(1)} collective-permute-done((bf16[224,256]{1,0:T(8,128)(2,1)}, bf16[224,256]{1,0:T(8,128)(2,1)S(1)}, u32[]{:S(2)}, u32[]{:S(2)}) %collective-permute-start.9) | collective-permute-done | bytes 114720 | tf_op jit(solution)/shard_map/ppermute | solution.py:82
  168.0 9.8 %all-to-all-start.4 = ((bf16[64,48,128]{2,1,0:T(8,128)(2,1)}), bf16[64,48,128]{2,1,0:T(8,128)(2,1)S(1)}, u32[]{:S(2)}, u32[]{:S(2)}) async-start(bf16[64,48,128]{2,1,0:T(8,128)(2,1)} %pad_maximum_fusion), calls=%async_computation.4 | async-start | bytes 1572864 | tf_op jit(solution)/shard_map/all_to_all | solution.py:561
  177.8 2.9 %collective-permute-start.10 = (bf16[128,256]{1,0:T(8,128)(2,1)S(1)}, bf16[128,256]{1,0:T(8,128)(2,1)S(1)}, u32[]{:S(2)}, u32[]{:S(2)}) collective-permute-start(bf16[128,256]{1,0:T(8,128)(2,1)S(1)} %pad_maximum_fusion.7), channel_id=1, source_target_pairs={{0,1},{1,2},{2,3},{3,4},{4,5},{5,6},{6,7},{7,8},{8,9},{9,10},{10,1... | collective-permute-start | bytes 196616 | tf_op jit(solution)/shard_map/ppermute | solution.py:92
  182.1 13.1 %kernel_grad.1 = f32[49,256]{1,0:T(8,128)} custom-call(f32[38,14,8,256]{3,2,1,0:T(8,128)} %get-tuple-element.96.wide, bf16[2048,256]{1,0:T(8,128)(2,1)} %get-tuple-element.103.d_mixed), custom_call_target="tpu_custom_call" | custom-call | flops 14000000000 | bytes 16000000 | tf_op jit(solution)/shard_map/kernel_grad/pallas_call | solution.py:465
  198.7 10.8 %all-to-all-start.5 = ((bf16[64,24,128]{2,1,0:T(8,128)(2,1)}), bf16[64,24,128]{2,1,0:T(8,128)(2,1)S(1)}, u32[]{:S(2)}, u32[]{:S(2)}) async-start(bf16[64,24,128]{2,1,0:T(8,128)(2,1)} %broadcast_in_dim.18), calls=%async_computation.5 | async-start | bytes 786432 | tf_op jit(solution)/shard_map/all_to_all | solution.py:561
  209.5 12.2 %conv_back.1 = (f32[4,16,256]{2,1,0:T(8,128)}, f32[1,256]{1,0:T(1,128)}) custom-call(bf16[2048,256]{1,0:T(8,128)(2,1)} %get-tuple-element.103.d_mixed, bf16[224,256]{1,0:T(8,128)(2,1)} %copy-done.11, bf16[224,256]{1,0:T(8,128)(2,1)} %copy-done.12, bf16[128,256]{1,0:T(8,128)(2,1)} %copy-done.13, bf16[128,256]{1,0:T(8,128)(2,1)} %copy-done.14, ...), custom_call_target="tpu_custom_call" | custom-call | flops 14000000000 | bytes 16000000 | tf_op jit(solution)/shard_map/conv_back/pallas_call | solution.py:503
  226.0 4.0 %all-to-all-start.6 = ((f32[4,120,256]{2,1,0:T(8,128)}), f32[4,120,256]{2,1,0:T(8,128)S(1)}, u32[]{:S(2)}, u32[]{:S(2)}) async-start(f32[4,120,256]{2,1,0:T(8,128)} %broadcast_in_dim.19), calls=%async_computation.6 | async-start | bytes 983040 | tf_op jit(solution)/shard_map/all_to_all | solution.py:525
  230.8 7.8 %all-to-all-done.6 = f32[4,120,256]{2,1,0:T(8,128)S(1)} async-done(((f32[4,120,256]{2,1,0:T(8,128)}), f32[4,120,256]{2,1,0:T(8,128)S(1)}, u32[]{:S(2)}, u32[]{:S(2)}) %all-to-all-start.6) | async-done | bytes 491552 | tf_op jit(solution)/shard_map/all_to_all | solution.py:525
  240.1 6.6 %all-to-all-start.7 = ((f32[16,120,256]{2,1,0:T(8,128)}), f32[16,120,256]{2,1,0:T(8,128)}, u32[]{:S(2)}, u32[]{:S(2)}) async-start(f32[16,120,256]{2,1,0:T(8,128)} %broadcast_in_dim.20), calls=%async_computation.7 | async-start | bytes 3932160 | tf_op jit(solution)/shard_map/all_to_all | solution.py:525
  248.5 1.8 collective-permute-start.13
  252.2 1.8 copy.53
  254.0 2.9 %copy.57 = f32[256,2048]{1,0:T(8,128)} copy(f32[256,2048]{0,1:T(8,128)} %bitcast.131) | data formatting | bytes 4194304
  258.6 12.4 %all-to-all-done.7 = f32[16,120,256]{2,1,0:T(8,128)} async-done(((f32[16,120,256]{2,1,0:T(8,128)}), f32[16,120,256]{2,1,0:T(8,128)}, u32[]{:S(2)}, u32[]{:S(2)}) %all-to-all-start.7) | async-done | bytes 1966112 | tf_op jit(solution)/shard_map/all_to_all | solution.py:525
  (115 shorter events, 37.4 us)
Async XLA Ops:
  5.2 7.0 %collective-permute-start = (bf16[224,256]{1,0:T(8,128)(2,1)}, bf16[224,256]{1,0:T(8,128)(2,1)S(1)}, u32[]{:S(2)}, u32[]{:S(2)}) collective-permute-start(bf16[224,256]{1,0:T(8,128)(2,1)} %get-tuple-element.62), channel_id=1, source_target_pairs={{0,16},{16,32},{32,48},{48,64},{64,80},{80,96},{96,112},{1,17},{17... | collective-permute-start | bytes 344072 | tf_op jit(solution)/shard_map/ppermute | solution.py:81
  10.1 6.3 %collective-permute-start.1 = (bf16[224,256]{1,0:T(8,128)(2,1)}, bf16[224,256]{1,0:T(8,128)(2,1)S(1)}, u32[]{:S(2)}, u32[]{:S(2)}) collective-permute-start(bf16[224,256]{1,0:T(8,128)(2,1)} %get-tuple-element.63), channel_id=1, source_target_pairs={{16,0},{32,16},{48,32},{64,48},{80,64},{96,80},{112,96},{17,1},{33... | collective-permute-start | bytes 344072 | tf_op jit(solution)/shard_map/ppermute | solution.py:82
  12.2 14.1 %copy-start.4 = (bf16[224,256]{1,0:T(8,128)(2,1)}, bf16[224,256]{1,0:T(8,128)(2,1)S(1)}, u32[]{:S(2)}) copy-start(bf16[224,256]{1,0:T(8,128)(2,1)S(1)} %collective-permute-done.above) | copy-start | bytes 344068
  16.4 9.8 %copy-start.5 = (bf16[224,256]{1,0:T(8,128)(2,1)}, bf16[224,256]{1,0:T(8,128)(2,1)S(1)}, u32[]{:S(2)}) copy-start(bf16[224,256]{1,0:T(8,128)(2,1)S(1)} %collective-permute-done.1.below) | copy-start | bytes 344068
  17.2 5.3 %collective-permute-start.2 = (bf16[128,256]{1,0:T(8,128)(2,1)S(1)}, bf16[128,256]{1,0:T(8,128)(2,1)S(1)}, u32[]{:S(2)}, u32[]{:S(2)}) collective-permute-start(bf16[128,256]{1,0:T(8,128)(2,1)S(1)} %pad_maximum_fusion.5), channel_id=1, source_target_pairs={{0,1},{1,2},{2,3},{3,4},{4,5},{5,6},{6,7},{7,8},{8,9},{9,10},{10,1... | collective-permute-start | bytes 196616 | tf_op jit(solution)/shard_map/ppermute | solution.py:92
  21.3 5.0 %collective-permute-start.3 = (bf16[128,256]{1,0:T(8,128)(2,1)S(1)}, bf16[128,256]{1,0:T(8,128)(2,1)S(1)}, u32[]{:S(2)}, u32[]{:S(2)}) collective-permute-start(bf16[128,256]{1,0:T(8,128)(2,1)S(1)} %pad_maximum_fusion.6), channel_id=1, source_target_pairs={{1,0},{2,1},{3,2},{4,3},{5,4},{6,5},{7,6},{8,7},{9,8},{10,9},{11,1... | collective-permute-start | bytes 196616 | tf_op jit(solution)/shard_map/ppermute | solution.py:93
  62.2 30.2 %copy-start.2 = (f32[8,256,128]{2,1,0:T(8,128)S(1)}, f32[8,256,128]{2,1,0:T(8,128)}, u32[]{:S(2)}) copy-start(f32[8,256,128]{2,1,0:T(8,128)} %get-tuple-element.70) | copy-start | bytes 3145732
  74.9 16.1 %all-to-all-start.1 = ((f32[16,3,8,256]{3,2,1,0:T(8,128)}), f32[16,3,8,256]{3,2,1,0:T(8,128)S(1)}, u32[]{:S(2)}, u32[]{:S(2)}) async-start(f32[16,3,8,256]{3,2,1,0:T(8,128)} %broadcast_in_dim.15), calls=%async_computation.1 | async-start | bytes 786432 | tf_op jit(solution)/shard_map/all_to_all | solution.py:525
  92.8 4.3 %collective-permute-start.4 = (f32[64,16,128]{2,1,0:T(8,128)S(1)}, f32[64,16,128]{2,1,0:T(8,128)S(1)}, u32[]{:S(2)}, u32[]{:S(2)}) collective-permute-start(f32[64,16,128]{2,1,0:T(8,128)S(1)} %dynamic-slice_bitcast_fusion.2), channel_id=1, source_target_pairs={{0,16},{16,0},{1,17},{17,1},{2,18},{18,2},{3,19},{19,3},{4,20},{20... | collective-permute-start | bytes 1572872 | tf_op jit(solution)/shard_map/ppermute | solution.py:543
  97.9 19.9 %all-to-all-start.2 = ((bf16[64,16,128]{2,1,0:T(8,128)(2,1)}), bf16[64,16,128]{2,1,0:T(8,128)(2,1)S(1)}, u32[]{:S(2)}, u32[]{:S(2)}) async-start(bf16[64,16,128]{2,1,0:T(8,128)(2,1)} %fusion.2), calls=%async_computation.2 | async-start | bytes 524288 | tf_op jit(solution)/shard_map/all_to_all | solution.py:561
  119.0 2.6 collective-permute-start.5
  122.7 34.0 %all-to-all-start.3 = ((bf16[64,40,128]{2,1,0:T(8,128)(2,1)}), bf16[64,40,128]{2,1,0:T(8,128)(2,1)S(1)}, u32[]{:S(2)}, u32[]{:S(2)}) async-start(bf16[64,40,128]{2,1,0:T(8,128)(2,1)} %pad_maximum_fusion.3), calls=%async_computation.3 | async-start | bytes 1310720 | tf_op jit(solution)/shard_map/all_to_all | solution.py:561
  156.7 7.0 %copy-start = (f32[3,4,256,128]{3,2,1,0:T(8,128)S(1)}, f32[3,4,256,128]{3,2,1,0:T(8,128)}, u32[]{:S(2)}) copy-start(f32[3,4,256,128]{3,2,1,0:T(8,128)} %get-tuple-element.91) | copy-start | bytes 4718596
  158.0 5.7 %collective-permute-start.7 = (f32[64,24,128]{2,1,0:T(8,128)S(1)}, f32[64,24,128]{2,1,0:T(8,128)S(1)}, u32[]{:S(2)}, u32[]{:S(2)}) collective-permute-start(f32[64,24,128]{2,1,0:T(8,128)S(1)} %dynamic-slice_bitcast_fusion), channel_id=1, source_target_pairs={{0,16},{16,0},{1,17},{17,1},{2,18},{18,2},{3,19},{19,3},{4,20},{20... | collective-permute-start | bytes 2359304 | tf_op jit(solution)/shard_map/ppermute | solution.py:543
  158.8 6.1 %collective-permute-start.8 = (bf16[224,256]{1,0:T(8,128)(2,1)}, bf16[224,256]{1,0:T(8,128)(2,1)S(1)}, u32[]{:S(2)}, u32[]{:S(2)}) collective-permute-start(bf16[224,256]{1,0:T(8,128)(2,1)} %get-tuple-element.92), channel_id=1, source_target_pairs={{0,16},{16,32},{32,48},{48,64},{64,80},{80,96},{96,112},{1,17},{17... | collective-permute-start | bytes 344072 | tf_op jit(solution)/shard_map/ppermute | solution.py:81
  161.7 6.3 %collective-permute-start.9 = (bf16[224,256]{1,0:T(8,128)(2,1)}, bf16[224,256]{1,0:T(8,128)(2,1)S(1)}, u32[]{:S(2)}, u32[]{:S(2)}) collective-permute-start(bf16[224,256]{1,0:T(8,128)(2,1)} %get-tuple-element.93), channel_id=1, source_target_pairs={{16,0},{32,16},{48,32},{64,48},{80,64},{96,80},{112,96},{17,1},{33... | collective-permute-start | bytes 344072 | tf_op jit(solution)/shard_map/ppermute | solution.py:82
  163.8 14.0 %copy-start.9 = (bf16[96,256]{1,0:T(8,128)(2,1)S(1)}, bf16[96,256]{1,0:T(8,128)(2,1)}, u32[]{:S(2)}) copy-start(bf16[96,256]{1,0:T(8,128)(2,1)} %get-tuple-element.97) | copy-start | bytes 147460
  163.9 16.9 %copy-start.8 = (bf16[96,256]{1,0:T(8,128)(2,1)S(1)}, bf16[96,256]{1,0:T(8,128)(2,1)}, u32[]{:S(2)}) copy-start(bf16[96,256]{1,0:T(8,128)(2,1)} %get-tuple-element.100) | copy-start | bytes 147460
  164.9 30.3 %copy-start.11 = (bf16[224,256]{1,0:T(8,128)(2,1)}, bf16[224,256]{1,0:T(8,128)(2,1)S(1)}, u32[]{:S(2)}) copy-start(bf16[224,256]{1,0:T(8,128)(2,1)S(1)} %collective-permute-done.8.above) | copy-start | bytes 344068
  168.0 27.1 %copy-start.12 = (bf16[224,256]{1,0:T(8,128)(2,1)}, bf16[224,256]{1,0:T(8,128)(2,1)S(1)}, u32[]{:S(2)}) copy-start(bf16[224,256]{1,0:T(8,128)(2,1)S(1)} %collective-permute-done.9.below) | copy-start | bytes 344068
  168.0 27.2 %all-to-all-start.4 = ((bf16[64,48,128]{2,1,0:T(8,128)(2,1)}), bf16[64,48,128]{2,1,0:T(8,128)(2,1)S(1)}, u32[]{:S(2)}, u32[]{:S(2)}) async-start(bf16[64,48,128]{2,1,0:T(8,128)(2,1)} %pad_maximum_fusion), calls=%async_computation.4 | async-start | bytes 1572864 | tf_op jit(solution)/shard_map/all_to_all | solution.py:561
  177.8 17.3 %collective-permute-start.10 = (bf16[128,256]{1,0:T(8,128)(2,1)S(1)}, bf16[128,256]{1,0:T(8,128)(2,1)S(1)}, u32[]{:S(2)}, u32[]{:S(2)}) collective-permute-start(bf16[128,256]{1,0:T(8,128)(2,1)S(1)} %pad_maximum_fusion.7), channel_id=1, source_target_pairs={{0,1},{1,2},{2,3},{3,4},{4,5},{5,6},{6,7},{7,8},{8,9},{9,10},{10,1... | collective-permute-start | bytes 196616 | tf_op jit(solution)/shard_map/ppermute | solution.py:92
  180.8 14.4 %collective-permute-start.11 = (bf16[128,256]{1,0:T(8,128)(2,1)S(1)}, bf16[128,256]{1,0:T(8,128)(2,1)S(1)}, u32[]{:S(2)}, u32[]{:S(2)}) collective-permute-start(bf16[128,256]{1,0:T(8,128)(2,1)S(1)} %pad_maximum_fusion.8), channel_id=1, source_target_pairs={{1,0},{2,1},{3,2},{4,3},{5,4},{6,5},{7,6},{8,7},{9,8},{10,9},{11,1... | collective-permute-start | bytes 196616 | tf_op jit(solution)/shard_map/ppermute | solution.py:93
  195.9 1.8 collective-permute-start.12
  198.7 23.0 %all-to-all-start.5 = ((bf16[64,24,128]{2,1,0:T(8,128)(2,1)}), bf16[64,24,128]{2,1,0:T(8,128)(2,1)S(1)}, u32[]{:S(2)}, u32[]{:S(2)}) async-start(bf16[64,24,128]{2,1,0:T(8,128)(2,1)} %broadcast_in_dim.18), calls=%async_computation.5 | async-start | bytes 786432 | tf_op jit(solution)/shard_map/all_to_all | solution.py:561
  209.5 12.2 %copy-start.3 = (f32[49,256]{1,0:T(8,128)S(1)}, f32[49,256]{1,0:T(8,128)}, u32[]{:S(2)}) copy-start(f32[49,256]{1,0:T(8,128)} %kernel_grad.1) | copy-start | bytes 150532
  209.5 12.2 %copy-start.10 = (f32[1,256]{1,0:T(1,128)S(1)}, f32[1,256]{1,0:T(1,128)}, u32[]{:S(2)}) copy-start(f32[1,256]{1,0:T(1,128)} %get-tuple-element.113) | copy-start | bytes 3076
  222.6 1.7 collective-permute-start.14
  226.0 12.6 %all-to-all-start.6 = ((f32[4,120,256]{2,1,0:T(8,128)}), f32[4,120,256]{2,1,0:T(8,128)S(1)}, u32[]{:S(2)}, u32[]{:S(2)}) async-start(f32[4,120,256]{2,1,0:T(8,128)} %broadcast_in_dim.19), calls=%async_computation.6 | async-start | bytes 983040 | tf_op jit(solution)/shard_map/all_to_all | solution.py:525
  230.1 16.6 %collective-permute-start.6 = (bf16[64,16,128]{2,1,0:T(8,128)(2,1)S(1)}, bf16[64,16,128]{2,1,0:T(8,128)(2,1)S(1)}, u32[]{:S(2)}, u32[]{:S(2)}) collective-permute-start(bf16[64,16,128]{2,1,0:T(8,128)(2,1)S(1)} %slice.85), channel_id=1, source_target_pairs={{0,16},{16,0},{1,17},{17,1},{2,18},{18,2},{3,19},{19,3},{4,20},{20... | collective-permute-start | bytes 786440 | tf_op jit(solution)/shard_map/ppermute | solution.py:547
  240.1 30.9 %all-to-all-start.7 = ((f32[16,120,256]{2,1,0:T(8,128)}), f32[16,120,256]{2,1,0:T(8,128)}, u32[]{:S(2)}, u32[]{:S(2)}) async-start(f32[16,120,256]{2,1,0:T(8,128)} %broadcast_in_dim.20), calls=%async_computation.7 | async-start | bytes 3932160 | tf_op jit(solution)/shard_map/all_to_all | solution.py:525
  248.5 3.1 %collective-permute-start.13 = (bf16[64,24,128]{2,1,0:T(8,128)(2,1)S(1)}, bf16[64,24,128]{2,1,0:T(8,128)(2,1)S(1)}, u32[]{:S(2)}, u32[]{:S(2)}) collective-permute-start(bf16[64,24,128]{2,1,0:T(8,128)(2,1)S(1)} %all-to-all-done.5), channel_id=1, source_target_pairs={{0,16},{16,0},{1,17},{17,1},{2,18},{18,2},{3,19},{19,3},{4,20},{20... | collective-permute-start | bytes 1179656 | tf_op jit(solution)/shard_map/ppermute | solution.py:547
  (5 other events, 9.6 us)

commit v3 on v2

--- a/solution.py
+++ b/solution.py
@@ -21,6 +21,7 @@
 CH = 256
 TOK = ROWS * COLS
 WIDE = 14
+BLOCK = 256
 WIRE = BF
 ROW_AXES = ("z", "core")
 COL_AXES = ("x", "y")
@@ -144,15 +145,18 @@
         w_sc[n] = jnp.broadcast_to(kernel_ref[n : n + 1, :], (8, CH))
 
 
-def conv_row(wide, w_sc, a, half, flip):
+def conv_rows(wide, w_sc, a, half, flip):
     lanes = pl.ds(half * 128, 128)
-    acc = [wide[a + HALO, HALO + cb, :, lanes] for cb in range(8)]
-    for i in range(KSIZE):
+    acc = [[wide[a + r + HALO, HALO + cb, :, lanes] for cb in range(8)] for r in range(2)]
+    for i in range(KSIZE + 1):
         xs = [wide[a + i, c, :, lanes] for c in range(WIDE)]
-        for j in range(KSIZE):
-            n = i * KSIZE + j
-            w = w_sc[KSIZE * KSIZE - 1 - n if flip else n, :, lanes]
-            acc = [acc[cb] + xs[cb + j] * w for cb in range(8)]
+        for r in range(2):
+            if not 0 <= i - r < KSIZE:
+                continue
+            for j in range(KSIZE):
+                n = (i - r) * KSIZE + j
+                w = w_sc[KSIZE * KSIZE - 1 - n if flip else n, :, lanes]
+                acc[r] = [acc[r][cb] + xs[cb + j] * w for cb in range(8)]
     return acc
 
 
@@ -209,27 +213,30 @@
     return outs[0], outs[1], outs[2:]
 
 
-def conv_kernel_body(emb, above, below, lh, rh, kern, gain, wide, mixed, normed, w_sc, l_sc, r_sc, c_sc):
+def conv_kernel_body(emb, above, below, lh, rh, kern, gain, wide, centred, inverse, normed, w_sc, l_sc, r_sc, c_sc):
     assemble(wide, emb, (above, below, lh, rh), l_sc, r_sc, c_sc)
     spread_weights(kern, w_sc)
 
-    def body(a, carry):
+    def body(n, carry):
         for half in range(2):
-            acc = conv_row(wide, w_sc, a, half, False)
-            for cb in range(8):
-                rows = pl.ds(pl.multiple_of(a * COLS + cb * 8, 8), 8)
-                mixed[rows, pl.ds(half * 128, 128)] = acc[cb]
+            acc = conv_rows(wide, w_sc, 2 * n, half, False)
+            for r in range(2):
+                for cb in range(8):
+                    rows = pl.ds(pl.multiple_of((2 * n + r) * COLS + cb * 8, 8), 8)
+                    centred[rows, pl.ds(half * 128, 128)] = acc[r][cb]
         return carry
 
-    lax.fori_loop(0, ROWS, body, 0)
-
-    def norm_body(a, carry):
-        rows = pl.ds(pl.multiple_of(a * COLS, COLS), COLS)
-        centred, _ = norm_rows(mixed[rows, :])
-        normed[rows, :] = (centred * gain[...]).astype(BF)
+    lax.fori_loop(0, ROWS // 2, body, 0)
+
+    def norm_body(n, carry):
+        rows = pl.ds(pl.multiple_of(n * BLOCK, BLOCK), BLOCK)
+        out, inv = norm_rows(centred[rows, :])
+        centred[rows, :] = out
+        inverse[rows, :] = jnp.broadcast_to(inv, (BLOCK, 128))
+        normed[rows, :] = (out * gain[...]).astype(BF)
         return carry
 
-    lax.fori_loop(0, ROWS, norm_body, 0)
+    lax.fori_loop(0, TOK // BLOCK, norm_body, 0)
 
 
 def conv_forward(emb, halo, conv_kernel, gain):
@@ -239,6 +246,7 @@
         out_shape=[
             jax.ShapeDtypeStruct((ROWS + 2 * HALO, WIDE, 8, CH), F32),
             jax.ShapeDtypeStruct((TOK, CH), F32),
+            jax.ShapeDtypeStruct((TOK, 128), F32),
             jax.ShapeDtypeStruct((TOK, CH), BF),
         ],
         scratch_shapes=[pltpu.VMEM((KSIZE * KSIZE, 8, CH), F32)] + EDGE_SCRATCH,
@@ -248,6 +256,7 @@
 
 CHUNK = 512
 SCALE = 128**-0.5
+SCALE2 = SCALE * 1.4426950408889634
 COST = pl.CostEstimate(flops=14_000_000_000, transcendentals=0, bytes_accessed=16_000_000)
 
 
@@ -260,20 +269,21 @@
         kv = dot(normed[rows, :], w).astype(BF)
         k_out[rows, :] = kv[:, :128]
         v_out[rows, :] = kv[:, 128:]
-        s = dot(kv[:, :128], q[...], NT) * SCALE
+        s = dot(kv[:, :128], q[...], NT)
         s_sc[rows, :] = s
         top = jnp.max(s, axis=0, keepdims=True)
         peak = top if peak is None else jnp.maximum(peak, top)
+    level = peak * SCALE2
     total = jnp.zeros((1, 256), F32)
     acc = jnp.zeros((128, 256), F32)
     for c in range(TOK // CHUNK):
         rows = slice(c * CHUNK, (c + 1) * CHUNK)
-        p = jnp.exp(s_sc[rows, :] - peak)
+        p = jnp.exp2(s_sc[rows, :] * SCALE2 - level)
         total = total + jnp.sum(p, axis=0, keepdims=True)
         acc = acc + dot(v_out[rows, :], p.astype(BF), TN)
     weighted[0] = acc.T
     dots = jnp.sum(acc * up[...].astype(F32).T, axis=0, keepdims=True)
-    stats[0, pl.ds(h, 1), :] = peak
+    stats[0, pl.ds(h, 1), :] = level
     stats[1, pl.ds(h, 1), :] = total
     stats[2, pl.ds(h, 1), :] = dots
 
@@ -315,7 +325,17 @@
     )(normed, kv_weight, kv_weight, latents, d_attended)
 
 
-def head_grads(h, normed, k_in, v_in, wk, wv, q, up, lse, dots, grads, dn_sc, nt_sc):
+def attend_grad_kernel(
+    normed, k_in, v_in, wk, wv, q, up, lse, dots, centred, inverse, gain,
+    grads, d_mixed, gain_grad, top, bot, left, right, dn_sc, nt_sc, l_sc, r_sc, c_sc,
+):
+    h = pl.program_id(0)
+
+    @pl.when(h == 0)
+    def _():
+        nt_sc[...] = normed[...].T
+        dn_sc[...] = jnp.zeros_like(dn_sc)
+
     w = jnp.concatenate([wk[...], wv[...]], axis=1)
     level = lse[pl.ds(h, 1), :]
     row_dots = dots[pl.ds(h, 1), :]
@@ -324,117 +344,73 @@
     for c in range(TOK // CHUNK):
         rows = slice(c * CHUNK, (c + 1) * CHUNK)
         k = k_in[rows, :]
-        p = jnp.exp(dot(k, q[...], NT) * SCALE - level)
+        p = jnp.exp2(dot(k, q[...], NT) * SCALE2 - level)
         dp = dot(v_in[rows, :], up[...], NT)
-        ds = (p * (dp - row_dots) * SCALE).astype(BF)
+        ds = (p * (dp - row_dots)).astype(BF)
         qg = qg + dot(k, ds, TN)
-        kg = dot(ds, q[...]).astype(BF)
+        kg = (dot(ds, q[...]) * SCALE).astype(BF)
         vg = dot(p.astype(BF), up[...]).astype(BF)
         d_proj = jnp.concatenate([kg, vg], axis=1)
         wg = wg + dot(nt_sc[:, rows], d_proj)
         dn_sc[rows, :] += dot(d_proj, w, NT)
-    grads[0, 0] = qg.T
+    grads[0, 0] = qg.T * SCALE
     grads[1, 0] = wg[:, :128]
     grads[2, 0] = wg[:, 128:]
 
-
-def first_half_kernel(normed, k_in, v_in, wk, wv, q, up, lse, dots, grads, dn, nt):
-    h = pl.program_id(0)
-
-    @pl.when(h == 0)
+    @pl.when(h == HEADS - 1)
     def _():
-        nt[...] = normed[...].astype(F32).T.astype(BF)
-        dn[...] = jnp.zeros_like(dn)
-
-    head_grads(h, normed, k_in, v_in, wk, wv, q, up, lse, dots, grads, dn, nt)
-
-
-def second_half_kernel(
-    nt, k_in, v_in, wk, wv, q, up, lse, dots, dn_in, mixed, gain,
-    grads, d_mixed, gain_grad, top, bot, left, right, dn_sc, l_sc, r_sc, c_sc,
-):
-    h = pl.program_id(0)
-
-    @pl.when(h == 0)
-    def _():
-        dn_sc[...] = dn_in[...]
-
-    head_grads(h + HEADS // 2, None, k_in, v_in, wk, wv, q, up, lse, dots, grads, dn_sc, nt)
-
-    @pl.when(h == HEADS // 2 - 1)
-    def _():
-        def body(a, total):
-            rows = pl.ds(pl.multiple_of(a * COLS, COLS), COLS)
-            centred, inverse = norm_rows(mixed[rows, :])
+        def body(n, total):
+            rows = pl.ds(pl.multiple_of(n * BLOCK, BLOCK), BLOCK)
+            x = centred[rows, :]
+            inv = inverse[rows, :]
             dn = dn_sc[rows, :]
-            total = total + jnp.sum(dn * centred, axis=0, keepdims=True)
+            total = total + jnp.sum(dn * x, axis=0, keepdims=True)
             g = dn * gain[...]
             mean = jnp.sum(g, axis=-1, keepdims=True) * (1.0 / CH)
-            slope = jnp.sum(g * centred, axis=-1, keepdims=True) * (1.0 / CH)
-            d_mixed[rows, :] = (inverse * (g - mean - centred * slope)).astype(BF)
+            slope = jnp.sum(g * x, axis=-1, keepdims=True) * (1.0 / CH)
+            inv = jnp.concatenate([inv, inv], axis=1)
+            d_mixed[rows, :] = (inv * (g - mean - x * slope)).astype(BF)
             return total
 
-        gain_grad[...] = lax.fori_loop(0, ROWS, body, jnp.zeros((1, CH), F32))
+        gain_grad[...] = lax.fori_loop(0, TOK // BLOCK, body, jnp.zeros((1, CH), F32))
         write_edges(d_mixed, top, bot, left, right, l_sc, r_sc, c_sc)
 
 
-HALF = HEADS // 2
-
-
-def head_specs(first):
-    return [
-        column(TOK, 128, first),
-        column(TOK, 128, first),
-        column(CH, 128, first),
-        column(CH, 128, HEADS + first),
-        column(256, 128, first),
-        column(256, 128, first),
-        whole((HEADS, 256)),
-        whole((HEADS, 256)),
-    ]
-
-
-GRADS_SPEC = pl.BlockSpec((3, 1, 256, 128), lambda h: (0, h, 0, 0))
-GRADS = jax.ShapeDtypeStruct((3, HALF, 256, 128), F32)
-
-
-def first_half(normed, k, v, kv_weight, latents, d_attended, lse, dots):
-    return pl.pallas_call(
-        first_half_kernel,
-        name="first_half",
-        grid=(HALF,),
-        in_specs=[whole((TOK, CH))] + head_specs(0),
-        out_specs=[GRADS_SPEC, whole((TOK, CH)), whole((CH, TOK))],
-        out_shape=[
-            GRADS,
-            jax.ShapeDtypeStruct((TOK, CH), F32),
-            jax.ShapeDtypeStruct((CH, TOK), BF),
+def attend_grad(normed, k, v, kv_weight, latents, d_attended, lse, dots, centred, inverse, gain):
+    outs = pl.pallas_call(
+        attend_grad_kernel,
+        name="attend_grad",
+        grid=(HEADS,),
+        in_specs=[
+            whole((TOK, CH)),
+            column(TOK, 128),
+            column(TOK, 128),
+            column(CH, 128),
+            column(CH, 128, HEADS),
+            column(256, 128),
+            column(256, 128),
+            whole((HEADS, 256)),
+            whole((HEADS, 256)),
+            whole((TOK, CH)),
+            whole((TOK, 128)),
+            whole((1, CH)),
         ],
-        compiler_params=VMEM,
-        cost_estimate=COST,
-    )(normed, k, v, kv_weight, kv_weight, latents, d_attended, lse, dots)
-
-
-def second_half(nt, k, v, kv_weight, latents, d_attended, lse, dots, dn, mixed, gain):
-    outs = pl.pallas_call(
-        second_half_kernel,
-        name="second_half",
-        grid=(HALF,),
-        in_specs=[whole((CH, TOK))]
-        + head_specs(HALF)
-        + [whole((TOK, CH)), whole((TOK, CH)), whole((1, CH))],
-        out_specs=[GRADS_SPEC, whole((TOK, CH)), whole((1, CH))]
+        out_specs=[
+            pl.BlockSpec((3, 1, 256, 128), lambda h: (0, h, 0, 0)),
+            whole((TOK, CH)),
+            whole((1, CH)),
+        ]
         + [whole(s.shape) for s in EDGE_SHAPES],
         out_shape=[
-            GRADS,
+            jax.ShapeDtypeStruct((3, HEADS, 256, 128), F32),
             jax.ShapeDtypeStruct((TOK, CH), BF),
             jax.ShapeDtypeStruct((1, CH), F32),
         ]
         + EDGE_SHAPES,
-        scratch_shapes=[pltpu.VMEM((TOK, CH), F32)] + EDGE_SCRATCH,
+        scratch_shapes=[pltpu.VMEM((TOK, CH), F32), pltpu.VMEM((CH, TOK), BF)] + EDGE_SCRATCH,
         compiler_params=VMEM,
         cost_estimate=COST,
-    )(nt, k, v, kv_weight, kv_weight, latents, d_attended, lse, dots, dn, mixed, gain)
+    )(normed, k, v, kv_weight, kv_weight, latents, d_attended, lse, dots, centred, inverse, gain)
     return outs[:3], outs[3:]
 
 
@@ -444,18 +420,20 @@
         lanes = pl.ds(half * 128, 128)
         for i in range(KSIZE):
 
-            def body(a, acc):
-                xs = [wide[a + i, c, :, lanes] for c in range(WIDE)]
-                base = pl.multiple_of(a * COLS, COLS)
-                ds = [d_sc[pl.ds(base + cb * 8, 8), lanes] for cb in range(8)]
+            def body(n, acc):
                 acc = list(acc)
-                for cb in range(8):
-                    for j in range(KSIZE):
-                        acc[j] = acc[j] + xs[cb + j] * ds[cb]
+                for r in range(4):
+                    a = 4 * n + r
+                    xs = [wide[a + i, c, :, lanes] for c in range(WIDE)]
+                    base = pl.multiple_of(a * COLS, COLS)
+                    ds = [d_sc[pl.ds(base + cb * 8, 8), lanes] for cb in range(8)]
+                    for cb in range(8):
+                        for j in range(KSIZE):
+                            acc[j] = acc[j] + xs[cb + j] * ds[cb]
                 return tuple(acc)
 
             zero = jnp.zeros((8, 128), F32)
-            acc = lax.fori_loop(0, ROWS, body, (zero,) * KSIZE)
+            acc = lax.fori_loop(0, ROWS // 4, body, (zero,) * KSIZE)
             for j in range(KSIZE):
                 n = i * KSIZE + j
                 out[n : n + 1, lanes] = jnp.sum(acc[j], axis=0, keepdims=True)
@@ -477,16 +455,18 @@
     spread_weights(kern, w_sc)
     zero = jnp.zeros((8, 128), F32)
 
-    def body(a, bias):
+    def body(n, bias):
         bias = list(bias)
         for half in range(2):
-            acc = conv_row(wide, w_sc, a, half, True)
-            acc = jnp.concatenate(acc, axis=0).astype(BF)
-            d_sc[a & 7, pl.ds(pl.multiple_of((a >> 3) * 64, 64), 64), pl.ds(half * 128, 128)] = acc
-            bias[half] = bias[half] + jnp.sum(acc.astype(F32).reshape(8, 8, 128), axis=0)
+            accs = conv_rows(wide, w_sc, 2 * n, half, True)
+            for r in range(2):
+                a = 2 * n + r
+                acc = jnp.concatenate(accs[r], axis=0).astype(BF)
+                d_sc[a & 7, pl.ds(pl.multiple_of((a >> 3) * 64, 64), 64), pl.ds(half * 128, 128)] = acc
+                bias[half] = bias[half] + jnp.sum(acc.astype(F32).reshape(8, 8, 128), axis=0)
         return tuple(bias)
 
-    bias = lax.fori_loop(0, ROWS, body, (zero, zero))
+    bias = lax.fori_loop(0, ROWS // 2, body, (zero, zero))
     for half in range(2):
         bias_grad[:, half * 128 : (half + 1) * 128] = jnp.sum(bias[half], axis=0, keepdims=True)
     total = [jnp.zeros((16, CH), F32) for _ in range(4)]
@@ -516,6 +496,7 @@
 
 
 CHIPS = ("z", "x", "y")
+ALL = ("z", "core", "x", "y")
 PAIR = [(0, 1), (1, 0)]
 
 
@@ -529,7 +510,7 @@
     for axes in (("z", "core"), ("x", "y")):
         group = gather(stats, axes)
         peak = jnp.max(group[:, 0], axis=0)
-        factors = jnp.exp(group[:, 0] - peak)
+        factors = jnp.exp2(group[:, 0] - peak)
         total = jnp.sum(group[:, 1] * factors, axis=0)
         dots = jnp.sum(group[:, 2] * factors, axis=0)
         stats = jnp.stack([peak, total, dots])
@@ -562,9 +543,8 @@
 
 
 def small_sum(x):
-    x = x + lax.ppermute(x, "core", PAIR)
-    x = jnp.sum(gather(x, ("z",)), axis=0)
-    return jnp.sum(gather(x, ("x", "y")), axis=0)
+    mine = jnp.sum(lax.all_to_all(x[:, None], ALL, 0, 0, tiled=True), axis=0)
+    return lax.all_to_all(jnp.broadcast_to(mine[None], (128,) + mine.shape), ALL, 0, 0, tiled=True)[:, 0]
 
 
 def blocks(x):
@@ -586,54 +566,36 @@
     emb, z, edges = embed(pixels, patch_weight, patch_bias)
     rows = exchange_rows(edges)
     halo = rows + exchange_cols(edges, *rows)
-    wide, mixed, normed = conv_forward(emb, halo, conv_kernel, gain)
+    wide, centred, inverse, normed = conv_forward(emb, halo, conv_kernel, gain)
     k, v, weighted, local = attend(normed, kv_weight, latents, d_attended)
     stats = combine_stats(local)
-    lse = stats[0] + jnp.log(stats[1])
+    lse = stats[0] + jnp.log2(stats[1])
     row_dots = stats[2] / stats[1]
-    factor = jnp.exp(local[0] - stats[0]) / stats[1]
-    attended = pair_sum(blocks((weighted * factor[:, :, None]).reshape(2048, 128)))
-    lse, attended = tie(lse, attended)
-    attended = send(attended)
-    grads_a, dn, nt = first_half(normed, k, v, kv_weight, latents, d_attended, lse, row_dots)
-    dn, nt, grads_a, attended = tie(dn, nt, grads_a, attended)
-    sums_a = pair_sum(blocks(grads_a.reshape(3072, 128)))
-    message = jnp.concatenate([sums_a, copies(block_sum(attended))], axis=1)
-    dn, message = tie(dn, message)
-    message = send(message)
-    (grads_b, d_mixed, gain_grad), d_edges = second_half(
-        nt, k, v, kv_weight, latents, d_attended, lse, row_dots, dn, mixed, gain
+    factor = jnp.exp2(local[0] - stats[0]) / stats[1]
+    (grads, d_mixed, gain_grad), d_edges = attend_grad(
+        normed, k, v, kv_weight, latents, d_attended, lse, row_dots, centred, inverse, gain
     )
-    grads_b, d_mixed, message, *d_edges = tie(grads_b, d_mixed, message, *d_edges)
-    attended = message[:, 24:]
     d_rows = exchange_rows(d_edges)
-    sums_b = pair_sum(blocks(grads_b.reshape(3072, 128)))
-    message = jnp.concatenate([sums_b, copies(block_sum(message[:, :24]))], axis=1)
+    sums = jnp.concatenate([(weighted * factor[:, :, None])[None], grads], axis=0)
+    message = pair_sum(blocks(sums.reshape(8192, 128)))
     d_mixed, message, *d_rows = tie(d_mixed, message, *d_rows)
     message = send(message)
     d_cols = exchange_cols(d_edges, *d_rows)
     kern = kernel_grad(wide, d_mixed)
     d_mixed, message, kern, *d_cols = tie(d_mixed, message, kern, *d_cols)
-    grads_a = message[:, 24:]
-    grads_b = copies(block_sum(message[:, :24]))
-    d_mixed, grads_b = tie(d_mixed, grads_b)
-    grads_b = send(grads_b)
+    message = copies(block_sum(message))
+    d_mixed, message = tie(d_mixed, message)
+    message = send(message)
     patch, bias = conv_back(d_mixed, tuple(d_rows) + tuple(d_cols), conv_kernel, z)
-    patch, bias, grads_b = tie(patch, bias, grads_b)
+    patch, bias, message = tie(patch, bias, message)
     small = jnp.concatenate([patch.reshape(64, CH), kern, gain_grad, bias], axis=0)
-    small = small_sum(jnp.pad(small, ((0, 5), (0, 0))))
-    attended = swap(attended)
-    grads = [
-        jnp.concatenate([a, b], axis=0)
-        for a, b in zip(
-            swap(grads_a).reshape(3, HALF, 256, 128), swap(grads_b).reshape(3, HALF, 256, 128)
-        )
-    ]
+    small = small_sum(jnp.pad(small, ((0, 13), (0, 0))))
+    sums = swap(message).reshape(4, HEADS, 256, 128)
     patch = small[:64].reshape(4, 16, CH)[:, :12].transpose(1, 0, 2).reshape(48, CH)
     return (
-        columns(attended.reshape(HEADS, 256, 128)),
-        columns(grads[0]),
-        columns(jnp.concatenate([grads[1], grads[2]], axis=0)),
+        columns(sums[0]),
+        columns(sums[1]),
+        columns(sums[2:].reshape(2 * HEADS, 256, 128)),
         small[64 + 49],
         small[64 : 64 + 49],
         patch,

time: 280 us -> 234 us (0.84); the launches traced: 275 us -> 233 us
  starting transfers between devices: 82.2 us -> 54.1 us
  Pallas kernels: 102 us -> 85.8 us
  blocking collectives: 11 us -> 24.5 us
  waiting for transfers between devices: 46.6 us -> 35.5 us
    all_to_all x4 -> x2, starting transfers between devices: 35.8 us -> 12.6 us  [send(): return lax.all_to_all(x, CHIPS, 0, 0, tiled=True)]
    all_to_all x3 -> x1, waiting for transfers between devices: 28.3 us -> 8.13 us  [gather(): return lax.all_to_all(copies, axes, 0, 0, tiled=True)]
    all_to_all x0 -> x1, blocking collectives: none -> 13.8 us  [small_sum(): mine = jnp.sum(lax.all_to_all(x[:, None], ALL, 0, 0, tiled=True), axis=0)]
    pallas_call x2 -> x1, Pallas kernels: 38.6 us -> 27.6 us  [attend_grad(): pl.pallas_call(attend_grad_kernel, name='attend_grad', grid=(HEADS,), in_...]
    all_to_all x4 -> x2, waiting for transfers between devices: 0.01 us -> 10.7 us  [send(): return lax.all_to_all(x, CHIPS, 0, 0, tiled=True)]
    all_to_all x0 -> x1, waiting for transfers between devices: none -> 10.1 us  [small_sum(): lax.all_to_all(jnp.broadcast_to(mine[None], (128,) + mine.shape), ALL, 0,...]
    all_to_all x3 -> x1, starting transfers between devices: 18.6 us -> 9.57 us  [gather(): return lax.all_to_all(copies, axes, 0, 0, tiled=True)]
    all_to_all x0 -> x1, starting transfers between devices: none -> 4.21 us  [small_sum(): lax.all_to_all(jnp.broadcast_to(mine[None], (128,) + mine.shape), ALL, 0,...]
  transfers between devices with their start and end apart: 22 -> 14, of which waited for: 12 -> 8; matrix products, arithmetic and copies ran while one was open for 5% -> 3% of each run, Pallas kernels for 23% -> 10%
where the time goes in v3:
time: 234 us; the launch traced here: 233 us
  Pallas kernels  85.8 us (37%)
  starting transfers between devices  54.1 us (23%)
  waiting for transfers between devices  35.5 us (15%)
  blocking collectives  24.5 us (10%)
  local copies, waits for them, and re-layouts  20.6 us (9%)
  other arithmetic  11 us (5%)
    pallas_call x1, Pallas kernels, attend_grad(): pl.pallas_call(attend_grad_kernel, name='attend_grad', grid=(HEADS,), in_...  27.6 us
    pallas_call x1, Pallas kernels, attend(): pl.pallas_call(attend_kernel, name='attend', grid=(HEADS,), in_specs=[who...  16.9 us
    pallas_call x1, Pallas kernels, conv_forward(): pl.pallas_call(conv_kernel_body, name='conv_forward', out_shape=[jax.Shap...  14.7 us
    all_to_all x1, blocking collectives, small_sum(): mine = jnp.sum(lax.all_to_all(x[:, None], ALL, 0, 0, tiled=True), axis=0)  13.8 us
    pallas_call x1, Pallas kernels, conv_back(): pl.pallas_call(conv_back_body, name='conv_back', out_shape=[jax.ShapeDtyp...  12.7 us
    all_to_all x2, starting transfers between devices, send(): return lax.all_to_all(x, CHIPS, 0, 0, tiled=True)  12.6 us
    pallas_call x1, Pallas kernels, kernel_grad(): pl.pallas_call(kernel_grad_body, name='kernel_grad', out_shape=jax.ShapeD...  10.8 us
    all_to_all x1, blocking collectives, gather(): return lax.all_to_all(copies, axes, 0, 0, tiled=True)  10.7 us
  transfers between devices with their start and end apart: 14, of which 8 were waited for; matrix products, arithmetic and copies ran while one was open for 3% of the time, Pallas kernels for 10%

profile of v3, /device:TPU:1, one launch (start us, length us, event | category | flops | bytes accessed | tf_op | source)
XLA Modules:
  0.0 232.6 jit_solution(10118193892654339936)
XLA Ops:
  2.0 3.2 %embed.1 = (bf16[2048,256]{1,0:T(8,128)(2,1)}, bf16[256,512]{1,0:T(8,128)(2,1)}, bf16[224,256]{1,0:T(8,128)(2,1)}, bf16[224,256]{1,0:T(8,128)(2,1)}, bf16[96,256]{1,0:T(8,128)(2,1)}, /*index=5*/bf16[96,256]{1,0:T(8,128)(2,1)}) custom-call(bf16[384,256]{1,0:T(8,128)(2,1)} %bitcast.120, bf16[4,16,256]{2,1,0:T(8,128)(2,1)} %pad.8.weights, f32[1,256]{1,0:T(1,128)} %bitcast.127), custom_call_target="tpu_custom_call" | custom-call | tf_op jit(solution)/shard_map/embed/pallas_call | solution.py:202
  5.2 4.9 %collective-permute-start = (bf16[224,256]{1,0:T(8,128)(2,1)}, bf16[224,256]{1,0:T(8,128)(2,1)S(1)}, u32[]{:S(2)}, u32[]{:S(2)}) collective-permute-start(bf16[224,256]{1,0:T(8,128)(2,1)} %get-tuple-element.45), channel_id=1, source_target_pairs={{0,16},{16,32},{32,48},{48,64},{64,80},{80,96},{96,112},{1,17},{17... | collective-permute-start | bytes 344072 | tf_op jit(solution)/shard_map/ppermute | solution.py:82
  10.1 1.9 collective-permute-start.1
  12.2 4.2 %collective-permute-done.1.below = bf16[224,256]{1,0:T(8,128)(2,1)S(1)} collective-permute-done((bf16[224,256]{1,0:T(8,128)(2,1)}, bf16[224,256]{1,0:T(8,128)(2,1)S(1)}, u32[]{:S(2)}, u32[]{:S(2)}) %collective-permute-start.1) | collective-permute-done | bytes 114720 | tf_op jit(solution)/shard_map/ppermute | solution.py:83
  19.4 4.0 %collective-permute-start.2 = (bf16[128,256]{1,0:T(8,128)(2,1)S(1)}, bf16[128,256]{1,0:T(8,128)(2,1)S(1)}, u32[]{:S(2)}, u32[]{:S(2)}) collective-permute-start(bf16[128,256]{1,0:T(8,128)(2,1)S(1)} %pad_maximum_fusion.2), channel_id=1, source_target_pairs={{0,1},{1,2},{2,3},{3,4},{4,5},{5,6},{6,7},{7,8},{8,9},{9,10},{10,1... | collective-permute-start | bytes 196616 | tf_op jit(solution)/shard_map/ppermute | solution.py:93
  25.3 14.7 %conv_forward.1 = (f32[38,14,8,256]{3,2,1,0:T(8,128)}, f32[2048,256]{1,0:T(8,128)}, f32[2048,128]{1,0:T(8,128)}, bf16[2048,256]{1,0:T(8,128)(2,1)}) custom-call(bf16[2048,256]{1,0:T(8,128)(2,1)} %get-tuple-element.44.emb, bf16[224,256]{1,0:T(8,128)(2,1)} %copy-done.2, bf16[224,256]{1,0:T(8,128)(2,1)} %copy-done.3, bf16[128,256]{1,0:T(8,128)(2,1)} %copy-done.5, ...), custom_call_target="tpu_custom_call" | custom-call | tf_op jit(solution)/shard_map/conv_forward/pallas_call | solution.py:243
  40.0 16.9 %attend.1 = (bf16[2048,1024]{1,0:T(8,128)(2,1)}, bf16[2048,1024]{1,0:T(8,128)(2,1)}, f32[8,256,128]{2,1,0:T(8,128)}, f32[3,8,256]{2,1,0:T(8,128)}) custom-call(bf16[2048,256]{1,0:T(8,128)(2,1)} %get-tuple-element.49.normed, bf16[256,2048]{1,0:T(8,128)(2,1)} %wv.3, bf16[256,2048]{1,0:T(8,128)(2,1)} %wv.3, bf16[256,1024]{1,0:T(8,128)(2,1)} %q.3, ...), custom_call_target="tpu_custom_call" | custom-call | tf_op jit(solution)/shard_map/attend/pallas_call | solution.py:300
  57.8 10.7 %all_to_all.30 = f32[8,3,8,256]{3,2,1,0:T(8,128)S(1)} all-to-all(f32[8,3,8,256]{3,2,1,0:T(8,128)S(1)} %broadcast_in_dim.12), channel_id=1, replica_groups=mesh['z'=4,'core'=2,'x'=4,'y'=4] {'z','core'}, dimensions={0} | all-to-all | bytes 393216 | tf_op jit(solution)/shard_map/all_to_all | solution.py:506
  69.4 9.6 %all-to-all-start.1 = ((f32[16,3,8,256]{3,2,1,0:T(8,128)}), f32[16,3,8,256]{3,2,1,0:T(8,128)S(1)}, u32[]{:S(2)}, u32[]{:S(2)}) async-start(f32[16,3,8,256]{3,2,1,0:T(8,128)} %broadcast_in_dim.13), calls=%async_computation.1 | async-start | bytes 786432 | tf_op jit(solution)/shard_map/all_to_all | solution.py:506
  78.9 8.1 %all-to-all-done.1 = f32[16,3,8,256]{3,2,1,0:T(8,128)S(1)} async-done(((f32[16,3,8,256]{3,2,1,0:T(8,128)}), f32[16,3,8,256]{3,2,1,0:T(8,128)S(1)}, u32[]{:S(2)}, u32[]{:S(2)}) %all-to-all-start.1) | async-done | bytes 393248 | tf_op jit(solution)/shard_map/all_to_all | solution.py:506
  87.2 1.3 fusion.15
  88.8 27.6 %attend_grad.1 = (f32[3,8,256,128]{3,2,1,0:T(8,128)}, bf16[2048,256]{1,0:T(8,128)(2,1)}, f32[1,256]{1,0:T(1,128)}, bf16[224,256]{1,0:T(8,128)(2,1)}, bf16[224,25...) custom-call(bf16[2048,256]{1,0:T(8,128)(2,1)} %get-tuple-element.49.normed, ...), custom_call_target="tpu_custom_call" | custom-call | flops 14000000000 | bytes 16000000 | tf_op jit(solution)/shard_map/attend_grad/pallas_call | solution.py:380
  116.4 2.3 %pad_maximum_fusion = f32[4,8,256,128]{3,2,1,0:T(8,128)S(1)} fusion(f32[3,8,256,128]{3,2,1,0:T(8,128)} %get-tuple-element.57, f32[1,8,256,128]{3,2,1,0:T(8,128)S(1)} %multiply_bitcast_fusion), kind=kLoop, calls=%fused_computation | loop fusion | flops 1048576 | bytes 8388608 | tf_op jit(solution)/shard_map/concatenate | solution.py:579
  118.7 1.6 dynamic-slice_bitcast_fusion
  121.4 2.6 %collective-permute-start.4 = (f32[64,64,128]{2,1,0:T(8,128)}, f32[64,64,128]{2,1,0:T(8,128)S(1)}, u32[]{:S(2)}, u32[]{:S(2)}) collective-permute-start(f32[64,64,128]{2,1,0:T(8,128)} %dynamic-slice_bitcast_fusion), channel_id=1, source_target_pairs={{0,16},{16,0},{1,17},{17,1},{2,18},{18,2},{3,19},{19,3},{4,20},{20... | collective-permute-start | bytes 6291464 | tf_op jit(solution)/shard_map/ppermute | solution.py:524
  124.0 2.1 collective-permute-start.5
  126.1 2.4 %collective-permute-start.6 = (bf16[224,256]{1,0:T(8,128)(2,1)S(1)}, bf16[224,256]{1,0:T(8,128)(2,1)S(1)}, u32[]{:S(2)}, u32[]{:S(2)}) collective-permute-start(bf16[224,256]{1,0:T(8,128)(2,1)S(1)} %copy-done.12), channel_id=1, source_target_pairs={{16,0},{32,16},{48,32},{64,48},{80,64},{96,80},{112,96},{17,1},{33... | collective-permute-start | bytes 344072 | tf_op jit(solution)/shard_map/ppermute | solution.py:83
  128.5 3.0 %fusion = bf16[64,64,128]{2,1,0:T(8,128)(2,1)} fusion(f32[64,64,128]{2,1,0:T(8,128)S(1)} %collective-permute-done.4, f32[2,64,64,128]{3,2,1,0:T(8,128)} %bitcast.112, s32[]{:T(128)S(6)} %select_n.20), kind=kLoop, calls=%fused_computation.4 | loop fusion | flops 1048576 | bytes 5242884 | tf_op jit(solution)/shard_map/convert_element_type | solution.py:524
  133.7 4.0 %collective-permute-start.7 = (bf16[128,256]{1,0:T(8,128)(2,1)S(1)}, bf16[128,256]{1,0:T(8,128)(2,1)S(1)}, u32[]{:S(2)}, u32[]{:S(2)}) collective-permute-start(bf16[128,256]{1,0:T(8,128)(2,1)S(1)} %pad_maximum_fusion.4), channel_id=1, source_target_pairs={{0,1},{1,2},{2,3},{3,4},{4,5},{5,6},{6,7},{7,8},{8,9},{9,10},{10,1... | collective-permute-start | bytes 196616 | tf_op jit(solution)/shard_map/ppermute | solution.py:93
  137.7 7.4 %all-to-all-start.2 = ((bf16[64,64,128]{2,1,0:T(8,128)(2,1)}), bf16[64,64,128]{2,1,0:T(8,128)(2,1)S(1)}, u32[]{:S(2)}, u32[]{:S(2)}) async-start(bf16[64,64,128]{2,1,0:T(8,128)(2,1)} %fusion), calls=%async_computation.2 | async-start | bytes 2097152 | tf_op jit(solution)/shard_map/all_to_all | solution.py:542
  145.2 10.8 %kernel_grad.1 = f32[49,256]{1,0:T(8,128)} custom-call(f32[38,14,8,256]{3,2,1,0:T(8,128)} %get-tuple-element.62.wide, bf16[2048,256]{1,0:T(8,128)(2,1)} %get-tuple-element.69.d_mixed), custom_call_target="tpu_custom_call" | custom-call | flops 14000000000 | bytes 16000000 | tf_op jit(solution)/shard_map/kernel_grad/pallas_call | solution.py:443
  156.0 7.1 %all-to-all-done.2 = bf16[64,64,128]{2,1,0:T(8,128)(2,1)S(1)} async-done(((bf16[64,64,128]{2,1,0:T(8,128)(2,1)}), bf16[64,64,128]{2,1,0:T(8,128)(2,1)S(1)}, u32[]{:S(2)}, u32[]{:S(2)}) %all-to-all-start.2) | async-done | bytes 1048608 | tf_op jit(solution)/shard_map/all_to_all | solution.py:542
  164.4 5.2 %all-to-all-start.3 = ((bf16[64,64,128]{2,1,0:T(8,128)(2,1)}), bf16[64,64,128]{2,1,0:T(8,128)(2,1)S(1)}, u32[]{:S(2)}, u32[]{:S(2)}) async-start(bf16[64,64,128]{2,1,0:T(8,128)(2,1)} %broadcast_in_dim.15), calls=%async_computation.3 | async-start | bytes 2097152 | tf_op jit(solution)/shard_map/all_to_all | solution.py:542
  169.7 12.7 %conv_back.1 = (f32[4,16,256]{2,1,0:T(8,128)}, f32[1,256]{1,0:T(1,128)}) custom-call(bf16[2048,256]{1,0:T(8,128)(2,1)} %get-tuple-element.69.d_mixed, bf16[224,256]{1,0:T(8,128)(2,1)} %copy-done.9, bf16[224,256]{1,0:T(8,128)(2,1)} %copy-done.10, bf16[128,256]{1,0:T(8,128)(2,1)} %copy-done.15, bf16[128,256]{1,0:T(8,128)(2,1)} %copy-done.14, f32[49,256]{1,0:T(8,128)} %kern.3, ...), custom_call_target="tpu_custom_call" | custom-call | flops 14000000000 | bytes 16000000 | tf_op jit(solution)/shard_map/conv_back/pallas_call | solution.py:483
  182.3 3.7 %all-to-all-done.3 = bf16[64,64,128]{2,1,0:T(8,128)(2,1)S(1)} async-done(((bf16[64,64,128]{2,1,0:T(8,128)(2,1)}), bf16[64,64,128]{2,1,0:T(8,128)(2,1)S(1)}, u32[]{:S(2)}, u32[]{:S(2)}) %all-to-all-start.3) | async-done | bytes 1048608 | tf_op jit(solution)/shard_map/all_to_all | solution.py:542
  186.0 3.3 %collective-permute-start.9 = (bf16[64,64,128]{2,1,0:T(8,128)(2,1)S(1)}, bf16[64,64,128]{2,1,0:T(8,128)(2,1)S(1)}, u32[]{:S(2)}, u32[]{:S(2)}) collective-permute-start(bf16[64,64,128]{2,1,0:T(8,128)(2,1)S(1)} %all-to-all-done.3), channel_id=1, source_target_pairs={{0,16},{16,0},{1,17},{17,1},{2,18},{18,2},{3,19},{19,3},{4,20},{20... | collective-permute-start | bytes 3145736 | tf_op jit(solution)/shard_map/ppermute | solution.py:528
  190.3 13.8 %all_to_all.31 = f32[128,1,256]{2,1,0:T(1,128)S(1)} all-to-all(f32[128,1,256]{2,1,0:T(1,128)S(1)} %broadcast_in_dim.16), channel_id=1, replica_groups=mesh['z'=4,'core'=2,'x'=4,'y'=4] {'z','core','x','y'}, dimensions={0} | all-to-all | bytes 262144 | tf_op jit(solution)/shard_map/all_to_all | solution.py:546
  204.9 4.2 %all-to-all-start.5 = ((f32[128,1,256]{2,1,0:T(1,128)}), f32[128,1,256]{2,1,0:T(1,128)S(1)}, u32[]{:S(2)}, u32[]{:S(2)}) async-start(f32[128,1,256]{2,1,0:T(1,128)} %broadcast_in_dim.17), calls=%async_computation.5 | async-start | bytes 262144 | tf_op jit(solution)/shard_map/all_to_all | solution.py:547
  209.1 10.1 %all-to-all-done.5 = f32[128,1,256]{2,1,0:T(1,128)S(1)} async-done(((f32[128,1,256]{2,1,0:T(1,128)}), f32[128,1,256]{2,1,0:T(1,128)S(1)}, u32[]{:S(2)}, u32[]{:S(2)}) %all-to-all-start.5) | async-done | bytes 131104 | tf_op jit(solution)/shard_map/all_to_all | solution.py:547
  223.1 1.6 copy.63
  227.9 1.8 copy.65
  229.7 2.9 %copy.69 = f32[256,2048]{1,0:T(8,128)} copy(f32[256,2048]{0,1:T(8,128)} %bitcast.116) | data formatting | bytes 4194304
  (83 shorter events, 22.0 us)
Async XLA Ops:
  5.2 7.0 %collective-permute-start = (bf16[224,256]{1,0:T(8,128)(2,1)}, bf16[224,256]{1,0:T(8,128)(2,1)S(1)}, u32[]{:S(2)}, u32[]{:S(2)}) collective-permute-start(bf16[224,256]{1,0:T(8,128)(2,1)} %get-tuple-element.45), channel_id=1, source_target_pairs={{0,16},{16,32},{32,48},{48,64},{64,80},{80,96},{96,112},{1,17},{17... | collective-permute-start | bytes 344072 | tf_op jit(solution)/shard_map/ppermute | solution.py:82
  10.1 6.3 %collective-permute-start.1 = (bf16[224,256]{1,0:T(8,128)(2,1)}, bf16[224,256]{1,0:T(8,128)(2,1)S(1)}, u32[]{:S(2)}, u32[]{:S(2)}) collective-permute-start(bf16[224,256]{1,0:T(8,128)(2,1)} %get-tuple-element.46), channel_id=1, source_target_pairs={{16,0},{32,16},{48,32},{64,48},{80,64},{96,80},{112,96},{17,1},{33... | collective-permute-start | bytes 344072 | tf_op jit(solution)/shard_map/ppermute | solution.py:83
  12.2 12.5 %copy-start.2 = (bf16[224,256]{1,0:T(8,128)(2,1)}, bf16[224,256]{1,0:T(8,128)(2,1)S(1)}, u32[]{:S(2)}) copy-start(bf16[224,256]{1,0:T(8,128)(2,1)S(1)} %collective-permute-done.above) | copy-start | bytes 344068
  16.4 8.2 %copy-start.3 = (bf16[224,256]{1,0:T(8,128)(2,1)}, bf16[224,256]{1,0:T(8,128)(2,1)S(1)}, u32[]{:S(2)}) copy-start(bf16[224,256]{1,0:T(8,128)(2,1)S(1)} %collective-permute-done.1.below) | copy-start | bytes 344068
  17.3 6.1 %collective-permute-start.3 = (bf16[128,256]{1,0:T(8,128)(2,1)S(1)}, bf16[128,256]{1,0:T(8,128)(2,1)S(1)}, u32[]{:S(2)}, u32[]{:S(2)}) collective-permute-start(bf16[128,256]{1,0:T(8,128)(2,1)S(1)} %pad_maximum_fusion.3), channel_id=1, source_target_pairs={{1,0},{2,1},{3,2},{4,3},{5,4},{6,5},{7,6},{8,7},{9,8},{10,9},{11,1... | collective-permute-start | bytes 196616 | tf_op jit(solution)/shard_map/ppermute | solution.py:94
  19.4 5.3 %collective-permute-start.2 = (bf16[128,256]{1,0:T(8,128)(2,1)S(1)}, bf16[128,256]{1,0:T(8,128)(2,1)S(1)}, u32[]{:S(2)}, u32[]{:S(2)}) collective-permute-start(bf16[128,256]{1,0:T(8,128)(2,1)S(1)} %pad_maximum_fusion.2), channel_id=1, source_target_pairs={{0,1},{1,2},{2,3},{3,4},{4,5},{5,6},{6,7},{7,8},{8,9},{9,10},{10,1... | collective-permute-start | bytes 196616 | tf_op jit(solution)/shard_map/ppermute | solution.py:93
  23.4 1.3 copy-start.4
  24.7 0.6 copy-start.5
  56.9 31.6 %copy-start.1 = (f32[8,256,128]{2,1,0:T(8,128)S(1)}, f32[8,256,128]{2,1,0:T(8,128)}, u32[]{:S(2)}) copy-start(f32[8,256,128]{2,1,0:T(8,128)} %get-tuple-element.56) | copy-start | bytes 3145732
  69.4 17.7 %all-to-all-start.1 = ((f32[16,3,8,256]{3,2,1,0:T(8,128)}), f32[16,3,8,256]{3,2,1,0:T(8,128)S(1)}, u32[]{:S(2)}, u32[]{:S(2)}) async-start(f32[16,3,8,256]{3,2,1,0:T(8,128)} %broadcast_in_dim.13), calls=%async_computation.1 | async-start | bytes 786432 | tf_op jit(solution)/shard_map/all_to_all | solution.py:506
  118.7 2.7 %copy-start = (f32[4,8,256,128]{3,2,1,0:T(8,128)}, f32[4,8,256,128]{3,2,1,0:T(8,128)S(1)}, u32[]{:S(2)}) copy-start(f32[4,8,256,128]{3,2,1,0:T(8,128)S(1)} %pad_maximum_fusion) | copy-start | bytes 12582916
  118.7 5.3 %copy-start.13 = (bf16[224,256]{1,0:T(8,128)(2,1)S(1)}, bf16[224,256]{1,0:T(8,128)(2,1)}, u32[]{:S(2)}) copy-start(bf16[224,256]{1,0:T(8,128)(2,1)} %get-tuple-element.58) | copy-start | bytes 344068
  118.7 7.4 %copy-start.12 = (bf16[224,256]{1,0:T(8,128)(2,1)S(1)}, bf16[224,256]{1,0:T(8,128)(2,1)}, u32[]{:S(2)}) copy-start(bf16[224,256]{1,0:T(8,128)(2,1)} %get-tuple-element.59) | copy-start | bytes 344068
  121.4 7.1 %collective-permute-start.4 = (f32[64,64,128]{2,1,0:T(8,128)}, f32[64,64,128]{2,1,0:T(8,128)S(1)}, u32[]{:S(2)}, u32[]{:S(2)}) collective-permute-start(f32[64,64,128]{2,1,0:T(8,128)} %dynamic-slice_bitcast_fusion), channel_id=1, source_target_pairs={{0,16},{16,0},{1,17},{17,1},{2,18},{18,2},{3,19},{19,3},{4,20},{20... | collective-permute-start | bytes 6291464 | tf_op jit(solution)/shard_map/ppermute | solution.py:524
  124.0 7.5 %collective-permute-start.5 = (bf16[224,256]{1,0:T(8,128)(2,1)S(1)}, bf16[224,256]{1,0:T(8,128)(2,1)S(1)}, u32[]{:S(2)}, u32[]{:S(2)}) collective-permute-start(bf16[224,256]{1,0:T(8,128)(2,1)S(1)} %copy-done.13), channel_id=1, source_target_pairs={{0,16},{16,32},{32,48},{48,64},{64,80},{80,96},{96,112},{1,17},{17... | collective-permute-start | bytes 344072 | tf_op jit(solution)/shard_map/ppermute | solution.py:82
  126.1 6.3 %copy-start.8 = (bf16[96,256]{1,0:T(8,128)(2,1)S(1)}, bf16[96,256]{1,0:T(8,128)(2,1)}, u32[]{:S(2)}) copy-start(bf16[96,256]{1,0:T(8,128)(2,1)} %get-tuple-element.66) | copy-start | bytes 147460
  126.1 7.6 %copy-start.7 = (bf16[96,256]{1,0:T(8,128)(2,1)S(1)}, bf16[96,256]{1,0:T(8,128)(2,1)}, u32[]{:S(2)}) copy-start(bf16[96,256]{1,0:T(8,128)(2,1)} %get-tuple-element.63) | copy-start | bytes 147460
  126.1 6.2 %collective-permute-start.6 = (bf16[224,256]{1,0:T(8,128)(2,1)S(1)}, bf16[224,256]{1,0:T(8,128)(2,1)S(1)}, u32[]{:S(2)}, u32[]{:S(2)}) collective-permute-start(bf16[224,256]{1,0:T(8,128)(2,1)S(1)} %copy-done.12), channel_id=1, source_target_pairs={{16,0},{32,16},{48,32},{64,48},{80,64},{96,80},{112,96},{17,1},{33... | collective-permute-start | bytes 344072 | tf_op jit(solution)/shard_map/ppermute | solution.py:83
  131.5 24.4 %copy-start.9 = (bf16[224,256]{1,0:T(8,128)(2,1)}, bf16[224,256]{1,0:T(8,128)(2,1)S(1)}, u32[]{:S(2)}) copy-start(bf16[224,256]{1,0:T(8,128)(2,1)S(1)} %collective-permute-done.5.above) | copy-start | bytes 344068
  132.4 23.6 %copy-start.10 = (bf16[224,256]{1,0:T(8,128)(2,1)}, bf16[224,256]{1,0:T(8,128)(2,1)S(1)}, u32[]{:S(2)}) copy-start(bf16[224,256]{1,0:T(8,128)(2,1)S(1)} %collective-permute-done.6.below) | copy-start | bytes 344068
  132.4 23.5 %collective-permute-start.8 = (bf16[128,256]{1,0:T(8,128)(2,1)S(1)}, bf16[128,256]{1,0:T(8,128)(2,1)S(1)}, u32[]{:S(2)}, u32[]{:S(2)}) collective-permute-start(bf16[128,256]{1,0:T(8,128)(2,1)S(1)} %pad_maximum_fusion.5), channel_id=1, source_target_pairs={{1,0},{2,1},{3,2},{4,3},{5,4},{6,5},{7,6},{8,7},{9,8},{10,9},{11,1... | collective-permute-start | bytes 196616 | tf_op jit(solution)/shard_map/ppermute | solution.py:94
  133.7 22.2 %collective-permute-start.7 = (bf16[128,256]{1,0:T(8,128)(2,1)S(1)}, bf16[128,256]{1,0:T(8,128)(2,1)S(1)}, u32[]{:S(2)}, u32[]{:S(2)}) collective-permute-start(bf16[128,256]{1,0:T(8,128)(2,1)S(1)} %pad_maximum_fusion.4), channel_id=1, source_target_pairs={{0,1},{1,2},{2,3},{3,4},{4,5},{5,6},{6,7},{7,8},{8,9},{9,10},{10,1... | collective-permute-start | bytes 196616 | tf_op jit(solution)/shard_map/ppermute | solution.py:93
  137.7 25.3 %all-to-all-start.2 = ((bf16[64,64,128]{2,1,0:T(8,128)(2,1)}), bf16[64,64,128]{2,1,0:T(8,128)(2,1)S(1)}, u32[]{:S(2)}, u32[]{:S(2)}) async-start(bf16[64,64,128]{2,1,0:T(8,128)(2,1)} %fusion), calls=%async_computation.2 | async-start | bytes 2097152 | tf_op jit(solution)/shard_map/all_to_all | solution.py:542
  155.9 8.5 %copy-start.14 = (bf16[128,256]{1,0:T(8,128)(2,1)}, bf16[128,256]{1,0:T(8,128)(2,1)S(1)}, u32[]{:S(2)}) copy-start(bf16[128,256]{1,0:T(8,128)(2,1)S(1)} %collective-permute-done.8.rh) | copy-start | bytes 196612
  156.0 8.5 %copy-start.15 = (bf16[128,256]{1,0:T(8,128)(2,1)}, bf16[128,256]{1,0:T(8,128)(2,1)S(1)}, u32[]{:S(2)}) copy-start(bf16[128,256]{1,0:T(8,128)(2,1)S(1)} %collective-permute-done.7.lh) | copy-start | bytes 196612
  164.4 21.6 %all-to-all-start.3 = ((bf16[64,64,128]{2,1,0:T(8,128)(2,1)}), bf16[64,64,128]{2,1,0:T(8,128)(2,1)S(1)}, u32[]{:S(2)}, u32[]{:S(2)}) async-start(bf16[64,64,128]{2,1,0:T(8,128)(2,1)} %broadcast_in_dim.15), calls=%async_computation.3 | async-start | bytes 2097152 | tf_op jit(solution)/shard_map/all_to_all | solution.py:542
  169.6 19.7 %copy-start.6 = (f32[49,256]{1,0:T(8,128)S(1)}, f32[49,256]{1,0:T(8,128)}, u32[]{:S(2)}) copy-start(f32[49,256]{1,0:T(8,128)} %kernel_grad.1) | copy-start | bytes 150532
  169.6 19.7 %copy-start.11 = (f32[1,256]{1,0:T(1,128)S(1)}, f32[1,256]{1,0:T(1,128)}, u32[]{:S(2)}) copy-start(f32[1,256]{1,0:T(1,128)} %get-tuple-element.79) | copy-start | bytes 3076
  186.0 35.2 %collective-permute-start.9 = (bf16[64,64,128]{2,1,0:T(8,128)(2,1)S(1)}, bf16[64,64,128]{2,1,0:T(8,128)(2,1)S(1)}, u32[]{:S(2)}, u32[]{:S(2)}) collective-permute-start(bf16[64,64,128]{2,1,0:T(8,128)(2,1)S(1)} %all-to-all-done.3), channel_id=1, source_target_pairs={{0,16},{16,0},{1,17},{17,1},{2,18},{18,2},{3,19},{19,3},{4,20},{20... | collective-permute-start | bytes 3145736 | tf_op jit(solution)/shard_map/ppermute | solution.py:528
  204.9 14.3 %all-to-all-start.5 = ((f32[128,1,256]{2,1,0:T(1,128)}), f32[128,1,256]{2,1,0:T(1,128)S(1)}, u32[]{:S(2)}, u32[]{:S(2)}) async-start(f32[128,1,256]{2,1,0:T(1,128)} %broadcast_in_dim.17), calls=%async_computation.5 | async-start | bytes 262144 | tf_op jit(solution)/shard_map/all_to_all | solution.py:547

commit v4 on v3

--- a/solution.py
+++ b/solution.py
@@ -281,7 +281,7 @@
         p = jnp.exp2(s_sc[rows, :] * SCALE2 - level)
         total = total + jnp.sum(p, axis=0, keepdims=True)
         acc = acc + dot(v_out[rows, :], p.astype(BF), TN)
-    weighted[0] = acc.T
+    weighted[0] = acc
     dots = jnp.sum(acc * up[...].astype(F32).T, axis=0, keepdims=True)
     stats[0, pl.ds(h, 1), :] = level
     stats[1, pl.ds(h, 1), :] = total
@@ -311,13 +311,13 @@
         out_specs=[
             column(TOK, 128),
             column(TOK, 128),
-            pl.BlockSpec((1, 256, 128), lambda h: (h, 0, 0)),
+            pl.BlockSpec((1, 128, 256), lambda h: (h, 0, 0)),
             whole((3, HEADS, 256)),
         ],
         out_shape=[
             jax.ShapeDtypeStruct((TOK, 1024), BF),
             jax.ShapeDtypeStruct((TOK, 1024), BF),
-            jax.ShapeDtypeStruct((HEADS, 256, 128), F32),
+            jax.ShapeDtypeStruct((HEADS, 128, 256), F32),
             jax.ShapeDtypeStruct((3, HEADS, 256), F32),
         ],
         scratch_shapes=[pltpu.VMEM((TOK, 256), F32)],
@@ -325,13 +325,18 @@
     )(normed, kv_weight, kv_weight, latents, d_attended)
 
 
+def head_at(step, core):
+    return (step + HEADS // 2 * (1 - core[0])) & (HEADS - 1)
+
+
 def attend_grad_kernel(
-    normed, k_in, v_in, wk, wv, q, up, lse, dots, centred, inverse, gain,
-    grads, d_mixed, gain_grad, top, bot, left, right, dn_sc, nt_sc, l_sc, r_sc, c_sc,
+    core, normed, k_in, v_in, wk, wv, q, up, lse, dots, factor, weighted, centred, inverse, gain,
+    send, keep, d_mixed, gain_grad, top, bot, left, right, dn_sc, nt_sc, l_sc, r_sc, c_sc,
 ):
-    h = pl.program_id(0)
-
-    @pl.when(h == 0)
+    step = pl.program_id(0)
+    h = head_at(step, core)
+
+    @pl.when(step == 0)
     def _():
         nt_sc[...] = normed[...].T
         dn_sc[...] = jnp.zeros_like(dn_sc)
@@ -353,11 +358,24 @@
         d_proj = jnp.concatenate([kg, vg], axis=1)
         wg = wg + dot(nt_sc[:, rows], d_proj)
         dn_sc[rows, :] += dot(d_proj, w, NT)
-    grads[0, 0] = qg.T * SCALE
-    grads[1, 0] = wg[:, :128]
-    grads[2, 0] = wg[:, 128:]
-
-    @pl.when(h == HEADS - 1)
+    att = (weighted[0] * factor[pl.ds(h, 1), :]).T
+    qg = (qg * SCALE).T
+
+    def put(out):
+        out[0, 0] = att
+        out[1, 0] = qg
+        out[2, 0] = wg[:, :128]
+        out[3, 0] = wg[:, 128:]
+
+    @pl.when(step < HEADS // 2)
+    def _():
+        put(send)
+
+    @pl.when(step >= HEADS // 2)
+    def _():
+        put(keep)
+
+    @pl.when(step == HEADS - 1)
     def _():
         def body(n, total):
             rows = pl.ds(pl.multiple_of(n * BLOCK, BLOCK), BLOCK)
@@ -376,42 +394,59 @@
         write_edges(d_mixed, top, bot, left, right, l_sc, r_sc, c_sc)
 
 
-def attend_grad(normed, k, v, kv_weight, latents, d_attended, lse, dots, centred, inverse, gain):
+def attend_grad(
+    core, normed, k, v, kv_weight, latents, d_attended, lse, dots, factor, weighted, centred, inverse, gain
+):
+    def full(shape):
+        return pl.BlockSpec(shape, lambda n, core: (0,) * len(shape))
+
+    def head(rows, first=0):
+        return pl.BlockSpec((rows, 128), lambda n, core: (0, head_at(n, core) + first))
+
+    half = HEADS // 2
+    part = jax.ShapeDtypeStruct((4, half, 256, 128), F32)
     outs = pl.pallas_call(
         attend_grad_kernel,
         name="attend_grad",
-        grid=(HEADS,),
-        in_specs=[
-            whole((TOK, CH)),
-            column(TOK, 128),
-            column(TOK, 128),
-            column(CH, 128),
-            column(CH, 128, HEADS),
-            column(256, 128),
-            column(256, 128),
-            whole((HEADS, 256)),
-            whole((HEADS, 256)),
-            whole((TOK, CH)),
-            whole((TOK, 128)),
-            whole((1, CH)),
-        ],
-        out_specs=[
-            pl.BlockSpec((3, 1, 256, 128), lambda h: (0, h, 0, 0)),
-            whole((TOK, CH)),
-            whole((1, CH)),
-        ]
-        + [whole(s.shape) for s in EDGE_SHAPES],
+        grid_spec=pltpu.PrefetchScalarGridSpec(
+            num_scalar_prefetch=1,
+            grid=(HEADS,),
+            in_specs=[
+                full((TOK, CH)),
+                head(TOK),
+                head(TOK),
+                head(CH),
+                head(CH, HEADS),
+                head(256),
+                head(256),
+                full((HEADS, 256)),
+                full((HEADS, 256)),
+                full((HEADS, 256)),
+                pl.BlockSpec((1, 128, 256), lambda n, core: (head_at(n, core), 0, 0)),
+                full((TOK, CH)),
+                full((TOK, 128)),
+                full((1, CH)),
+            ],
+            out_specs=[
+                pl.BlockSpec((4, 1, 256, 128), lambda n, core: (0, jnp.minimum(n, half - 1), 0, 0)),
+                pl.BlockSpec((4, 1, 256, 128), lambda n, core: (0, jnp.maximum(n - half, 0), 0, 0)),
+                full((TOK, CH)),
+                full((1, CH)),
+            ]
+            + [full(s.shape) for s in EDGE_SHAPES],
+            scratch_shapes=[pltpu.VMEM((TOK, CH), F32), pltpu.VMEM((CH, TOK), BF)] + EDGE_SCRATCH,
+        ),
         out_shape=[
-            jax.ShapeDtypeStruct((3, HEADS, 256, 128), F32),
+            part,
+            part,
             jax.ShapeDtypeStruct((TOK, CH), BF),
             jax.ShapeDtypeStruct((1, CH), F32),
         ]
         + EDGE_SHAPES,
-        scratch_shapes=[pltpu.VMEM((TOK, CH), F32), pltpu.VMEM((CH, TOK), BF)] + EDGE_SCRATCH,
         compiler_params=VMEM,
         cost_estimate=COST,
-    )(normed, k, v, kv_weight, kv_weight, latents, d_attended, lse, dots, centred, inverse, gain)
-    return outs[:3], outs[3:]
+    )(core, normed, k, v, kv_weight, kv_weight, latents, d_attended, lse, dots, factor, weighted, centred, inverse, gain)
+    return outs[:4], outs[4:]
 
 
 def kernel_grad_body(wide, d_mixed, out, d_sc):
@@ -517,17 +552,11 @@
     return stats
 
 
-def pair_sum(x):
-    core = lax.axis_index("core")
-    keep = lax.dynamic_index_in_dim(x, core, 0, keepdims=False)
-    send = lax.dynamic_index_in_dim(x, 1 - core, 0, keepdims=False)
-    return (keep + lax.ppermute(send, "core", PAIR)).astype(WIRE)
-
-
 def swap(half):
     other = lax.ppermute(half, "core", PAIR)
     first = lax.axis_index("core") == 0
-    return jnp.stack([jnp.where(first, half, other), jnp.where(first, other, half)]).astype(F32)
+    pair = [jnp.where(first, half, other), jnp.where(first, other, half)]
+    return jnp.stack([x.reshape(4, HEADS // 2, 256, 128) for x in pair], axis=1)
 
 
 def block_sum(parts):
@@ -542,13 +571,8 @@
     return lax.all_to_all(x, CHIPS, 0, 0, tiled=True)
 
 
-def small_sum(x):
-    mine = jnp.sum(lax.all_to_all(x[:, None], ALL, 0, 0, tiled=True), axis=0)
-    return lax.all_to_all(jnp.broadcast_to(mine[None], (128,) + mine.shape), ALL, 0, 0, tiled=True)[:, 0]
-
-
-def blocks(x):
-    return x.reshape(2, 64, -1, x.shape[-1])
+def send_all(x):
+    return lax.all_to_all(x, ALL, 0, 0, tiled=True)
 
 
 def tie(x, *others):
@@ -572,12 +596,13 @@
     lse = stats[0] + jnp.log2(stats[1])
     row_dots = stats[2] / stats[1]
     factor = jnp.exp2(local[0] - stats[0]) / stats[1]
-    (grads, d_mixed, gain_grad), d_edges = attend_grad(
-        normed, k, v, kv_weight, latents, d_attended, lse, row_dots, centred, inverse, gain
+    core = lax.axis_index("core").astype(jnp.int32).reshape(1)
+    (away, keep, d_mixed, gain_grad), d_edges = attend_grad(
+        core, normed, k, v, kv_weight, latents, d_attended, lse, row_dots, factor, weighted,
+        centred, inverse, gain,
     )
     d_rows = exchange_rows(d_edges)
-    sums = jnp.concatenate([(weighted * factor[:, :, None])[None], grads], axis=0)
-    message = pair_sum(blocks(sums.reshape(8192, 128)))
+    message = (keep + lax.ppermute(away, "core", PAIR)).astype(BF).reshape(64, 64, 128)
     d_mixed, message, *d_rows = tie(d_mixed, message, *d_rows)
     message = send(message)
     d_cols = exchange_cols(d_edges, *d_rows)
@@ -589,13 +614,15 @@
     patch, bias = conv_back(d_mixed, tuple(d_rows) + tuple(d_cols), conv_kernel, z)
     patch, bias, message = tie(patch, bias, message)
     small = jnp.concatenate([patch.reshape(64, CH), kern, gain_grad, bias], axis=0)
-    small = small_sum(jnp.pad(small, ((0, 13), (0, 0))))
-    sums = swap(message).reshape(4, HEADS, 256, 128)
+    mine = block_sum(send_all(jnp.pad(small, ((0, 13), (0, 0)))[:, None]))
+    small = send_all(jnp.broadcast_to(mine[None], (128,) + mine.shape))
+    sums = swap(message).astype(F32).reshape(4, HEADS, 256, 128)
+    outs = (columns(sums[0]), columns(sums[1]), columns(sums[2:].reshape(2 * HEADS, 256, 128)))
+    small, *outs = tie(small, *outs)
+    small = small[:, 0]
     patch = small[:64].reshape(4, 16, CH)[:, :12].transpose(1, 0, 2).reshape(48, CH)
     return (
-        columns(sums[0]),
-        columns(sums[1]),
-        columns(sums[2:].reshape(2 * HEADS, 256, 128)),
+        *outs,
         small[64 + 49],
         small[64 : 64 + 49],
         patch,

time: 234 us -> 220 us (0.940)
  blocking collectives: 24.5 us -> 10.7 us
  local copies, waits for them, and re-layouts: 20.6 us -> 16.6 us
  waiting for transfers between devices: 35.5 us -> 38.7 us
  starting transfers between devices: 54.1 us -> 56.7 us
    all_to_all x1 -> x0, blocking collectives: 13.8 us -> none  [small_sum(): mine = jnp.sum(lax.all_to_all(x[:, None], ALL, 0, 0, tiled=True), axis=0)]
    unnamed x37 -> x29, local copies, waits for them, and re-layouts: 7.86 us -> 3.1 us
    all_to_all x1 -> x2, starting transfers between devices: 4.21 us -> 7.66 us  [send_all(): return lax.all_to_all(x, ALL, 0, 0, tiled=True)]
    all_to_all x1 -> x2, waiting for transfers between devices: 10.1 us -> 11.9 us  [send_all(): return lax.all_to_all(x, ALL, 0, 0, tiled=True)]
  transfers between devices with their start and end apart: 14 -> 15, of which waited for: 8 -> 9; matrix products, arithmetic and copies ran while one was open for 3% -> 7% of each run, Pallas kernels for 10% -> 11%
where the time goes in v4:
time: 220 us; the launch traced here: 219 us
  Pallas kernels  86.3 us (39%)
  starting transfers between devices  56.7 us (26%)
  waiting for transfers between devices  38.7 us (18%)
  local copies, waits for them, and re-layouts  16.6 us (8%)
  blocking collectives  10.7 us (5%)
  other arithmetic  8.77 us (4%)
    pallas_call x1, Pallas kernels, attend_grad(): pl.pallas_call(attend_grad_kernel, name='attend_grad', grid_spec=pltpu.Pr...  28.9 us
    pallas_call x1, Pallas kernels, attend(): pl.pallas_call(attend_kernel, name='attend', grid=(HEADS,), in_specs=[who...  16 us
    pallas_call x1, Pallas kernels, conv_forward(): pl.pallas_call(conv_kernel_body, name='conv_forward', out_shape=[jax.Shap...  14.7 us
    pallas_call x1, Pallas kernels, conv_back(): pl.pallas_call(conv_back_body, name='conv_back', out_shape=[jax.ShapeDtyp...  12.7 us
    all_to_all x2, starting transfers between devices, send(): return lax.all_to_all(x, CHIPS, 0, 0, tiled=True)  12.4 us
    all_to_all x2, waiting for transfers between devices, send_all(): return lax.all_to_all(x, ALL, 0, 0, tiled=True)  11.9 us
    all_to_all x2, waiting for transfers between devices, send(): return lax.all_to_all(x, CHIPS, 0, 0, tiled=True)  11.8 us
    pallas_call x1, Pallas kernels, kernel_grad(): pl.pallas_call(kernel_grad_body, name='kernel_grad', out_shape=jax.ShapeD...  10.8 us
  transfers between devices with their start and end apart: 15, of which 9 were waited for; matrix products, arithmetic and copies ran while one was open for 7% of the time, Pallas kernels for 11%

profile of v4, /device:TPU:1, one launch (start us, length us, event | category | flops | bytes accessed | tf_op | source)
XLA Modules:
  0.0 218.8 jit_solution(3357166564048590163)
XLA Ops:
  2.0 3.2 %embed.1 = (bf16[2048,256]{1,0:T(8,128)(2,1)}, bf16[256,512]{1,0:T(8,128)(2,1)}, bf16[224,256]{1,0:T(8,128)(2,1)}, bf16[224,256]{1,0:T(8,128)(2,1)}, bf16[96,256]{1,0:T(8,128)(2,1)}, /*index=5*/bf16[96,256]{1,0:T(8,128)(2,1)}) custom-call(bf16[384,256]{1,0:T(8,128)(2,1)} %bitcast.113, bf16[4,16,256]{2,1,0:T(8,128)(2,1)} %pad.8.weights, f32[1,256]{1,0:T(1,128)} %bitcast.120), custom_call_target="tpu_custom_call" | custom-call | tf_op jit(solution)/shard_map/embed/pallas_call | solution.py:202
  5.2 4.9 %collective-permute-start = (bf16[224,256]{1,0:T(8,128)(2,1)}, bf16[224,256]{1,0:T(8,128)(2,1)S(1)}, u32[]{:S(2)}, u32[]{:S(2)}) collective-permute-start(bf16[224,256]{1,0:T(8,128)(2,1)} %get-tuple-element.50), channel_id=1, source_target_pairs={{0,16},{16,32},{32,48},{48,64},{64,80},{80,96},{96,112},{1,17},{17... | collective-permute-start | bytes 344072 | tf_op jit(solution)/shard_map/ppermute | solution.py:82
  10.1 1.9 collective-permute-start.1
  12.2 4.2 %collective-permute-done.1.below = bf16[224,256]{1,0:T(8,128)(2,1)S(1)} collective-permute-done((bf16[224,256]{1,0:T(8,128)(2,1)}, bf16[224,256]{1,0:T(8,128)(2,1)S(1)}, u32[]{:S(2)}, u32[]{:S(2)}) %collective-permute-start.1) | collective-permute-done | bytes 114720 | tf_op jit(solution)/shard_map/ppermute | solution.py:83
  19.3 4.0 %collective-permute-start.2 = (bf16[128,256]{1,0:T(8,128)(2,1)S(1)}, bf16[128,256]{1,0:T(8,128)(2,1)S(1)}, u32[]{:S(2)}, u32[]{:S(2)}) collective-permute-start(bf16[128,256]{1,0:T(8,128)(2,1)S(1)} %pad_maximum_fusion.1), channel_id=1, source_target_pairs={{0,1},{1,2},{2,3},{3,4},{4,5},{5,6},{6,7},{7,8},{8,9},{9,10},{10,1... | collective-permute-start | bytes 196616 | tf_op jit(solution)/shard_map/ppermute | solution.py:93
  25.3 14.7 %conv_forward.1 = (f32[38,14,8,256]{3,2,1,0:T(8,128)}, f32[2048,256]{1,0:T(8,128)}, f32[2048,128]{1,0:T(8,128)}, bf16[2048,256]{1,0:T(8,128)(2,1)}) custom-call(bf16[2048,256]{1,0:T(8,128)(2,1)} %get-tuple-element.49.emb, bf16[224,256]{1,0:T(8,128)(2,1)} %copy-done.1, bf16[224,256]{1,0:T(8,128)(2,1)} %copy-done.2, bf16[128,256]{1,0:T(8,128)(2,1)} %copy-done.4, ...), custom_call_target="tpu_custom_call" | custom-call | tf_op jit(solution)/shard_map/conv_forward/pallas_call | solution.py:243
  40.0 16.0 %attend.1 = (bf16[2048,1024]{1,0:T(8,128)(2,1)}, bf16[2048,1024]{1,0:T(8,128)(2,1)}, f32[8,128,256]{2,1,0:T(8,128)}, f32[3,8,256]{2,1,0:T(8,128)}) custom-call(bf16[2048,256]{1,0:T(8,128)(2,1)} %get-tuple-element.54.normed, bf16[256,2048]{1,0:T(8,128)(2,1)} %wv.3, bf16[256,2048]{1,0:T(8,128)(2,1)} %wv.3, bf16[256,1024]{1,0:T(8,128)(2,1)} %q.3, ...), custom_call_target="tpu_custom_call" | custom-call | tf_op jit(solution)/shard_map/attend/pallas_call | solution.py:300
  56.8 10.7 %all_to_all.30 = f32[8,3,8,256]{3,2,1,0:T(8,128)S(1)} all-to-all(f32[8,3,8,256]{3,2,1,0:T(8,128)S(1)} %broadcast_in_dim.10), channel_id=1, replica_groups=mesh['z'=4,'core'=2,'x'=4,'y'=4] {'z','core'}, dimensions={0} | all-to-all | bytes 393216 | tf_op jit(solution)/shard_map/all_to_all | solution.py:541
  68.4 9.6 %all-to-all-start.1 = ((f32[16,3,8,256]{3,2,1,0:T(8,128)}), f32[16,3,8,256]{3,2,1,0:T(8,128)S(1)}, u32[]{:S(2)}, u32[]{:S(2)}) async-start(f32[16,3,8,256]{3,2,1,0:T(8,128)} %broadcast_in_dim.11), calls=%async_computation.1 | async-start | bytes 786432 | tf_op jit(solution)/shard_map/all_to_all | solution.py:541
  78.0 8.1 %all-to-all-done.1 = f32[16,3,8,256]{3,2,1,0:T(8,128)S(1)} async-done(((f32[16,3,8,256]{3,2,1,0:T(8,128)}), f32[16,3,8,256]{3,2,1,0:T(8,128)S(1)}, u32[]{:S(2)}, u32[]{:S(2)}) %all-to-all-start.1) | async-done | bytes 393248 | tf_op jit(solution)/shard_map/all_to_all | solution.py:541
  86.2 1.3 fusion.15
  87.5 28.9 %attend_grad.1 = (f32[4,4,256,128]{3,2,1,0:T(8,128)}, f32[4,4,256,128]{3,2,1,0:T(8,128)}, bf16[2048,256]{1,0:T(8,128)(2,1)}, f32[1,256]{1,0:T(1,128)}, bf16[224,...) custom-call(s32[1]{0:T(128)} %bitcast.core, ...), custom_call_target="tpu_custom_call" | custom-call | flops 14000000000 | bytes 16000000 | tf_op jit(solution)/shard_map/attend_grad/pallas_call | solution.py:408
  116.4 2.7 %collective-permute-start.4 = (f32[4,4,256,128]{3,2,1,0:T(8,128)}, f32[4,4,256,128]{3,2,1,0:T(8,128)S(1)}, u32[]{:S(2)}, u32[]{:S(2)}) collective-permute-start(f32[4,4,256,128]{3,2,1,0:T(8,128)} %get-tuple-element.63), channel_id=1, source_target_pairs={{0,16},{16,0},{1,17},{17,1},{2,18},{18,2},{3,19},{19,3},{4,20},{20... | collective-permute-start | bytes 6291464 | tf_op jit(solution)/shard_map/ppermute | solution.py:605
  119.2 2.1 collective-permute-start.5
  121.3 2.2 %collective-permute-start.6 = (bf16[224,256]{1,0:T(8,128)(2,1)}, bf16[224,256]{1,0:T(8,128)(2,1)S(1)}, u32[]{:S(2)}, u32[]{:S(2)}) collective-permute-start(bf16[224,256]{1,0:T(8,128)(2,1)} %get-tuple-element.65), channel_id=1, source_target_pairs={{16,0},{32,16},{48,32},{64,48},{80,64},{96,80},{112,96},{17,1},{33... | collective-permute-start | bytes 344072 | tf_op jit(solution)/shard_map/ppermute | solution.py:83
  123.5 2.9 %add_convert_fusion = bf16[4,4,256,128]{3,2,1,0:T(8,128)(2,1)} fusion(f32[4,4,256,128]{3,2,1,0:T(8,128)} %get-tuple-element.62, f32[4,4,256,128]{3,2,1,0:T(8,128)S(1)} %collective-permute-done.4), kind=kLoop, calls=%fused_computation | loop fusion | flops 1048576 | bytes 5242880 | tf_op jit(solution)/shard_map/convert_element_type | solution.py:605
  128.9 4.0 %collective-permute-start.7 = (bf16[128,256]{1,0:T(8,128)(2,1)S(1)}, bf16[128,256]{1,0:T(8,128)(2,1)S(1)}, u32[]{:S(2)}, u32[]{:S(2)}) collective-permute-start(bf16[128,256]{1,0:T(8,128)(2,1)S(1)} %pad_maximum_fusion.3), channel_id=1, source_target_pairs={{0,1},{1,2},{2,3},{3,4},{4,5},{5,6},{6,7},{7,8},{8,9},{9,10},{10,1... | collective-permute-start | bytes 196616 | tf_op jit(solution)/shard_map/ppermute | solution.py:93
  132.9 7.4 %all-to-all-start.2 = ((bf16[64,64,128]{2,1,0:T(8,128)(2,1)}), bf16[64,64,128]{2,1,0:T(8,128)(2,1)S(1)}, u32[]{:S(2)}, u32[]{:S(2)}) async-start(bf16[64,64,128]{2,1,0:T(8,128)(2,1)} %bitcast.15), calls=%async_computation.2 | async-start | bytes 2097152 | tf_op jit(solution)/shard_map/all_to_all | solution.py:571
  140.4 10.8 %kernel_grad.1 = f32[49,256]{1,0:T(8,128)} custom-call(f32[38,14,8,256]{3,2,1,0:T(8,128)} %get-tuple-element.68.wide, bf16[2048,256]{1,0:T(8,128)(2,1)} %get-tuple-element.75.d_mixed), custom_call_target="tpu_custom_call" | custom-call | flops 14000000000 | bytes 16000000 | tf_op jit(solution)/shard_map/kernel_grad/pallas_call | solution.py:478
  151.2 7.7 %all-to-all-done.2 = bf16[64,64,128]{2,1,0:T(8,128)(2,1)S(1)} async-done(((bf16[64,64,128]{2,1,0:T(8,128)(2,1)}), bf16[64,64,128]{2,1,0:T(8,128)(2,1)S(1)}, u32[]{:S(2)}, u32[]{:S(2)}) %all-to-all-start.2) | async-done | bytes 1048608 | tf_op jit(solution)/shard_map/all_to_all | solution.py:571
  160.3 5.0 %all-to-all-start.3 = ((bf16[64,64,128]{2,1,0:T(8,128)(2,1)}), bf16[64,64,128]{2,1,0:T(8,128)(2,1)S(1)}, u32[]{:S(2)}, u32[]{:S(2)}) async-start(bf16[64,64,128]{2,1,0:T(8,128)(2,1)} %broadcast_in_dim.12), calls=%async_computation.3 | async-start | bytes 2097152 | tf_op jit(solution)/shard_map/all_to_all | solution.py:571
  165.3 12.7 %conv_back.1 = (f32[4,16,256]{2,1,0:T(8,128)}, f32[1,256]{1,0:T(1,128)}) custom-call(bf16[2048,256]{1,0:T(8,128)(2,1)} %get-tuple-element.75.d_mixed, bf16[224,256]{1,0:T(8,128)(2,1)} %copy-done.8, bf16[224,256]{1,0:T(8,128)(2,1)} %copy-done.9, bf16[128,256]{1,0:T(8,128)(2,1)} %copy-done.12, bf16[128,256]{1,0:T(8,128)(2,1)} %copy-done.11, f32[49,256]{1,0:T(8,128)} %kern.3, ...), custom_call_target="tpu_custom_call" | custom-call | flops 14000000000 | bytes 16000000 | tf_op jit(solution)/shard_map/conv_back/pallas_call | solution.py:518
  177.9 4.1 %all-to-all-done.3 = bf16[64,64,128]{2,1,0:T(8,128)(2,1)S(1)} async-done(((bf16[64,64,128]{2,1,0:T(8,128)(2,1)}), bf16[64,64,128]{2,1,0:T(8,128)(2,1)S(1)}, u32[]{:S(2)}, u32[]{:S(2)}) %all-to-all-start.3) | async-done | bytes 1048608 | tf_op jit(solution)/shard_map/all_to_all | solution.py:571
  182.0 2.7 %collective-permute-start.9 = (bf16[64,64,128]{2,1,0:T(8,128)(2,1)S(1)}, bf16[64,64,128]{2,1,0:T(8,128)(2,1)}, u32[]{:S(2)}, u32[]{:S(2)}) collective-permute-start(bf16[64,64,128]{2,1,0:T(8,128)(2,1)S(1)} %all-to-all-done.3), channel_id=1, source_target_pairs={{0,16},{16,0},{1,17},{17,1},{2,18},{18,2},{3,19},{19,3},{4,20},{20... | collective-permute-start | bytes 3145736 | tf_op jit(solution)/shard_map/ppermute | solution.py:556
  186.4 3.5 %all-to-all-start.4 = ((f32[128,1,256]{2,1,0:T(1,128)}), f32[128,1,256]{2,1,0:T(1,128)S(1)}, u32[]{:S(2)}, u32[]{:S(2)}) async-start(f32[128,1,256]{2,1,0:T(1,128)} %broadcast_in_dim.13), calls=%async_computation.4 | async-start | bytes 262144 | tf_op jit(solution)/shard_map/all_to_all | solution.py:575
  189.9 10.1 %all-to-all-done.4 = f32[128,1,256]{2,1,0:T(1,128)S(1)} async-done(((f32[128,1,256]{2,1,0:T(1,128)}), f32[128,1,256]{2,1,0:T(1,128)S(1)}, u32[]{:S(2)}, u32[]{:S(2)}) %all-to-all-start.4) | async-done | bytes 131104 | tf_op jit(solution)/shard_map/all_to_all | solution.py:575
  200.9 4.1 %all-to-all-start.5 = ((f32[128,1,256]{2,1,0:T(1,128)}), f32[128,1,256]{2,1,0:T(1,128)S(1)}, u32[]{:S(2)}, u32[]{:S(2)}) async-start(f32[128,1,256]{2,1,0:T(1,128)} %broadcast_in_dim.14), calls=%async_computation.5 | async-start | bytes 262144 | tf_op jit(solution)/shard_map/all_to_all | solution.py:575
  205.0 1.4 broadcast_select_fusion.1
  206.5 1.5 copy.73
  208.0 2.9 %copy.74 = f32[256,16,128]{0,2,1:T(8,128)} copy(f32[256,16,128]{2,0,1:T(8,128)} %bitcast.107) | data formatting | bytes 4194304 | tf_op jit(solution)/shard_map/transpose | solution.py:583
  213.2 1.8 all-to-all-done.5
  215.6 1.8 copy.76
  (72 shorter events, 18.9 us)
Async XLA Ops:
  5.2 7.0 %collective-permute-start = (bf16[224,256]{1,0:T(8,128)(2,1)}, bf16[224,256]{1,0:T(8,128)(2,1)S(1)}, u32[]{:S(2)}, u32[]{:S(2)}) collective-permute-start(bf16[224,256]{1,0:T(8,128)(2,1)} %get-tuple-element.50), channel_id=1, source_target_pairs={{0,16},{16,32},{32,48},{48,64},{64,80},{80,96},{96,112},{1,17},{17... | collective-permute-start | bytes 344072 | tf_op jit(solution)/shard_map/ppermute | solution.py:82
  10.1 6.3 %collective-permute-start.1 = (bf16[224,256]{1,0:T(8,128)(2,1)}, bf16[224,256]{1,0:T(8,128)(2,1)S(1)}, u32[]{:S(2)}, u32[]{:S(2)}) collective-permute-start(bf16[224,256]{1,0:T(8,128)(2,1)} %get-tuple-element.51), channel_id=1, source_target_pairs={{16,0},{32,16},{48,32},{64,48},{80,64},{96,80},{112,96},{17,1},{33... | collective-permute-start | bytes 344072 | tf_op jit(solution)/shard_map/ppermute | solution.py:83
  12.2 12.5 %copy-start.1 = (bf16[224,256]{1,0:T(8,128)(2,1)}, bf16[224,256]{1,0:T(8,128)(2,1)S(1)}, u32[]{:S(2)}) copy-start(bf16[224,256]{1,0:T(8,128)(2,1)S(1)} %collective-permute-done.above) | copy-start | bytes 344068
  16.4 8.2 %copy-start.2 = (bf16[224,256]{1,0:T(8,128)(2,1)}, bf16[224,256]{1,0:T(8,128)(2,1)S(1)}, u32[]{:S(2)}) copy-start(bf16[224,256]{1,0:T(8,128)(2,1)S(1)} %collective-permute-done.1.below) | copy-start | bytes 344068
  17.2 6.1 %collective-permute-start.3 = (bf16[128,256]{1,0:T(8,128)(2,1)S(1)}, bf16[128,256]{1,0:T(8,128)(2,1)S(1)}, u32[]{:S(2)}, u32[]{:S(2)}) collective-permute-start(bf16[128,256]{1,0:T(8,128)(2,1)S(1)} %pad_maximum_fusion.2), channel_id=1, source_target_pairs={{1,0},{2,1},{3,2},{4,3},{5,4},{6,5},{7,6},{8,7},{9,8},{10,9},{11,1... | collective-permute-start | bytes 196616 | tf_op jit(solution)/shard_map/ppermute | solution.py:94
  19.3 5.3 %collective-permute-start.2 = (bf16[128,256]{1,0:T(8,128)(2,1)S(1)}, bf16[128,256]{1,0:T(8,128)(2,1)S(1)}, u32[]{:S(2)}, u32[]{:S(2)}) collective-permute-start(bf16[128,256]{1,0:T(8,128)(2,1)S(1)} %pad_maximum_fusion.1), channel_id=1, source_target_pairs={{0,1},{1,2},{2,3},{3,4},{4,5},{5,6},{6,7},{7,8},{8,9},{9,10},{10,1... | collective-permute-start | bytes 196616 | tf_op jit(solution)/shard_map/ppermute | solution.py:93
  23.3 1.3 copy-start.3
  24.6 0.6 copy-start.4
  68.4 17.7 %all-to-all-start.1 = ((f32[16,3,8,256]{3,2,1,0:T(8,128)}), f32[16,3,8,256]{3,2,1,0:T(8,128)S(1)}, u32[]{:S(2)}, u32[]{:S(2)}) async-start(f32[16,3,8,256]{3,2,1,0:T(8,128)} %broadcast_in_dim.11), calls=%async_computation.1 | async-start | bytes 786432 | tf_op jit(solution)/shard_map/all_to_all | solution.py:541
  116.4 7.0 %collective-permute-start.4 = (f32[4,4,256,128]{3,2,1,0:T(8,128)}, f32[4,4,256,128]{3,2,1,0:T(8,128)S(1)}, u32[]{:S(2)}, u32[]{:S(2)}) collective-permute-start(f32[4,4,256,128]{3,2,1,0:T(8,128)} %get-tuple-element.63), channel_id=1, source_target_pairs={{0,16},{16,0},{1,17},{17,1},{2,18},{18,2},{3,19},{19,3},{4,20},{20... | collective-permute-start | bytes 6291464 | tf_op jit(solution)/shard_map/ppermute | solution.py:605
  119.2 7.2 %collective-permute-start.5 = (bf16[224,256]{1,0:T(8,128)(2,1)}, bf16[224,256]{1,0:T(8,128)(2,1)S(1)}, u32[]{:S(2)}, u32[]{:S(2)}) collective-permute-start(bf16[224,256]{1,0:T(8,128)(2,1)} %get-tuple-element.64), channel_id=1, source_target_pairs={{0,16},{16,32},{32,48},{48,64},{64,80},{80,96},{96,112},{1,17},{17... | collective-permute-start | bytes 344072 | tf_op jit(solution)/shard_map/ppermute | solution.py:82
  121.3 6.3 %collective-permute-start.6 = (bf16[224,256]{1,0:T(8,128)(2,1)}, bf16[224,256]{1,0:T(8,128)(2,1)S(1)}, u32[]{:S(2)}, u32[]{:S(2)}) collective-permute-start(bf16[224,256]{1,0:T(8,128)(2,1)} %get-tuple-element.65), channel_id=1, source_target_pairs={{16,0},{32,16},{48,32},{64,48},{80,64},{96,80},{112,96},{17,1},{33... | collective-permute-start | bytes 344072 | tf_op jit(solution)/shard_map/ppermute | solution.py:83
  123.5 4.1 %copy-start.7 = (bf16[96,256]{1,0:T(8,128)(2,1)S(1)}, bf16[96,256]{1,0:T(8,128)(2,1)}, u32[]{:S(2)}) copy-start(bf16[96,256]{1,0:T(8,128)(2,1)} %get-tuple-element.72) | copy-start | bytes 147460
  123.5 5.4 %copy-start.6 = (bf16[96,256]{1,0:T(8,128)(2,1)S(1)}, bf16[96,256]{1,0:T(8,128)(2,1)}, u32[]{:S(2)}) copy-start(bf16[96,256]{1,0:T(8,128)(2,1)} %get-tuple-element.69) | copy-start | bytes 147460
  126.4 24.8 %copy-start.8 = (bf16[224,256]{1,0:T(8,128)(2,1)}, bf16[224,256]{1,0:T(8,128)(2,1)S(1)}, u32[]{:S(2)}) copy-start(bf16[224,256]{1,0:T(8,128)(2,1)S(1)} %collective-permute-done.5.above) | copy-start | bytes 344068
  127.6 23.6 %copy-start.9 = (bf16[224,256]{1,0:T(8,128)(2,1)}, bf16[224,256]{1,0:T(8,128)(2,1)S(1)}, u32[]{:S(2)}) copy-start(bf16[224,256]{1,0:T(8,128)(2,1)S(1)} %collective-permute-done.6.below) | copy-start | bytes 344068
  127.6 23.5 %collective-permute-start.8 = (bf16[128,256]{1,0:T(8,128)(2,1)S(1)}, bf16[128,256]{1,0:T(8,128)(2,1)S(1)}, u32[]{:S(2)}, u32[]{:S(2)}) collective-permute-start(bf16[128,256]{1,0:T(8,128)(2,1)S(1)} %pad_maximum_fusion.4), channel_id=1, source_target_pairs={{1,0},{2,1},{3,2},{4,3},{5,4},{6,5},{7,6},{8,7},{9,8},{10,9},{11,1... | collective-permute-start | bytes 196616 | tf_op jit(solution)/shard_map/ppermute | solution.py:94
  128.9 22.2 %collective-permute-start.7 = (bf16[128,256]{1,0:T(8,128)(2,1)S(1)}, bf16[128,256]{1,0:T(8,128)(2,1)S(1)}, u32[]{:S(2)}, u32[]{:S(2)}) collective-permute-start(bf16[128,256]{1,0:T(8,128)(2,1)S(1)} %pad_maximum_fusion.3), channel_id=1, source_target_pairs={{0,1},{1,2},{2,3},{3,4},{4,5},{5,6},{6,7},{7,8},{8,9},{9,10},{10,1... | collective-permute-start | bytes 196616 | tf_op jit(solution)/shard_map/ppermute | solution.py:93
  132.9 25.9 %all-to-all-start.2 = ((bf16[64,64,128]{2,1,0:T(8,128)(2,1)}), bf16[64,64,128]{2,1,0:T(8,128)(2,1)S(1)}, u32[]{:S(2)}, u32[]{:S(2)}) async-start(bf16[64,64,128]{2,1,0:T(8,128)(2,1)} %bitcast.15), calls=%async_computation.2 | async-start | bytes 2097152 | tf_op jit(solution)/shard_map/all_to_all | solution.py:571
  151.1 9.1 %copy-start.11 = (bf16[128,256]{1,0:T(8,128)(2,1)}, bf16[128,256]{1,0:T(8,128)(2,1)S(1)}, u32[]{:S(2)}) copy-start(bf16[128,256]{1,0:T(8,128)(2,1)S(1)} %collective-permute-done.8.rh) | copy-start | bytes 196612
  151.2 9.1 %copy-start.12 = (bf16[128,256]{1,0:T(8,128)(2,1)}, bf16[128,256]{1,0:T(8,128)(2,1)S(1)}, u32[]{:S(2)}) copy-start(bf16[128,256]{1,0:T(8,128)(2,1)S(1)} %collective-permute-done.7.lh) | copy-start | bytes 196612
  160.3 21.8 %all-to-all-start.3 = ((bf16[64,64,128]{2,1,0:T(8,128)(2,1)}), bf16[64,64,128]{2,1,0:T(8,128)(2,1)S(1)}, u32[]{:S(2)}, u32[]{:S(2)}) async-start(bf16[64,64,128]{2,1,0:T(8,128)(2,1)} %broadcast_in_dim.12), calls=%async_computation.3 | async-start | bytes 2097152 | tf_op jit(solution)/shard_map/all_to_all | solution.py:571
  165.3 19.5 %copy-start.5 = (f32[49,256]{1,0:T(8,128)S(1)}, f32[49,256]{1,0:T(8,128)}, u32[]{:S(2)}) copy-start(f32[49,256]{1,0:T(8,128)} %kernel_grad.1) | copy-start | bytes 150532
  165.3 19.5 %copy-start.10 = (f32[1,256]{1,0:T(1,128)S(1)}, f32[1,256]{1,0:T(1,128)}, u32[]{:S(2)}) copy-start(f32[1,256]{1,0:T(1,128)} %get-tuple-element.84) | copy-start | bytes 3076
  182.0 23.0 %collective-permute-start.9 = (bf16[64,64,128]{2,1,0:T(8,128)(2,1)S(1)}, bf16[64,64,128]{2,1,0:T(8,128)(2,1)}, u32[]{:S(2)}, u32[]{:S(2)}) collective-permute-start(bf16[64,64,128]{2,1,0:T(8,128)(2,1)S(1)} %all-to-all-done.3), channel_id=1, source_target_pairs={{0,16},{16,0},{1,17},{17,1},{2,18},{18,2},{3,19},{19,3},{4,20},{20... | collective-permute-start | bytes 3145736 | tf_op jit(solution)/shard_map/ppermute | solution.py:556
  186.4 13.6 %all-to-all-start.4 = ((f32[128,1,256]{2,1,0:T(1,128)}), f32[128,1,256]{2,1,0:T(1,128)S(1)}, u32[]{:S(2)}, u32[]{:S(2)}) async-start(f32[128,1,256]{2,1,0:T(1,128)} %broadcast_in_dim.13), calls=%async_computation.4 | async-start | bytes 262144 | tf_op jit(solution)/shard_map/all_to_all | solution.py:575
  200.9 14.2 %all-to-all-start.5 = ((f32[128,1,256]{2,1,0:T(1,128)}), f32[128,1,256]{2,1,0:T(1,128)S(1)}, u32[]{:S(2)}, u32[]{:S(2)}) async-start(f32[128,1,256]{2,1,0:T(1,128)} %broadcast_in_dim.14), calls=%async_computation.5 | async-start | bytes 262144 | tf_op jit(solution)/shard_map/all_to_all | solution.py:575
  211.0 4.6 %copy-start = (f32[256,16,128]{0,2,1:T(8,128)S(1)}, f32[256,16,128]{0,2,1:T(8,128)}, u32[]{:S(2)}) copy-start(f32[256,16,128]{0,2,1:T(8,128)} %copy.74) | copy-start | bytes 6291460

commit v5 on v4

--- a/solution.py
+++ b/solution.py
@@ -21,7 +21,7 @@
 CH = 256
 TOK = ROWS * COLS
 WIDE = 14
-BLOCK = 256
+BLOCK = 1024
 WIRE = BF
 ROW_AXES = ("z", "core")
 COL_AXES = ("x", "y")
@@ -254,64 +254,77 @@
     )(emb, *halo, conv_kernel, gain)
 
 
-CHUNK = 512
+CHUNK = 1024
+GROUP = 2
+ACHUNK = 1024
+WIDTH = 4
 SCALE = 128**-0.5
 SCALE2 = SCALE * 1.4426950408889634
 COST = pl.CostEstimate(flops=14_000_000_000, transcendentals=0, bytes_accessed=16_000_000)
 
 
+def lane(n):
+    return slice(n * 128, (n + 1) * 128)
+
+
 def attend_kernel(normed, wk, wv, q, up, k_out, v_out, weighted, stats, s_sc):
-    h = pl.program_id(0)
-    w = jnp.concatenate([wk[...], wv[...]], axis=1)
-    peak = None
-    for c in range(TOK // CHUNK):
-        rows = slice(c * CHUNK, (c + 1) * CHUNK)
-        kv = dot(normed[rows, :], w).astype(BF)
-        k_out[rows, :] = kv[:, :128]
-        v_out[rows, :] = kv[:, 128:]
-        s = dot(kv[:, :128], q[...], NT)
-        s_sc[rows, :] = s
-        top = jnp.max(s, axis=0, keepdims=True)
-        peak = top if peak is None else jnp.maximum(peak, top)
-    level = peak * SCALE2
-    total = jnp.zeros((1, 256), F32)
-    acc = jnp.zeros((128, 256), F32)
-    for c in range(TOK // CHUNK):
-        rows = slice(c * CHUNK, (c + 1) * CHUNK)
-        p = jnp.exp2(s_sc[rows, :] * SCALE2 - level)
-        total = total + jnp.sum(p, axis=0, keepdims=True)
-        acc = acc + dot(v_out[rows, :], p.astype(BF), TN)
-    weighted[0] = acc
-    dots = jnp.sum(acc * up[...].astype(F32).T, axis=0, keepdims=True)
-    stats[0, pl.ds(h, 1), :] = level
-    stats[1, pl.ds(h, 1), :] = total
-    stats[2, pl.ds(h, 1), :] = dots
+    step = pl.program_id(0)
+    peak = [None] * WIDTH
+    level = None
+    for n in range(WIDTH + 1):
+        total = jnp.zeros((1, 256), F32)
+        acc = jnp.zeros((128, 256), F32)
+        if n < WIDTH:
+            w = jnp.concatenate([wk[:, lane(n)], wv[:, lane(n)]], axis=1)
+        for c in range(TOK // ACHUNK):
+            rows = slice(c * ACHUNK, (c + 1) * ACHUNK)
+            if n < WIDTH:
+                kv = dot(normed[rows, :], w).astype(BF)
+                k_out[rows, lane(n)] = kv[:, :128]
+                v_out[rows, lane(n)] = kv[:, 128:]
+                s = dot(kv[:, :128], q[:, lane(n)], NT)
+                s_sc[n % 2, rows, :] = s
+                top = jnp.max(s, axis=0, keepdims=True)
+                peak[n] = top if peak[n] is None else jnp.maximum(peak[n], top)
+            if n > 0:
+                p = jnp.exp2(s_sc[1 - n % 2, rows, :] * SCALE2 - level)
+                total = total + jnp.sum(p, axis=0, keepdims=True)
+                acc = acc + dot(v_out[rows, lane(n - 1)], p.astype(BF), TN)
+        if n > 0:
+            weighted[n - 1] = acc
+            dots = jnp.sum(acc * up[:, lane(n - 1)].astype(F32).T, axis=0, keepdims=True)
+            h = step * WIDTH + n - 1
+            stats[0, pl.ds(h, 1), :] = level
+            stats[1, pl.ds(h, 1), :] = total
+            stats[2, pl.ds(h, 1), :] = dots
+        if n < WIDTH:
+            level = peak[n] * SCALE2
 
 
 def whole(shape):
     return pl.BlockSpec(shape, lambda h: (0,) * len(shape))
 
 
-def column(rows, width, first=0):
-    return pl.BlockSpec((rows, width), lambda h: (0, h + first))
+def column(rows, first=0):
+    return pl.BlockSpec((rows, 128 * WIDTH), lambda h: (0, h + first))
 
 
 def attend(normed, kv_weight, latents, d_attended):
     return pl.pallas_call(
         attend_kernel,
         name="attend",
-        grid=(HEADS,),
+        grid=(HEADS // WIDTH,),
         in_specs=[
             whole((TOK, CH)),
-            column(CH, 128),
-            column(CH, 128, HEADS),
-            column(256, 128),
-            column(256, 128),
+            column(CH),
+            column(CH, HEADS // WIDTH),
+            column(256),
+            column(256),
         ],
         out_specs=[
-            column(TOK, 128),
-            column(TOK, 128),
-            pl.BlockSpec((1, 128, 256), lambda h: (h, 0, 0)),
+            column(TOK),
+            column(TOK),
+            pl.BlockSpec((WIDTH, 128, 256), lambda h: (h, 0, 0)),
             whole((3, HEADS, 256)),
         ],
         out_shape=[
@@ -320,13 +333,16 @@
             jax.ShapeDtypeStruct((HEADS, 128, 256), F32),
             jax.ShapeDtypeStruct((3, HEADS, 256), F32),
         ],
-        scratch_shapes=[pltpu.VMEM((TOK, 256), F32)],
+        scratch_shapes=[pltpu.VMEM((2, TOK, 256), F32)],
         compiler_params=VMEM,
     )(normed, kv_weight, kv_weight, latents, d_attended)
 
 
-def head_at(step, core):
-    return (step + HEADS // 2 * (1 - core[0])) & (HEADS - 1)
+STEPS = HEADS // GROUP
+
+
+def step_at(step, core):
+    return (step + STEPS // 2 * (1 - core[0])) & (STEPS - 1)
 
 
 def attend_grad_kernel(
@@ -334,48 +350,63 @@
     send, keep, d_mixed, gain_grad, top, bot, left, right, dn_sc, nt_sc, l_sc, r_sc, c_sc,
 ):
     step = pl.program_id(0)
-    h = head_at(step, core)
+    first = step_at(step, core) * GROUP
 
     @pl.when(step == 0)
     def _():
         nt_sc[...] = normed[...].T
         dn_sc[...] = jnp.zeros_like(dn_sc)
 
-    w = jnp.concatenate([wk[...], wv[...]], axis=1)
-    level = lse[pl.ds(h, 1), :]
-    row_dots = dots[pl.ds(h, 1), :]
-    qg = jnp.zeros((128, 256), F32)
-    wg = jnp.zeros((256, 256), F32)
-    for c in range(TOK // CHUNK):
+    w = jnp.concatenate([x[:, lane(n)] for n in range(GROUP) for x in (wk, wv)], axis=1)
+    level = [lse[pl.ds(first + n, 1), :] for n in range(GROUP)]
+    row_dots = [dots[pl.ds(first + n, 1), :] for n in range(GROUP)]
+    qg = [jnp.zeros((128, 256), F32)] * GROUP
+    wg = jnp.zeros((256, 256 * GROUP), F32)
+    units = [(c, n) for c in range(TOK // CHUNK) for n in range(GROUP)]
+
+    def products(c, n):
         rows = slice(c * CHUNK, (c + 1) * CHUNK)
-        k = k_in[rows, :]
-        p = jnp.exp2(dot(k, q[...], NT) * SCALE2 - level)
-        dp = dot(v_in[rows, :], up[...], NT)
-        ds = (p * (dp - row_dots)).astype(BF)
-        qg = qg + dot(k, ds, TN)
-        kg = (dot(ds, q[...]) * SCALE).astype(BF)
-        vg = dot(p.astype(BF), up[...]).astype(BF)
-        d_proj = jnp.concatenate([kg, vg], axis=1)
-        wg = wg + dot(nt_sc[:, rows], d_proj)
-        dn_sc[rows, :] += dot(d_proj, w, NT)
-    att = (weighted[0] * factor[pl.ds(h, 1), :]).T
-    qg = (qg * SCALE).T
+        return (
+            dot(k_in[rows, lane(n)], q[:, lane(n)], NT),
+            dot(v_in[rows, lane(n)], up[:, lane(n)], NT),
+        )
+
+    d_proj = []
+    ahead = products(*units[0])
+    for at, (c, n) in enumerate(units):
+        rows = slice(c * CHUNK, (c + 1) * CHUNK)
+        s, dp = ahead
+        if at + 1 < len(units):
+            ahead = products(*units[at + 1])
+        p = jnp.exp2(s * SCALE2 - level[n])
+        ds = (p * (dp - row_dots[n])).astype(BF)
+        qg[n] = qg[n] + dot(k_in[rows, lane(n)], ds, TN)
+        d_proj.append((dot(ds, q[:, lane(n)]) * SCALE).astype(BF))
+        d_proj.append(dot(p.astype(BF), up[:, lane(n)]).astype(BF))
+        if n == GROUP - 1:
+            d_proj = jnp.concatenate(d_proj, axis=1)
+            wg = wg + dot(nt_sc[:, rows], d_proj)
+            dn_sc[rows, :] += dot(d_proj, w, NT)
+            d_proj = []
+    att = [(weighted[n] * factor[pl.ds(first + n, 1), :]).T for n in range(GROUP)]
+    qg = [(x * SCALE).T for x in qg]
 
     def put(out):
-        out[0, 0] = att
-        out[1, 0] = qg
-        out[2, 0] = wg[:, :128]
-        out[3, 0] = wg[:, 128:]
-
-    @pl.when(step < HEADS // 2)
+        for n in range(GROUP):
+            out[0, n] = att[n]
+            out[1, n] = qg[n]
+            out[2, n] = wg[:, lane(2 * n)]
+            out[3, n] = wg[:, lane(2 * n + 1)]
+
+    @pl.when(step < STEPS // 2)
     def _():
         put(send)
 
-    @pl.when(step >= HEADS // 2)
+    @pl.when(step >= STEPS // 2)
     def _():
         put(keep)
 
-    @pl.when(step == HEADS - 1)
+    @pl.when(step == STEPS - 1)
     def _():
         def body(n, total):
             rows = pl.ds(pl.multiple_of(n * BLOCK, BLOCK), BLOCK)
@@ -401,35 +432,36 @@
         return pl.BlockSpec(shape, lambda n, core: (0,) * len(shape))
 
     def head(rows, first=0):
-        return pl.BlockSpec((rows, 128), lambda n, core: (0, head_at(n, core) + first))
-
-    half = HEADS // 2
-    part = jax.ShapeDtypeStruct((4, half, 256, 128), F32)
+        return pl.BlockSpec((rows, 128 * GROUP), lambda n, core: (0, step_at(n, core) + first))
+
+    half = STEPS // 2
+    block = (4, GROUP, 256, 128)
+    part = jax.ShapeDtypeStruct((4, HEADS // 2, 256, 128), F32)
     outs = pl.pallas_call(
         attend_grad_kernel,
         name="attend_grad",
         grid_spec=pltpu.PrefetchScalarGridSpec(
             num_scalar_prefetch=1,
-            grid=(HEADS,),
+            grid=(STEPS,),
             in_specs=[
                 full((TOK, CH)),
                 head(TOK),
                 head(TOK),
                 head(CH),
-                head(CH, HEADS),
+                head(CH, STEPS),
                 head(256),
                 head(256),
                 full((HEADS, 256)),
                 full((HEADS, 256)),
                 full((HEADS, 256)),
-                pl.BlockSpec((1, 128, 256), lambda n, core: (head_at(n, core), 0, 0)),
+                pl.BlockSpec((GROUP, 128, 256), lambda n, core: (step_at(n, core), 0, 0)),
                 full((TOK, CH)),
                 full((TOK, 128)),
                 full((1, CH)),
             ],
             out_specs=[
-                pl.BlockSpec((4, 1, 256, 128), lambda n, core: (0, jnp.minimum(n, half - 1), 0, 0)),
-                pl.BlockSpec((4, 1, 256, 128), lambda n, core: (0, jnp.maximum(n - half, 0), 0, 0)),
+                pl.BlockSpec(block, lambda n, core: (0, jnp.minimum(n, half - 1), 0, 0)),
+                pl.BlockSpec(block, lambda n, core: (0, jnp.maximum(n - half, 0), 0, 0)),
                 full((TOK, CH)),
                 full((1, CH)),
             ]

time: 220 us -> 210 us (0.955)
  Pallas kernels: 86.3 us -> 75.8 us
    pallas_call x1, Pallas kernels: 28.9 us -> 23.4 us  [attend_grad(): pl.pallas_call(attend_grad_kernel, name='attend_grad', grid_spec=pltpu.Pr...]
    pallas_call x1, Pallas kernels: 16 us -> 12.1 us  [attend(): pl.pallas_call(attend_kernel, name='attend', grid=(HEADS // WIDTH,), in_s...]
where the time goes in v5:
time: 210 us; the launch traced here: 208 us
  Pallas kernels  75.8 us (36%)
  starting transfers between devices  56.8 us (27%)
  waiting for transfers between devices  38.7 us (18%)
  local copies, waits for them, and re-layouts  16.6 us (8%)
  blocking collectives  10.7 us (5%)
  other arithmetic  8.77 us (4%)
    pallas_call x1, Pallas kernels, attend_grad(): pl.pallas_call(attend_grad_kernel, name='attend_grad', grid_spec=pltpu.Pr...  23.4 us
    pallas_call x1, Pallas kernels, conv_forward(): pl.pallas_call(conv_kernel_body, name='conv_forward', out_shape=[jax.Shap...  13.7 us
    pallas_call x1, Pallas kernels, conv_back(): pl.pallas_call(conv_back_body, name='conv_back', out_shape=[jax.ShapeDtyp...  12.7 us
    all_to_all x2, starting transfers between devices, send(): return lax.all_to_all(x, CHIPS, 0, 0, tiled=True)  12.2 us
    pallas_call x1, Pallas kernels, attend(): pl.pallas_call(attend_kernel, name='attend', grid=(HEADS // WIDTH,), in_s...  12.1 us
    all_to_all x2, waiting for transfers between devices, send(): return lax.all_to_all(x, CHIPS, 0, 0, tiled=True)  12 us
    all_to_all x2, waiting for transfers between devices, send_all(): return lax.all_to_all(x, ALL, 0, 0, tiled=True)  11.7 us
    pallas_call x1, Pallas kernels, kernel_grad(): pl.pallas_call(kernel_grad_body, name='kernel_grad', out_shape=jax.ShapeD...  10.8 us
  transfers between devices with their start and end apart: 15, of which 9 were waited for; matrix products, arithmetic and copies ran while one was open for 7% of the time, Pallas kernels for 11%

profile of v5, /device:TPU:1, one launch (start us, length us, event | category | flops | bytes accessed | tf_op | source)
XLA Modules:
  0.0 208.3 jit_solution(4954456360723529924)
XLA Ops:
  2.0 3.2 %embed.1 = (bf16[2048,256]{1,0:T(8,128)(2,1)}, bf16[256,512]{1,0:T(8,128)(2,1)}, bf16[224,256]{1,0:T(8,128)(2,1)}, bf16[224,256]{1,0:T(8,128)(2,1)}, bf16[96,256]{1,0:T(8,128)(2,1)}, /*index=5*/bf16[96,256]{1,0:T(8,128)(2,1)}) custom-call(bf16[384,256]{1,0:T(8,128)(2,1)} %bitcast.113, bf16[4,16,256]{2,1,0:T(8,128)(2,1)} %pad.8.weights, f32[1,256]{1,0:T(1,128)} %bitcast.120), custom_call_target="tpu_custom_call" | custom-call | tf_op jit(solution)/shard_map/embed/pallas_call | solution.py:202
  5.2 4.9 %collective-permute-start = (bf16[224,256]{1,0:T(8,128)(2,1)}, bf16[224,256]{1,0:T(8,128)(2,1)S(1)}, u32[]{:S(2)}, u32[]{:S(2)}) collective-permute-start(bf16[224,256]{1,0:T(8,128)(2,1)} %get-tuple-element.50), channel_id=1, source_target_pairs={{0,16},{16,32},{32,48},{48,64},{64,80},{80,96},{96,112},{1,17},{17... | collective-permute-start | bytes 344072 | tf_op jit(solution)/shard_map/ppermute | solution.py:82
  10.1 1.9 collective-permute-start.1
  12.2 4.2 %collective-permute-done.1.below = bf16[224,256]{1,0:T(8,128)(2,1)S(1)} collective-permute-done((bf16[224,256]{1,0:T(8,128)(2,1)}, bf16[224,256]{1,0:T(8,128)(2,1)S(1)}, u32[]{:S(2)}, u32[]{:S(2)}) %collective-permute-start.1) | collective-permute-done | bytes 114720 | tf_op jit(solution)/shard_map/ppermute | solution.py:83
  19.3 4.0 %collective-permute-start.2 = (bf16[128,256]{1,0:T(8,128)(2,1)S(1)}, bf16[128,256]{1,0:T(8,128)(2,1)S(1)}, u32[]{:S(2)}, u32[]{:S(2)}) collective-permute-start(bf16[128,256]{1,0:T(8,128)(2,1)S(1)} %pad_maximum_fusion.1), channel_id=1, source_target_pairs={{0,1},{1,2},{2,3},{3,4},{4,5},{5,6},{6,7},{7,8},{8,9},{9,10},{10,1... | collective-permute-start | bytes 196616 | tf_op jit(solution)/shard_map/ppermute | solution.py:93
  25.3 13.7 %conv_forward.1 = (f32[38,14,8,256]{3,2,1,0:T(8,128)}, f32[2048,256]{1,0:T(8,128)}, f32[2048,128]{1,0:T(8,128)}, bf16[2048,256]{1,0:T(8,128)(2,1)}) custom-call(bf16[2048,256]{1,0:T(8,128)(2,1)} %get-tuple-element.49.emb, bf16[224,256]{1,0:T(8,128)(2,1)} %copy-done.1, bf16[224,256]{1,0:T(8,128)(2,1)} %copy-done.2, bf16[128,256]{1,0:T(8,128)(2,1)} %copy-done.4, ...), custom_call_target="tpu_custom_call" | custom-call | tf_op jit(solution)/shard_map/conv_forward/pallas_call | solution.py:243
  38.9 12.1 %attend.1 = (bf16[2048,1024]{1,0:T(8,128)(2,1)}, bf16[2048,1024]{1,0:T(8,128)(2,1)}, f32[8,128,256]{2,1,0:T(8,128)}, f32[3,8,256]{2,1,0:T(8,128)}) custom-call(bf16[2048,256]{1,0:T(8,128)(2,1)} %get-tuple-element.54.normed, bf16[256,2048]{1,0:T(8,128)(2,1)} %wv.3, bf16[256,2048]{1,0:T(8,128)(2,1)} %wv.3, bf16[256,1024]{1,0:T(8,128)(2,1)} %q.3, ...), custom_call_target="tpu_custom_call" | custom-call | tf_op jit(solution)/shard_map/attend/pallas_call | solution.py:313
  51.8 10.7 %all_to_all.30 = f32[8,3,8,256]{3,2,1,0:T(8,128)S(1)} all-to-all(f32[8,3,8,256]{3,2,1,0:T(8,128)S(1)} %broadcast_in_dim.10), channel_id=1, replica_groups=mesh['z'=4,'core'=2,'x'=4,'y'=4] {'z','core'}, dimensions={0} | all-to-all | bytes 393216 | tf_op jit(solution)/shard_map/all_to_all | solution.py:573
  63.5 9.6 %all-to-all-start.1 = ((f32[16,3,8,256]{3,2,1,0:T(8,128)}), f32[16,3,8,256]{3,2,1,0:T(8,128)S(1)}, u32[]{:S(2)}, u32[]{:S(2)}) async-start(f32[16,3,8,256]{3,2,1,0:T(8,128)} %broadcast_in_dim.11), calls=%async_computation.1 | async-start | bytes 786432 | tf_op jit(solution)/shard_map/all_to_all | solution.py:573
  73.1 8.1 %all-to-all-done.1 = f32[16,3,8,256]{3,2,1,0:T(8,128)S(1)} async-done(((f32[16,3,8,256]{3,2,1,0:T(8,128)}), f32[16,3,8,256]{3,2,1,0:T(8,128)S(1)}, u32[]{:S(2)}, u32[]{:S(2)}) %all-to-all-start.1) | async-done | bytes 393248 | tf_op jit(solution)/shard_map/all_to_all | solution.py:573
  81.3 1.3 fusion.15
  82.6 23.4 %attend_grad.1 = (f32[4,4,256,128]{3,2,1,0:T(8,128)}, f32[4,4,256,128]{3,2,1,0:T(8,128)}, bf16[2048,256]{1,0:T(8,128)(2,1)}, f32[1,256]{1,0:T(1,128)}, bf16[224,...) custom-call(s32[1]{0:T(128)} %bitcast.core, ...), custom_call_target="tpu_custom_call" | custom-call | flops 14000000000 | bytes 16000000 | tf_op jit(solution)/shard_map/attend_grad/pallas_call | solution.py:440
  106.0 2.7 %collective-permute-start.4 = (f32[4,4,256,128]{3,2,1,0:T(8,128)}, f32[4,4,256,128]{3,2,1,0:T(8,128)S(1)}, u32[]{:S(2)}, u32[]{:S(2)}) collective-permute-start(f32[4,4,256,128]{3,2,1,0:T(8,128)} %get-tuple-element.63), channel_id=1, source_target_pairs={{0,16},{16,0},{1,17},{17,1},{2,18},{18,2},{3,19},{19,3},{4,20},{20... | collective-permute-start | bytes 6291464 | tf_op jit(solution)/shard_map/ppermute | solution.py:637
  108.7 2.1 %collective-permute-start.5 = (bf16[224,256]{1,0:T(8,128)(2,1)}, bf16[224,256]{1,0:T(8,128)(2,1)S(1)}, u32[]{:S(2)}, u32[]{:S(2)}) collective-permute-start(bf16[224,256]{1,0:T(8,128)(2,1)} %get-tuple-element.64), channel_id=1, source_target_pairs={{0,16},{16,32},{32,48},{48,64},{64,80},{80,96},{96,112},{1,17},{17... | collective-permute-start | bytes 344072 | tf_op jit(solution)/shard_map/ppermute | solution.py:82
  110.8 2.2 %collective-permute-start.6 = (bf16[224,256]{1,0:T(8,128)(2,1)}, bf16[224,256]{1,0:T(8,128)(2,1)S(1)}, u32[]{:S(2)}, u32[]{:S(2)}) collective-permute-start(bf16[224,256]{1,0:T(8,128)(2,1)} %get-tuple-element.65), channel_id=1, source_target_pairs={{16,0},{32,16},{48,32},{64,48},{80,64},{96,80},{112,96},{17,1},{33... | collective-permute-start | bytes 344072 | tf_op jit(solution)/shard_map/ppermute | solution.py:83
  113.1 2.9 %add_convert_fusion = bf16[4,4,256,128]{3,2,1,0:T(8,128)(2,1)} fusion(f32[4,4,256,128]{3,2,1,0:T(8,128)} %get-tuple-element.62, f32[4,4,256,128]{3,2,1,0:T(8,128)S(1)} %collective-permute-done.4), kind=kLoop, calls=%fused_computation | loop fusion | flops 1048576 | bytes 5242880 | tf_op jit(solution)/shard_map/convert_element_type | solution.py:637
  118.5 4.0 %collective-permute-start.7 = (bf16[128,256]{1,0:T(8,128)(2,1)S(1)}, bf16[128,256]{1,0:T(8,128)(2,1)S(1)}, u32[]{:S(2)}, u32[]{:S(2)}) collective-permute-start(bf16[128,256]{1,0:T(8,128)(2,1)S(1)} %pad_maximum_fusion.3), channel_id=1, source_target_pairs={{0,1},{1,2},{2,3},{3,4},{4,5},{5,6},{6,7},{7,8},{8,9},{9,10},{10,1... | collective-permute-start | bytes 196616 | tf_op jit(solution)/shard_map/ppermute | solution.py:93
  122.5 7.4 %all-to-all-start.2 = ((bf16[64,64,128]{2,1,0:T(8,128)(2,1)}), bf16[64,64,128]{2,1,0:T(8,128)(2,1)S(1)}, u32[]{:S(2)}, u32[]{:S(2)}) async-start(bf16[64,64,128]{2,1,0:T(8,128)(2,1)} %bitcast.15), calls=%async_computation.2 | async-start | bytes 2097152 | tf_op jit(solution)/shard_map/all_to_all | solution.py:603
  129.9 10.8 %kernel_grad.1 = f32[49,256]{1,0:T(8,128)} custom-call(f32[38,14,8,256]{3,2,1,0:T(8,128)} %get-tuple-element.68.wide, bf16[2048,256]{1,0:T(8,128)(2,1)} %get-tuple-element.75.d_mixed), custom_call_target="tpu_custom_call" | custom-call | flops 14000000000 | bytes 16000000 | tf_op jit(solution)/shard_map/kernel_grad/pallas_call | solution.py:510
  140.7 7.7 %all-to-all-done.2 = bf16[64,64,128]{2,1,0:T(8,128)(2,1)S(1)} async-done(((bf16[64,64,128]{2,1,0:T(8,128)(2,1)}), bf16[64,64,128]{2,1,0:T(8,128)(2,1)S(1)}, u32[]{:S(2)}, u32[]{:S(2)}) %all-to-all-start.2) | async-done | bytes 1048608 | tf_op jit(solution)/shard_map/all_to_all | solution.py:603
  149.8 4.8 %all-to-all-start.3 = ((bf16[64,64,128]{2,1,0:T(8,128)(2,1)}), bf16[64,64,128]{2,1,0:T(8,128)(2,1)S(1)}, u32[]{:S(2)}, u32[]{:S(2)}) async-start(bf16[64,64,128]{2,1,0:T(8,128)(2,1)} %broadcast_in_dim.12), calls=%async_computation.3 | async-start | bytes 2097152 | tf_op jit(solution)/shard_map/all_to_all | solution.py:603
  154.6 12.7 %conv_back.1 = (f32[4,16,256]{2,1,0:T(8,128)}, f32[1,256]{1,0:T(1,128)}) custom-call(bf16[2048,256]{1,0:T(8,128)(2,1)} %get-tuple-element.75.d_mixed, bf16[224,256]{1,0:T(8,128)(2,1)} %copy-done.8, bf16[224,256]{1,0:T(8,128)(2,1)} %copy-done.9, bf16[128,256]{1,0:T(8,128)(2,1)} %copy-done.12, bf16[128,256]{1,0:T(8,128)(2,1)} %copy-done.11, f32[49,256]{1,0:T(8,128)} %kern.3, ...), custom_call_target="tpu_custom_call" | custom-call | flops 14000000000 | bytes 16000000 | tf_op jit(solution)/shard_map/conv_back/pallas_call | solution.py:550
  167.3 4.3 %all-to-all-done.3 = bf16[64,64,128]{2,1,0:T(8,128)(2,1)S(1)} async-done(((bf16[64,64,128]{2,1,0:T(8,128)(2,1)}), bf16[64,64,128]{2,1,0:T(8,128)(2,1)S(1)}, u32[]{:S(2)}, u32[]{:S(2)}) %all-to-all-start.3) | async-done | bytes 1048608 | tf_op jit(solution)/shard_map/all_to_all | solution.py:603
  171.6 2.7 %collective-permute-start.9 = (bf16[64,64,128]{2,1,0:T(8,128)(2,1)S(1)}, bf16[64,64,128]{2,1,0:T(8,128)(2,1)}, u32[]{:S(2)}, u32[]{:S(2)}) collective-permute-start(bf16[64,64,128]{2,1,0:T(8,128)(2,1)S(1)} %all-to-all-done.3), channel_id=1, source_target_pairs={{0,16},{16,0},{1,17},{17,1},{2,18},{18,2},{3,19},{19,3},{4,20},{20... | collective-permute-start | bytes 3145736 | tf_op jit(solution)/shard_map/ppermute | solution.py:588
  175.9 3.8 %all-to-all-start.4 = ((f32[128,1,256]{2,1,0:T(1,128)}), f32[128,1,256]{2,1,0:T(1,128)S(1)}, u32[]{:S(2)}, u32[]{:S(2)}) async-start(f32[128,1,256]{2,1,0:T(1,128)} %broadcast_in_dim.13), calls=%async_computation.4 | async-start | bytes 262144 | tf_op jit(solution)/shard_map/all_to_all | solution.py:607
  179.7 9.8 %all-to-all-done.4 = f32[128,1,256]{2,1,0:T(1,128)S(1)} async-done(((f32[128,1,256]{2,1,0:T(1,128)}), f32[128,1,256]{2,1,0:T(1,128)S(1)}, u32[]{:S(2)}, u32[]{:S(2)}) %all-to-all-start.4) | async-done | bytes 131104 | tf_op jit(solution)/shard_map/all_to_all | solution.py:607
  190.4 4.1 %all-to-all-start.5 = ((f32[128,1,256]{2,1,0:T(1,128)}), f32[128,1,256]{2,1,0:T(1,128)S(1)}, u32[]{:S(2)}, u32[]{:S(2)}) async-start(f32[128,1,256]{2,1,0:T(1,128)} %broadcast_in_dim.14), calls=%async_computation.5 | async-start | bytes 262144 | tf_op jit(solution)/shard_map/all_to_all | solution.py:607
  194.6 1.4 broadcast_select_fusion.1
  196.1 1.5 copy.73
  197.5 2.9 %copy.74 = f32[256,16,128]{0,2,1:T(8,128)} copy(f32[256,16,128]{2,0,1:T(8,128)} %bitcast.107) | data formatting | bytes 4194304 | tf_op jit(solution)/shard_map/transpose | solution.py:615
  202.8 1.8 all-to-all-done.5
  205.2 1.8 copy.76
  (72 shorter events, 18.9 us)
Async XLA Ops:
  5.2 7.0 %collective-permute-start = (bf16[224,256]{1,0:T(8,128)(2,1)}, bf16[224,256]{1,0:T(8,128)(2,1)S(1)}, u32[]{:S(2)}, u32[]{:S(2)}) collective-permute-start(bf16[224,256]{1,0:T(8,128)(2,1)} %get-tuple-element.50), channel_id=1, source_target_pairs={{0,16},{16,32},{32,48},{48,64},{64,80},{80,96},{96,112},{1,17},{17... | collective-permute-start | bytes 344072 | tf_op jit(solution)/shard_map/ppermute | solution.py:82
  10.1 6.3 %collective-permute-start.1 = (bf16[224,256]{1,0:T(8,128)(2,1)}, bf16[224,256]{1,0:T(8,128)(2,1)S(1)}, u32[]{:S(2)}, u32[]{:S(2)}) collective-permute-start(bf16[224,256]{1,0:T(8,128)(2,1)} %get-tuple-element.51), channel_id=1, source_target_pairs={{16,0},{32,16},{48,32},{64,48},{80,64},{96,80},{112,96},{17,1},{33... | collective-permute-start | bytes 344072 | tf_op jit(solution)/shard_map/ppermute | solution.py:83
  12.2 12.5 %copy-start.1 = (bf16[224,256]{1,0:T(8,128)(2,1)}, bf16[224,256]{1,0:T(8,128)(2,1)S(1)}, u32[]{:S(2)}) copy-start(bf16[224,256]{1,0:T(8,128)(2,1)S(1)} %collective-permute-done.above) | copy-start | bytes 344068
  16.4 8.2 %copy-start.2 = (bf16[224,256]{1,0:T(8,128)(2,1)}, bf16[224,256]{1,0:T(8,128)(2,1)S(1)}, u32[]{:S(2)}) copy-start(bf16[224,256]{1,0:T(8,128)(2,1)S(1)} %collective-permute-done.1.below) | copy-start | bytes 344068
  17.2 6.1 %collective-permute-start.3 = (bf16[128,256]{1,0:T(8,128)(2,1)S(1)}, bf16[128,256]{1,0:T(8,128)(2,1)S(1)}, u32[]{:S(2)}, u32[]{:S(2)}) collective-permute-start(bf16[128,256]{1,0:T(8,128)(2,1)S(1)} %pad_maximum_fusion.2), channel_id=1, source_target_pairs={{1,0},{2,1},{3,2},{4,3},{5,4},{6,5},{7,6},{8,7},{9,8},{10,9},{11,1... | collective-permute-start | bytes 196616 | tf_op jit(solution)/shard_map/ppermute | solution.py:94
  19.3 5.3 %collective-permute-start.2 = (bf16[128,256]{1,0:T(8,128)(2,1)S(1)}, bf16[128,256]{1,0:T(8,128)(2,1)S(1)}, u32[]{:S(2)}, u32[]{:S(2)}) collective-permute-start(bf16[128,256]{1,0:T(8,128)(2,1)S(1)} %pad_maximum_fusion.1), channel_id=1, source_target_pairs={{0,1},{1,2},{2,3},{3,4},{4,5},{5,6},{6,7},{7,8},{8,9},{9,10},{10,1... | collective-permute-start | bytes 196616 | tf_op jit(solution)/shard_map/ppermute | solution.py:93
  23.3 1.3 copy-start.3
  24.6 0.6 copy-start.4
  63.5 17.7 %all-to-all-start.1 = ((f32[16,3,8,256]{3,2,1,0:T(8,128)}), f32[16,3,8,256]{3,2,1,0:T(8,128)S(1)}, u32[]{:S(2)}, u32[]{:S(2)}) async-start(f32[16,3,8,256]{3,2,1,0:T(8,128)} %broadcast_in_dim.11), calls=%async_computation.1 | async-start | bytes 786432 | tf_op jit(solution)/shard_map/all_to_all | solution.py:573
  106.0 7.0 %collective-permute-start.4 = (f32[4,4,256,128]{3,2,1,0:T(8,128)}, f32[4,4,256,128]{3,2,1,0:T(8,128)S(1)}, u32[]{:S(2)}, u32[]{:S(2)}) collective-permute-start(f32[4,4,256,128]{3,2,1,0:T(8,128)} %get-tuple-element.63), channel_id=1, source_target_pairs={{0,16},{16,0},{1,17},{17,1},{2,18},{18,2},{3,19},{19,3},{4,20},{20... | collective-permute-start | bytes 6291464 | tf_op jit(solution)/shard_map/ppermute | solution.py:637
  108.7 7.2 %collective-permute-start.5 = (bf16[224,256]{1,0:T(8,128)(2,1)}, bf16[224,256]{1,0:T(8,128)(2,1)S(1)}, u32[]{:S(2)}, u32[]{:S(2)}) collective-permute-start(bf16[224,256]{1,0:T(8,128)(2,1)} %get-tuple-element.64), channel_id=1, source_target_pairs={{0,16},{16,32},{32,48},{48,64},{64,80},{80,96},{96,112},{1,17},{17... | collective-permute-start | bytes 344072 | tf_op jit(solution)/shard_map/ppermute | solution.py:82
  110.8 6.3 %collective-permute-start.6 = (bf16[224,256]{1,0:T(8,128)(2,1)}, bf16[224,256]{1,0:T(8,128)(2,1)S(1)}, u32[]{:S(2)}, u32[]{:S(2)}) collective-permute-start(bf16[224,256]{1,0:T(8,128)(2,1)} %get-tuple-element.65), channel_id=1, source_target_pairs={{16,0},{32,16},{48,32},{64,48},{80,64},{96,80},{112,96},{17,1},{33... | collective-permute-start | bytes 344072 | tf_op jit(solution)/shard_map/ppermute | solution.py:83
  113.0 4.1 %copy-start.7 = (bf16[96,256]{1,0:T(8,128)(2,1)S(1)}, bf16[96,256]{1,0:T(8,128)(2,1)}, u32[]{:S(2)}) copy-start(bf16[96,256]{1,0:T(8,128)(2,1)} %get-tuple-element.72) | copy-start | bytes 147460
  113.1 5.4 %copy-start.6 = (bf16[96,256]{1,0:T(8,128)(2,1)S(1)}, bf16[96,256]{1,0:T(8,128)(2,1)}, u32[]{:S(2)}) copy-start(bf16[96,256]{1,0:T(8,128)(2,1)} %get-tuple-element.69) | copy-start | bytes 147460
  115.9 24.8 %copy-start.8 = (bf16[224,256]{1,0:T(8,128)(2,1)}, bf16[224,256]{1,0:T(8,128)(2,1)S(1)}, u32[]{:S(2)}) copy-start(bf16[224,256]{1,0:T(8,128)(2,1)S(1)} %collective-permute-done.5.above) | copy-start | bytes 344068
  117.1 23.6 %copy-start.9 = (bf16[224,256]{1,0:T(8,128)(2,1)}, bf16[224,256]{1,0:T(8,128)(2,1)S(1)}, u32[]{:S(2)}) copy-start(bf16[224,256]{1,0:T(8,128)(2,1)S(1)} %collective-permute-done.6.below) | copy-start | bytes 344068
  117.2 23.5 %collective-permute-start.8 = (bf16[128,256]{1,0:T(8,128)(2,1)S(1)}, bf16[128,256]{1,0:T(8,128)(2,1)S(1)}, u32[]{:S(2)}, u32[]{:S(2)}) collective-permute-start(bf16[128,256]{1,0:T(8,128)(2,1)S(1)} %pad_maximum_fusion.4), channel_id=1, source_target_pairs={{1,0},{2,1},{3,2},{4,3},{5,4},{6,5},{7,6},{8,7},{9,8},{10,9},{11,1... | collective-permute-start | bytes 196616 | tf_op jit(solution)/shard_map/ppermute | solution.py:94
  118.5 22.2 %collective-permute-start.7 = (bf16[128,256]{1,0:T(8,128)(2,1)S(1)}, bf16[128,256]{1,0:T(8,128)(2,1)S(1)}, u32[]{:S(2)}, u32[]{:S(2)}) collective-permute-start(bf16[128,256]{1,0:T(8,128)(2,1)S(1)} %pad_maximum_fusion.3), channel_id=1, source_target_pairs={{0,1},{1,2},{2,3},{3,4},{4,5},{5,6},{6,7},{7,8},{8,9},{9,10},{10,1... | collective-permute-start | bytes 196616 | tf_op jit(solution)/shard_map/ppermute | solution.py:93
  122.5 25.9 %all-to-all-start.2 = ((bf16[64,64,128]{2,1,0:T(8,128)(2,1)}), bf16[64,64,128]{2,1,0:T(8,128)(2,1)S(1)}, u32[]{:S(2)}, u32[]{:S(2)}) async-start(bf16[64,64,128]{2,1,0:T(8,128)(2,1)} %bitcast.15), calls=%async_computation.2 | async-start | bytes 2097152 | tf_op jit(solution)/shard_map/all_to_all | solution.py:603
  140.7 9.1 %copy-start.11 = (bf16[128,256]{1,0:T(8,128)(2,1)}, bf16[128,256]{1,0:T(8,128)(2,1)S(1)}, u32[]{:S(2)}) copy-start(bf16[128,256]{1,0:T(8,128)(2,1)S(1)} %collective-permute-done.8.rh) | copy-start | bytes 196612
  140.7 9.1 %copy-start.12 = (bf16[128,256]{1,0:T(8,128)(2,1)}, bf16[128,256]{1,0:T(8,128)(2,1)S(1)}, u32[]{:S(2)}) copy-start(bf16[128,256]{1,0:T(8,128)(2,1)S(1)} %collective-permute-done.7.lh) | copy-start | bytes 196612
  149.8 21.8 %all-to-all-start.3 = ((bf16[64,64,128]{2,1,0:T(8,128)(2,1)}), bf16[64,64,128]{2,1,0:T(8,128)(2,1)S(1)}, u32[]{:S(2)}, u32[]{:S(2)}) async-start(bf16[64,64,128]{2,1,0:T(8,128)(2,1)} %broadcast_in_dim.12), calls=%async_computation.3 | async-start | bytes 2097152 | tf_op jit(solution)/shard_map/all_to_all | solution.py:603
  154.6 19.7 %copy-start.5 = (f32[49,256]{1,0:T(8,128)S(1)}, f32[49,256]{1,0:T(8,128)}, u32[]{:S(2)}) copy-start(f32[49,256]{1,0:T(8,128)} %kernel_grad.1) | copy-start | bytes 150532
  154.6 19.7 %copy-start.10 = (f32[1,256]{1,0:T(1,128)S(1)}, f32[1,256]{1,0:T(1,128)}, u32[]{:S(2)}) copy-start(f32[1,256]{1,0:T(1,128)} %get-tuple-element.84) | copy-start | bytes 3076
  171.6 23.0 %collective-permute-start.9 = (bf16[64,64,128]{2,1,0:T(8,128)(2,1)S(1)}, bf16[64,64,128]{2,1,0:T(8,128)(2,1)}, u32[]{:S(2)}, u32[]{:S(2)}) collective-permute-start(bf16[64,64,128]{2,1,0:T(8,128)(2,1)S(1)} %all-to-all-done.3), channel_id=1, source_target_pairs={{0,16},{16,0},{1,17},{17,1},{2,18},{18,2},{3,19},{19,3},{4,20},{20... | collective-permute-start | bytes 3145736 | tf_op jit(solution)/shard_map/ppermute | solution.py:588
  175.9 13.6 %all-to-all-start.4 = ((f32[128,1,256]{2,1,0:T(1,128)}), f32[128,1,256]{2,1,0:T(1,128)S(1)}, u32[]{:S(2)}, u32[]{:S(2)}) async-start(f32[128,1,256]{2,1,0:T(1,128)} %broadcast_in_dim.13), calls=%async_computation.4 | async-start | bytes 262144 | tf_op jit(solution)/shard_map/all_to_all | solution.py:607
  190.4 14.2 %all-to-all-start.5 = ((f32[128,1,256]{2,1,0:T(1,128)}), f32[128,1,256]{2,1,0:T(1,128)S(1)}, u32[]{:S(2)}, u32[]{:S(2)}) async-start(f32[128,1,256]{2,1,0:T(1,128)} %broadcast_in_dim.14), calls=%async_computation.5 | async-start | bytes 262144 | tf_op jit(solution)/shard_map/all_to_all | solution.py:607
  200.6 4.6 %copy-start = (f32[256,16,128]{0,2,1:T(8,128)S(1)}, f32[256,16,128]{0,2,1:T(8,128)}, u32[]{:S(2)}) copy-start(f32[256,16,128]{0,2,1:T(8,128)} %copy.74) | copy-start | bytes 6291460

commit v6 on v5

--- a/solution.py
+++ b/solution.py
@@ -517,7 +517,7 @@
     )(wide, d_mixed)
 
 
-def conv_back_body(d_mixed, above, below, lh, rh, kern, z, patch_grad, bias_grad, wide, d_sc, w_sc, l_sc, r_sc, c_sc):
+def conv_back_body(d_mixed, above, below, lh, rh, kern, z, kern_grad, gain_grad, small, wide, d_sc, w_sc, l_sc, r_sc, c_sc):
     assemble(wide, d_mixed, (above, below, lh, rh), l_sc, r_sc, c_sc)
     spread_weights(kern, w_sc)
     zero = jnp.zeros((8, 128), F32)
@@ -535,7 +535,11 @@
 
     bias = lax.fori_loop(0, ROWS // 2, body, (zero, zero))
     for half in range(2):
-        bias_grad[:, half * 128 : (half + 1) * 128] = jnp.sum(bias[half], axis=0, keepdims=True)
+        small[98, :, half * 128 : (half + 1) * 128] = jnp.sum(bias[half], axis=0, keepdims=True)
+    for n in range(KSIZE * KSIZE):
+        small[48 + n] = kern_grad[n : n + 1, :]
+    small[97] = gain_grad[...]
+    small[99:128] = jnp.zeros((29, 1, CH), F32)
     total = [jnp.zeros((16, CH), F32) for _ in range(4)]
     for a8 in range(8):
         part = dot(z[...], d_sc[a8], TN)
@@ -543,14 +547,15 @@
             first = v * 128 + a8 * 16
             total[v] = total[v] + part[first : first + 16, :]
     for v in range(4):
-        patch_grad[v] = total[v]
-
-
-def conv_back(d_mixed, halo, conv_kernel, z):
+        for fu in range(12):
+            small[fu * 4 + v] = total[v][fu : fu + 1, :]
+
+
+def conv_back(d_mixed, halo, conv_kernel, z, kern_grad, gain_grad):
     return pl.pallas_call(
         conv_back_body,
         name="conv_back",
-        out_shape=[jax.ShapeDtypeStruct((4, 16, CH), F32), jax.ShapeDtypeStruct((1, CH), F32)],
+        out_shape=jax.ShapeDtypeStruct((128, 1, CH), F32),
         scratch_shapes=[
             pltpu.VMEM((ROWS + 2 * HALO, WIDE, 8, CH), F32),
             pltpu.VMEM((8, 256, CH), BF),
@@ -559,12 +564,13 @@
         + EDGE_SCRATCH,
         compiler_params=VMEM,
         cost_estimate=COST,
-    )(d_mixed, *halo, conv_kernel, z)
+    )(d_mixed, *halo, conv_kernel, z, kern_grad, gain_grad)
 
 
 CHIPS = ("z", "x", "y")
 ALL = ("z", "core", "x", "y")
 PAIR = [(0, 1), (1, 0)]
+STAGES = (("z", "core"), ("x", "y"))
 
 
 def gather(x, axes):
@@ -574,7 +580,7 @@
 
 
 def combine_stats(stats):
-    for axes in (("z", "core"), ("x", "y")):
+    for axes in STAGES:
         group = gather(stats, axes)
         peak = jnp.max(group[:, 0], axis=0)
         factors = jnp.exp2(group[:, 0] - peak)
@@ -584,11 +590,68 @@
     return stats
 
 
-def swap(half):
-    other = lax.ppermute(half, "core", PAIR)
-    first = lax.axis_index("core") == 0
-    pair = [jnp.where(first, half, other), jnp.where(first, other, half)]
-    return jnp.stack([x.reshape(4, HEADS // 2, 256, 128) for x in pair], axis=1)
+def collect_body(core, own, other, attended, q_grad, kv_grad):
+    h = pl.program_id(0)
+    mine = (h // (HEADS // 2)) == core[0]
+
+    def put(x):
+        attended[...] = x[0, 0].astype(F32)
+        q_grad[...] = x[1, 0].astype(F32)
+        kv_grad[:, pl.ds(pl.multiple_of(h * 128, 128), 128)] = x[2, 0].astype(F32)
+        kv_grad[:, pl.ds(pl.multiple_of((HEADS + h) * 128, 128), 128)] = x[3, 0].astype(F32)
+
+    @pl.when(mine)
+    def _():
+        put(own)
+
+    @pl.when(jnp.logical_not(mine))
+    def _():
+        put(other)
+
+
+def collect(core, own, other):
+    shape = (4, HEADS // 2, 256, 128)
+    block = pl.BlockSpec((4, 1, 256, 128), lambda h, core: (0, h % (HEADS // 2), 0, 0))
+    heads = pl.BlockSpec((256, 128), lambda h, core: (0, h))
+    return pl.pallas_call(
+        collect_body,
+        name="collect",
+        grid_spec=pltpu.PrefetchScalarGridSpec(
+            num_scalar_prefetch=1,
+            grid=(HEADS,),
+            in_specs=[block, block],
+            out_specs=[heads, heads, pl.BlockSpec((256, 2048), lambda h, core: (0, 0))],
+        ),
+        out_shape=[
+            jax.ShapeDtypeStruct((256, 1024), F32),
+            jax.ShapeDtypeStruct((256, 1024), F32),
+            jax.ShapeDtypeStruct((256, 2048), F32),
+        ],
+        compiler_params=VMEM,
+    )(core, own.reshape(shape), other.reshape(shape))
+
+
+def split_small_body(small, patch, kern, gain, bias):
+    for n in range(48):
+        patch[n : n + 1, :] = small[n]
+    for n in range(KSIZE * KSIZE):
+        kern[n : n + 1, :] = small[48 + n]
+    gain[...] = small[97, 0]
+    bias[...] = small[98, 0]
+
+
+def split_small(small):
+    return pl.pallas_call(
+        split_small_body,
+        name="split_small",
+        out_shape=[
+            jax.ShapeDtypeStruct((48, CH), F32),
+            jax.ShapeDtypeStruct((KSIZE * KSIZE, CH), F32),
+            jax.ShapeDtypeStruct((CH,), F32),
+            jax.ShapeDtypeStruct((CH,), F32),
+        ],
+        compiler_params=VMEM,
+    )(small)
 
 
 def block_sum(parts):
@@ -609,10 +672,6 @@
 
 def tie(x, *others):
     return lax.optimization_barrier((x,) + others)
-
-
-def columns(x):
-    return x.transpose(1, 0, 2).reshape(256, -1)
 
 
 def per_device(
@@ -637,29 +696,20 @@
     message = (keep + lax.ppermute(away, "core", PAIR)).astype(BF).reshape(64, 64, 128)
     d_mixed, message, *d_rows = tie(d_mixed, message, *d_rows)
     message = send(message)
+    kern = kernel_grad(wide, d_mixed)
+    d_mixed, message, kern = tie(d_mixed, message, kern)
+    message = copies(block_sum(message))
+    d_mixed, message, *d_rows = tie(d_mixed, message, *d_rows)
+    message = send(message)
     d_cols = exchange_cols(d_edges, *d_rows)
-    kern = kernel_grad(wide, d_mixed)
-    d_mixed, message, kern, *d_cols = tie(d_mixed, message, kern, *d_cols)
-    message = copies(block_sum(message))
-    d_mixed, message = tie(d_mixed, message)
-    message = send(message)
-    patch, bias = conv_back(d_mixed, tuple(d_rows) + tuple(d_cols), conv_kernel, z)
-    patch, bias, message = tie(patch, bias, message)
-    small = jnp.concatenate([patch.reshape(64, CH), kern, gain_grad, bias], axis=0)
-    mine = block_sum(send_all(jnp.pad(small, ((0, 13), (0, 0)))[:, None]))
+    small = conv_back(d_mixed, tuple(d_rows) + tuple(d_cols), conv_kernel, z, kern, gain_grad)
+    small, message = tie(small, message)
+    mine = block_sum(send_all(small))
     small = send_all(jnp.broadcast_to(mine[None], (128,) + mine.shape))
-    sums = swap(message).astype(F32).reshape(4, HEADS, 256, 128)
-    outs = (columns(sums[0]), columns(sums[1]), columns(sums[2:].reshape(2 * HEADS, 256, 128)))
+    outs = collect(core, message, lax.ppermute(message, "core", PAIR))
     small, *outs = tie(small, *outs)
-    small = small[:, 0]
-    patch = small[:64].reshape(4, 16, CH)[:, :12].transpose(1, 0, 2).reshape(48, CH)
-    return (
-        *outs,
-        small[64 + 49],
-        small[64 : 64 + 49],
-        patch,
-        small[64 + 50],
-    )
+    patch, kern, gain, bias = split_small(small)
+    return (*outs, gain, kern, patch, bias)
 
 
 def solution(mesh):

time: 210 us -> 208 us (level)
  blocking collectives: 10.7 us -> 25.4 us
  local copies, waits for them, and re-layouts: 16.6 us -> 7.78 us
  Pallas kernels: 75.8 us -> 84.4 us
  waiting for transfers between devices: 38.7 us -> 31.2 us
  starting transfers between devices: 56.8 us -> 50.5 us
  other arithmetic: 8.77 us -> 6.22 us
    all_to_all x0 -> x1, blocking collectives: none -> 14.3 us  [send_all(): return lax.all_to_all(x, ALL, 0, 0, tiled=True)]
    all_to_all x2 -> x1, waiting for transfers between devices: 11.7 us -> 2.24 us  [send_all(): return lax.all_to_all(x, ALL, 0, 0, tiled=True)]
    pallas_call x1 -> x3, Pallas kernels: 12.7 us -> 21.2 us  [the longest x1 12.8 us: conv_back(): pl.pallas_call(conv_back_body, name='conv_back', out_shape=jax.ShapeDtype...]
    all_to_all x2 -> x1, starting transfers between devices: 7.88 us -> 4.12 us  [send_all(): return lax.all_to_all(x, ALL, 0, 0, tiled=True)]
    ppermute x2, waiting for transfers between devices: 0.01 us -> 3.69 us  [exchange_cols(): lax.ppermute(left, COL_AXES, [(i + 1, i) for i in range(n - 1)])]
    transpose x3 -> x0, local copies, waits for them, and re-layouts: 2.93 us -> none  [the longest x1 2.89 us: columns(): return x.transpose(1, 0, 2).reshape(256, -1)]
    reshape x3 -> x0, local copies, waits for them, and re-layouts: 2.84 us -> none  [the longest x2 2.2 us: columns(): return x.transpose(1, 0, 2).reshape(256, -1)]
    ppermute x2, starting transfers between devices: 7.97 us -> 5.74 us  [exchange_cols(): lax.ppermute(right, COL_AXES, [(i, i + 1) for i in range(n - 1)])]
  transfers between devices with their start and end apart: 15 -> 14, of which waited for: 9 -> 8; matrix products, arithmetic and copies ran while one was open for 7% -> 2% of each run, Pallas kernels for 11% -> 15%
where the time goes in v6:
time: 208 us; the launch traced here: 206 us
  Pallas kernels  84.4 us (41%)
  starting transfers between devices  50.5 us (24%)
  waiting for transfers between devices  31.2 us (15%)
  blocking collectives  25.4 us (12%)
  local copies, waits for them, and re-layouts  7.78 us (4%)
  other arithmetic  6.22 us (3%)
    pallas_call x1, Pallas kernels, attend_grad(): pl.pallas_call(attend_grad_kernel, name='attend_grad', grid_spec=pltpu.Pr...  23.4 us
    all_to_all x1, blocking collectives, send_all(): return lax.all_to_all(x, ALL, 0, 0, tiled=True)  14.3 us
    pallas_call x1, Pallas kernels, conv_forward(): pl.pallas_call(conv_kernel_body, name='conv_forward', out_shape=[jax.Shap...  13.7 us
    all_to_all x2, starting transfers between devices, send(): return lax.all_to_all(x, CHIPS, 0, 0, tiled=True)  13.5 us
    pallas_call x1, Pallas kernels, conv_back(): pl.pallas_call(conv_back_body, name='conv_back', out_shape=jax.ShapeDtype...  12.8 us
    pallas_call x1, Pallas kernels, attend(): pl.pallas_call(attend_kernel, name='attend', grid=(HEADS // WIDTH,), in_s...  12.1 us
    all_to_all x2, waiting for transfers between devices, send(): return lax.all_to_all(x, CHIPS, 0, 0, tiled=True)  11.5 us
    all_to_all x1, blocking collectives, gather(): return lax.all_to_all(copies, axes, 0, 0, tiled=True)  11 us
  transfers between devices with their start and end apart: 14, of which 8 were waited for; matrix products, arithmetic and copies ran while one was open for 2% of the time, Pallas kernels for 15%

profile of v6, /device:TPU:1, one launch (start us, length us, event | category | flops | bytes accessed | tf_op | source)
XLA Modules:
  0.0 206.3 jit_solution(12327414306490257248)
XLA Ops:
  2.0 3.2 %embed.1 = (bf16[2048,256]{1,0:T(8,128)(2,1)}, bf16[256,512]{1,0:T(8,128)(2,1)}, bf16[224,256]{1,0:T(8,128)(2,1)}, bf16[224,256]{1,0:T(8,128)(2,1)}, bf16[96,256]{1,0:T(8,128)(2,1)}, /*index=5*/bf16[96,256]{1,0:T(8,128)(2,1)}) custom-call(bf16[384,256]{1,0:T(8,128)(2,1)} %bitcast.77, bf16[4,16,256]{2,1,0:T(8,128)(2,1)} %pad.4.weights, f32[1,256]{1,0:T(1,128)} %bitcast.82), custom_call_target="tpu_custom_call" | custom-call | tf_op jit(solution)/shard_map/embed/pallas_call | solution.py:202
  5.2 4.9 %collective-permute-start = (bf16[224,256]{1,0:T(8,128)(2,1)}, bf16[224,256]{1,0:T(8,128)(2,1)S(1)}, u32[]{:S(2)}, u32[]{:S(2)}) collective-permute-start(bf16[224,256]{1,0:T(8,128)(2,1)} %get-tuple-element.54), channel_id=1, source_target_pairs={{0,16},{16,32},{32,48},{48,64},{64,80},{80,96},{96,112},{1,17},{17... | collective-permute-start | bytes 344072 | tf_op jit(solution)/shard_map/ppermute | solution.py:82
  10.1 1.9 collective-permute-start.1
  12.2 4.2 %collective-permute-done.1.below = bf16[224,256]{1,0:T(8,128)(2,1)S(1)} collective-permute-done((bf16[224,256]{1,0:T(8,128)(2,1)}, bf16[224,256]{1,0:T(8,128)(2,1)S(1)}, u32[]{:S(2)}, u32[]{:S(2)}) %collective-permute-start.1) | collective-permute-done | bytes 114720 | tf_op jit(solution)/shard_map/ppermute | solution.py:83
  17.3 3.2 %collective-permute-start.2 = (bf16[128,256]{1,0:T(8,128)(2,1)S(1)}, bf16[128,256]{1,0:T(8,128)(2,1)S(1)}, u32[]{:S(2)}, u32[]{:S(2)}) collective-permute-start(bf16[128,256]{1,0:T(8,128)(2,1)S(1)} %pad_maximum_fusion), channel_id=1, source_target_pairs={{0,1},{1,2},{2,3},{3,4},{4,5},{5,6},{6,7},{7,8},{8,9},{9,10},{10,1... | collective-permute-start | bytes 196616 | tf_op jit(solution)/shard_map/ppermute | solution.py:93
  21.3 1.3 collective-permute-start.3
  22.6 3.7 %collective-permute-done.3.rh = bf16[128,256]{1,0:T(8,128)(2,1)S(1)} collective-permute-done((bf16[128,256]{1,0:T(8,128)(2,1)S(1)}, bf16[128,256]{1,0:T(8,128)(2,1)S(1)}, u32[]{:S(2)}, u32[]{:S(2)}) %collective-permute-start.3) | collective-permute-done | bytes 65568 | tf_op jit(solution)/shard_map/ppermute | solution.py:94
  26.9 13.7 %conv_forward.1 = (f32[38,14,8,256]{3,2,1,0:T(8,128)}, f32[2048,256]{1,0:T(8,128)}, f32[2048,128]{1,0:T(8,128)}, bf16[2048,256]{1,0:T(8,128)(2,1)}) custom-call(bf16[2048,256]{1,0:T(8,128)(2,1)} %get-tuple-element.53.emb, bf16[224,256]{1,0:T(8,128)(2,1)} %copy-done.3, bf16[224,256]{1,0:T(8,128)(2,1)} %copy-done.4, bf16[128,256]{1,0:T(8,128)(2,1)} %copy-done.5, ...), custom_call_target="tpu_custom_call" | custom-call | tf_op jit(solution)/shard_map/conv_forward/pallas_call | solution.py:243
  40.6 12.1 %attend.1 = (bf16[2048,1024]{1,0:T(8,128)(2,1)}, bf16[2048,1024]{1,0:T(8,128)(2,1)}, f32[8,128,256]{2,1,0:T(8,128)}, f32[3,8,256]{2,1,0:T(8,128)}) custom-call(bf16[2048,256]{1,0:T(8,128)(2,1)} %get-tuple-element.58.normed, bf16[256,2048]{1,0:T(8,128)(2,1)} %wv.3, bf16[256,2048]{1,0:T(8,128)(2,1)} %wv.3, bf16[256,1024]{1,0:T(8,128)(2,1)} %q.3, ...), custom_call_target="tpu_custom_call" | custom-call | tf_op jit(solution)/shard_map/attend/pallas_call | solution.py:313
  53.5 11.0 %all_to_all.30 = f32[8,3,8,256]{3,2,1,0:T(8,128)S(1)} all-to-all(f32[8,3,8,256]{3,2,1,0:T(8,128)S(1)} %broadcast_in_dim.8), channel_id=1, replica_groups=mesh['z'=4,'core'=2,'x'=4,'y'=4] {'z','core'}, dimensions={0} | all-to-all | bytes 393216 | tf_op jit(solution)/shard_map/all_to_all | solution.py:579
  65.4 8.0 %all-to-all-start.1 = ((f32[16,3,8,256]{3,2,1,0:T(8,128)}), f32[16,3,8,256]{3,2,1,0:T(8,128)S(1)}, u32[]{:S(2)}, u32[]{:S(2)}) async-start(f32[16,3,8,256]{3,2,1,0:T(8,128)} %broadcast_in_dim.9), calls=%async_computation.1 | async-start | bytes 786432 | tf_op jit(solution)/shard_map/all_to_all | solution.py:579
  73.4 8.1 %all-to-all-done.1 = f32[16,3,8,256]{3,2,1,0:T(8,128)S(1)} async-done(((f32[16,3,8,256]{3,2,1,0:T(8,128)}), f32[16,3,8,256]{3,2,1,0:T(8,128)S(1)}, u32[]{:S(2)}, u32[]{:S(2)}) %all-to-all-start.1) | async-done | bytes 393248 | tf_op jit(solution)/shard_map/all_to_all | solution.py:579
  81.6 1.3 fusion.14
  82.9 23.4 %attend_grad.1 = (f32[4,4,256,128]{3,2,1,0:T(8,128)}, f32[4,4,256,128]{3,2,1,0:T(8,128)}, bf16[2048,256]{1,0:T(8,128)(2,1)}, f32[1,256]{1,0:T(1,128)}, bf16[224,...) custom-call(s32[1]{0:T(128)} %bitcast.core, ...), custom_call_target="tpu_custom_call" | custom-call | flops 14000000000 | bytes 16000000 | tf_op jit(solution)/shard_map/attend_grad/pallas_call | solution.py:440
  106.3 2.7 %collective-permute-start.4 = (f32[4,4,256,128]{3,2,1,0:T(8,128)}, f32[4,4,256,128]{3,2,1,0:T(8,128)S(1)}, u32[]{:S(2)}, u32[]{:S(2)}) collective-permute-start(f32[4,4,256,128]{3,2,1,0:T(8,128)} %get-tuple-element.67), channel_id=1, source_target_pairs={{0,16},{16,0},{1,17},{17,1},{2,18},{18,2},{3,19},{19,3},{4,20},{20... | collective-permute-start | bytes 6291464 | tf_op jit(solution)/shard_map/ppermute | solution.py:696
  109.0 2.1 %collective-permute-start.5 = (bf16[224,256]{1,0:T(8,128)(2,1)}, bf16[224,256]{1,0:T(8,128)(2,1)S(1)}, u32[]{:S(2)}, u32[]{:S(2)}) collective-permute-start(bf16[224,256]{1,0:T(8,128)(2,1)} %get-tuple-element.68), channel_id=1, source_target_pairs={{0,16},{16,32},{32,48},{48,64},{64,80},{80,96},{96,112},{1,17},{17... | collective-permute-start | bytes 344072 | tf_op jit(solution)/shard_map/ppermute | solution.py:82
  111.1 2.2 %collective-permute-start.6 = (bf16[224,256]{1,0:T(8,128)(2,1)}, bf16[224,256]{1,0:T(8,128)(2,1)S(1)}, u32[]{:S(2)}, u32[]{:S(2)}) collective-permute-start(bf16[224,256]{1,0:T(8,128)(2,1)} %get-tuple-element.69), channel_id=1, source_target_pairs={{16,0},{32,16},{48,32},{64,48},{80,64},{96,80},{112,96},{17,1},{33... | collective-permute-start | bytes 344072 | tf_op jit(solution)/shard_map/ppermute | solution.py:83
  113.3 2.8 %add_convert_fusion = bf16[4,4,256,128]{3,2,1,0:T(8,128)(2,1)} fusion(f32[4,4,256,128]{3,2,1,0:T(8,128)} %get-tuple-element.66, f32[4,4,256,128]{3,2,1,0:T(8,128)S(1)} %collective-permute-done.4), kind=kLoop, calls=%fused_computation | loop fusion | flops 1048576 | bytes 5242880 | tf_op jit(solution)/shard_map/convert_element_type | solution.py:696
  117.4 5.8 %all-to-all-start.2 = ((bf16[64,64,128]{2,1,0:T(8,128)(2,1)}), bf16[64,64,128]{2,1,0:T(8,128)(2,1)S(1)}, u32[]{:S(2)}, u32[]{:S(2)}) async-start(bf16[64,64,128]{2,1,0:T(8,128)(2,1)} %bitcast.15), calls=%async_computation.2 | async-start | bytes 2097152 | tf_op jit(solution)/shard_map/all_to_all | solution.py:666
  123.3 10.8 %kernel_grad.1.kern_grad = f32[49,256]{1,0:T(8,128)} custom-call(f32[38,14,8,256]{3,2,1,0:T(8,128)} %get-tuple-element.72.wide, bf16[2048,256]{1,0:T(8,128)(2,1)} %get-tuple-element.77.d_mixed), custom_call_target="tpu_custom_call" | custom-call | flops 14000000000 | bytes 16000000 | tf_op jit(solution)/shard_map/kernel_grad/pallas_call | solution.py:510
  134.0 7.9 %all-to-all-done.2 = bf16[64,64,128]{2,1,0:T(8,128)(2,1)S(1)} async-done(((bf16[64,64,128]{2,1,0:T(8,128)(2,1)}), bf16[64,64,128]{2,1,0:T(8,128)(2,1)S(1)}, u32[]{:S(2)}, u32[]{:S(2)}) %all-to-all-start.2) | async-done | bytes 1048608 | tf_op jit(solution)/shard_map/all_to_all | solution.py:666
  143.4 2.5 %collective-permute-start.7 = (bf16[128,256]{1,0:T(8,128)(2,1)S(1)}, bf16[128,256]{1,0:T(8,128)(2,1)S(1)}, u32[]{:S(2)}, u32[]{:S(2)}) collective-permute-start(bf16[128,256]{1,0:T(8,128)(2,1)S(1)} %pad_maximum_fusion.2), channel_id=1, source_target_pairs={{0,1},{1,2},{2,3},{3,4},{4,5},{5,6},{6,7},{7,8},{8,9},{9,10},{10,1... | collective-permute-start | bytes 196616 | tf_op jit(solution)/shard_map/ppermute | solution.py:93
  146.0 1.3 collective-permute-start.8
  147.3 7.7 %all-to-all-start.3 = ((bf16[64,64,128]{2,1,0:T(8,128)(2,1)}), bf16[64,64,128]{2,1,0:T(8,128)(2,1)S(1)}, u32[]{:S(2)}, u32[]{:S(2)}) async-start(bf16[64,64,128]{2,1,0:T(8,128)(2,1)} %broadcast_in_dim.10), calls=%async_computation.3 | async-start | bytes 2097152 | tf_op jit(solution)/shard_map/all_to_all | solution.py:666
  155.6 12.8 %conv_back.1 = f32[128,1,256]{2,1,0:T(1,128)} custom-call(bf16[2048,256]{1,0:T(8,128)(2,1)} %get-tuple-element.77.d_mixed, bf16[224,256]{1,0:T(8,128)(2,1)} %copy-done.9, bf16[224,256]{1,0:T(8,128)(2,1)} %copy-done.10, bf16[128,256]{1,0:T(8,128)(2,1)} %copy-done.11, bf16[128,256]{1,0:T(8,128)(2,1)} %copy-done.12, f32[49,256]{1,0:T(8,128)} %kern.3, ...), custom_call_target="tpu_custom_call" | custom-call | flops 14000000000 | bytes 16000000 | tf_op jit(solution)/shard_map/conv_back/pallas_call | solution.py:555
  168.4 3.5 %all-to-all-done.3 = bf16[64,64,128]{2,1,0:T(8,128)(2,1)S(1)} async-done(((bf16[64,64,128]{2,1,0:T(8,128)(2,1)}), bf16[64,64,128]{2,1,0:T(8,128)(2,1)S(1)}, u32[]{:S(2)}, u32[]{:S(2)}) %all-to-all-start.3) | async-done | bytes 1048608 | tf_op jit(solution)/shard_map/all_to_all | solution.py:666
  171.9 2.7 %collective-permute-start.9 = (bf16[64,64,128]{2,1,0:T(8,128)(2,1)S(1)}, bf16[64,64,128]{2,1,0:T(8,128)(2,1)S(1)}, u32[]{:S(2)}, u32[]{:S(2)}) collective-permute-start(bf16[64,64,128]{2,1,0:T(8,128)(2,1)S(1)} %all-to-all-done.3), channel_id=1, source_target_pairs={{0,16},{16,0},{1,17},{17,1},{2,18},{18,2},{3,19},{19,3},{4,20},{20... | collective-permute-start | bytes 3145736 | tf_op jit(solution)/shard_map/ppermute | solution.py:709
  174.6 14.3 %all_to_all.31 = f32[128,1,256]{2,1,0:T(1,128)S(1)} all-to-all(f32[128,1,256]{2,1,0:T(1,128)} %conv_back.1), channel_id=1, replica_groups=mesh['z'=4,'core'=2,'x'=4,'y'=4] {'z','core','x','y'}, dimensions={0} | all-to-all | bytes 262144 | tf_op jit(solution)/shard_map/all_to_all | solution.py:670
  189.8 4.1 %all-to-all-start.5 = ((f32[128,1,256]{2,1,0:T(1,128)}), f32[128,1,256]{2,1,0:T(1,128)S(1)}, u32[]{:S(2)}, u32[]{:S(2)}) async-start(f32[128,1,256]{2,1,0:T(1,128)} %broadcast_in_dim.11), calls=%async_computation.5 | async-start | bytes 262144 | tf_op jit(solution)/shard_map/all_to_all | solution.py:670
  195.0 6.8 %collect.1 = (f32[256,1024]{1,0:T(8,128)}, f32[256,1024]{1,0:T(8,128)}, f32[256,2048]{1,0:T(8,128)}) custom-call(s32[1]{0:T(128)} %bitcast.core, bf16[4,4,256,128]{3,2,1,0:T(8,128)(2,1)} %bitcast.75, bf16[4,4,256,128]{3,2,1,0:T(8,128)(2,1)} %bitcast.76), custom_call_target="tpu_custom_call" | custom-call | tf_op jit(solution)/shard_map/collect/pallas_call | solution.py:616
  201.8 2.2 %all-to-all-done.5.small = f32[128,1,256]{2,1,0:T(1,128)S(1)} async-done(((f32[128,1,256]{2,1,0:T(1,128)}), f32[128,1,256]{2,1,0:T(1,128)S(1)}, u32[]{:S(2)}, u32[]{:S(2)}) %all-to-all-start.5) | async-done | bytes 131104 | tf_op jit(solution)/shard_map/all_to_all | solution.py:670
  204.7 1.6 split_small.1
  (55 shorter events, 11.3 us)
Async XLA Ops:
  5.2 7.0 %collective-permute-start = (bf16[224,256]{1,0:T(8,128)(2,1)}, bf16[224,256]{1,0:T(8,128)(2,1)S(1)}, u32[]{:S(2)}, u32[]{:S(2)}) collective-permute-start(bf16[224,256]{1,0:T(8,128)(2,1)} %get-tuple-element.54), channel_id=1, source_target_pairs={{0,16},{16,32},{32,48},{48,64},{64,80},{80,96},{96,112},{1,17},{17... | collective-permute-start | bytes 344072 | tf_op jit(solution)/shard_map/ppermute | solution.py:82
  10.1 6.3 %collective-permute-start.1 = (bf16[224,256]{1,0:T(8,128)(2,1)}, bf16[224,256]{1,0:T(8,128)(2,1)S(1)}, u32[]{:S(2)}, u32[]{:S(2)}) collective-permute-start(bf16[224,256]{1,0:T(8,128)(2,1)} %get-tuple-element.55), channel_id=1, source_target_pairs={{16,0},{32,16},{48,32},{64,48},{80,64},{96,80},{112,96},{17,1},{33... | collective-permute-start | bytes 344072 | tf_op jit(solution)/shard_map/ppermute | solution.py:83
  12.2 14.1 %copy-start.3 = (bf16[224,256]{1,0:T(8,128)(2,1)}, bf16[224,256]{1,0:T(8,128)(2,1)S(1)}, u32[]{:S(2)}) copy-start(bf16[224,256]{1,0:T(8,128)(2,1)S(1)} %collective-permute-done.above) | copy-start | bytes 344068
  16.4 9.8 %copy-start.4 = (bf16[224,256]{1,0:T(8,128)(2,1)}, bf16[224,256]{1,0:T(8,128)(2,1)S(1)}, u32[]{:S(2)}) copy-start(bf16[224,256]{1,0:T(8,128)(2,1)S(1)} %collective-permute-done.1.below) | copy-start | bytes 344068
  17.3 5.3 %collective-permute-start.2 = (bf16[128,256]{1,0:T(8,128)(2,1)S(1)}, bf16[128,256]{1,0:T(8,128)(2,1)S(1)}, u32[]{:S(2)}, u32[]{:S(2)}) collective-permute-start(bf16[128,256]{1,0:T(8,128)(2,1)S(1)} %pad_maximum_fusion), channel_id=1, source_target_pairs={{0,1},{1,2},{2,3},{3,4},{4,5},{5,6},{6,7},{7,8},{8,9},{9,10},{10,1... | collective-permute-start | bytes 196616 | tf_op jit(solution)/shard_map/ppermute | solution.py:93
  21.3 5.0 %collective-permute-start.3 = (bf16[128,256]{1,0:T(8,128)(2,1)S(1)}, bf16[128,256]{1,0:T(8,128)(2,1)S(1)}, u32[]{:S(2)}, u32[]{:S(2)}) collective-permute-start(bf16[128,256]{1,0:T(8,128)(2,1)S(1)} %pad_maximum_fusion.1), channel_id=1, source_target_pairs={{1,0},{2,1},{3,2},{4,3},{5,4},{6,5},{7,6},{8,7},{9,8},{10,9},{11,1... | collective-permute-start | bytes 196616 | tf_op jit(solution)/shard_map/ppermute | solution.py:94
  22.6 3.7 %copy-start.5 = (bf16[128,256]{1,0:T(8,128)(2,1)}, bf16[128,256]{1,0:T(8,128)(2,1)S(1)}, u32[]{:S(2)}) copy-start(bf16[128,256]{1,0:T(8,128)(2,1)S(1)} %collective-permute-done.2.lh) | copy-start | bytes 196612
  26.3 0.6 copy-start.6
  65.4 16.1 %all-to-all-start.1 = ((f32[16,3,8,256]{3,2,1,0:T(8,128)}), f32[16,3,8,256]{3,2,1,0:T(8,128)S(1)}, u32[]{:S(2)}, u32[]{:S(2)}) async-start(f32[16,3,8,256]{3,2,1,0:T(8,128)} %broadcast_in_dim.9), calls=%async_computation.1 | async-start | bytes 786432 | tf_op jit(solution)/shard_map/all_to_all | solution.py:579
  106.3 7.0 %collective-permute-start.4 = (f32[4,4,256,128]{3,2,1,0:T(8,128)}, f32[4,4,256,128]{3,2,1,0:T(8,128)S(1)}, u32[]{:S(2)}, u32[]{:S(2)}) collective-permute-start(f32[4,4,256,128]{3,2,1,0:T(8,128)} %get-tuple-element.67), channel_id=1, source_target_pairs={{0,16},{16,0},{1,17},{17,1},{2,18},{18,2},{3,19},{19,3},{4,20},{20... | collective-permute-start | bytes 6291464 | tf_op jit(solution)/shard_map/ppermute | solution.py:696
  109.0 7.2 %collective-permute-start.5 = (bf16[224,256]{1,0:T(8,128)(2,1)}, bf16[224,256]{1,0:T(8,128)(2,1)S(1)}, u32[]{:S(2)}, u32[]{:S(2)}) collective-permute-start(bf16[224,256]{1,0:T(8,128)(2,1)} %get-tuple-element.68), channel_id=1, source_target_pairs={{0,16},{16,32},{32,48},{48,64},{64,80},{80,96},{96,112},{1,17},{17... | collective-permute-start | bytes 344072 | tf_op jit(solution)/shard_map/ppermute | solution.py:82
  111.1 6.3 %collective-permute-start.6 = (bf16[224,256]{1,0:T(8,128)(2,1)}, bf16[224,256]{1,0:T(8,128)(2,1)S(1)}, u32[]{:S(2)}, u32[]{:S(2)}) collective-permute-start(bf16[224,256]{1,0:T(8,128)(2,1)} %get-tuple-element.69), channel_id=1, source_target_pairs={{16,0},{32,16},{48,32},{64,48},{80,64},{96,80},{112,96},{17,1},{33... | collective-permute-start | bytes 344072 | tf_op jit(solution)/shard_map/ppermute | solution.py:83
  116.2 27.2 %copy-start.9 = (bf16[224,256]{1,0:T(8,128)(2,1)}, bf16[224,256]{1,0:T(8,128)(2,1)S(1)}, u32[]{:S(2)}) copy-start(bf16[224,256]{1,0:T(8,128)(2,1)S(1)} %collective-permute-done.5.above) | copy-start | bytes 344068
  117.4 25.9 %copy-start.10 = (bf16[224,256]{1,0:T(8,128)(2,1)}, bf16[224,256]{1,0:T(8,128)(2,1)S(1)}, u32[]{:S(2)}) copy-start(bf16[224,256]{1,0:T(8,128)(2,1)S(1)} %collective-permute-done.6.below) | copy-start | bytes 344068
  117.4 24.5 %all-to-all-start.2 = ((bf16[64,64,128]{2,1,0:T(8,128)(2,1)}), bf16[64,64,128]{2,1,0:T(8,128)(2,1)S(1)}, u32[]{:S(2)}, u32[]{:S(2)}) async-start(bf16[64,64,128]{2,1,0:T(8,128)(2,1)} %bitcast.15), calls=%async_computation.2 | async-start | bytes 2097152 | tf_op jit(solution)/shard_map/all_to_all | solution.py:666
  134.0 9.3 %copy-start.8 = (bf16[96,256]{1,0:T(8,128)(2,1)S(1)}, bf16[96,256]{1,0:T(8,128)(2,1)}, u32[]{:S(2)}) copy-start(bf16[96,256]{1,0:T(8,128)(2,1)} %get-tuple-element.80) | copy-start | bytes 147460
  134.0 11.9 %copy-start.7 = (bf16[96,256]{1,0:T(8,128)(2,1)S(1)}, bf16[96,256]{1,0:T(8,128)(2,1)}, u32[]{:S(2)}) copy-start(bf16[96,256]{1,0:T(8,128)(2,1)} %get-tuple-element.81) | copy-start | bytes 147460
  143.4 11.6 %collective-permute-start.7 = (bf16[128,256]{1,0:T(8,128)(2,1)S(1)}, bf16[128,256]{1,0:T(8,128)(2,1)S(1)}, u32[]{:S(2)}, u32[]{:S(2)}) collective-permute-start(bf16[128,256]{1,0:T(8,128)(2,1)S(1)} %pad_maximum_fusion.2), channel_id=1, source_target_pairs={{0,1},{1,2},{2,3},{3,4},{4,5},{5,6},{6,7},{7,8},{8,9},{9,10},{10,1... | collective-permute-start | bytes 196616 | tf_op jit(solution)/shard_map/ppermute | solution.py:93
  146.0 9.0 %collective-permute-start.8 = (bf16[128,256]{1,0:T(8,128)(2,1)S(1)}, bf16[128,256]{1,0:T(8,128)(2,1)S(1)}, u32[]{:S(2)}, u32[]{:S(2)}) collective-permute-start(bf16[128,256]{1,0:T(8,128)(2,1)S(1)} %pad_maximum_fusion.3), channel_id=1, source_target_pairs={{1,0},{2,1},{3,2},{4,3},{5,4},{6,5},{7,6},{8,7},{9,8},{10,9},{11,1... | collective-permute-start | bytes 196616 | tf_op jit(solution)/shard_map/ppermute | solution.py:94
  147.3 24.7 %all-to-all-start.3 = ((bf16[64,64,128]{2,1,0:T(8,128)(2,1)}), bf16[64,64,128]{2,1,0:T(8,128)(2,1)S(1)}, u32[]{:S(2)}, u32[]{:S(2)}) async-start(bf16[64,64,128]{2,1,0:T(8,128)(2,1)} %broadcast_in_dim.10), calls=%async_computation.3 | async-start | bytes 2097152 | tf_op jit(solution)/shard_map/all_to_all | solution.py:666
  155.0 0.6 copy-start.11
  155.0 0.6 copy-start.12
  171.9 22.1 %copy-start = (bf16[64,64,128]{2,1,0:T(8,128)(2,1)}, bf16[64,64,128]{2,1,0:T(8,128)(2,1)S(1)}, u32[]{:S(2)}) copy-start(bf16[64,64,128]{2,1,0:T(8,128)(2,1)S(1)} %all-to-all-done.3) | copy-start | bytes 3145732
  171.9 22.0 %collective-permute-start.9 = (bf16[64,64,128]{2,1,0:T(8,128)(2,1)S(1)}, bf16[64,64,128]{2,1,0:T(8,128)(2,1)S(1)}, u32[]{:S(2)}, u32[]{:S(2)}) collective-permute-start(bf16[64,64,128]{2,1,0:T(8,128)(2,1)S(1)} %all-to-all-done.3), channel_id=1, source_target_pairs={{0,16},{16,0},{1,17},{17,1},{2,18},{18,2},{3,19},{19,3},{4,20},{20... | collective-permute-start | bytes 3145736 | tf_op jit(solution)/shard_map/ppermute | solution.py:709
  189.8 14.2 %all-to-all-start.5 = ((f32[128,1,256]{2,1,0:T(1,128)}), f32[128,1,256]{2,1,0:T(1,128)S(1)}, u32[]{:S(2)}, u32[]{:S(2)}) async-start(f32[128,1,256]{2,1,0:T(1,128)} %broadcast_in_dim.11), calls=%async_computation.5 | async-start | bytes 262144 | tf_op jit(solution)/shard_map/all_to_all | solution.py:670
  194.0 1.0 copy-start.1
  204.0 0.7 copy-start.2

commit v7 on v6

--- a/solution.py
+++ b/solution.py
@@ -346,8 +346,8 @@
 
 
 def attend_grad_kernel(
-    core, normed, k_in, v_in, wk, wv, q, up, lse, dots, factor, weighted, centred, inverse, gain,
-    send, keep, d_mixed, gain_grad, top, bot, left, right, dn_sc, nt_sc, l_sc, r_sc, c_sc,
+    core, normed, k_in, v_in, wk, wv, q, up, lse, dots, factor, weighted,
+    send, keep, dn_sc, nt_sc,
 ):
     step = pl.program_id(0)
     first = step_at(step, core) * GROUP
@@ -406,27 +406,39 @@
     def _():
         put(keep)
 
-    @pl.when(step == STEPS - 1)
-    def _():
-        def body(n, total):
-            rows = pl.ds(pl.multiple_of(n * BLOCK, BLOCK), BLOCK)
-            x = centred[rows, :]
-            inv = inverse[rows, :]
-            dn = dn_sc[rows, :]
-            total = total + jnp.sum(dn * x, axis=0, keepdims=True)
-            g = dn * gain[...]
-            mean = jnp.sum(g, axis=-1, keepdims=True) * (1.0 / CH)
-            slope = jnp.sum(g * x, axis=-1, keepdims=True) * (1.0 / CH)
-            inv = jnp.concatenate([inv, inv], axis=1)
-            d_mixed[rows, :] = (inv * (g - mean - x * slope)).astype(BF)
-            return total
-
-        gain_grad[...] = lax.fori_loop(0, TOK // BLOCK, body, jnp.zeros((1, CH), F32))
-        write_edges(d_mixed, top, bot, left, right, l_sc, r_sc, c_sc)
+
+def norm_grad_kernel(dn_in, centred, inverse, gain, d_mixed, gain_grad, top, bot, left, right, l_sc, r_sc, c_sc):
+    def body(n, total):
+        rows = pl.ds(pl.multiple_of(n * BLOCK, BLOCK), BLOCK)
+        x = centred[rows, :]
+        inv = inverse[rows, :]
+        dn = dn_in[rows, :]
+        total = total + jnp.sum(dn * x, axis=0, keepdims=True)
+        g = dn * gain[...]
+        mean = jnp.sum(g, axis=-1, keepdims=True) * (1.0 / CH)
+        slope = jnp.sum(g * x, axis=-1, keepdims=True) * (1.0 / CH)
+        inv = jnp.concatenate([inv, inv], axis=1)
+        d_mixed[rows, :] = (inv * (g - mean - x * slope)).astype(BF)
+        return total
+
+    gain_grad[...] = lax.fori_loop(0, TOK // BLOCK, body, jnp.zeros((1, CH), F32))
+    write_edges(d_mixed, top, bot, left, right, l_sc, r_sc, c_sc)
+
+
+def norm_grad(dn, centred, inverse, gain):
+    outs = pl.pallas_call(
+        norm_grad_kernel,
+        name="norm_grad",
+        out_shape=[jax.ShapeDtypeStruct((TOK, CH), BF), jax.ShapeDtypeStruct((1, CH), F32)] + EDGE_SHAPES,
+        scratch_shapes=EDGE_SCRATCH,
+        compiler_params=VMEM,
+        cost_estimate=COST,
+    )(dn, centred, inverse, gain)
+    return outs[0], outs[1], outs[2:]
 
 
 def attend_grad(
-    core, normed, k, v, kv_weight, latents, d_attended, lse, dots, factor, weighted, centred, inverse, gain
+    core, normed, k, v, kv_weight, latents, d_attended, lse, dots, factor, weighted
 ):
     def full(shape):
         return pl.BlockSpec(shape, lambda n, core: (0,) * len(shape))
@@ -455,30 +467,23 @@
                 full((HEADS, 256)),
                 full((HEADS, 256)),
                 pl.BlockSpec((GROUP, 128, 256), lambda n, core: (step_at(n, core), 0, 0)),
-                full((TOK, CH)),
-                full((TOK, 128)),
-                full((1, CH)),
             ],
             out_specs=[
                 pl.BlockSpec(block, lambda n, core: (0, jnp.minimum(n, half - 1), 0, 0)),
                 pl.BlockSpec(block, lambda n, core: (0, jnp.maximum(n - half, 0), 0, 0)),
                 full((TOK, CH)),
-                full((1, CH)),
-            ]
-            + [full(s.shape) for s in EDGE_SHAPES],
-            scratch_shapes=[pltpu.VMEM((TOK, CH), F32), pltpu.VMEM((CH, TOK), BF)] + EDGE_SCRATCH,
+            ],
+            scratch_shapes=[pltpu.VMEM((CH, TOK), BF)],
         ),
         out_shape=[
             part,
             part,
-            jax.ShapeDtypeStruct((TOK, CH), BF),
-            jax.ShapeDtypeStruct((1, CH), F32),
-        ]
-        + EDGE_SHAPES,
+            jax.ShapeDtypeStruct((TOK, CH), F32),
+        ],
         compiler_params=VMEM,
         cost_estimate=COST,
-    )(core, normed, k, v, kv_weight, kv_weight, latents, d_attended, lse, dots, factor, weighted, centred, inverse, gain)
-    return outs[:4], outs[4:]
+    )(core, normed, k, v, kv_weight, kv_weight, latents, d_attended, lse, dots, factor, weighted)
+    return outs
 
 
 def kernel_grad_body(wide, d_mixed, out, d_sc):
@@ -688,16 +693,18 @@
     row_dots = stats[2] / stats[1]
     factor = jnp.exp2(local[0] - stats[0]) / stats[1]
     core = lax.axis_index("core").astype(jnp.int32).reshape(1)
-    (away, keep, d_mixed, gain_grad), d_edges = attend_grad(
-        core, normed, k, v, kv_weight, latents, d_attended, lse, row_dots, factor, weighted,
-        centred, inverse, gain,
+    away, keep, dn = attend_grad(
+        core, normed, k, v, kv_weight, latents, d_attended, lse, row_dots, factor, weighted
     )
+    away = lax.ppermute(away, "core", PAIR)
+    d_mixed, gain_grad, d_edges = norm_grad(dn, centred, inverse, gain)
+    d_mixed, away, *d_edges = tie(d_mixed, away, *d_edges)
+    message = (keep + away).astype(BF).reshape(64, 64, 128)
+    d_mixed, message, *d_edges = tie(d_mixed, message, *d_edges)
+    message = send(message)
     d_rows = exchange_rows(d_edges)
-    message = (keep + lax.ppermute(away, "core", PAIR)).astype(BF).reshape(64, 64, 128)
-    d_mixed, message, *d_rows = tie(d_mixed, message, *d_rows)
-    message = send(message)
     kern = kernel_grad(wide, d_mixed)
-    d_mixed, message, kern = tie(d_mixed, message, kern)
+    d_mixed, message, kern, *d_rows = tie(d_mixed, message, kern, *d_rows)
     message = copies(block_sum(message))
     d_mixed, message, *d_rows = tie(d_mixed, message, *d_rows)
     message = send(message)

time: 208 us -> 203 us (0.976)
  waiting for transfers between devices: 31.2 us -> 23.7 us
  starting transfers between devices: 50.5 us -> 53 us
  Pallas kernels: 84.4 us -> 86.8 us
    all_to_all x2, waiting for transfers between devices: 11.5 us -> 4.81 us  [send(): return lax.all_to_all(x, CHIPS, 0, 0, tiled=True)]
    pallas_call x0 -> x1, Pallas kernels: none -> 4.57 us  [norm_grad(): pl.pallas_call(norm_grad_kernel, name='norm_grad', out_shape=[jax.ShapeDt...]
    pallas_call x1, Pallas kernels: 23.4 us -> 21.2 us  [attend_grad(): pl.pallas_call(attend_grad_kernel, name='attend_grad', grid_spec=pltpu.Pr...]
  transfers between devices with their start and end apart: 14 -> 14, of which waited for: 8 -> 8; matrix products, arithmetic and copies ran while one was open for 2% -> 1% of each run, Pallas kernels for 15% -> 17%
where the time goes in v7:
time: 203 us; the launch traced here: 202 us
  Pallas kernels  86.8 us (43%)
  starting transfers between devices  53 us (26%)
  blocking collectives  25.4 us (13%)
  waiting for transfers between devices  23.7 us (12%)
  local copies, waits for them, and re-layouts  7.76 us (4%)
  other arithmetic  4.61 us (2%)
    pallas_call x1, Pallas kernels, attend_grad(): pl.pallas_call(attend_grad_kernel, name='attend_grad', grid_spec=pltpu.Pr...  21.2 us
    all_to_all x2, starting transfers between devices, send(): return lax.all_to_all(x, CHIPS, 0, 0, tiled=True)  14.5 us
    all_to_all x1, blocking collectives, send_all(): return lax.all_to_all(x, ALL, 0, 0, tiled=True)  14.4 us
    pallas_call x1, Pallas kernels, conv_forward(): pl.pallas_call(conv_kernel_body, name='conv_forward', out_shape=[jax.Shap...  13.7 us
    pallas_call x1, Pallas kernels, conv_back(): pl.pallas_call(conv_back_body, name='conv_back', out_shape=jax.ShapeDtype...  12.8 us
    pallas_call x1, Pallas kernels, attend(): pl.pallas_call(attend_kernel, name='attend', grid=(HEADS // WIDTH,), in_s...  12.1 us
    all_to_all x1, blocking collectives, gather(): return lax.all_to_all(copies, axes, 0, 0, tiled=True)  11 us
    pallas_call x1, Pallas kernels, kernel_grad(): pl.pallas_call(kernel_grad_body, name='kernel_grad', out_shape=jax.ShapeD...  10.8 us
  transfers between devices with their start and end apart: 14, of which 8 were waited for; matrix products, arithmetic and copies ran while one was open for 1% of the time, Pallas kernels for 17%

profile of v7, /device:TPU:1, one launch (start us, length us, event | category | flops | bytes accessed | tf_op | source)
XLA Modules:
  0.0 202.2 jit_solution(11622557066216806874)
XLA Ops:
  2.0 3.2 %embed.1 = (bf16[2048,256]{1,0:T(8,128)(2,1)}, bf16[256,512]{1,0:T(8,128)(2,1)}, bf16[224,256]{1,0:T(8,128)(2,1)}, bf16[224,256]{1,0:T(8,128)(2,1)}, bf16[96,256]{1,0:T(8,128)(2,1)}, /*index=5*/bf16[96,256]{1,0:T(8,128)(2,1)}) custom-call(bf16[384,256]{1,0:T(8,128)(2,1)} %bitcast.77, bf16[4,16,256]{2,1,0:T(8,128)(2,1)} %pad.4.weights, f32[1,256]{1,0:T(1,128)} %bitcast.82), custom_call_target="tpu_custom_call" | custom-call | tf_op jit(solution)/shard_map/embed/pallas_call | solution.py:202
  5.2 4.9 %collective-permute-start = (bf16[224,256]{1,0:T(8,128)(2,1)}, bf16[224,256]{1,0:T(8,128)(2,1)S(1)}, u32[]{:S(2)}, u32[]{:S(2)}) collective-permute-start(bf16[224,256]{1,0:T(8,128)(2,1)} %get-tuple-element.65), channel_id=1, source_target_pairs={{0,16},{16,32},{32,48},{48,64},{64,80},{80,96},{96,112},{1,17},{17... | collective-permute-start | bytes 344072 | tf_op jit(solution)/shard_map/ppermute | solution.py:82
  10.1 1.9 collective-permute-start.1
  12.2 4.2 %collective-permute-done.1.below = bf16[224,256]{1,0:T(8,128)(2,1)S(1)} collective-permute-done((bf16[224,256]{1,0:T(8,128)(2,1)}, bf16[224,256]{1,0:T(8,128)(2,1)S(1)}, u32[]{:S(2)}, u32[]{:S(2)}) %collective-permute-start.1) | collective-permute-done | bytes 114720 | tf_op jit(solution)/shard_map/ppermute | solution.py:83
  17.2 3.2 %collective-permute-start.2 = (bf16[128,256]{1,0:T(8,128)(2,1)S(1)}, bf16[128,256]{1,0:T(8,128)(2,1)S(1)}, u32[]{:S(2)}, u32[]{:S(2)}) collective-permute-start(bf16[128,256]{1,0:T(8,128)(2,1)S(1)} %pad_maximum_fusion), channel_id=1, source_target_pairs={{0,1},{1,2},{2,3},{3,4},{4,5},{5,6},{6,7},{7,8},{8,9},{9,10},{10,1... | collective-permute-start | bytes 196616 | tf_op jit(solution)/shard_map/ppermute | solution.py:93
  21.3 1.3 collective-permute-start.3
  22.6 3.7 %collective-permute-done.3.rh = bf16[128,256]{1,0:T(8,128)(2,1)S(1)} collective-permute-done((bf16[128,256]{1,0:T(8,128)(2,1)S(1)}, bf16[128,256]{1,0:T(8,128)(2,1)S(1)}, u32[]{:S(2)}, u32[]{:S(2)}) %collective-permute-start.3) | collective-permute-done | bytes 65568 | tf_op jit(solution)/shard_map/ppermute | solution.py:94
  26.9 13.7 %conv_forward.1 = (f32[38,14,8,256]{3,2,1,0:T(8,128)}, f32[2048,256]{1,0:T(8,128)}, f32[2048,128]{1,0:T(8,128)}, bf16[2048,256]{1,0:T(8,128)(2,1)}) custom-call(bf16[2048,256]{1,0:T(8,128)(2,1)} %get-tuple-element.64.emb, bf16[224,256]{1,0:T(8,128)(2,1)} %copy-done.4, bf16[224,256]{1,0:T(8,128)(2,1)} %copy-done.5, bf16[128,256]{1,0:T(8,128)(2,1)} %copy-done.6, ...), custom_call_target="tpu_custom_call" | custom-call | tf_op jit(solution)/shard_map/conv_forward/pallas_call | solution.py:243
  40.6 12.1 %attend.1 = (bf16[2048,1024]{1,0:T(8,128)(2,1)}, bf16[2048,1024]{1,0:T(8,128)(2,1)}, f32[8,128,256]{2,1,0:T(8,128)}, f32[3,8,256]{2,1,0:T(8,128)}) custom-call(bf16[2048,256]{1,0:T(8,128)(2,1)} %get-tuple-element.69.normed, bf16[256,2048]{1,0:T(8,128)(2,1)} %wv.3, bf16[256,2048]{1,0:T(8,128)(2,1)} %wv.3, bf16[256,1024]{1,0:T(8,128)(2,1)} %q.3, ...), custom_call_target="tpu_custom_call" | custom-call | tf_op jit(solution)/shard_map/attend/pallas_call | solution.py:313
  53.5 11.0 %all_to_all.30 = f32[8,3,8,256]{3,2,1,0:T(8,128)S(1)} all-to-all(f32[8,3,8,256]{3,2,1,0:T(8,128)S(1)} %broadcast_in_dim.8), channel_id=1, replica_groups=mesh['z'=4,'core'=2,'x'=4,'y'=4] {'z','core'}, dimensions={0} | all-to-all | bytes 393216 | tf_op jit(solution)/shard_map/all_to_all | solution.py:584
  65.4 8.0 %all-to-all-start.1 = ((f32[16,3,8,256]{3,2,1,0:T(8,128)}), f32[16,3,8,256]{3,2,1,0:T(8,128)S(1)}, u32[]{:S(2)}, u32[]{:S(2)}) async-start(f32[16,3,8,256]{3,2,1,0:T(8,128)} %broadcast_in_dim.9), calls=%async_computation.1 | async-start | bytes 786432 | tf_op jit(solution)/shard_map/all_to_all | solution.py:584
  73.4 8.1 %all-to-all-done.1 = f32[16,3,8,256]{3,2,1,0:T(8,128)S(1)} async-done(((f32[16,3,8,256]{3,2,1,0:T(8,128)}), f32[16,3,8,256]{3,2,1,0:T(8,128)S(1)}, u32[]{:S(2)}, u32[]{:S(2)}) %all-to-all-start.1) | async-done | bytes 393248 | tf_op jit(solution)/shard_map/all_to_all | solution.py:584
  81.6 1.3 fusion.14
  82.9 21.2 %attend_grad.1 = (f32[4,4,256,128]{3,2,1,0:T(8,128)}, f32[4,4,256,128]{3,2,1,0:T(8,128)}, f32[2048,256]{1,0:T(8,128)}) custom-call(s32[1]{0:T(128)} %bitcast.core, bf16[2048,256]{1,0:T(8,128)(2,1)} %get-tuple-element.69.normed, bf16[2048,1024]{1,0:T(8,128)(2,1)} %get-tuple-element.70.k_in, bf16[2048,1024]{1,0:T(8,128)(2,1)} %get-tuple-element.71.v_in, ...), custom_call_target="tpu_custom_call" | custom-call | flops 14000000000 | bytes 16000000 | tf_op jit(solution)/shard_map/attend_grad/pallas_call | solution.py:452
  104.1 2.9 %collective-permute-start.4 = (f32[4,4,256,128]{3,2,1,0:T(8,128)}, f32[4,4,256,128]{3,2,1,0:T(8,128)S(1)}, u32[]{:S(2)}, u32[]{:S(2)}) collective-permute-start(f32[4,4,256,128]{3,2,1,0:T(8,128)} %get-tuple-element.78), channel_id=1, source_target_pairs={{0,16},{16,0},{1,17},{17,1},{2,18},{18,2},{3,19},{19,3},{4,20},{20... | collective-permute-start | bytes 6291464 | tf_op jit(solution)/shard_map/ppermute | solution.py:699
  107.0 4.6 %norm_grad.1 = (bf16[2048,256]{1,0:T(8,128)(2,1)}, f32[1,256]{1,0:T(1,128)}, bf16[224,256]{1,0:T(8,128)(2,1)}, bf16[224,256]{1,0:T(8,128)(2,1)}, bf16[96,256]{1,0:T(8,128)(2,1)}, /*index=5*/bf16[96,256]{1,0:T(8,128)(2,1)}) custom-call(f32[2048,256]{1,0:T(8,128)} %get-tuple-element.74.dn_in, f32[2048,256]{1,0:T(8,128)} %get-tuple-element.75.centred, ...), custom_call_target="tpu_custom_call" | custom-call | flops 14000000000 | bytes 16000000 | tf_op jit(solution)/shard_map/norm_grad/pallas_call | solution.py:429
  112.8 5.0 %all-to-all-start.2 = ((bf16[64,64,128]{2,1,0:T(8,128)(2,1)}), bf16[64,64,128]{2,1,0:T(8,128)(2,1)S(1)}, u32[]{:S(2)}, u32[]{:S(2)}) async-start(bf16[64,64,128]{2,1,0:T(8,128)(2,1)} %bitcast.15), calls=%async_computation.2 | async-start | bytes 2097152 | tf_op jit(solution)/shard_map/all_to_all | solution.py:671
  117.9 3.4 %collective-permute-start.5 = (bf16[224,256]{1,0:T(8,128)(2,1)S(1)}, bf16[224,256]{1,0:T(8,128)(2,1)S(1)}, u32[]{:S(2)}, u32[]{:S(2)}) collective-permute-start(bf16[224,256]{1,0:T(8,128)(2,1)S(1)} %copy-done.13), channel_id=1, source_target_pairs={{0,16},{16,32},{32,48},{48,64},{64,80},{80,96},{96,112},{1,17},{17... | collective-permute-start | bytes 344072 | tf_op jit(solution)/shard_map/ppermute | solution.py:82
  121.3 1.9 collective-permute-start.6
  123.2 10.8 %kernel_grad.1.kern_grad = f32[49,256]{1,0:T(8,128)} custom-call(f32[38,14,8,256]{3,2,1,0:T(8,128)} %get-tuple-element.92.wide, bf16[2048,256]{1,0:T(8,128)(2,1)} %get-tuple-element.99.d_mixed), custom_call_target="tpu_custom_call" | custom-call | flops 14000000000 | bytes 16000000 | tf_op jit(solution)/shard_map/kernel_grad/pallas_call | solution.py:515
  134.4 1.3 all-to-all-done.2
  137.2 2.8 %collective-permute-start.7 = (bf16[128,256]{1,0:T(8,128)(2,1)S(1)}, bf16[128,256]{1,0:T(8,128)(2,1)S(1)}, u32[]{:S(2)}, u32[]{:S(2)}) collective-permute-start(bf16[128,256]{1,0:T(8,128)(2,1)S(1)} %pad_maximum_fusion.2), channel_id=1, source_target_pairs={{0,1},{1,2},{2,3},{3,4},{4,5},{5,6},{6,7},{7,8},{8,9},{9,10},{10,1... | collective-permute-start | bytes 196616 | tf_op jit(solution)/shard_map/ppermute | solution.py:93
  140.1 1.3 collective-permute-start.8
  141.4 9.4 %all-to-all-start.3 = ((bf16[64,64,128]{2,1,0:T(8,128)(2,1)}), bf16[64,64,128]{2,1,0:T(8,128)(2,1)S(1)}, u32[]{:S(2)}, u32[]{:S(2)}) async-start(bf16[64,64,128]{2,1,0:T(8,128)(2,1)} %broadcast_in_dim.10), calls=%async_computation.3 | async-start | bytes 2097152 | tf_op jit(solution)/shard_map/all_to_all | solution.py:671
  151.5 12.8 %conv_back.1 = f32[128,1,256]{2,1,0:T(1,128)} custom-call(bf16[2048,256]{1,0:T(8,128)(2,1)} %get-tuple-element.99.d_mixed, bf16[224,256]{1,0:T(8,128)(2,1)} %copy-done.10, bf16[224,256]{1,0:T(8,128)(2,1)} %copy-done.11, bf16[128,256]{1,0:T(8,128)(2,1)} %copy-done.14, bf16[128,256]{1,0:T(8,128)(2,1)} %copy-done.15, f32[49,256]{1,0:T(8,128)} %kern.3, ...), custom_call_target="tpu_custom_call" | custom-call | flops 14000000000 | bytes 16000000 | tf_op jit(solution)/shard_map/conv_back/pallas_call | solution.py:560
  164.3 3.5 %all-to-all-done.3 = bf16[64,64,128]{2,1,0:T(8,128)(2,1)S(1)} async-done(((bf16[64,64,128]{2,1,0:T(8,128)(2,1)}), bf16[64,64,128]{2,1,0:T(8,128)(2,1)S(1)}, u32[]{:S(2)}, u32[]{:S(2)}) %all-to-all-start.3) | async-done | bytes 1048608 | tf_op jit(solution)/shard_map/all_to_all | solution.py:671
  167.7 2.8 %collective-permute-start.9 = (bf16[64,64,128]{2,1,0:T(8,128)(2,1)S(1)}, bf16[64,64,128]{2,1,0:T(8,128)(2,1)S(1)}, u32[]{:S(2)}, u32[]{:S(2)}) collective-permute-start(bf16[64,64,128]{2,1,0:T(8,128)(2,1)S(1)} %all-to-all-done.3), channel_id=1, source_target_pairs={{0,16},{16,0},{1,17},{17,1},{2,18},{18,2},{3,19},{19,3},{4,20},{20... | collective-permute-start | bytes 3145736 | tf_op jit(solution)/shard_map/ppermute | solution.py:716
  170.5 14.4 %all_to_all.31 = f32[128,1,256]{2,1,0:T(1,128)S(1)} all-to-all(f32[128,1,256]{2,1,0:T(1,128)} %conv_back.1), channel_id=1, replica_groups=mesh['z'=4,'core'=2,'x'=4,'y'=4] {'z','core','x','y'}, dimensions={0} | all-to-all | bytes 262144 | tf_op jit(solution)/shard_map/all_to_all | solution.py:675
  185.8 4.1 %all-to-all-start.5 = ((f32[128,1,256]{2,1,0:T(1,128)}), f32[128,1,256]{2,1,0:T(1,128)S(1)}, u32[]{:S(2)}, u32[]{:S(2)}) async-start(f32[128,1,256]{2,1,0:T(1,128)} %broadcast_in_dim.11), calls=%async_computation.5 | async-start | bytes 262144 | tf_op jit(solution)/shard_map/all_to_all | solution.py:675
  190.9 6.8 %collect.1 = (f32[256,1024]{1,0:T(8,128)}, f32[256,1024]{1,0:T(8,128)}, f32[256,2048]{1,0:T(8,128)}) custom-call(s32[1]{0:T(128)} %bitcast.core, bf16[4,4,256,128]{3,2,1,0:T(8,128)(2,1)} %bitcast.75, bf16[4,4,256,128]{3,2,1,0:T(8,128)(2,1)} %bitcast.76), custom_call_target="tpu_custom_call" | custom-call | tf_op jit(solution)/shard_map/collect/pallas_call | solution.py:621
  197.7 2.2 %all-to-all-done.5.small = f32[128,1,256]{2,1,0:T(1,128)S(1)} async-done(((f32[128,1,256]{2,1,0:T(1,128)}), f32[128,1,256]{2,1,0:T(1,128)S(1)}, u32[]{:S(2)}, u32[]{:S(2)}) %all-to-all-start.5) | async-done | bytes 131104 | tf_op jit(solution)/shard_map/all_to_all | solution.py:675
  200.6 1.6 split_small.1
  (62 shorter events, 11.7 us)
Async XLA Ops:
  5.2 7.0 %collective-permute-start = (bf16[224,256]{1,0:T(8,128)(2,1)}, bf16[224,256]{1,0:T(8,128)(2,1)S(1)}, u32[]{:S(2)}, u32[]{:S(2)}) collective-permute-start(bf16[224,256]{1,0:T(8,128)(2,1)} %get-tuple-element.65), channel_id=1, source_target_pairs={{0,16},{16,32},{32,48},{48,64},{64,80},{80,96},{96,112},{1,17},{17... | collective-permute-start | bytes 344072 | tf_op jit(solution)/shard_map/ppermute | solution.py:82
  10.1 6.3 %collective-permute-start.1 = (bf16[224,256]{1,0:T(8,128)(2,1)}, bf16[224,256]{1,0:T(8,128)(2,1)S(1)}, u32[]{:S(2)}, u32[]{:S(2)}) collective-permute-start(bf16[224,256]{1,0:T(8,128)(2,1)} %get-tuple-element.66), channel_id=1, source_target_pairs={{16,0},{32,16},{48,32},{64,48},{80,64},{96,80},{112,96},{17,1},{33... | collective-permute-start | bytes 344072 | tf_op jit(solution)/shard_map/ppermute | solution.py:83
  12.2 14.1 %copy-start.4 = (bf16[224,256]{1,0:T(8,128)(2,1)}, bf16[224,256]{1,0:T(8,128)(2,1)S(1)}, u32[]{:S(2)}) copy-start(bf16[224,256]{1,0:T(8,128)(2,1)S(1)} %collective-permute-done.above) | copy-start | bytes 344068
  16.4 9.8 %copy-start.5 = (bf16[224,256]{1,0:T(8,128)(2,1)}, bf16[224,256]{1,0:T(8,128)(2,1)S(1)}, u32[]{:S(2)}) copy-start(bf16[224,256]{1,0:T(8,128)(2,1)S(1)} %collective-permute-done.1.below) | copy-start | bytes 344068
  17.2 5.3 %collective-permute-start.2 = (bf16[128,256]{1,0:T(8,128)(2,1)S(1)}, bf16[128,256]{1,0:T(8,128)(2,1)S(1)}, u32[]{:S(2)}, u32[]{:S(2)}) collective-permute-start(bf16[128,256]{1,0:T(8,128)(2,1)S(1)} %pad_maximum_fusion), channel_id=1, source_target_pairs={{0,1},{1,2},{2,3},{3,4},{4,5},{5,6},{6,7},{7,8},{8,9},{9,10},{10,1... | collective-permute-start | bytes 196616 | tf_op jit(solution)/shard_map/ppermute | solution.py:93
  21.3 5.0 %collective-permute-start.3 = (bf16[128,256]{1,0:T(8,128)(2,1)S(1)}, bf16[128,256]{1,0:T(8,128)(2,1)S(1)}, u32[]{:S(2)}, u32[]{:S(2)}) collective-permute-start(bf16[128,256]{1,0:T(8,128)(2,1)S(1)} %pad_maximum_fusion.1), channel_id=1, source_target_pairs={{1,0},{2,1},{3,2},{4,3},{5,4},{6,5},{7,6},{8,7},{9,8},{10,9},{11,1... | collective-permute-start | bytes 196616 | tf_op jit(solution)/shard_map/ppermute | solution.py:94
  22.6 3.7 %copy-start.6 = (bf16[128,256]{1,0:T(8,128)(2,1)}, bf16[128,256]{1,0:T(8,128)(2,1)S(1)}, u32[]{:S(2)}) copy-start(bf16[128,256]{1,0:T(8,128)(2,1)S(1)} %collective-permute-done.2.lh) | copy-start | bytes 196612
  26.2 0.6 copy-start.7
  65.4 16.1 %all-to-all-start.1 = ((f32[16,3,8,256]{3,2,1,0:T(8,128)}), f32[16,3,8,256]{3,2,1,0:T(8,128)S(1)}, u32[]{:S(2)}, u32[]{:S(2)}) async-start(f32[16,3,8,256]{3,2,1,0:T(8,128)} %broadcast_in_dim.9), calls=%async_computation.1 | async-start | bytes 786432 | tf_op jit(solution)/shard_map/all_to_all | solution.py:584
  104.1 7.5 %collective-permute-start.4 = (f32[4,4,256,128]{3,2,1,0:T(8,128)}, f32[4,4,256,128]{3,2,1,0:T(8,128)S(1)}, u32[]{:S(2)}, u32[]{:S(2)}) collective-permute-start(f32[4,4,256,128]{3,2,1,0:T(8,128)} %get-tuple-element.78), channel_id=1, source_target_pairs={{0,16},{16,0},{1,17},{17,1},{2,18},{18,2},{3,19},{19,3},{4,20},{20... | collective-permute-start | bytes 6291464 | tf_op jit(solution)/shard_map/ppermute | solution.py:699
  107.0 4.6 %copy-start.1 = (f32[4,4,256,128]{3,2,1,0:T(8,128)S(1)}, f32[4,4,256,128]{3,2,1,0:T(8,128)}, u32[]{:S(2)}) copy-start(f32[4,4,256,128]{3,2,1,0:T(8,128)} %get-tuple-element.84) | copy-start | bytes 6291460
  112.8 5.1 %copy-start.13 = (bf16[224,256]{1,0:T(8,128)(2,1)S(1)}, bf16[224,256]{1,0:T(8,128)(2,1)}, u32[]{:S(2)}) copy-start(bf16[224,256]{1,0:T(8,128)(2,1)} %get-tuple-element.93) | copy-start | bytes 344068
  112.8 8.5 %copy-start.12 = (bf16[224,256]{1,0:T(8,128)(2,1)S(1)}, bf16[224,256]{1,0:T(8,128)(2,1)}, u32[]{:S(2)}) copy-start(bf16[224,256]{1,0:T(8,128)(2,1)} %get-tuple-element.94) | copy-start | bytes 344068
  112.8 23.0 %all-to-all-start.2 = ((bf16[64,64,128]{2,1,0:T(8,128)(2,1)}), bf16[64,64,128]{2,1,0:T(8,128)(2,1)S(1)}, u32[]{:S(2)}, u32[]{:S(2)}) async-start(bf16[64,64,128]{2,1,0:T(8,128)(2,1)} %bitcast.15), calls=%async_computation.2 | async-start | bytes 2097152 | tf_op jit(solution)/shard_map/all_to_all | solution.py:671
  117.9 16.1 %collective-permute-start.5 = (bf16[224,256]{1,0:T(8,128)(2,1)S(1)}, bf16[224,256]{1,0:T(8,128)(2,1)S(1)}, u32[]{:S(2)}, u32[]{:S(2)}) collective-permute-start(bf16[224,256]{1,0:T(8,128)(2,1)S(1)} %copy-done.13), channel_id=1, source_target_pairs={{0,16},{16,32},{32,48},{48,64},{64,80},{80,96},{96,112},{1,17},{17... | collective-permute-start | bytes 344072 | tf_op jit(solution)/shard_map/ppermute | solution.py:82
  121.3 13.1 %collective-permute-start.6 = (bf16[224,256]{1,0:T(8,128)(2,1)S(1)}, bf16[224,256]{1,0:T(8,128)(2,1)S(1)}, u32[]{:S(2)}, u32[]{:S(2)}) collective-permute-start(bf16[224,256]{1,0:T(8,128)(2,1)S(1)} %copy-done.12), channel_id=1, source_target_pairs={{16,0},{32,16},{48,32},{64,48},{80,64},{96,80},{112,96},{17,1},{33... | collective-permute-start | bytes 344072 | tf_op jit(solution)/shard_map/ppermute | solution.py:83
  134.0 3.2 %copy-start.9 = (bf16[96,256]{1,0:T(8,128)(2,1)S(1)}, bf16[96,256]{1,0:T(8,128)(2,1)}, u32[]{:S(2)}) copy-start(bf16[96,256]{1,0:T(8,128)(2,1)} %get-tuple-element.102) | copy-start | bytes 147460
  134.0 6.0 %copy-start.8 = (bf16[96,256]{1,0:T(8,128)(2,1)S(1)}, bf16[96,256]{1,0:T(8,128)(2,1)}, u32[]{:S(2)}) copy-start(bf16[96,256]{1,0:T(8,128)(2,1)} %get-tuple-element.103) | copy-start | bytes 147460
  134.0 7.4 %copy-start.10 = (bf16[224,256]{1,0:T(8,128)(2,1)}, bf16[224,256]{1,0:T(8,128)(2,1)S(1)}, u32[]{:S(2)}) copy-start(bf16[224,256]{1,0:T(8,128)(2,1)S(1)} %collective-permute-done.5.above) | copy-start | bytes 344068
  134.4 6.9 %copy-start.11 = (bf16[224,256]{1,0:T(8,128)(2,1)}, bf16[224,256]{1,0:T(8,128)(2,1)S(1)}, u32[]{:S(2)}) copy-start(bf16[224,256]{1,0:T(8,128)(2,1)S(1)} %collective-permute-done.6.below) | copy-start | bytes 344068
  137.2 13.6 %collective-permute-start.7 = (bf16[128,256]{1,0:T(8,128)(2,1)S(1)}, bf16[128,256]{1,0:T(8,128)(2,1)S(1)}, u32[]{:S(2)}, u32[]{:S(2)}) collective-permute-start(bf16[128,256]{1,0:T(8,128)(2,1)S(1)} %pad_maximum_fusion.2), channel_id=1, source_target_pairs={{0,1},{1,2},{2,3},{3,4},{4,5},{5,6},{6,7},{7,8},{8,9},{9,10},{10,1... | collective-permute-start | bytes 196616 | tf_op jit(solution)/shard_map/ppermute | solution.py:93
  140.1 10.8 %collective-permute-start.8 = (bf16[128,256]{1,0:T(8,128)(2,1)S(1)}, bf16[128,256]{1,0:T(8,128)(2,1)S(1)}, u32[]{:S(2)}, u32[]{:S(2)}) collective-permute-start(bf16[128,256]{1,0:T(8,128)(2,1)S(1)} %pad_maximum_fusion.3), channel_id=1, source_target_pairs={{1,0},{2,1},{3,2},{4,3},{5,4},{6,5},{7,6},{8,7},{9,8},{10,9},{11,1... | collective-permute-start | bytes 196616 | tf_op jit(solution)/shard_map/ppermute | solution.py:94
  141.4 26.4 %all-to-all-start.3 = ((bf16[64,64,128]{2,1,0:T(8,128)(2,1)}), bf16[64,64,128]{2,1,0:T(8,128)(2,1)S(1)}, u32[]{:S(2)}, u32[]{:S(2)}) async-start(bf16[64,64,128]{2,1,0:T(8,128)(2,1)} %broadcast_in_dim.10), calls=%async_computation.3 | async-start | bytes 2097152 | tf_op jit(solution)/shard_map/all_to_all | solution.py:671
  150.8 0.6 copy-start.14
  150.9 0.6 copy-start.15
  167.7 22.2 %copy-start = (bf16[64,64,128]{2,1,0:T(8,128)(2,1)}, bf16[64,64,128]{2,1,0:T(8,128)(2,1)S(1)}, u32[]{:S(2)}) copy-start(bf16[64,64,128]{2,1,0:T(8,128)(2,1)S(1)} %all-to-all-done.3) | copy-start | bytes 3145732
  167.7 22.1 %collective-permute-start.9 = (bf16[64,64,128]{2,1,0:T(8,128)(2,1)S(1)}, bf16[64,64,128]{2,1,0:T(8,128)(2,1)S(1)}, u32[]{:S(2)}, u32[]{:S(2)}) collective-permute-start(bf16[64,64,128]{2,1,0:T(8,128)(2,1)S(1)} %all-to-all-done.3), channel_id=1, source_target_pairs={{0,16},{16,0},{1,17},{17,1},{2,18},{18,2},{3,19},{19,3},{4,20},{20... | collective-permute-start | bytes 3145736 | tf_op jit(solution)/shard_map/ppermute | solution.py:716
  185.8 14.2 %all-to-all-start.5 = ((f32[128,1,256]{2,1,0:T(1,128)}), f32[128,1,256]{2,1,0:T(1,128)S(1)}, u32[]{:S(2)}, u32[]{:S(2)}) async-start(f32[128,1,256]{2,1,0:T(1,128)} %broadcast_in_dim.11), calls=%async_computation.5 | async-start | bytes 262144 | tf_op jit(solution)/shard_map/all_to_all | solution.py:675
  189.9 1.0 copy-start.2
  199.9 0.7 copy-start.3

commit v8 on v7

--- a/solution.py
+++ b/solution.py
@@ -213,7 +213,7 @@
     return outs[0], outs[1], outs[2:]
 
 
-def conv_kernel_body(emb, above, below, lh, rh, kern, gain, wide, centred, inverse, normed, w_sc, l_sc, r_sc, c_sc):
+def conv_kernel_body(emb, above, below, lh, rh, kern, gain, centred, inverse, normed, wide, w_sc, l_sc, r_sc, c_sc):
     assemble(wide, emb, (above, below, lh, rh), l_sc, r_sc, c_sc)
     spread_weights(kern, w_sc)
 
@@ -244,12 +244,15 @@
         conv_kernel_body,
         name="conv_forward",
         out_shape=[
-            jax.ShapeDtypeStruct((ROWS + 2 * HALO, WIDE, 8, CH), F32),
             jax.ShapeDtypeStruct((TOK, CH), F32),
             jax.ShapeDtypeStruct((TOK, 128), F32),
             jax.ShapeDtypeStruct((TOK, CH), BF),
         ],
-        scratch_shapes=[pltpu.VMEM((KSIZE * KSIZE, 8, CH), F32)] + EDGE_SCRATCH,
+        scratch_shapes=[
+            pltpu.VMEM((ROWS + 2 * HALO, WIDE, 8, CH), F32),
+            pltpu.VMEM((KSIZE * KSIZE, 8, CH), F32),
+        ]
+        + EDGE_SCRATCH,
         compiler_params=VMEM,
     )(emb, *halo, conv_kernel, gain)
 
@@ -486,7 +489,8 @@
     return outs
 
 
-def kernel_grad_body(wide, d_mixed, out, d_sc):
+def kernel_grad_body(emb, above, below, lh, rh, d_mixed, out, wide, d_sc, l_sc, r_sc, c_sc):
+    assemble(wide, emb, (above, below, lh, rh), l_sc, r_sc, c_sc)
     d_sc[...] = d_mixed[...].astype(F32)
     for half in range(2):
         lanes = pl.ds(half * 128, 128)
@@ -511,15 +515,16 @@
                 out[n : n + 1, lanes] = jnp.sum(acc[j], axis=0, keepdims=True)
 
 
-def kernel_grad(wide, d_mixed):
+def kernel_grad(emb, halo, d_mixed):
     return pl.pallas_call(
         kernel_grad_body,
         name="kernel_grad",
         out_shape=jax.ShapeDtypeStruct((KSIZE * KSIZE, CH), F32),
-        scratch_shapes=[pltpu.VMEM((TOK, CH), F32)],
+        scratch_shapes=[pltpu.VMEM((ROWS + 2 * HALO, WIDE, 8, CH), F32), pltpu.VMEM((TOK, CH), F32)]
+        + EDGE_SCRATCH,
         compiler_params=VMEM,
         cost_estimate=COST,
-    )(wide, d_mixed)
+    )(emb, *halo, d_mixed)
 
 
 def conv_back_body(d_mixed, above, below, lh, rh, kern, z, kern_grad, gain_grad, small, wide, d_sc, w_sc, l_sc, r_sc, c_sc):
@@ -686,7 +691,7 @@
     emb, z, edges = embed(pixels, patch_weight, patch_bias)
     rows = exchange_rows(edges)
     halo = rows + exchange_cols(edges, *rows)
-    wide, centred, inverse, normed = conv_forward(emb, halo, conv_kernel, gain)
+    centred, inverse, normed = conv_forward(emb, halo, conv_kernel, gain)
     k, v, weighted, local = attend(normed, kv_weight, latents, d_attended)
     stats = combine_stats(local)
     lse = stats[0] + jnp.log2(stats[1])
@@ -703,7 +708,7 @@
     d_mixed, message, *d_edges = tie(d_mixed, message, *d_edges)
     message = send(message)
     d_rows = exchange_rows(d_edges)
-    kern = kernel_grad(wide, d_mixed)
+    kern = kernel_grad(emb, halo, d_mixed)
     d_mixed, message, kern, *d_rows = tie(d_mixed, message, kern, *d_rows)
     message = copies(block_sum(message))
     d_mixed, message, *d_rows = tie(d_mixed, message, *d_rows)

time: 203 us -> 202 us (level)
  no operation moved by 1% of the time
where the time goes in v8:
time: 202 us; the launch traced here: 201 us
  Pallas kernels  85.5 us (42%)
  starting transfers between devices  52.9 us (26%)
  blocking collectives  25.1 us (12%)
  waiting for transfers between devices  24.1 us (12%)
  local copies, waits for them, and re-layouts  7.77 us (4%)
  other arithmetic  4.62 us (2%)
    pallas_call x1, Pallas kernels, attend_grad(): pl.pallas_call(attend_grad_kernel, name='attend_grad', grid_spec=pltpu.Pr...  21.2 us
    all_to_all x2, starting transfers between devices, send(): return lax.all_to_all(x, CHIPS, 0, 0, tiled=True)  14.5 us
    all_to_all x1, blocking collectives, send_all(): return lax.all_to_all(x, ALL, 0, 0, tiled=True)  14.1 us
    pallas_call x1, Pallas kernels, conv_back(): pl.pallas_call(conv_back_body, name='conv_back', out_shape=jax.ShapeDtype...  12.8 us
    pallas_call x1, Pallas kernels, conv_forward(): pl.pallas_call(conv_kernel_body, name='conv_forward', out_shape=[jax.Shap...  12.7 us
    pallas_call x1, Pallas kernels, attend(): pl.pallas_call(attend_kernel, name='attend', grid=(HEADS // WIDTH,), in_s...  12.2 us
    all_to_all x1, blocking collectives, gather(): return lax.all_to_all(copies, axes, 0, 0, tiled=True)  11 us
    pallas_call x1, Pallas kernels, kernel_grad(): pl.pallas_call(kernel_grad_body, name='kernel_grad', out_shape=jax.ShapeD...  10.5 us
  transfers between devices with their start and end apart: 14, of which 8 were waited for; matrix products, arithmetic and copies ran while one was open for 1% of the time, Pallas kernels for 17%

profile of v8, /device:TPU:1, one launch (start us, length us, event | category | flops | bytes accessed | tf_op | source)
XLA Modules:
  0.0 201.0 jit_solution(2627897293827301363)
XLA Ops:
  2.0 3.2 %embed.1 = (bf16[2048,256]{1,0:T(8,128)(2,1)}, bf16[256,512]{1,0:T(8,128)(2,1)}, bf16[224,256]{1,0:T(8,128)(2,1)}, bf16[224,256]{1,0:T(8,128)(2,1)}, bf16[96,256]{1,0:T(8,128)(2,1)}, /*index=5*/bf16[96,256]{1,0:T(8,128)(2,1)}) custom-call(bf16[384,256]{1,0:T(8,128)(2,1)} %bitcast.77, bf16[4,16,256]{2,1,0:T(8,128)(2,1)} %pad.4.weights, f32[1,256]{1,0:T(1,128)} %bitcast.82), custom_call_target="tpu_custom_call" | custom-call | tf_op jit(solution)/shard_map/embed/pallas_call | solution.py:202
  5.2 4.9 %collective-permute-start = (bf16[224,256]{1,0:T(8,128)(2,1)}, bf16[224,256]{1,0:T(8,128)(2,1)S(1)}, u32[]{:S(2)}, u32[]{:S(2)}) collective-permute-start(bf16[224,256]{1,0:T(8,128)(2,1)} %get-tuple-element.64), channel_id=1, source_target_pairs={{0,16},{16,32},{32,48},{48,64},{64,80},{80,96},{96,112},{1,17},{17... | collective-permute-start | bytes 344072 | tf_op jit(solution)/shard_map/ppermute | solution.py:82
  10.1 1.9 collective-permute-start.1
  12.2 4.2 %collective-permute-done.1.below = bf16[224,256]{1,0:T(8,128)(2,1)S(1)} collective-permute-done((bf16[224,256]{1,0:T(8,128)(2,1)}, bf16[224,256]{1,0:T(8,128)(2,1)S(1)}, u32[]{:S(2)}, u32[]{:S(2)}) %collective-permute-start.1) | collective-permute-done | bytes 114720 | tf_op jit(solution)/shard_map/ppermute | solution.py:83
  17.2 3.2 %collective-permute-start.2 = (bf16[128,256]{1,0:T(8,128)(2,1)S(1)}, bf16[128,256]{1,0:T(8,128)(2,1)S(1)}, u32[]{:S(2)}, u32[]{:S(2)}) collective-permute-start(bf16[128,256]{1,0:T(8,128)(2,1)S(1)} %pad_maximum_fusion), channel_id=1, source_target_pairs={{0,1},{1,2},{2,3},{3,4},{4,5},{5,6},{6,7},{7,8},{8,9},{9,10},{10,1... | collective-permute-start | bytes 196616 | tf_op jit(solution)/shard_map/ppermute | solution.py:93
  21.3 1.3 collective-permute-start.3
  22.6 3.7 %collective-permute-done.3.rh = bf16[128,256]{1,0:T(8,128)(2,1)S(1)} collective-permute-done((bf16[128,256]{1,0:T(8,128)(2,1)S(1)}, bf16[128,256]{1,0:T(8,128)(2,1)S(1)}, u32[]{:S(2)}, u32[]{:S(2)}) %collective-permute-start.3) | collective-permute-done | bytes 65568 | tf_op jit(solution)/shard_map/ppermute | solution.py:94
  26.9 12.7 %conv_forward.1 = (f32[2048,256]{1,0:T(8,128)}, f32[2048,128]{1,0:T(8,128)}, bf16[2048,256]{1,0:T(8,128)(2,1)}) custom-call(bf16[2048,256]{1,0:T(8,128)(2,1)} %get-tuple-element.63.emb, bf16[224,256]{1,0:T(8,128)(2,1)} %copy-done.4, bf16[224,256]{1,0:T(8,128)(2,1)} %copy-done.5, bf16[128,256]{1,0:T(8,128)(2,1)} %copy-done.6, bf16[128,256]{1,0:T(8,128)(2,1)} %copy-done.7, ...), custom_call_target="tpu_custom_call" | custom-call | tf_op jit(solution)/shard_map/conv_forward/pallas_call | solution.py:243
  39.6 12.2 %attend.1 = (bf16[2048,1024]{1,0:T(8,128)(2,1)}, bf16[2048,1024]{1,0:T(8,128)(2,1)}, f32[8,128,256]{2,1,0:T(8,128)}, f32[3,8,256]{2,1,0:T(8,128)}) custom-call(bf16[2048,256]{1,0:T(8,128)(2,1)} %get-tuple-element.68.normed, bf16[256,2048]{1,0:T(8,128)(2,1)} %wv.3, bf16[256,2048]{1,0:T(8,128)(2,1)} %wv.3, bf16[256,1024]{1,0:T(8,128)(2,1)} %q.3, ...), custom_call_target="tpu_custom_call" | custom-call | tf_op jit(solution)/shard_map/attend/pallas_call | solution.py:316
  52.5 11.0 %all_to_all.30 = f32[8,3,8,256]{3,2,1,0:T(8,128)S(1)} all-to-all(f32[8,3,8,256]{3,2,1,0:T(8,128)S(1)} %broadcast_in_dim.8), channel_id=1, replica_groups=mesh['z'=4,'core'=2,'x'=4,'y'=4] {'z','core'}, dimensions={0} | all-to-all | bytes 393216 | tf_op jit(solution)/shard_map/all_to_all | solution.py:589
  64.4 8.0 %all-to-all-start.1 = ((f32[16,3,8,256]{3,2,1,0:T(8,128)}), f32[16,3,8,256]{3,2,1,0:T(8,128)S(1)}, u32[]{:S(2)}, u32[]{:S(2)}) async-start(f32[16,3,8,256]{3,2,1,0:T(8,128)} %broadcast_in_dim.9), calls=%async_computation.1 | async-start | bytes 786432 | tf_op jit(solution)/shard_map/all_to_all | solution.py:589
  72.4 8.1 %all-to-all-done.1 = f32[16,3,8,256]{3,2,1,0:T(8,128)S(1)} async-done(((f32[16,3,8,256]{3,2,1,0:T(8,128)}), f32[16,3,8,256]{3,2,1,0:T(8,128)S(1)}, u32[]{:S(2)}, u32[]{:S(2)}) %all-to-all-start.1) | async-done | bytes 393248 | tf_op jit(solution)/shard_map/all_to_all | solution.py:589
  80.6 1.3 fusion.14
  81.9 21.2 %attend_grad.1 = (f32[4,4,256,128]{3,2,1,0:T(8,128)}, f32[4,4,256,128]{3,2,1,0:T(8,128)}, f32[2048,256]{1,0:T(8,128)}) custom-call(s32[1]{0:T(128)} %bitcast.core, bf16[2048,256]{1,0:T(8,128)(2,1)} %get-tuple-element.68.normed, bf16[2048,1024]{1,0:T(8,128)(2,1)} %get-tuple-element.69.k_in, bf16[2048,1024]{1,0:T(8,128)(2,1)} %get-tuple-element.70.v_in, ...), custom_call_target="tpu_custom_call" | custom-call | flops 14000000000 | bytes 16000000 | tf_op jit(solution)/shard_map/attend_grad/pallas_call | solution.py:455
  103.2 2.9 %collective-permute-start.4 = (f32[4,4,256,128]{3,2,1,0:T(8,128)}, f32[4,4,256,128]{3,2,1,0:T(8,128)S(1)}, u32[]{:S(2)}, u32[]{:S(2)}) collective-permute-start(f32[4,4,256,128]{3,2,1,0:T(8,128)} %get-tuple-element.77), channel_id=1, source_target_pairs={{0,16},{16,0},{1,17},{17,1},{2,18},{18,2},{3,19},{19,3},{4,20},{20... | collective-permute-start | bytes 6291464 | tf_op jit(solution)/shard_map/ppermute | solution.py:704
  106.1 4.5 %norm_grad.1 = (bf16[2048,256]{1,0:T(8,128)(2,1)}, f32[1,256]{1,0:T(1,128)}, bf16[224,256]{1,0:T(8,128)(2,1)}, bf16[224,256]{1,0:T(8,128)(2,1)}, bf16[96,256]{1,0:T(8,128)(2,1)}, /*index=5*/bf16[96,256]{1,0:T(8,128)(2,1)}) custom-call(f32[2048,256]{1,0:T(8,128)} %get-tuple-element.73.dn_in, f32[2048,256]{1,0:T(8,128)} %get-tuple-element.74.centred, ...), custom_call_target="tpu_custom_call" | custom-call | flops 14000000000 | bytes 16000000 | tf_op jit(solution)/shard_map/norm_grad/pallas_call | solution.py:432
  111.9 5.1 %all-to-all-start.2 = ((bf16[64,64,128]{2,1,0:T(8,128)(2,1)}), bf16[64,64,128]{2,1,0:T(8,128)(2,1)S(1)}, u32[]{:S(2)}, u32[]{:S(2)}) async-start(bf16[64,64,128]{2,1,0:T(8,128)(2,1)} %bitcast.15), calls=%async_computation.2 | async-start | bytes 2097152 | tf_op jit(solution)/shard_map/all_to_all | solution.py:676
  117.0 3.4 %collective-permute-start.5 = (bf16[224,256]{1,0:T(8,128)(2,1)S(1)}, bf16[224,256]{1,0:T(8,128)(2,1)S(1)}, u32[]{:S(2)}, u32[]{:S(2)}) collective-permute-start(bf16[224,256]{1,0:T(8,128)(2,1)S(1)} %copy-done.13), channel_id=1, source_target_pairs={{0,16},{16,32},{32,48},{48,64},{64,80},{80,96},{96,112},{1,17},{17... | collective-permute-start | bytes 344072 | tf_op jit(solution)/shard_map/ppermute | solution.py:82
  120.4 1.9 collective-permute-start.6
  122.3 10.5 %kernel_grad.1.kern_grad = f32[49,256]{1,0:T(8,128)} custom-call(bf16[2048,256]{1,0:T(8,128)(2,1)} %get-tuple-element.63.emb, bf16[224,256]{1,0:T(8,128)(2,1)} %copy-done.4, bf16[224,256]{1,0:T(8,128)(2,1)} %copy-done.5, bf16[128,256]{1,0:T(8,128)(2,1)} %copy-done.6, bf16[128,256]{1,0:T(8,128)(2,1)} %copy-done.7, bf16[2048,256]{1,0:T(8,128)(2,1)} %get-tuple-element.97.d_mixed), custom_call_target="tpu_custom_call" | custom-call | flops 14000000000 | bytes 16000000 | tf_op jit(solution)/shard_map/kernel_grad/pallas_call | solution.py:519
  133.5 1.3 all-to-all-done.2
  136.3 2.8 %collective-permute-start.7 = (bf16[128,256]{1,0:T(8,128)(2,1)S(1)}, bf16[128,256]{1,0:T(8,128)(2,1)S(1)}, u32[]{:S(2)}, u32[]{:S(2)}) collective-permute-start(bf16[128,256]{1,0:T(8,128)(2,1)S(1)} %pad_maximum_fusion.2), channel_id=1, source_target_pairs={{0,1},{1,2},{2,3},{3,4},{4,5},{5,6},{6,7},{7,8},{8,9},{9,10},{10,1... | collective-permute-start | bytes 196616 | tf_op jit(solution)/shard_map/ppermute | solution.py:93
  139.2 1.3 collective-permute-start.8
  140.5 9.4 %all-to-all-start.3 = ((bf16[64,64,128]{2,1,0:T(8,128)(2,1)}), bf16[64,64,128]{2,1,0:T(8,128)(2,1)S(1)}, u32[]{:S(2)}, u32[]{:S(2)}) async-start(bf16[64,64,128]{2,1,0:T(8,128)(2,1)} %broadcast_in_dim.10), calls=%async_computation.3 | async-start | bytes 2097152 | tf_op jit(solution)/shard_map/all_to_all | solution.py:676
  150.6 12.8 %conv_back.1 = f32[128,1,256]{2,1,0:T(1,128)} custom-call(bf16[2048,256]{1,0:T(8,128)(2,1)} %get-tuple-element.97.d_mixed, bf16[224,256]{1,0:T(8,128)(2,1)} %copy-done.10, bf16[224,256]{1,0:T(8,128)(2,1)} %copy-done.11, bf16[128,256]{1,0:T(8,128)(2,1)} %copy-done.14, bf16[128,256]{1,0:T(8,128)(2,1)} %copy-done.15, f32[49,256]{1,0:T(8,128)} %kern.3, ...), custom_call_target="tpu_custom_call" | custom-call | flops 14000000000 | bytes 16000000 | tf_op jit(solution)/shard_map/conv_back/pallas_call | solution.py:565
  163.3 3.6 %all-to-all-done.3 = bf16[64,64,128]{2,1,0:T(8,128)(2,1)S(1)} async-done(((bf16[64,64,128]{2,1,0:T(8,128)(2,1)}), bf16[64,64,128]{2,1,0:T(8,128)(2,1)S(1)}, u32[]{:S(2)}, u32[]{:S(2)}) %all-to-all-start.3) | async-done | bytes 1048608 | tf_op jit(solution)/shard_map/all_to_all | solution.py:676
  166.9 2.7 %collective-permute-start.9 = (bf16[64,64,128]{2,1,0:T(8,128)(2,1)S(1)}, bf16[64,64,128]{2,1,0:T(8,128)(2,1)S(1)}, u32[]{:S(2)}, u32[]{:S(2)}) collective-permute-start(bf16[64,64,128]{2,1,0:T(8,128)(2,1)S(1)} %all-to-all-done.3), channel_id=1, source_target_pairs={{0,16},{16,0},{1,17},{17,1},{2,18},{18,2},{3,19},{19,3},{4,20},{20... | collective-permute-start | bytes 3145736 | tf_op jit(solution)/shard_map/ppermute | solution.py:721
  169.6 14.1 %all_to_all.31 = f32[128,1,256]{2,1,0:T(1,128)S(1)} all-to-all(f32[128,1,256]{2,1,0:T(1,128)} %conv_back.1), channel_id=1, replica_groups=mesh['z'=4,'core'=2,'x'=4,'y'=4] {'z','core','x','y'}, dimensions={0} | all-to-all | bytes 262144 | tf_op jit(solution)/shard_map/all_to_all | solution.py:680
  184.5 4.1 %all-to-all-start.5 = ((f32[128,1,256]{2,1,0:T(1,128)}), f32[128,1,256]{2,1,0:T(1,128)S(1)}, u32[]{:S(2)}, u32[]{:S(2)}) async-start(f32[128,1,256]{2,1,0:T(1,128)} %broadcast_in_dim.11), calls=%async_computation.5 | async-start | bytes 262144 | tf_op jit(solution)/shard_map/all_to_all | solution.py:680
  189.6 6.8 %collect.1 = (f32[256,1024]{1,0:T(8,128)}, f32[256,1024]{1,0:T(8,128)}, f32[256,2048]{1,0:T(8,128)}) custom-call(s32[1]{0:T(128)} %bitcast.core, bf16[4,4,256,128]{3,2,1,0:T(8,128)(2,1)} %bitcast.75, bf16[4,4,256,128]{3,2,1,0:T(8,128)(2,1)} %bitcast.76), custom_call_target="tpu_custom_call" | custom-call | tf_op jit(solution)/shard_map/collect/pallas_call | solution.py:626
  196.5 2.2 %all-to-all-done.5.small = f32[128,1,256]{2,1,0:T(1,128)S(1)} async-done(((f32[128,1,256]{2,1,0:T(1,128)}), f32[128,1,256]{2,1,0:T(1,128)S(1)}, u32[]{:S(2)}, u32[]{:S(2)}) %all-to-all-start.5) | async-done | bytes 131104 | tf_op jit(solution)/shard_map/all_to_all | solution.py:680
  199.4 1.6 split_small.1
  (62 shorter events, 12.0 us)
Async XLA Ops:
  5.2 7.0 %collective-permute-start = (bf16[224,256]{1,0:T(8,128)(2,1)}, bf16[224,256]{1,0:T(8,128)(2,1)S(1)}, u32[]{:S(2)}, u32[]{:S(2)}) collective-permute-start(bf16[224,256]{1,0:T(8,128)(2,1)} %get-tuple-element.64), channel_id=1, source_target_pairs={{0,16},{16,32},{32,48},{48,64},{64,80},{80,96},{96,112},{1,17},{17... | collective-permute-start | bytes 344072 | tf_op jit(solution)/shard_map/ppermute | solution.py:82
  10.1 6.3 %collective-permute-start.1 = (bf16[224,256]{1,0:T(8,128)(2,1)}, bf16[224,256]{1,0:T(8,128)(2,1)S(1)}, u32[]{:S(2)}, u32[]{:S(2)}) collective-permute-start(bf16[224,256]{1,0:T(8,128)(2,1)} %get-tuple-element.65), channel_id=1, source_target_pairs={{16,0},{32,16},{48,32},{64,48},{80,64},{96,80},{112,96},{17,1},{33... | collective-permute-start | bytes 344072 | tf_op jit(solution)/shard_map/ppermute | solution.py:83
  12.2 14.1 %copy-start.4 = (bf16[224,256]{1,0:T(8,128)(2,1)}, bf16[224,256]{1,0:T(8,128)(2,1)S(1)}, u32[]{:S(2)}) copy-start(bf16[224,256]{1,0:T(8,128)(2,1)S(1)} %collective-permute-done.above) | copy-start | bytes 344068
  16.4 9.8 %copy-start.5 = (bf16[224,256]{1,0:T(8,128)(2,1)}, bf16[224,256]{1,0:T(8,128)(2,1)S(1)}, u32[]{:S(2)}) copy-start(bf16[224,256]{1,0:T(8,128)(2,1)S(1)} %collective-permute-done.1.below) | copy-start | bytes 344068
  17.2 5.3 %collective-permute-start.2 = (bf16[128,256]{1,0:T(8,128)(2,1)S(1)}, bf16[128,256]{1,0:T(8,128)(2,1)S(1)}, u32[]{:S(2)}, u32[]{:S(2)}) collective-permute-start(bf16[128,256]{1,0:T(8,128)(2,1)S(1)} %pad_maximum_fusion), channel_id=1, source_target_pairs={{0,1},{1,2},{2,3},{3,4},{4,5},{5,6},{6,7},{7,8},{8,9},{9,10},{10,1... | collective-permute-start | bytes 196616 | tf_op jit(solution)/shard_map/ppermute | solution.py:93
  21.3 5.0 %collective-permute-start.3 = (bf16[128,256]{1,0:T(8,128)(2,1)S(1)}, bf16[128,256]{1,0:T(8,128)(2,1)S(1)}, u32[]{:S(2)}, u32[]{:S(2)}) collective-permute-start(bf16[128,256]{1,0:T(8,128)(2,1)S(1)} %pad_maximum_fusion.1), channel_id=1, source_target_pairs={{1,0},{2,1},{3,2},{4,3},{5,4},{6,5},{7,6},{8,7},{9,8},{10,9},{11,1... | collective-permute-start | bytes 196616 | tf_op jit(solution)/shard_map/ppermute | solution.py:94
  22.6 3.7 %copy-start.6 = (bf16[128,256]{1,0:T(8,128)(2,1)}, bf16[128,256]{1,0:T(8,128)(2,1)S(1)}, u32[]{:S(2)}) copy-start(bf16[128,256]{1,0:T(8,128)(2,1)S(1)} %collective-permute-done.2.lh) | copy-start | bytes 196612
  26.2 0.6 copy-start.7
  64.4 16.1 %all-to-all-start.1 = ((f32[16,3,8,256]{3,2,1,0:T(8,128)}), f32[16,3,8,256]{3,2,1,0:T(8,128)S(1)}, u32[]{:S(2)}, u32[]{:S(2)}) async-start(f32[16,3,8,256]{3,2,1,0:T(8,128)} %broadcast_in_dim.9), calls=%async_computation.1 | async-start | bytes 786432 | tf_op jit(solution)/shard_map/all_to_all | solution.py:589
  103.2 7.5 %collective-permute-start.4 = (f32[4,4,256,128]{3,2,1,0:T(8,128)}, f32[4,4,256,128]{3,2,1,0:T(8,128)S(1)}, u32[]{:S(2)}, u32[]{:S(2)}) collective-permute-start(f32[4,4,256,128]{3,2,1,0:T(8,128)} %get-tuple-element.77), channel_id=1, source_target_pairs={{0,16},{16,0},{1,17},{17,1},{2,18},{18,2},{3,19},{19,3},{4,20},{20... | collective-permute-start | bytes 6291464 | tf_op jit(solution)/shard_map/ppermute | solution.py:704
  106.1 4.6 %copy-start.1 = (f32[4,4,256,128]{3,2,1,0:T(8,128)S(1)}, f32[4,4,256,128]{3,2,1,0:T(8,128)}, u32[]{:S(2)}) copy-start(f32[4,4,256,128]{3,2,1,0:T(8,128)} %get-tuple-element.83) | copy-start | bytes 6291460
  111.9 5.1 %copy-start.13 = (bf16[224,256]{1,0:T(8,128)(2,1)S(1)}, bf16[224,256]{1,0:T(8,128)(2,1)}, u32[]{:S(2)}) copy-start(bf16[224,256]{1,0:T(8,128)(2,1)} %get-tuple-element.91) | copy-start | bytes 344068
  111.9 8.5 %copy-start.12 = (bf16[224,256]{1,0:T(8,128)(2,1)S(1)}, bf16[224,256]{1,0:T(8,128)(2,1)}, u32[]{:S(2)}) copy-start(bf16[224,256]{1,0:T(8,128)(2,1)} %get-tuple-element.92) | copy-start | bytes 344068
  111.9 23.0 %all-to-all-start.2 = ((bf16[64,64,128]{2,1,0:T(8,128)(2,1)}), bf16[64,64,128]{2,1,0:T(8,128)(2,1)S(1)}, u32[]{:S(2)}, u32[]{:S(2)}) async-start(bf16[64,64,128]{2,1,0:T(8,128)(2,1)} %bitcast.15), calls=%async_computation.2 | async-start | bytes 2097152 | tf_op jit(solution)/shard_map/all_to_all | solution.py:676
  117.0 15.8 %collective-permute-start.5 = (bf16[224,256]{1,0:T(8,128)(2,1)S(1)}, bf16[224,256]{1,0:T(8,128)(2,1)S(1)}, u32[]{:S(2)}, u32[]{:S(2)}) collective-permute-start(bf16[224,256]{1,0:T(8,128)(2,1)S(1)} %copy-done.13), channel_id=1, source_target_pairs={{0,16},{16,32},{32,48},{48,64},{64,80},{80,96},{96,112},{1,17},{17... | collective-permute-start | bytes 344072 | tf_op jit(solution)/shard_map/ppermute | solution.py:82
  120.4 13.1 %collective-permute-start.6 = (bf16[224,256]{1,0:T(8,128)(2,1)S(1)}, bf16[224,256]{1,0:T(8,128)(2,1)S(1)}, u32[]{:S(2)}, u32[]{:S(2)}) collective-permute-start(bf16[224,256]{1,0:T(8,128)(2,1)S(1)} %copy-done.12), channel_id=1, source_target_pairs={{16,0},{32,16},{48,32},{64,48},{80,64},{96,80},{112,96},{17,1},{33... | collective-permute-start | bytes 344072 | tf_op jit(solution)/shard_map/ppermute | solution.py:83
  132.8 3.5 %copy-start.9 = (bf16[96,256]{1,0:T(8,128)(2,1)S(1)}, bf16[96,256]{1,0:T(8,128)(2,1)}, u32[]{:S(2)}) copy-start(bf16[96,256]{1,0:T(8,128)(2,1)} %get-tuple-element.100) | copy-start | bytes 147460
  132.8 6.3 %copy-start.8 = (bf16[96,256]{1,0:T(8,128)(2,1)S(1)}, bf16[96,256]{1,0:T(8,128)(2,1)}, u32[]{:S(2)}) copy-start(bf16[96,256]{1,0:T(8,128)(2,1)} %get-tuple-element.101) | copy-start | bytes 147460
  132.8 7.7 %copy-start.10 = (bf16[224,256]{1,0:T(8,128)(2,1)}, bf16[224,256]{1,0:T(8,128)(2,1)S(1)}, u32[]{:S(2)}) copy-start(bf16[224,256]{1,0:T(8,128)(2,1)S(1)} %collective-permute-done.5.above) | copy-start | bytes 344068
  133.5 6.9 %copy-start.11 = (bf16[224,256]{1,0:T(8,128)(2,1)}, bf16[224,256]{1,0:T(8,128)(2,1)S(1)}, u32[]{:S(2)}) copy-start(bf16[224,256]{1,0:T(8,128)(2,1)S(1)} %collective-permute-done.6.below) | copy-start | bytes 344068
  136.3 13.6 %collective-permute-start.7 = (bf16[128,256]{1,0:T(8,128)(2,1)S(1)}, bf16[128,256]{1,0:T(8,128)(2,1)S(1)}, u32[]{:S(2)}, u32[]{:S(2)}) collective-permute-start(bf16[128,256]{1,0:T(8,128)(2,1)S(1)} %pad_maximum_fusion.2), channel_id=1, source_target_pairs={{0,1},{1,2},{2,3},{3,4},{4,5},{5,6},{6,7},{7,8},{8,9},{9,10},{10,1... | collective-permute-start | bytes 196616 | tf_op jit(solution)/shard_map/ppermute | solution.py:93
  139.2 10.8 %collective-permute-start.8 = (bf16[128,256]{1,0:T(8,128)(2,1)S(1)}, bf16[128,256]{1,0:T(8,128)(2,1)S(1)}, u32[]{:S(2)}, u32[]{:S(2)}) collective-permute-start(bf16[128,256]{1,0:T(8,128)(2,1)S(1)} %pad_maximum_fusion.3), channel_id=1, source_target_pairs={{1,0},{2,1},{3,2},{4,3},{5,4},{6,5},{7,6},{8,7},{9,8},{10,9},{11,1... | collective-permute-start | bytes 196616 | tf_op jit(solution)/shard_map/ppermute | solution.py:94
  140.5 26.5 %all-to-all-start.3 = ((bf16[64,64,128]{2,1,0:T(8,128)(2,1)}), bf16[64,64,128]{2,1,0:T(8,128)(2,1)S(1)}, u32[]{:S(2)}, u32[]{:S(2)}) async-start(bf16[64,64,128]{2,1,0:T(8,128)(2,1)} %broadcast_in_dim.10), calls=%async_computation.3 | async-start | bytes 2097152 | tf_op jit(solution)/shard_map/all_to_all | solution.py:676
  149.9 0.6 copy-start.14
  150.0 0.6 copy-start.15
  166.9 21.8 %copy-start = (bf16[64,64,128]{2,1,0:T(8,128)(2,1)}, bf16[64,64,128]{2,1,0:T(8,128)(2,1)S(1)}, u32[]{:S(2)}) copy-start(bf16[64,64,128]{2,1,0:T(8,128)(2,1)S(1)} %all-to-all-done.3) | copy-start | bytes 3145732
  166.9 21.7 %collective-permute-start.9 = (bf16[64,64,128]{2,1,0:T(8,128)(2,1)S(1)}, bf16[64,64,128]{2,1,0:T(8,128)(2,1)S(1)}, u32[]{:S(2)}, u32[]{:S(2)}) collective-permute-start(bf16[64,64,128]{2,1,0:T(8,128)(2,1)S(1)} %all-to-all-done.3), channel_id=1, source_target_pairs={{0,16},{16,0},{1,17},{17,1},{2,18},{18,2},{3,19},{19,3},{4,20},{20... | collective-permute-start | bytes 3145736 | tf_op jit(solution)/shard_map/ppermute | solution.py:721
  184.5 14.2 %all-to-all-start.5 = ((f32[128,1,256]{2,1,0:T(1,128)}), f32[128,1,256]{2,1,0:T(1,128)S(1)}, u32[]{:S(2)}, u32[]{:S(2)}) async-start(f32[128,1,256]{2,1,0:T(1,128)} %broadcast_in_dim.11), calls=%async_computation.5 | async-start | bytes 262144 | tf_op jit(solution)/shard_map/all_to_all | solution.py:680
  188.7 1.0 copy-start.2
  198.7 0.7 copy-start.3

commit v9 on v8

--- a/solution.py
+++ b/solution.py
@@ -21,7 +21,7 @@
 CH = 256
 TOK = ROWS * COLS
 WIDE = 14
-BLOCK = 1024
+BLOCK = 2048
 WIRE = BF
 ROW_AXES = ("z", "core")
 COL_AXES = ("x", "y")

time: 202 us -> 202 us (level)
  no operation moved by 1% of the time
where the time goes in v9:
time: 202 us; the launch traced here: 201 us
  Pallas kernels  85.6 us (42%)
  starting transfers between devices  52.9 us (26%)
  blocking collectives  25.1 us (12%)
  waiting for transfers between devices  24.1 us (12%)
  local copies, waits for them, and re-layouts  7.77 us (4%)
  other arithmetic  4.62 us (2%)
    pallas_call x1, Pallas kernels, attend_grad(): pl.pallas_call(attend_grad_kernel, name='attend_grad', grid_spec=pltpu.Pr...  21.2 us
    all_to_all x2, starting transfers between devices, send(): return lax.all_to_all(x, CHIPS, 0, 0, tiled=True)  14.5 us
    all_to_all x1, blocking collectives, send_all(): return lax.all_to_all(x, ALL, 0, 0, tiled=True)  14.1 us
    pallas_call x1, Pallas kernels, conv_back(): pl.pallas_call(conv_back_body, name='conv_back', out_shape=jax.ShapeDtype...  12.8 us
    pallas_call x1, Pallas kernels, conv_forward(): pl.pallas_call(conv_kernel_body, name='conv_forward', out_shape=[jax.Shap...  12.6 us
    pallas_call x1, Pallas kernels, attend(): pl.pallas_call(attend_kernel, name='attend', grid=(HEADS // WIDTH,), in_s...  12.2 us
    all_to_all x1, blocking collectives, gather(): return lax.all_to_all(copies, axes, 0, 0, tiled=True)  11 us
    pallas_call x1, Pallas kernels, kernel_grad(): pl.pallas_call(kernel_grad_body, name='kernel_grad', out_shape=jax.ShapeD...  10.5 us
  transfers between devices with their start and end apart: 14, of which 8 were waited for; matrix products, arithmetic and copies ran while one was open for 1% of the time, Pallas kernels for 17%

profile of v9, /device:TPU:1, one launch (start us, length us, event | category | flops | bytes accessed | tf_op | source)
XLA Modules:
  0.0 201.1 jit_solution(3401597048085055290)
XLA Ops:
  2.0 3.2 %embed.1 = (bf16[2048,256]{1,0:T(8,128)(2,1)}, bf16[256,512]{1,0:T(8,128)(2,1)}, bf16[224,256]{1,0:T(8,128)(2,1)}, bf16[224,256]{1,0:T(8,128)(2,1)}, bf16[96,256]{1,0:T(8,128)(2,1)}, /*index=5*/bf16[96,256]{1,0:T(8,128)(2,1)}) custom-call(bf16[384,256]{1,0:T(8,128)(2,1)} %bitcast.77, bf16[4,16,256]{2,1,0:T(8,128)(2,1)} %pad.4.weights, f32[1,256]{1,0:T(1,128)} %bitcast.82), custom_call_target="tpu_custom_call" | custom-call | tf_op jit(solution)/shard_map/embed/pallas_call | solution.py:202
  5.2 4.9 %collective-permute-start = (bf16[224,256]{1,0:T(8,128)(2,1)}, bf16[224,256]{1,0:T(8,128)(2,1)S(1)}, u32[]{:S(2)}, u32[]{:S(2)}) collective-permute-start(bf16[224,256]{1,0:T(8,128)(2,1)} %get-tuple-element.64), channel_id=1, source_target_pairs={{0,16},{16,32},{32,48},{48,64},{64,80},{80,96},{96,112},{1,17},{17... | collective-permute-start | bytes 344072 | tf_op jit(solution)/shard_map/ppermute | solution.py:82
  10.1 1.9 collective-permute-start.1
  12.2 4.2 %collective-permute-done.1.below = bf16[224,256]{1,0:T(8,128)(2,1)S(1)} collective-permute-done((bf16[224,256]{1,0:T(8,128)(2,1)}, bf16[224,256]{1,0:T(8,128)(2,1)S(1)}, u32[]{:S(2)}, u32[]{:S(2)}) %collective-permute-start.1) | collective-permute-done | bytes 114720 | tf_op jit(solution)/shard_map/ppermute | solution.py:83
  17.2 3.2 %collective-permute-start.2 = (bf16[128,256]{1,0:T(8,128)(2,1)S(1)}, bf16[128,256]{1,0:T(8,128)(2,1)S(1)}, u32[]{:S(2)}, u32[]{:S(2)}) collective-permute-start(bf16[128,256]{1,0:T(8,128)(2,1)S(1)} %pad_maximum_fusion), channel_id=1, source_target_pairs={{0,1},{1,2},{2,3},{3,4},{4,5},{5,6},{6,7},{7,8},{8,9},{9,10},{10,1... | collective-permute-start | bytes 196616 | tf_op jit(solution)/shard_map/ppermute | solution.py:93
  21.3 1.3 collective-permute-start.3
  22.6 3.7 %collective-permute-done.3.rh = bf16[128,256]{1,0:T(8,128)(2,1)S(1)} collective-permute-done((bf16[128,256]{1,0:T(8,128)(2,1)S(1)}, bf16[128,256]{1,0:T(8,128)(2,1)S(1)}, u32[]{:S(2)}, u32[]{:S(2)}) %collective-permute-start.3) | collective-permute-done | bytes 65568 | tf_op jit(solution)/shard_map/ppermute | solution.py:94
  26.9 12.6 %conv_forward.1 = (f32[2048,256]{1,0:T(8,128)}, f32[2048,128]{1,0:T(8,128)}, bf16[2048,256]{1,0:T(8,128)(2,1)}) custom-call(bf16[2048,256]{1,0:T(8,128)(2,1)} %get-tuple-element.63.emb, bf16[224,256]{1,0:T(8,128)(2,1)} %copy-done.4, bf16[224,256]{1,0:T(8,128)(2,1)} %copy-done.5, bf16[128,256]{1,0:T(8,128)(2,1)} %copy-done.6, bf16[128,256]{1,0:T(8,128)(2,1)} %copy-done.7, ...), custom_call_target="tpu_custom_call" | custom-call | tf_op jit(solution)/shard_map/conv_forward/pallas_call | solution.py:243
  39.5 12.2 %attend.1 = (bf16[2048,1024]{1,0:T(8,128)(2,1)}, bf16[2048,1024]{1,0:T(8,128)(2,1)}, f32[8,128,256]{2,1,0:T(8,128)}, f32[3,8,256]{2,1,0:T(8,128)}) custom-call(bf16[2048,256]{1,0:T(8,128)(2,1)} %get-tuple-element.68.normed, bf16[256,2048]{1,0:T(8,128)(2,1)} %wv.3, bf16[256,2048]{1,0:T(8,128)(2,1)} %wv.3, bf16[256,1024]{1,0:T(8,128)(2,1)} %q.3, ...), custom_call_target="tpu_custom_call" | custom-call | tf_op jit(solution)/shard_map/attend/pallas_call | solution.py:316
  52.5 11.0 %all_to_all.30 = f32[8,3,8,256]{3,2,1,0:T(8,128)S(1)} all-to-all(f32[8,3,8,256]{3,2,1,0:T(8,128)S(1)} %broadcast_in_dim.8), channel_id=1, replica_groups=mesh['z'=4,'core'=2,'x'=4,'y'=4] {'z','core'}, dimensions={0} | all-to-all | bytes 393216 | tf_op jit(solution)/shard_map/all_to_all | solution.py:589
  64.4 8.0 %all-to-all-start.1 = ((f32[16,3,8,256]{3,2,1,0:T(8,128)}), f32[16,3,8,256]{3,2,1,0:T(8,128)S(1)}, u32[]{:S(2)}, u32[]{:S(2)}) async-start(f32[16,3,8,256]{3,2,1,0:T(8,128)} %broadcast_in_dim.9), calls=%async_computation.1 | async-start | bytes 786432 | tf_op jit(solution)/shard_map/all_to_all | solution.py:589
  72.3 8.1 %all-to-all-done.1 = f32[16,3,8,256]{3,2,1,0:T(8,128)S(1)} async-done(((f32[16,3,8,256]{3,2,1,0:T(8,128)}), f32[16,3,8,256]{3,2,1,0:T(8,128)S(1)}, u32[]{:S(2)}, u32[]{:S(2)}) %all-to-all-start.1) | async-done | bytes 393248 | tf_op jit(solution)/shard_map/all_to_all | solution.py:589
  80.5 1.3 fusion.14
  81.9 21.2 %attend_grad.1 = (f32[4,4,256,128]{3,2,1,0:T(8,128)}, f32[4,4,256,128]{3,2,1,0:T(8,128)}, f32[2048,256]{1,0:T(8,128)}) custom-call(s32[1]{0:T(128)} %bitcast.core, bf16[2048,256]{1,0:T(8,128)(2,1)} %get-tuple-element.68.normed, bf16[2048,1024]{1,0:T(8,128)(2,1)} %get-tuple-element.69.k_in, bf16[2048,1024]{1,0:T(8,128)(2,1)} %get-tuple-element.70.v_in, ...), custom_call_target="tpu_custom_call" | custom-call | flops 14000000000 | bytes 16000000 | tf_op jit(solution)/shard_map/attend_grad/pallas_call | solution.py:455
  103.1 2.9 %collective-permute-start.4 = (f32[4,4,256,128]{3,2,1,0:T(8,128)}, f32[4,4,256,128]{3,2,1,0:T(8,128)S(1)}, u32[]{:S(2)}, u32[]{:S(2)}) collective-permute-start(f32[4,4,256,128]{3,2,1,0:T(8,128)} %get-tuple-element.77), channel_id=1, source_target_pairs={{0,16},{16,0},{1,17},{17,1},{2,18},{18,2},{3,19},{19,3},{4,20},{20... | collective-permute-start | bytes 6291464 | tf_op jit(solution)/shard_map/ppermute | solution.py:704
  106.0 4.7 %norm_grad.1 = (bf16[2048,256]{1,0:T(8,128)(2,1)}, f32[1,256]{1,0:T(1,128)}, bf16[224,256]{1,0:T(8,128)(2,1)}, bf16[224,256]{1,0:T(8,128)(2,1)}, bf16[96,256]{1,0:T(8,128)(2,1)}, /*index=5*/bf16[96,256]{1,0:T(8,128)(2,1)}) custom-call(f32[2048,256]{1,0:T(8,128)} %get-tuple-element.73.dn_in, f32[2048,256]{1,0:T(8,128)} %get-tuple-element.74.centred, ...), custom_call_target="tpu_custom_call" | custom-call | flops 14000000000 | bytes 16000000 | tf_op jit(solution)/shard_map/norm_grad/pallas_call | solution.py:432
  112.0 5.1 %all-to-all-start.2 = ((bf16[64,64,128]{2,1,0:T(8,128)(2,1)}), bf16[64,64,128]{2,1,0:T(8,128)(2,1)S(1)}, u32[]{:S(2)}, u32[]{:S(2)}) async-start(bf16[64,64,128]{2,1,0:T(8,128)(2,1)} %bitcast.15), calls=%async_computation.2 | async-start | bytes 2097152 | tf_op jit(solution)/shard_map/all_to_all | solution.py:676
  117.1 3.4 %collective-permute-start.5 = (bf16[224,256]{1,0:T(8,128)(2,1)S(1)}, bf16[224,256]{1,0:T(8,128)(2,1)S(1)}, u32[]{:S(2)}, u32[]{:S(2)}) collective-permute-start(bf16[224,256]{1,0:T(8,128)(2,1)S(1)} %copy-done.13), channel_id=1, source_target_pairs={{0,16},{16,32},{32,48},{48,64},{64,80},{80,96},{96,112},{1,17},{17... | collective-permute-start | bytes 344072 | tf_op jit(solution)/shard_map/ppermute | solution.py:82
  120.5 1.9 collective-permute-start.6
  122.4 10.5 %kernel_grad.1.kern_grad = f32[49,256]{1,0:T(8,128)} custom-call(bf16[2048,256]{1,0:T(8,128)(2,1)} %get-tuple-element.63.emb, bf16[224,256]{1,0:T(8,128)(2,1)} %copy-done.4, bf16[224,256]{1,0:T(8,128)(2,1)} %copy-done.5, bf16[128,256]{1,0:T(8,128)(2,1)} %copy-done.6, bf16[128,256]{1,0:T(8,128)(2,1)} %copy-done.7, bf16[2048,256]{1,0:T(8,128)(2,1)} %get-tuple-element.97.d_mixed), custom_call_target="tpu_custom_call" | custom-call | flops 14000000000 | bytes 16000000 | tf_op jit(solution)/shard_map/kernel_grad/pallas_call | solution.py:519
  133.7 1.3 all-to-all-done.2
  136.4 2.8 %collective-permute-start.7 = (bf16[128,256]{1,0:T(8,128)(2,1)S(1)}, bf16[128,256]{1,0:T(8,128)(2,1)S(1)}, u32[]{:S(2)}, u32[]{:S(2)}) collective-permute-start(bf16[128,256]{1,0:T(8,128)(2,1)S(1)} %pad_maximum_fusion.2), channel_id=1, source_target_pairs={{0,1},{1,2},{2,3},{3,4},{4,5},{5,6},{6,7},{7,8},{8,9},{9,10},{10,1... | collective-permute-start | bytes 196616 | tf_op jit(solution)/shard_map/ppermute | solution.py:93
  139.3 1.3 collective-permute-start.8
  140.6 9.4 %all-to-all-start.3 = ((bf16[64,64,128]{2,1,0:T(8,128)(2,1)}), bf16[64,64,128]{2,1,0:T(8,128)(2,1)S(1)}, u32[]{:S(2)}, u32[]{:S(2)}) async-start(bf16[64,64,128]{2,1,0:T(8,128)(2,1)} %broadcast_in_dim.10), calls=%async_computation.3 | async-start | bytes 2097152 | tf_op jit(solution)/shard_map/all_to_all | solution.py:676
  150.7 12.8 %conv_back.1 = f32[128,1,256]{2,1,0:T(1,128)} custom-call(bf16[2048,256]{1,0:T(8,128)(2,1)} %get-tuple-element.97.d_mixed, bf16[224,256]{1,0:T(8,128)(2,1)} %copy-done.10, bf16[224,256]{1,0:T(8,128)(2,1)} %copy-done.11, bf16[128,256]{1,0:T(8,128)(2,1)} %copy-done.14, bf16[128,256]{1,0:T(8,128)(2,1)} %copy-done.15, f32[49,256]{1,0:T(8,128)} %kern.3, ...), custom_call_target="tpu_custom_call" | custom-call | flops 14000000000 | bytes 16000000 | tf_op jit(solution)/shard_map/conv_back/pallas_call | solution.py:565
  163.5 3.6 %all-to-all-done.3 = bf16[64,64,128]{2,1,0:T(8,128)(2,1)S(1)} async-done(((bf16[64,64,128]{2,1,0:T(8,128)(2,1)}), bf16[64,64,128]{2,1,0:T(8,128)(2,1)S(1)}, u32[]{:S(2)}, u32[]{:S(2)}) %all-to-all-start.3) | async-done | bytes 1048608 | tf_op jit(solution)/shard_map/all_to_all | solution.py:676
  167.1 2.7 %collective-permute-start.9 = (bf16[64,64,128]{2,1,0:T(8,128)(2,1)S(1)}, bf16[64,64,128]{2,1,0:T(8,128)(2,1)S(1)}, u32[]{:S(2)}, u32[]{:S(2)}) collective-permute-start(bf16[64,64,128]{2,1,0:T(8,128)(2,1)S(1)} %all-to-all-done.3), channel_id=1, source_target_pairs={{0,16},{16,0},{1,17},{17,1},{2,18},{18,2},{3,19},{19,3},{4,20},{20... | collective-permute-start | bytes 3145736 | tf_op jit(solution)/shard_map/ppermute | solution.py:721
  169.7 14.1 %all_to_all.31 = f32[128,1,256]{2,1,0:T(1,128)S(1)} all-to-all(f32[128,1,256]{2,1,0:T(1,128)} %conv_back.1), channel_id=1, replica_groups=mesh['z'=4,'core'=2,'x'=4,'y'=4] {'z','core','x','y'}, dimensions={0} | all-to-all | bytes 262144 | tf_op jit(solution)/shard_map/all_to_all | solution.py:680
  184.7 4.1 %all-to-all-start.5 = ((f32[128,1,256]{2,1,0:T(1,128)}), f32[128,1,256]{2,1,0:T(1,128)S(1)}, u32[]{:S(2)}, u32[]{:S(2)}) async-start(f32[128,1,256]{2,1,0:T(1,128)} %broadcast_in_dim.11), calls=%async_computation.5 | async-start | bytes 262144 | tf_op jit(solution)/shard_map/all_to_all | solution.py:680
  189.8 6.8 %collect.1 = (f32[256,1024]{1,0:T(8,128)}, f32[256,1024]{1,0:T(8,128)}, f32[256,2048]{1,0:T(8,128)}) custom-call(s32[1]{0:T(128)} %bitcast.core, bf16[4,4,256,128]{3,2,1,0:T(8,128)(2,1)} %bitcast.75, bf16[4,4,256,128]{3,2,1,0:T(8,128)(2,1)} %bitcast.76), custom_call_target="tpu_custom_call" | custom-call | tf_op jit(solution)/shard_map/collect/pallas_call | solution.py:626
  196.6 2.2 %all-to-all-done.5.small = f32[128,1,256]{2,1,0:T(1,128)S(1)} async-done(((f32[128,1,256]{2,1,0:T(1,128)}), f32[128,1,256]{2,1,0:T(1,128)S(1)}, u32[]{:S(2)}, u32[]{:S(2)}) %all-to-all-start.5) | async-done | bytes 131104 | tf_op jit(solution)/shard_map/all_to_all | solution.py:680
  199.5 1.6 split_small.1
  (62 shorter events, 12.0 us)
Async XLA Ops:
  5.2 7.0 %collective-permute-start = (bf16[224,256]{1,0:T(8,128)(2,1)}, bf16[224,256]{1,0:T(8,128)(2,1)S(1)}, u32[]{:S(2)}, u32[]{:S(2)}) collective-permute-start(bf16[224,256]{1,0:T(8,128)(2,1)} %get-tuple-element.64), channel_id=1, source_target_pairs={{0,16},{16,32},{32,48},{48,64},{64,80},{80,96},{96,112},{1,17},{17... | collective-permute-start | bytes 344072 | tf_op jit(solution)/shard_map/ppermute | solution.py:82
  10.1 6.3 %collective-permute-start.1 = (bf16[224,256]{1,0:T(8,128)(2,1)}, bf16[224,256]{1,0:T(8,128)(2,1)S(1)}, u32[]{:S(2)}, u32[]{:S(2)}) collective-permute-start(bf16[224,256]{1,0:T(8,128)(2,1)} %get-tuple-element.65), channel_id=1, source_target_pairs={{16,0},{32,16},{48,32},{64,48},{80,64},{96,80},{112,96},{17,1},{33... | collective-permute-start | bytes 344072 | tf_op jit(solution)/shard_map/ppermute | solution.py:83
  12.2 14.1 %copy-start.4 = (bf16[224,256]{1,0:T(8,128)(2,1)}, bf16[224,256]{1,0:T(8,128)(2,1)S(1)}, u32[]{:S(2)}) copy-start(bf16[224,256]{1,0:T(8,128)(2,1)S(1)} %collective-permute-done.above) | copy-start | bytes 344068
  16.4 9.8 %copy-start.5 = (bf16[224,256]{1,0:T(8,128)(2,1)}, bf16[224,256]{1,0:T(8,128)(2,1)S(1)}, u32[]{:S(2)}) copy-start(bf16[224,256]{1,0:T(8,128)(2,1)S(1)} %collective-permute-done.1.below) | copy-start | bytes 344068
  17.2 5.3 %collective-permute-start.2 = (bf16[128,256]{1,0:T(8,128)(2,1)S(1)}, bf16[128,256]{1,0:T(8,128)(2,1)S(1)}, u32[]{:S(2)}, u32[]{:S(2)}) collective-permute-start(bf16[128,256]{1,0:T(8,128)(2,1)S(1)} %pad_maximum_fusion), channel_id=1, source_target_pairs={{0,1},{1,2},{2,3},{3,4},{4,5},{5,6},{6,7},{7,8},{8,9},{9,10},{10,1... | collective-permute-start | bytes 196616 | tf_op jit(solution)/shard_map/ppermute | solution.py:93
  21.3 5.0 %collective-permute-start.3 = (bf16[128,256]{1,0:T(8,128)(2,1)S(1)}, bf16[128,256]{1,0:T(8,128)(2,1)S(1)}, u32[]{:S(2)}, u32[]{:S(2)}) collective-permute-start(bf16[128,256]{1,0:T(8,128)(2,1)S(1)} %pad_maximum_fusion.1), channel_id=1, source_target_pairs={{1,0},{2,1},{3,2},{4,3},{5,4},{6,5},{7,6},{8,7},{9,8},{10,9},{11,1... | collective-permute-start | bytes 196616 | tf_op jit(solution)/shard_map/ppermute | solution.py:94
  22.6 3.7 %copy-start.6 = (bf16[128,256]{1,0:T(8,128)(2,1)}, bf16[128,256]{1,0:T(8,128)(2,1)S(1)}, u32[]{:S(2)}) copy-start(bf16[128,256]{1,0:T(8,128)(2,1)S(1)} %collective-permute-done.2.lh) | copy-start | bytes 196612
  26.2 0.6 copy-start.7
  64.4 16.1 %all-to-all-start.1 = ((f32[16,3,8,256]{3,2,1,0:T(8,128)}), f32[16,3,8,256]{3,2,1,0:T(8,128)S(1)}, u32[]{:S(2)}, u32[]{:S(2)}) async-start(f32[16,3,8,256]{3,2,1,0:T(8,128)} %broadcast_in_dim.9), calls=%async_computation.1 | async-start | bytes 786432 | tf_op jit(solution)/shard_map/all_to_all | solution.py:589
  103.1 7.7 %collective-permute-start.4 = (f32[4,4,256,128]{3,2,1,0:T(8,128)}, f32[4,4,256,128]{3,2,1,0:T(8,128)S(1)}, u32[]{:S(2)}, u32[]{:S(2)}) collective-permute-start(f32[4,4,256,128]{3,2,1,0:T(8,128)} %get-tuple-element.77), channel_id=1, source_target_pairs={{0,16},{16,0},{1,17},{17,1},{2,18},{18,2},{3,19},{19,3},{4,20},{20... | collective-permute-start | bytes 6291464 | tf_op jit(solution)/shard_map/ppermute | solution.py:704
  106.0 4.8 %copy-start.1 = (f32[4,4,256,128]{3,2,1,0:T(8,128)S(1)}, f32[4,4,256,128]{3,2,1,0:T(8,128)}, u32[]{:S(2)}) copy-start(f32[4,4,256,128]{3,2,1,0:T(8,128)} %get-tuple-element.83) | copy-start | bytes 6291460
  112.0 5.1 %copy-start.13 = (bf16[224,256]{1,0:T(8,128)(2,1)S(1)}, bf16[224,256]{1,0:T(8,128)(2,1)}, u32[]{:S(2)}) copy-start(bf16[224,256]{1,0:T(8,128)(2,1)} %get-tuple-element.91) | copy-start | bytes 344068
  112.0 8.5 %copy-start.12 = (bf16[224,256]{1,0:T(8,128)(2,1)S(1)}, bf16[224,256]{1,0:T(8,128)(2,1)}, u32[]{:S(2)}) copy-start(bf16[224,256]{1,0:T(8,128)(2,1)} %get-tuple-element.92) | copy-start | bytes 344068
  112.0 23.0 %all-to-all-start.2 = ((bf16[64,64,128]{2,1,0:T(8,128)(2,1)}), bf16[64,64,128]{2,1,0:T(8,128)(2,1)S(1)}, u32[]{:S(2)}, u32[]{:S(2)}) async-start(bf16[64,64,128]{2,1,0:T(8,128)(2,1)} %bitcast.15), calls=%async_computation.2 | async-start | bytes 2097152 | tf_op jit(solution)/shard_map/all_to_all | solution.py:676
  117.1 15.8 %collective-permute-start.5 = (bf16[224,256]{1,0:T(8,128)(2,1)S(1)}, bf16[224,256]{1,0:T(8,128)(2,1)S(1)}, u32[]{:S(2)}, u32[]{:S(2)}) collective-permute-start(bf16[224,256]{1,0:T(8,128)(2,1)S(1)} %copy-done.13), channel_id=1, source_target_pairs={{0,16},{16,32},{32,48},{48,64},{64,80},{80,96},{96,112},{1,17},{17... | collective-permute-start | bytes 344072 | tf_op jit(solution)/shard_map/ppermute | solution.py:82
  120.5 13.1 %collective-permute-start.6 = (bf16[224,256]{1,0:T(8,128)(2,1)S(1)}, bf16[224,256]{1,0:T(8,128)(2,1)S(1)}, u32[]{:S(2)}, u32[]{:S(2)}) collective-permute-start(bf16[224,256]{1,0:T(8,128)(2,1)S(1)} %copy-done.12), channel_id=1, source_target_pairs={{16,0},{32,16},{48,32},{64,48},{80,64},{96,80},{112,96},{17,1},{33... | collective-permute-start | bytes 344072 | tf_op jit(solution)/shard_map/ppermute | solution.py:83
  132.9 3.5 %copy-start.9 = (bf16[96,256]{1,0:T(8,128)(2,1)S(1)}, bf16[96,256]{1,0:T(8,128)(2,1)}, u32[]{:S(2)}) copy-start(bf16[96,256]{1,0:T(8,128)(2,1)} %get-tuple-element.100) | copy-start | bytes 147460
  132.9 6.3 %copy-start.8 = (bf16[96,256]{1,0:T(8,128)(2,1)S(1)}, bf16[96,256]{1,0:T(8,128)(2,1)}, u32[]{:S(2)}) copy-start(bf16[96,256]{1,0:T(8,128)(2,1)} %get-tuple-element.101) | copy-start | bytes 147460
  132.9 7.7 %copy-start.10 = (bf16[224,256]{1,0:T(8,128)(2,1)}, bf16[224,256]{1,0:T(8,128)(2,1)S(1)}, u32[]{:S(2)}) copy-start(bf16[224,256]{1,0:T(8,128)(2,1)S(1)} %collective-permute-done.5.above) | copy-start | bytes 344068
  133.7 6.9 %copy-start.11 = (bf16[224,256]{1,0:T(8,128)(2,1)}, bf16[224,256]{1,0:T(8,128)(2,1)S(1)}, u32[]{:S(2)}) copy-start(bf16[224,256]{1,0:T(8,128)(2,1)S(1)} %collective-permute-done.6.below) | copy-start | bytes 344068
  136.4 13.6 %collective-permute-start.7 = (bf16[128,256]{1,0:T(8,128)(2,1)S(1)}, bf16[128,256]{1,0:T(8,128)(2,1)S(1)}, u32[]{:S(2)}, u32[]{:S(2)}) collective-permute-start(bf16[128,256]{1,0:T(8,128)(2,1)S(1)} %pad_maximum_fusion.2), channel_id=1, source_target_pairs={{0,1},{1,2},{2,3},{3,4},{4,5},{5,6},{6,7},{7,8},{8,9},{9,10},{10,1... | collective-permute-start | bytes 196616 | tf_op jit(solution)/shard_map/ppermute | solution.py:93
  139.3 10.8 %collective-permute-start.8 = (bf16[128,256]{1,0:T(8,128)(2,1)S(1)}, bf16[128,256]{1,0:T(8,128)(2,1)S(1)}, u32[]{:S(2)}, u32[]{:S(2)}) collective-permute-start(bf16[128,256]{1,0:T(8,128)(2,1)S(1)} %pad_maximum_fusion.3), channel_id=1, source_target_pairs={{1,0},{2,1},{3,2},{4,3},{5,4},{6,5},{7,6},{8,7},{9,8},{10,9},{11,1... | collective-permute-start | bytes 196616 | tf_op jit(solution)/shard_map/ppermute | solution.py:94
  140.6 26.5 %all-to-all-start.3 = ((bf16[64,64,128]{2,1,0:T(8,128)(2,1)}), bf16[64,64,128]{2,1,0:T(8,128)(2,1)S(1)}, u32[]{:S(2)}, u32[]{:S(2)}) async-start(bf16[64,64,128]{2,1,0:T(8,128)(2,1)} %broadcast_in_dim.10), calls=%async_computation.3 | async-start | bytes 2097152 | tf_op jit(solution)/shard_map/all_to_all | solution.py:676
  150.1 0.6 copy-start.14
  150.1 0.6 copy-start.15
  167.1 21.8 %copy-start = (bf16[64,64,128]{2,1,0:T(8,128)(2,1)}, bf16[64,64,128]{2,1,0:T(8,128)(2,1)S(1)}, u32[]{:S(2)}) copy-start(bf16[64,64,128]{2,1,0:T(8,128)(2,1)S(1)} %all-to-all-done.3) | copy-start | bytes 3145732
  167.1 21.7 %collective-permute-start.9 = (bf16[64,64,128]{2,1,0:T(8,128)(2,1)S(1)}, bf16[64,64,128]{2,1,0:T(8,128)(2,1)S(1)}, u32[]{:S(2)}, u32[]{:S(2)}) collective-permute-start(bf16[64,64,128]{2,1,0:T(8,128)(2,1)S(1)} %all-to-all-done.3), channel_id=1, source_target_pairs={{0,16},{16,0},{1,17},{17,1},{2,18},{18,2},{3,19},{19,3},{4,20},{20... | collective-permute-start | bytes 3145736 | tf_op jit(solution)/shard_map/ppermute | solution.py:721
  184.7 14.2 %all-to-all-start.5 = ((f32[128,1,256]{2,1,0:T(1,128)}), f32[128,1,256]{2,1,0:T(1,128)S(1)}, u32[]{:S(2)}, u32[]{:S(2)}) async-start(f32[128,1,256]{2,1,0:T(1,128)} %broadcast_in_dim.11), calls=%async_computation.5 | async-start | bytes 262144 | tf_op jit(solution)/shard_map/all_to_all | solution.py:680
  188.8 1.0 copy-start.2
  198.9 0.7 copy-start.3
